TPU v7x, 256 devices: a whole 4x4x8 slice. The times are simulated.
256 devices in a mesh: seq: 64 (over z_lo, x, y), round: 4 (over z_hi, core).
Axes of the slice: x: 4, y: 4, z: 8 (z_hi: 2, z_lo: 4; z = z_hi * 4 + z_lo), core: 2. Of those that a mesh axis runs over, the one named last changes fastest.
Arguments:
- tokens_x: bfloat16 [131072, 1024], P('seq'), may hold values from -208 to 208
- w_qk: bfloat16 [1024, 128], replicated, may hold values from -0.25 to 0.25
- w_v: bfloat16 [1024, 128], replicated, may hold values from -0.1875 to 0.1875
- w_out: bfloat16 [128, 1024], replicated, may hold values from -2 to 2
- send_slot: int32 [8, 131072], P('round', 'seq'), may hold values from 0 to 4095, as said below
- recv_row: int32 [8, 131072], P('round', 'seq'), may hold values from 0 to 4095, as said below
- look_back: int32 [8, 512], P('round', 'seq'), may hold values from 0 to 511, as said below
Outputs:
- mixed: bfloat16 [131072, 1024], P(('seq', 'round'))
Inputs may be any that keep to these rules, and one draw needn't show every extreme that they name: `send_slot`: in each round each device of seq gives its 2048 tokens distinct slots; slot // 64 names the receiving device of seq, and a device sends at most 64 tokens to one device, reaching it for some pair in every round; every device of seq receives exactly 2048 tokens a round, in slots 0 to count - 1 of each source. recv_row // 64 is the source device and recv_row % 64 its slot; in each round every received row of a device of seq is taken by exactly one of its sorted positions. look_back[r, c] is c - 1 or c - 2, modulo 512.
All inputs are finite; a program needn't handle non-finite values.
Results may differ from a plain program's by a relative error of at most 0.014.
The roundings to bfloat16 on the way count: a program that leaves them out, or rounds other values in their place, can miss the bound.
Values may be sent and summed in bfloat16 or wider, within the bound.
No kernel may reach another device: no remote copies, remote signals or barrier semaphores. Data moves between devices by JAX's collectives and lax.ppermute only.
A program may use at most 64 MiB of HBM per device.

v0:
```python
import jax
import jax.numpy as jnp
from jax import lax
from jax.sharding import PartitionSpec as P

BLOCK_LEN = 256


masked_score = -1000000000.0


def from_behind(block, axis, distance):
    devices = range(lax.axis_size(axis))
    route = [((i - distance) % len(devices), i) for i in devices]
    return lax.ppermute(block, axis, route)


def joined_2(value, axis, join):
    pieces = jax.tree.map(lambda part: lax.all_gather(part, axis), value)
    head = jax.tree.map(lambda part: part[0], pieces)
    tail = jax.tree.map(lambda part: part[1:], pieces)
    total, _ = lax.scan(lambda total, piece: (join(total, piece), None), head, tail)
    return total


def project_rows(rows_x, w_both):
    return jnp.dot(rows_x, w_both, preferred_element_type=jnp.float32).astype(jnp.bfloat16)


def unit_keys(qk_rows):
    floats = qk_rows.astype(jnp.float32)
    return (floats * lax.rsqrt(jnp.sum(floats * floats, axis=-1, keepdims=True) + 1e-06)).astype(
        jnp.bfloat16
    )


def attend(query_rows_in, every_key_row, every_value_row):
    block_len = query_rows_in.shape[-2]
    logit_scores = jnp.einsum(
        "gbqd,gbkd->gbqk", query_rows_in, every_key_row, preferred_element_type=jnp.float32
    )
    itself = jnp.arange(block_len)[:, None] == jnp.arange(2 * block_len)[None, :]
    logit_scores = jnp.where(itself, masked_score, logit_scores)
    top = jnp.max(logit_scores, axis=-1)
    expon = jnp.exp(logit_scores - top[..., None])
    total = jnp.sum(expon, axis=-1)
    softmax_weights = expon.astype(jnp.bfloat16)
    weighted_value_sum = jnp.einsum(
        "gbqk,gbkd->gbqd", softmax_weights, every_value_row, preferred_element_type=jnp.float32
    )
    return ((weighted_value_sum / total[..., None]).astype(jnp.bfloat16), top + jnp.log(total))


def combine_states(first_state, second_state):
    top = jnp.maximum(first_state[0], second_state[0])
    scale_first = jnp.exp(first_state[0] - top)
    scale_second = jnp.exp(second_state[0] - top)
    total = first_state[1] * scale_first + second_state[1] * scale_second
    weighted_value_sum = (
        first_state[2] * scale_first[..., None] + second_state[2] * scale_second[..., None]
    )
    return (top, total, weighted_value_sum)


def body(tokens_x, w_qk, w_v, w_out, send_slot, recv_row, look_back):
    tok_rows = tokens_x.shape[0]
    head_dim = w_qk.shape[1]
    seq_count = lax.axis_size("seq")
    round_count = lax.axis_size("round")
    rounds_here = send_slot.shape[0]
    capacity = 2 * tok_rows // seq_count
    buffer_rows = seq_count * capacity
    blocks_here = tok_rows // BLOCK_LEN
    quarter = tok_rows // round_count
    w_both = jnp.concatenate([w_qk, w_v], axis=1)
    packed = project_rows(tokens_x, w_both)
    spans = [(first, 1) for first in range(rounds_here)]
    global_block = lax.axis_index("seq") * blocks_here + jnp.arange(blocks_here, dtype=jnp.int32)
    state = None
    for first, members in spans:
        slots = send_slot[first : first + members]
        taken = recv_row[first : first + members]
        looks = look_back[first : first + members]
        outgoing = jax.vmap(
            lambda where_to: jnp.zeros((buffer_rows, 2 * head_dim), jnp.bfloat16)
            .at[where_to]
            .set(packed)
        )(slots)
        arrived = lax.all_to_all(
            outgoing.reshape(members, seq_count, capacity, 2 * head_dim),
            "seq",
            split_axis=1,
            concat_axis=1,
            tiled=True,
        )
        arrived = arrived.reshape(members, buffer_rows, 2 * head_dim)
        ordered = jnp.take_along_axis(arrived, taken[:, :, None], axis=1)
        query_rows_in = ordered[..., :head_dim]
        keyed = jnp.concatenate([unit_keys(query_rows_in), ordered[..., head_dim:]], axis=-1)
        keyed = keyed.reshape(members, blocks_here, BLOCK_LEN, 2 * head_dim)
        prior = from_behind(keyed[:, blocks_here - 2 :], "seq", 1)
        extended = jnp.concatenate([prior, keyed], axis=1)
        distance = (global_block[None, :] - looks) % (seq_count * blocks_here)
        behind = jnp.where(
            (distance == 1)[:, :, None, None],
            extended[:, 1 : blocks_here + 1],
            extended[:, :blocks_here],
        )
        joined = jnp.concatenate([keyed, behind], axis=2)
        result, log_total = attend(
            query_rows_in.reshape(members, blocks_here, BLOCK_LEN, head_dim),
            joined[..., :head_dim],
            joined[..., head_dim:],
        )
        result = result.reshape(members, tok_rows, head_dim)
        log_total = log_total.reshape(members, tok_rows)
        back_out = jax.vmap(
            lambda where_from, rows_out: jnp.zeros((buffer_rows, head_dim), jnp.bfloat16)
            .at[where_from]
            .set(rows_out)
        )(taken, result)
        back_log = jax.vmap(
            lambda where_from, rows_log: jnp.zeros((buffer_rows,), jnp.float32)
            .at[where_from]
            .set(rows_log)
        )(taken, log_total)
        home_out, home_log = (
            lax.all_to_all(
                back_out.reshape(members, seq_count, capacity, head_dim).astype(jnp.float32),
                "seq",
                split_axis=1,
                concat_axis=1,
                tiled=True,
            ).astype(jnp.bfloat16),
            lax.all_to_all(
                back_log.reshape(members, seq_count, capacity),
                "seq",
                split_axis=1,
                concat_axis=1,
                tiled=True,
            ),
        )
        home_out = jnp.take_along_axis(
            home_out.reshape(members, buffer_rows, head_dim), slots[:, :, None], axis=1
        )
        home_log = jnp.take_along_axis(home_log.reshape(members, buffer_rows), slots, axis=1)
        fresh = (home_log[0], jnp.ones_like(home_log[0]), home_out[0].astype(jnp.float32))
        state = fresh if state is None else combine_states(state, fresh)
    merged = joined_2(state, "round", combine_states)
    start = lax.axis_index("round") * quarter
    total = lax.dynamic_slice_in_dim(merged[1], start, quarter, 0)
    weighted_value_sum = lax.dynamic_slice_in_dim(merged[2], start, quarter, 0)
    blended = (weighted_value_sum / total[:, None]).astype(jnp.bfloat16)
    return jnp.dot(blended, w_out, preferred_element_type=jnp.float32).astype(jnp.bfloat16)


def solution(mesh):
    in_specs = (
        P("seq", None),
        P(),
        P(),
        P(),
        P("round", "seq"),
        P("round", "seq"),
        P("round", "seq"),
    )
    out_specs = P(("seq", "round"), None)
    return jax.shard_map(body, mesh=mesh, in_specs=in_specs, out_specs=out_specs, check_vma=False)
```

profile of v0, /device:TPU:35, one launch (start us, length us, event | category | flops | bytes accessed | tf_op | source)
XLA Modules:
  0.0 395.5 jit_solution(2337298448488271071)
XLA Ops:
  14.7 10.9 %scatter_custom_fusion.2 = bf16[4096,256]{1,0:T(8,128)(2,1)} fusion(s32[2048]{0:T(1024)S(1)} %get-tuple-element.108, bf16[2048,256]{1,0:T(8,128)(2,1)S(1)} %copy.12, bf16[]{:T(256)} %constant.59.clone.1), kind=kCustom, calls=%fused_computation.77 | custom fusion | bytes 2097154
  25.5 11.1 %all-to-all-start.2 = ((bf16[1,64,64,256]{3,2,0,1:T(8,128)(2,1)}), bf16[1,64,64,256]{3,2,0,1:T(8,128)(2,1)S(1)}, u32[]{:S(2)}, u32[]{:S(2)}) async-start(bf16[1,64,64,256]{3,2,0,1:T(8,128)(2,1)} %bitcast.142), calls=%async_computation.2 | async-start | bytes 4194304 | tf_op jit(solution)/shard_map/all_to_all | solution.py:89
  37.2 10.9 %scatter_custom_fusion = bf16[4096,256]{1,0:T(8,128)(2,1)} fusion(s32[2048]{0:T(1024)S(1)} %get-tuple-element.110, bf16[2048,256]{1,0:T(8,128)(2,1)S(1)} %copy.12, bf16[]{:T(256)} %constant.59.clone.1), kind=kCustom, calls=%fused_computation.79 | custom fusion | bytes 2097154
  48.1 34.7 %all-to-all-done.2 = bf16[1,64,64,256]{3,2,0,1:T(8,128)(2,1)S(1)} async-done(((bf16[1,64,64,256]{3,2,0,1:T(8,128)(2,1)}), bf16[1,64,64,256]{3,2,0,1:T(8,128)(2,1)S(1)}, u32[]{:S(2)}, u32[]{:S(2)}) %all-to-all-start.2) | async-done | bytes 2097184 | tf_op jit(solution)/shard_map/all_to_all | solution.py:89
  82.8 9.8 %all-to-all-start = ((bf16[1,64,64,256]{3,2,0,1:T(8,128)(2,1)}), bf16[1,64,64,256]{3,2,0,1:T(8,128)(2,1)}, u32[]{:S(2)}, u32[]{:S(2)}) async-start(bf16[1,64,64,256]{3,2,0,1:T(8,128)(2,1)} %bitcast.141), calls=%async_computation | async-start | bytes 4194304 | tf_op jit(solution)/shard_map/all_to_all | solution.py:89
  95.1 8.5 %gather_fusion.2 = bf16[2048,256]{1,0:T(8,128)(2,1)S(1)} fusion(bf16[4096,256]{1,0:T(8,128)(2,1)S(1)} %bitcast.130, s32[2048]{0:T(1024)} %broadcast_clamp_fusion.3), kind=kCustom, calls=%fused_computation.3.clone | custom fusion | bytes 2105344 | tf_op jit(solution)/shard_map/jit(take_along_axis)/gather | solution.py:97
  106.0 32.6 %all-to-all-done = bf16[1,64,64,256]{3,2,0,1:T(8,128)(2,1)} async-done(((bf16[1,64,64,256]{3,2,0,1:T(8,128)(2,1)}), bf16[1,64,64,256]{3,2,0,1:T(8,128)(2,1)}, u32[]{:S(2)}, u32[]{:S(2)}) %all-to-all-start) | async-done | bytes 2097184 | tf_op jit(solution)/shard_map/all_to_all | solution.py:89
  138.6 8.5 %gather_fusion = bf16[2048,256]{1,0:T(8,128)(2,1)S(1)} fusion(bf16[4096,256]{1,0:T(8,128)(2,1)} %bitcast.10, s32[2048]{0:T(1024)S(1)} %copy-done.11), kind=kCustom, calls=%fused_computation.clone | custom fusion | bytes 2105344 | tf_op jit(solution)/shard_map/jit(take_along_axis)/gather | solution.py:97
  165.9 8.8 %scatter_custom_fusion.1 = f32[4096]{0:T(1024)} fusion(s32[2048]{0:T(1024)} %get-tuple-element.111, f32[2048]{0:T(1024)} %bitcast.166, f32[]{:T(128)} %constant.50.clone.1), kind=kCustom, calls=%fused_computation.132 | custom fusion | bytes 16896
  176.0 12.4 %all-to-all-start.1 = ((f32[1,64,64]{2,0,1:T(1,128)}), f32[1,64,64]{2,0,1:T(1,128)}, u32[]{:S(2)}, u32[]{:S(2)}) async-start(f32[1,64,64]{2,0,1:T(1,128)} %reshape.377), calls=%async_computation.1 | async-start | bytes 65536 | tf_op jit(solution)/shard_map/all_to_all | solution.py:135
  189.7 8.8 %scatter_custom_fusion.3 = f32[4096]{0:T(1024)} fusion(s32[2048]{0:T(1024)} %get-tuple-element.109, f32[2048]{0:T(1024)} %bitcast.165, f32[]{:T(128)} %constant.50.clone.1), kind=kCustom, calls=%fused_computation.130 | custom fusion | bytes 16896
  199.9 10.4 %all-to-all-start.3 = ((f32[1,64,64]{2,0,1:T(1,128)}), f32[1,64,64]{2,0,1:T(1,128)}, u32[]{:S(2)}, u32[]{:S(2)}) async-start(f32[1,64,64]{2,0,1:T(1,128)} %reshape.384), calls=%async_computation.3 | async-start | bytes 65536 | tf_op jit(solution)/shard_map/all_to_all | solution.py:135
  214.6 7.2 %scatter_custom_fusion.4 = bf16[4096,128]{1,0:T(8,128)(2,1)} fusion(s32[2048]{0:T(1024)} %get-tuple-element.111, bf16[2048,128]{1,0:T(8,128)(2,1)} %bitcast.168, bf16[]{:T(256)} %constant.59.clone.1), kind=kCustom, calls=%fused_computation.91 | custom fusion | bytes 1049088
  221.8 10.2 %all-to-all-start.4 = ((bf16[1,64,64,128]{3,2,0,1:T(8,128)(2,1)}), bf16[1,64,64,128]{3,2,0,1:T(8,128)(2,1)S(1)}, u32[]{:S(2)}, u32[]{:S(2)}) async-start(bf16[1,64,64,128]{3,2,0,1:T(8,128)(2,1)} %bitcast.61), calls=%async_computation.4 | async-start | bytes 2097152 | tf_op jit(solution)/shard_map/all_to_all | solution.py:128
  236.3 7.1 %scatter_custom_fusion.5 = bf16[4096,128]{1,0:T(8,128)(2,1)} fusion(s32[2048]{0:T(1024)} %get-tuple-element.109, bf16[2048,128]{1,0:T(8,128)(2,1)} %bitcast.167, bf16[]{:T(256)} %constant.59.clone.1), kind=kCustom, calls=%fused_computation.89 | custom fusion | bytes 1049088
  243.5 12.6 %all-to-all-done.4 = bf16[1,64,64,128]{3,2,0,1:T(8,128)(2,1)S(1)} async-done(((bf16[1,64,64,128]{3,2,0,1:T(8,128)(2,1)}), bf16[1,64,64,128]{3,2,0,1:T(8,128)(2,1)S(1)}, u32[]{:S(2)}, u32[]{:S(2)}) %all-to-all-start.4) | async-done | bytes 1048608 | tf_op jit(solution)/shard_map/all_to_all | solution.py:128
  256.1 7.9 %all-to-all-start.5 = ((bf16[1,64,64,128]{3,2,0,1:T(8,128)(2,1)}), bf16[1,64,64,128]{3,2,0,1:T(8,128)(2,1)S(1)}, u32[]{:S(2)}, u32[]{:S(2)}) async-start(bf16[1,64,64,128]{3,2,0,1:T(8,128)(2,1)} %bitcast.63), calls=%async_computation.5 | async-start | bytes 2097152 | tf_op jit(solution)/shard_map/all_to_all | solution.py:128
  268.0 11.8 %gather_fusion.1 = f32[2048]{0:T(1024)S(1)} fusion(f32[4096]{0:T(1024)S(1)} %reshape.584, s32[2048]{0:T(1024)S(1)} %broadcast_clamp_fusion.4), kind=kCustom, calls=%fused_computation.1.clone | custom fusion | bytes 24576 | tf_op jit(solution)/shard_map/jit(take_along_axis)/gather | solution.py:146
  279.8 11.8 %gather_fusion.3 = f32[2048]{0:T(1024)S(1)} fusion(f32[4096]{0:T(1024)S(1)} %reshape.594, s32[2048]{0:T(1024)S(1)} %broadcast_clamp_fusion.2), kind=kCustom, calls=%fused_computation.4.clone | custom fusion | bytes 24576 | tf_op jit(solution)/shard_map/jit(take_along_axis)/gather | solution.py:146
  291.7 6.2 %gather_fusion.4 = bf16[2048,128]{1,0:T(8,128)(2,1)S(1)} fusion(bf16[4096,128]{1,0:T(8,128)(2,1)S(1)} %bitcast.131, s32[2048]{0:T(1024)S(1)} %broadcast_clamp_fusion.1), kind=kCustom, calls=%fused_computation.2.clone | custom fusion | bytes 1056768 | tf_op jit(solution)/shard_map/jit(take_along_axis)/gather | solution.py:143
  306.9 11.9 %all-gather = f32[4,1,2048]{2,1,0:T(1,128)S(1)} all-gather(f32[1,1,2048]{2,1,0:T(1,128)S(1)} %maximum_bitcast_fusion), channel_id=1, replica_groups=mesh['seq'=64,'round'=4] {'round'}, dimensions={0}, use_global_device_ids=true | all-gather | bytes 40960 | tf_op jit(solution)/shard_map/all_gather | solution.py:19
  318.8 9.2 %all-gather.1 = f32[4,1,2048]{2,1,0:T(1,128)S(1)} all-gather(f32[1,1,2048]{2,1,0:T(1,128)S(1)} %get-tuple-element.82), channel_id=1, replica_groups=mesh['seq'=64,'round'=4] {'round'}, dimensions={0}, use_global_device_ids=true | all-gather | bytes 40960 | tf_op jit(solution)/shard_map/all_gather | solution.py:19
  328.1 47.5 %all-gather.4.cloned.1.call-done = f32[4,2048,128]{2,1,0:T(8,128)} async-done(((f32[1,2048,128]{2,1,0:T(8,128)}), f32[4,2048,128]{2,1,0:T(8,128)}) %all-gather.4.cloned.1.call-update) | async-done | bytes 4194320 | tf_op jit(solution)/shard_map/all_gather | solution.py:19
  380.6 6.5 %while.14 = (s32[]{:T(128)}, f32[2048]{0:T(1024)S(1)}, f32[2048]{0:T(1024)S(1)}, f32[2048,128]{1,0:T(8,128)S(1)}, f32[3,2048]{1,0:T(4,128)S(1)}, /*index=5*/f32[...) while((s32[]{:T(128)}, f32[2048]{0:T(1024)S(1)}, f32[2048]{0:T(1024)S(1)}, f32[2048,128]{1,0:T(8,128)S(1)}, ...), condition=%wide.region_13.17_spmd, body=%wide.region_12.16_spmd.sunk | while | flops 798722 | bytes 3260509 | solution.py:22
  (115 shorter events, 70.9 us)
Async XLA Ops:
  6.5 380.6 %copy-start = (bf16[128,1024]{1,0:T(8,128)(2,1)S(1)}, bf16[128,1024]{1,0:T(8,128)(2,1)}, u32[]{:S(2)}) copy-start(bf16[128,1024]{1,0:T(8,128)(2,1)} %param.18) | copy-start | bytes 786436
  25.5 57.3 %all-to-all-start.2 = ((bf16[1,64,64,256]{3,2,0,1:T(8,128)(2,1)}), bf16[1,64,64,256]{3,2,0,1:T(8,128)(2,1)S(1)}, u32[]{:S(2)}, u32[]{:S(2)}) async-start(bf16[1,64,64,256]{3,2,0,1:T(8,128)(2,1)} %bitcast.142), calls=%async_computation.2 | async-start | bytes 4194304 | tf_op jit(solution)/shard_map/all_to_all | solution.py:89
  82.8 9.9 %copy-start.15 = (s32[2,8]{1,0:T(2,128)S(1)}, s32[2,8]{1,0:T(2,128)}, u32[]{:S(2)}) copy-start(s32[2,8]{1,0:T(2,128)} %param.21) | copy-start | bytes 196
  82.8 10.5 %copy-start.8 = (s32[2,2048]{1,0:T(2,128)S(1)}, s32[2,2048]{1,0:T(2,128)}, u32[]{:S(2)}) copy-start(s32[2,2048]{1,0:T(2,128)} %param.20) | copy-start | bytes 49156
  82.8 55.8 %all-to-all-start = ((bf16[1,64,64,256]{3,2,0,1:T(8,128)(2,1)}), bf16[1,64,64,256]{3,2,0,1:T(8,128)(2,1)}, u32[]{:S(2)}, u32[]{:S(2)}) async-start(bf16[1,64,64,256]{3,2,0,1:T(8,128)(2,1)} %bitcast.141), calls=%async_computation | async-start | bytes 4194304 | tf_op jit(solution)/shard_map/all_to_all | solution.py:89
  104.7 33.9 %copy-start.11 = (s32[2048]{0:T(1024)S(1)}, s32[2048]{0:T(1024)}, u32[]{:S(2)}) copy-start(s32[2048]{0:T(1024)} %broadcast_clamp_fusion.5) | copy-start | bytes 24580
  138.6 8.5 %copy-start.12 = (pred[2048]{0:T(1024)(128)(4,1)S(1)}, pred[2048]{0:T(1024)(128)(4,1)}, u32[]{:S(2)}) copy-start(pred[2048]{0:T(1024)(128)(4,1)} %get-tuple-element.85) | copy-start | bytes 6148
  148.5 7.4 %copy-start.14 = (pred[8]{0:T(512)(128)(4,1)S(1)}, pred[8]{0:T(512)(128)(4,1)}, u32[]{:S(2)}) copy-start(pred[8]{0:T(512)(128)(4,1)} %get-tuple-element.105) | copy-start | bytes 28
  148.5 7.4 %collective-permute-start = (bf16[1,2,256,256]{3,2,1,0:T(8,128)(2,1)S(1)}, bf16[1,2,256,256]{3,2,1,0:T(8,128)(2,1)S(1)}, u32[]{:S(2)}, u32[]{:S(2)}) collective-permute-start(bf16[1,2,256,256]{3,2,1,0:T(8,128)(2,1)S(1)} %slice.122), channel_id=1, source_target_pairs={{252,0},{0,4},{4,8},{8,12},{12,16},{16,20},{20,24},{24,28},{28,32}... | collective-permute-start | bytes 786440 | tf_op jit(solution)/shard_map/ppermute | solution.py:15
  150.1 11.1 %collective-permute-start.1 = (bf16[1,2,256,256]{3,2,1,0:T(8,128)(2,1)S(1)}, bf16[1,2,256,256]{3,2,1,0:T(8,128)(2,1)S(1)}, u32[]{:S(2)}, u32[]{:S(2)}) collective-permute-start(bf16[1,2,256,256]{3,2,1,0:T(8,128)(2,1)S(1)} %slice.129), channel_id=1, source_target_pairs={{252,0},{0,4},{4,8},{8,12},{12,16},{16,20},{20,24},{24,28},{28,32}... | collective-permute-start | bytes 786440 | tf_op jit(solution)/shard_map/ppermute | solution.py:15
  156.2 5.0 %copy-start.13 = (pred[8]{0:T(512)(128)(4,1)S(1)}, pred[8]{0:T(512)(128)(4,1)}, u32[]{:S(2)}) copy-start(pred[8]{0:T(512)(128)(4,1)} %get-tuple-element.106) | copy-start | bytes 28
  156.9 5.7 %copy-start.1 = (f32[8,256,512]{2,1,0:T(8,128)}, f32[8,256,512]{2,1,0:T(8,128)S(1)}, u32[]{:S(2)}) copy-start(f32[8,256,512]{2,1,0:T(8,128)S(1)} %fusion.30) | copy-start | bytes 12582916
  156.9 4.5 %copy-start.5 = (bf16[1,2048,128]{2,1,0:T(8,128)(2,1)S(1)}, bf16[1,2048,128]{2,1,0:T(8,128)(2,1)}, u32[]{:S(2)}) copy-start(bf16[1,2048,128]{2,1,0:T(8,128)(2,1)} %get-tuple-element.94) | copy-start | bytes 1572868
  161.4 1.1 copy-start.3
  162.5 2.7 copy-start.2
  162.5 2.7 copy-start.6
  162.5 2.7 copy-start.7
  176.0 23.9 %all-to-all-start.1 = ((f32[1,64,64]{2,0,1:T(1,128)}), f32[1,64,64]{2,0,1:T(1,128)}, u32[]{:S(2)}, u32[]{:S(2)}) async-start(f32[1,64,64]{2,0,1:T(1,128)} %reshape.377), calls=%async_computation.1 | async-start | bytes 65536 | tf_op jit(solution)/shard_map/all_to_all | solution.py:135
  199.9 21.9 %all-to-all-start.3 = ((f32[1,64,64]{2,0,1:T(1,128)}), f32[1,64,64]{2,0,1:T(1,128)}, u32[]{:S(2)}, u32[]{:S(2)}) async-start(f32[1,64,64]{2,0,1:T(1,128)} %reshape.384), calls=%async_computation.3 | async-start | bytes 65536 | tf_op jit(solution)/shard_map/all_to_all | solution.py:135
  214.6 17.4 %copy-start.4 = (bf16[1,8,256,256]{3,2,1,0:T(8,128)(2,1)S(1)}, bf16[1,8,256,256]{3,2,1,0:T(8,128)(2,1)}, u32[]{:S(2)}) copy-start(bf16[1,8,256,256]{3,2,1,0:T(8,128)(2,1)} %copy-done.3) | copy-start | bytes 3145732
  221.8 34.3 %all-to-all-start.4 = ((bf16[1,64,64,128]{3,2,0,1:T(8,128)(2,1)}), bf16[1,64,64,128]{3,2,0,1:T(8,128)(2,1)S(1)}, u32[]{:S(2)}, u32[]{:S(2)}) async-start(bf16[1,64,64,128]{3,2,0,1:T(8,128)(2,1)} %bitcast.61), calls=%async_computation.4 | async-start | bytes 2097152 | tf_op jit(solution)/shard_map/all_to_all | solution.py:128
  236.3 27.8 %copy-start.9 = (s32[2,2048]{1,0:T(2,128)S(1)}, s32[2,2048]{1,0:T(2,128)}, u32[]{:S(2)}) copy-start(s32[2,2048]{1,0:T(2,128)} %param.19) | copy-start | bytes 49156
  256.1 41.8 %all-to-all-start.5 = ((bf16[1,64,64,128]{3,2,0,1:T(8,128)(2,1)}), bf16[1,64,64,128]{3,2,0,1:T(8,128)(2,1)S(1)}, u32[]{:S(2)}, u32[]{:S(2)}) async-start(bf16[1,64,64,128]{3,2,0,1:T(8,128)(2,1)} %bitcast.63), calls=%async_computation.5 | async-start | bytes 2097152 | tf_op jit(solution)/shard_map/all_to_all | solution.py:128
  264.0 111.5 %all-gather.4.cloned.1.call-start = ((), (), s32[]{:S(2)}) async-start(), calls=%async_computation.6 | async-start | bytes 5242880 | tf_op jit(solution)/shard_map/all_gather | solution.py:19
  (1 other events, 0.6 us)
Sparse Core Ops, SparseCore 0:
  307.0 68.5 all-gather.3
where the time goes:
time: 399 us; the launch traced here: 395 us
  waiting for transfers between devices  136 us (34%)
  local copies, waits for them, and re-layouts  118 us (30%)
  starting transfers between devices  64.4 us (16%)
  other arithmetic  26.3 us (7%)
  blocking collectives  21.1 us (5%)
  matrix products  15.6 us (4%)
  between operations  13.9 us (3%)
    all_to_all x2, waiting for transfers between devices, body(): lax.all_to_all(outgoing.reshape(members, seq_count, capacity, 2 * head_di...  67.3 us
    unnamed x42, local copies, waits for them, and re-layouts  54.9 us
    all_gather x1, waiting for transfers between devices, joined_2(): pieces = jax.tree.map(lambda part: lax.all_gather(part, axis), value)  47.5 us
    gather x2, local copies, waits for them, and re-layouts, body(): jnp.take_along_axis(home_log.reshape(members, buffer_rows), slots, axis=1)  23.6 us
    all_to_all x2, starting transfers between devices, body(): lax.all_to_all(back_log.reshape(members, seq_count, capacity), 'seq', spl...  22.7 us
    all_gather x2, blocking collectives, joined_2(): pieces = jax.tree.map(lambda part: lax.all_gather(part, axis), value)  21.1 us
    all_to_all x2, starting transfers between devices, body(): lax.all_to_all(outgoing.reshape(members, seq_count, capacity, 2 * head_di...  20.9 us
    all_to_all x2, starting transfers between devices, body(): lax.all_to_all(back_out.reshape(members, seq_count, capacity, head_dim).a...  18.1 us
  transfers between devices with their start and end apart: 9, of which 6 were waited for; matrix products, arithmetic and copies ran while one was open for 24% of the time, Pallas kernels for 0%

commit v1 on v0

v1 whole, which is shorter than its diff:
```python
import functools

import jax
import jax.numpy as jnp
from jax import lax
from jax.experimental import pallas as pl
from jax.experimental.pallas import tpu as pltpu
from jax.sharding import Mesh
from jax.sharding import PartitionSpec as P

BLOCK = 256
MASKED = -1000000000.0
SEQ = ("zl", "x", "y")
ROUND = ("zh", "c")
BF = jnp.bfloat16
F32 = jnp.float32
VMEM_BYTES = 48 * 1024 * 1024


def params(n=1):
    return pltpu.CompilerParams(
        dimension_semantics=("arbitrary",) * n, vmem_limit_bytes=VMEM_BYTES
    )


def whole(shape):
    return pl.BlockSpec(shape, lambda *_: (0,) * len(shape))


def one_hot(a, b):
    return jnp.where(a == b, 1.0, 0.0).astype(BF)


def column(row):
    return jnp.transpose(jnp.broadcast_to(row, (8, row.shape[1])))[:, :1]


def project_kernel(x_ref, wqk_ref, wv_ref, out_ref, w_ref):
    @pl.when(pl.program_id(0) == 0)
    def _():
        w_ref[:, :128] = wqk_ref[...]
        w_ref[:, 128:] = wv_ref[...]

    out_ref[...] = jnp.dot(x_ref[...], w_ref[...], preferred_element_type=F32).astype(BF)


def project(x, w_qk, w_v):
    rows, model = x.shape
    step = 512
    return pl.pallas_call(
        project_kernel,
        grid=(rows // step,),
        in_specs=[
            pl.BlockSpec((step, model), lambda i: (i, 0)),
            whole(w_qk.shape),
            whole(w_v.shape),
        ],
        out_specs=pl.BlockSpec((step, 256), lambda i: (i, 0)),
        out_shape=jax.ShapeDtypeStruct((rows, 256), BF),
        scratch_shapes=[pltpu.VMEM((model, 256), BF)],
        compiler_params=params(),
        name="project",
    )(x, w_qk, w_v)


def scatter_kernel(idx_ref, rows_ref, out_ref):
    n = out_ref.shape[0] * out_ref.shape[1]
    base = pl.program_id(0) * n
    place = lax.broadcasted_iota(jnp.int32, (n, rows_ref.shape[0]), 0)
    hot = one_hot(idx_ref[...] - base, place)
    got = jnp.dot(hot, rows_ref[...], preferred_element_type=F32).astype(BF)
    out_ref[...] = got.reshape(out_ref.shape)


def scatter_rows(idx, rows, peers, cap):
    per = 8
    return pl.pallas_call(
        scatter_kernel,
        grid=(peers // per,),
        in_specs=[whole(idx.shape), whole(rows.shape)],
        out_specs=pl.BlockSpec((per, cap, 256), lambda i: (i, 0, 0)),
        out_shape=jax.ShapeDtypeStruct((peers, cap, 256), BF),
        compiler_params=params(),
        name="scatter_rows",
    )(idx, rows)


def sort_kernel(idx_ref, rows_ref, q_ref, kv_ref):
    n = rows_ref.shape[0]
    col = column(idx_ref[0])
    place = lax.broadcasted_iota(jnp.int32, (BLOCK, n), 1)
    got = jnp.dot(one_hot(col, place), rows_ref[...], preferred_element_type=F32)
    qk = got[:, :128]
    keys = qk * lax.rsqrt(jnp.sum(qk * qk, axis=-1, keepdims=True) + 1e-06)
    q_ref[...] = qk.astype(BF)
    kv_ref[:, :128] = keys.astype(BF)
    kv_ref[:, 128:] = got[:, 128:].astype(BF)


def sort_rows(idx, rows):
    count = idx.shape[-1]
    blocks = count // BLOCK
    return pl.pallas_call(
        sort_kernel,
        grid=(blocks,),
        in_specs=[pl.BlockSpec((1, 1, BLOCK), lambda i: (i, 0, 0)), whole(rows.shape)],
        out_specs=[
            pl.BlockSpec((BLOCK, 128), lambda i: (i, 0)),
            pl.BlockSpec((BLOCK, 256), lambda i: (i, 0)),
        ],
        out_shape=[
            jax.ShapeDtypeStruct((count, 128), BF),
            jax.ShapeDtypeStruct((count, 256), BF),
        ],
        compiler_params=params(),
        name="sort_rows",
    )(idx.reshape(blocks, 1, BLOCK), rows)


def three_terms(v):
    hi = v.astype(BF).astype(F32)
    mid = (v - hi).astype(BF).astype(F32)
    lo = v - hi - mid
    return hi, mid, lo


def term_lanes(v, rows):
    hi, mid, lo = three_terms(v)
    group = lax.broadcasted_iota(jnp.int32, (rows, 128), 1) // 32
    return jnp.where(
        group == 0, hi, jnp.where(group == 1, mid, jnp.where(group == 2, lo, 1.0))
    ).astype(BF)


def attend_kernel(dist_ref, q_ref, kv_ref, halo_ref, out_ref, ext_ref):
    c = pl.program_id(0)

    @pl.when(c == 0)
    def _():
        ext_ref[: 2 * BLOCK] = halo_ref[...]
        ext_ref[2 * BLOCK :] = kv_ref[...]

    own = ext_ref[pl.ds(pl.multiple_of((c + 2) * BLOCK, BLOCK), BLOCK), :]
    behind = ext_ref[pl.ds(pl.multiple_of((c + 2 - dist_ref[c]) * BLOCK, BLOCK), BLOCK), :]
    q = q_ref[...]
    nt = (((1,), (1,)), ((), ()))
    s1 = lax.dot_general(q, own[:, :128], nt, preferred_element_type=F32)
    s2 = lax.dot_general(q, behind[:, :128], nt, preferred_element_type=F32)
    r = lax.broadcasted_iota(jnp.int32, (BLOCK, BLOCK), 0)
    k = lax.broadcasted_iota(jnp.int32, (BLOCK, BLOCK), 1)
    s1 = jnp.where(r == k, MASKED, s1)
    top = jnp.maximum(
        jnp.max(s1, axis=-1, keepdims=True), jnp.max(s2, axis=-1, keepdims=True)
    )
    e1 = jnp.exp(s1 - top)
    e2 = jnp.exp(s2 - top)
    total = jnp.sum(e1, axis=-1, keepdims=True) + jnp.sum(e2, axis=-1, keepdims=True)
    o = jnp.dot(e1.astype(BF), own[:, 128:], preferred_element_type=F32) + jnp.dot(
        e2.astype(BF), behind[:, 128:], preferred_element_type=F32
    )
    out_ref[:, :128] = (o / total).astype(BF)
    out_ref[:, 128:] = term_lanes(top + jnp.log(total), BLOCK)


def attend(dist, q, kv, halo):
    count = q.shape[0]
    return pl.pallas_call(
        attend_kernel,
        grid_spec=pltpu.PrefetchScalarGridSpec(
            num_scalar_prefetch=1,
            grid=(count // BLOCK,),
            in_specs=[
                pl.BlockSpec((BLOCK, 128), lambda i, d: (i, 0)),
                whole(kv.shape),
                whole(halo.shape),
            ],
            out_specs=pl.BlockSpec((BLOCK, 256), lambda i, d: (i, 0)),
            scratch_shapes=[pltpu.VMEM((count + 2 * BLOCK, 256), BF)],
        ),
        out_shape=jax.ShapeDtypeStruct((count, 256), BF),
        compiler_params=params(),
        name="attend",
    )(dist, q, kv, halo)


def back_kernel(idx_ref, res_ref, out_ref):
    per, ext, _ = out_ref.shape
    cap = ext - 8
    n = per * cap
    base = pl.program_id(0) * n
    place = lax.broadcasted_iota(jnp.int32, (n, res_ref.shape[0]), 0)
    hot = one_hot(idx_ref[...] - base, place)
    got = jnp.dot(hot, res_ref[...], preferred_element_type=F32)
    out_ref[:, :cap, :] = got[:, :128].astype(BF).reshape(per, cap, 128)
    terms = got[:, 128:].reshape(per * cap // 32, 32, 128)
    slot = lax.broadcasted_iota(jnp.int32, terms.shape, 1)
    lane = lax.broadcasted_iota(jnp.int32, terms.shape, 2) % 32
    line = jnp.sum(jnp.where(slot == lane, terms, 0.0), axis=1, keepdims=True)
    line = line.reshape(per, cap // 32, 1, 128)
    row = lax.broadcasted_iota(jnp.int32, (per, 8, 128), 1)
    tail = jnp.zeros((per, 8, 128), F32)
    for part in range(cap // 32):
        tail = jnp.where(row == part, line[:, part], tail)
    out_ref[:, cap:, :] = tail.astype(BF)


def back_rows(idx, res, peers, cap):
    per = 8
    return pl.pallas_call(
        back_kernel,
        grid=(peers // per,),
        in_specs=[whole(idx.shape), whole(res.shape)],
        out_specs=pl.BlockSpec((per, cap + 8, 128), lambda i: (i, 0, 0)),
        out_shape=jax.ShapeDtypeStruct((peers, cap + 8, 128), BF),
        compiler_params=params(),
        name="back_rows",
    )(idx, res)


def home_kernel(idx_ref, *refs):
    (*home_refs, out_ref, x_ref) = refs
    peers, ext, _ = home_refs[0].shape
    cap = ext - 8
    n = peers * cap

    @pl.when(pl.program_id(0) == 0)
    def _():
        lane = lax.broadcasted_iota(jnp.int32, (128, 128), 0) // 32
        pick = one_hot(lane, lax.broadcasted_iota(jnp.int32, (128, 128), 1))
        for i, ref in enumerate(home_refs):
            x_ref[i, :, :128] = ref[:, :cap, :].reshape(n, 128)
            tail = ref[:, cap:, :].astype(F32)
            shape = (peers, 32, 128)
            slot = lax.broadcasted_iota(jnp.int32, shape, 1)
            at = lax.broadcasted_iota(jnp.int32, shape, 2) % 32
            spread = [
                jnp.where(slot == at, tail[:, part : part + 1], 0.0)
                for part in range(cap // 32)
            ]
            spread = jnp.concatenate(spread, axis=1).reshape(n, 128).astype(BF)
            x_ref[i, :, 128:] = jnp.dot(spread, pick, preferred_element_type=F32).astype(BF)

    step = out_ref.shape[1]
    place = lax.broadcasted_iota(jnp.int32, (step, n), 1)
    parts, logs = [], []
    for i in range(len(home_refs)):
        hot = one_hot(column(idx_ref[0, i : i + 1]), place)
        got = jnp.dot(hot, x_ref[i], preferred_element_type=F32)
        parts.append(got[:, :128])
        logs.append(got[:, 128:129] + got[:, 129:130] + got[:, 130:131])
    top = functools.reduce(jnp.maximum, logs)
    scales = [jnp.exp(v - top) for v in logs]
    total = sum(scales)
    summed = sum(s * p for s, p in zip(scales, parts))
    out_ref[0, :, :128] = summed
    lane = lax.broadcasted_iota(jnp.int32, (step, 128), 1)
    out_ref[0, :, 128:] = jnp.where(lane < 64, top, total)


def home_rows(idx, homes):
    rounds, count = idx.shape
    step = BLOCK
    steps = count // step
    quarters = 4
    per = steps // quarters
    peers, ext, _ = homes[0].shape
    n = peers * (ext - 8)
    return pl.pallas_call(
        home_kernel,
        grid=(steps,),
        in_specs=[pl.BlockSpec((1, rounds, step), lambda i: (i, 0, 0))]
        + [whole(h.shape) for h in homes],
        out_specs=pl.BlockSpec((1, step, 256), lambda i: (i // per, i % per, 0)),
        out_shape=jax.ShapeDtypeStruct((quarters, count // quarters, 256), F32),
        scratch_shapes=[pltpu.VMEM((rounds, n, 256), BF)],
        compiler_params=params(),
        name="home_rows",
    )(idx.reshape(rounds, steps, step).transpose(1, 0, 2), *homes)


def finish_kernel(m_ref, w_ref, out_ref):
    tops = [m_ref[i, :, 128:129] for i in range(4)]
    totals = [m_ref[i, :, 192:193] for i in range(4)]
    top = functools.reduce(jnp.maximum, tops)
    scales = [jnp.exp(t - top) for t in tops]
    total = sum(s * t for s, t in zip(scales, totals))
    summed = sum(s * m_ref[i, :, :128] for i, s in enumerate(scales))
    blended = (summed / total).astype(BF)
    out_ref[...] = jnp.dot(blended, w_ref[...], preferred_element_type=F32).astype(BF)


def finish(merged, w_out):
    parts, rows, wide = merged.shape
    step = 256
    return pl.pallas_call(
        finish_kernel,
        grid=(rows // step,),
        in_specs=[pl.BlockSpec((parts, step, wide), lambda i: (0, i, 0)), whole(w_out.shape)],
        out_specs=pl.BlockSpec((step, w_out.shape[1]), lambda i: (i, 0)),
        out_shape=jax.ShapeDtypeStruct((rows, w_out.shape[1]), BF),
        compiler_params=params(),
        name="finish",
    )(merged, w_out)


def body(x, w_qk, w_v, w_out, slots, taken, looks):
    rounds, count = slots.shape
    peers = lax.axis_size(SEQ)
    cap = 2 * count // peers
    blocks = count // BLOCK
    packed = project(x, w_qk, w_v)
    mine = lax.axis_index(SEQ) * blocks + jnp.arange(blocks, dtype=jnp.int32)
    dist = (mine[None, :] - looks) % (peers * blocks)
    ring = [(i, (i + 1) % peers) for i in range(peers)]
    arrived = []
    for i in range(rounds):
        out = scatter_rows(slots[i : i + 1], packed, peers, cap)
        arrived.append(lax.all_to_all(out, SEQ, 0, 0, tiled=True))
    homes = []
    for i in range(rounds):
        q, kv = sort_rows(taken[i], arrived[i].reshape(peers * cap, 256))
        halo = lax.ppermute(kv[count - 2 * BLOCK :], SEQ, ring)
        res = attend(dist[i], q, kv, halo)
        back = back_rows(taken[i : i + 1], res, peers, cap)
        homes.append(lax.all_to_all(back, SEQ, 0, 0, tiled=True))
    state = home_rows(slots, homes)
    merged = lax.all_to_all(state, ROUND, 0, 0, tiled=True)
    return finish(merged, w_out)


def solution(mesh):
    fine = Mesh(mesh.devices.reshape(4, 4, 4, 2, 2), SEQ + ROUND)
    in_specs = (P(SEQ, None), P(), P(), P()) + (P(ROUND, SEQ),) * 3
    return jax.shard_map(
        body, mesh=fine, in_specs=in_specs, out_specs=P(SEQ + ROUND, None), check_vma=False
    )
```

time: 399 us -> 308 us (0.77)
  local copies, waits for them, and re-layouts: 118 us -> 10.5 us
  blocking collectives: 21.1 us -> 107 us
  Pallas kernels: 0 us -> 67.4 us
  waiting for transfers between devices: 136 us -> 74.3 us
  other arithmetic: 26.3 us -> 0.01 us
  starting transfers between devices: 64.4 us -> 47.8 us
  matrix products: 15.6 us -> 0 us
  between operations: 13.9 us -> 0.23 us
    all_to_all x0 -> x2, blocking collectives: none -> 107 us  [the longest x1 60.1 us: body(): merged = lax.all_to_all(state, ROUND, 0, 0, tiled=True)]
    pallas_call x0 -> x11, Pallas kernels: none -> 67.4 us  [the longest x2 15.8 us: sort_rows(): pl.pallas_call(sort_kernel, grid=(blocks,), in_specs=[pl.BlockSpec((1, 1,...]
    gather x6 -> x0, local copies, waits for them, and re-layouts: 52.9 us -> none  [the longest x2 23.6 us: body(): jnp.take_along_axis(home_log.reshape(members, buffer_rows), slots, axis=1)]
    all_gather x1 -> x0, waiting for transfers between devices: 47.5 us -> none  [joined_2(): pieces = jax.tree.map(lambda part: lax.all_gather(part, axis), value)]
    unnamed x42 -> x22, local copies, waits for them, and re-layouts: 54.9 us -> 9.59 us
    all_to_all x6 -> x3, waiting for transfers between devices: 79.9 us -> 51.4 us  [the longest x2 51.4 us: body(): arrived.append(lax.all_to_all(out, SEQ, 0, 0, tiled=True))]
    all_gather x2 -> x0, blocking collectives: 21.1 us -> none  [joined_2(): pieces = jax.tree.map(lambda part: lax.all_gather(part, axis), value)]
    all_to_all x6 -> x3, starting transfers between devices: 61.8 us -> 45.2 us  [the longest x1 24.7 us: body(): homes.append(lax.all_to_all(back, SEQ, 0, 0, tiled=True))]
  transfers between devices with their start and end apart: 9 -> 5, of which waited for: 6 -> 4; matrix products, arithmetic and copies ran while one was open for 24% -> 0% of each run, Pallas kernels for 0% -> 14%
where the time goes in v1:
time: 308 us
  blocking collectives  107 us (35%)
  waiting for transfers between devices  74.3 us (24%)
  Pallas kernels  67.4 us (22%)
  starting transfers between devices  47.8 us (16%)
  local copies, waits for them, and re-layouts  10.5 us (3%)
    all_to_all x1, blocking collectives, body(): merged = lax.all_to_all(state, ROUND, 0, 0, tiled=True)  60.1 us
    all_to_all x2, waiting for transfers between devices, body(): arrived.append(lax.all_to_all(out, SEQ, 0, 0, tiled=True))  51.4 us
    all_to_all x1, blocking collectives, body(): homes.append(lax.all_to_all(back, SEQ, 0, 0, tiled=True))  47.3 us
    all_to_all x1, starting transfers between devices, body(): homes.append(lax.all_to_all(back, SEQ, 0, 0, tiled=True))  24.7 us
    ppermute x2, waiting for transfers between devices, body(): halo = lax.ppermute(kv[count - 2 * BLOCK:], SEQ, ring)  22.9 us
    all_to_all x2, starting transfers between devices, body(): arrived.append(lax.all_to_all(out, SEQ, 0, 0, tiled=True))  20.6 us
    pallas_call x2, Pallas kernels, sort_rows(): pl.pallas_call(sort_kernel, grid=(blocks,), in_specs=[pl.BlockSpec((1, 1,...  15.8 us
    pallas_call x1, Pallas kernels, home_rows(): pl.pallas_call(home_kernel, grid=(steps,), in_specs=[pl.BlockSpec((1, rou...  15 us
  transfers between devices with their start and end apart: 5, of which 4 were waited for; matrix products, arithmetic and copies ran while one was open for 0% of the time, Pallas kernels for 14%

profile of v1, /device:TPU:35, one launch (start us, length us, event | category | flops | bytes accessed | tf_op | source)
XLA Modules:
  0.0 307.5 jit_solution(3478886355262799655)
XLA Ops:
  0.8 2.2 copy-done.4
  4.9 1.9 project.1.rows_ref
  6.8 5.7 %scatter_rows.3 = bf16[64,64,256]{2,1,0:T(8,128)(2,1)S(1)} custom-call(s32[1,2048]{1,0:T(1,128)S(1)} %get-tuple-element.13.idx_ref, bf16[2048,256]{1,0:T(8,128)(2,1)S(1)} %project.1.rows_ref), custom_call_target="tpu_custom_call" | custom-call | tf_op jit(solution)/shard_map/scatter_rows/pallas_call | solution.py:77
  13.8 11.1 %all-to-all-start.2 = ((bf16[64,64,256]{2,1,0:T(8,128)(2,1)}), bf16[64,64,256]{2,1,0:T(8,128)(2,1)S(1)}, u32[]{:S(2)}, u32[]{:S(2)}) async-start(bf16[64,64,256]{2,1,0:T(8,128)(2,1)} %copy-done.3), calls=%async_computation.2 | async-start | bytes 4194304 | tf_op jit(solution)/shard_map/all_to_all | solution.py:318
  24.9 5.7 %scatter_rows.2 = bf16[64,64,256]{2,1,0:T(8,128)(2,1)S(1)} custom-call(s32[1,2048]{1,0:T(1,128)S(1)} %get-tuple-element.14.idx_ref, bf16[2048,256]{1,0:T(8,128)(2,1)S(1)} %project.1.rows_ref), custom_call_target="tpu_custom_call" | custom-call | tf_op jit(solution)/shard_map/scatter_rows/pallas_call | solution.py:77
  30.6 1.3 copy-done
  32.0 39.2 %all-to-all-done.2 = bf16[64,64,256]{2,1,0:T(8,128)(2,1)S(1)} async-done(((bf16[64,64,256]{2,1,0:T(8,128)(2,1)}), bf16[64,64,256]{2,1,0:T(8,128)(2,1)S(1)}, u32[]{:S(2)}, u32[]{:S(2)}) %all-to-all-start.2) | async-done | bytes 2097184 | tf_op jit(solution)/shard_map/all_to_all | solution.py:318
  71.1 1.3 copy-done.1
  72.4 9.5 %all-to-all-start = ((bf16[64,64,256]{2,1,0:T(8,128)(2,1)}), bf16[64,64,256]{2,1,0:T(8,128)(2,1)S(1)}, u32[]{:S(2)}, u32[]{:S(2)}) async-start(bf16[64,64,256]{2,1,0:T(8,128)(2,1)} %copy-done), calls=%async_computation | async-start | bytes 4194304 | tf_op jit(solution)/shard_map/all_to_all | solution.py:318
  82.0 1.6 copy-done.2
  83.6 7.9 %sort_rows.3 = (bf16[2048,128]{1,0:T(8,128)(2,1)S(1)}, bf16[2048,256]{1,0:T(8,128)(2,1)S(1)}) custom-call(s32[8,1,256]{2,1,0:T(1,128)S(1)} %bitcast.14, bf16[4096,256]{1,0:T(8,128)(2,1)S(1)} %bitcast.12), custom_call_target="tpu_custom_call" | custom-call | tf_op jit(solution)/shard_map/sort_rows/pallas_call | solution.py:103
  92.8 12.0 %collective-permute-done.1.halo_ref = bf16[512,256]{1,0:T(8,128)(2,1)S(1)} collective-permute-done((bf16[512,256]{1,0:T(8,128)(2,1)S(1)}, bf16[512,256]{1,0:T(8,128)(2,1)S(1)}, u32[]{:S(2)}, u32[]{:S(2)}) %collective-permute-start.1) | collective-permute-done | bytes 262176 | tf_op jit(solution)/shard_map/ppermute | solution.py:322
  104.8 4.4 %attend.3.res_ref = bf16[2048,256]{1,0:T(8,128)(2,1)S(1)} custom-call(s32[8]{0:T(128)S(1)} %get-tuple-element.17.dist_ref, bf16[2048,128]{1,0:T(8,128)(2,1)S(1)} %get-tuple-element.11.q_ref, bf16[2048,256]{1,0:T(8,128)(2,1)S(1)} %get-tuple-element.12.kv_ref, bf16[512,256]{1,0:T(8,128)(2,1)S(1)} %collective-permute-done.1.halo_ref), custom_call_target="tpu_custom_call" | custom-call | tf_op jit(solution)/shard_map/attend/pallas_call | solution.py:167
  109.2 6.5 %back_rows.3 = bf16[64,72,128]{2,1,0:T(8,128)(2,1)} custom-call(s32[1,2048]{1,0:T(1,128)S(1)} %get-tuple-element.15.idx_ref, bf16[2048,256]{1,0:T(8,128)(2,1)S(1)} %attend.3.res_ref), custom_call_target="tpu_custom_call" | custom-call | tf_op jit(solution)/shard_map/back_rows/pallas_call | solution.py:209
  115.7 12.2 %all-to-all-done = bf16[64,64,256]{2,1,0:T(8,128)(2,1)S(1)} async-done(((bf16[64,64,256]{2,1,0:T(8,128)(2,1)}), bf16[64,64,256]{2,1,0:T(8,128)(2,1)S(1)}, u32[]{:S(2)}, u32[]{:S(2)}) %all-to-all-start) | async-done | bytes 2097184 | tf_op jit(solution)/shard_map/all_to_all | solution.py:318
  127.9 24.7 %all-to-all-start.3 = ((bf16[64,72,128]{2,1,0:T(8,128)(2,1)}), bf16[64,72,128]{2,1,0:T(8,128)(2,1)S(1)}, u32[]{:S(2)}, u32[]{:S(2)}) async-start(bf16[64,72,128]{2,1,0:T(8,128)(2,1)} %back_rows.3), calls=%async_computation.3 | async-start | bytes 2359296 | tf_op jit(solution)/shard_map/all_to_all | solution.py:325
  152.6 7.9 %sort_rows.2 = (bf16[2048,128]{1,0:T(8,128)(2,1)S(1)}, bf16[2048,256]{1,0:T(8,128)(2,1)S(1)}) custom-call(s32[8,1,256]{2,1,0:T(1,128)S(1)} %bitcast.13, bf16[4096,256]{1,0:T(8,128)(2,1)S(1)} %bitcast.11), custom_call_target="tpu_custom_call" | custom-call | tf_op jit(solution)/shard_map/sort_rows/pallas_call | solution.py:103
  161.8 10.9 %collective-permute-done.halo_ref = bf16[512,256]{1,0:T(8,128)(2,1)S(1)} collective-permute-done((bf16[512,256]{1,0:T(8,128)(2,1)S(1)}, bf16[512,256]{1,0:T(8,128)(2,1)S(1)}, u32[]{:S(2)}, u32[]{:S(2)}) %collective-permute-start) | collective-permute-done | bytes 262176 | tf_op jit(solution)/shard_map/ppermute | solution.py:322
  172.7 4.5 %attend.2.res_ref = bf16[2048,256]{1,0:T(8,128)(2,1)S(1)} custom-call(s32[8]{0:T(128)S(1)} %get-tuple-element.18.dist_ref, bf16[2048,128]{1,0:T(8,128)(2,1)S(1)} %get-tuple-element.9.q_ref, bf16[2048,256]{1,0:T(8,128)(2,1)S(1)} %get-tuple-element.10.kv_ref, bf16[512,256]{1,0:T(8,128)(2,1)S(1)} %collective-permute-done.halo_ref), custom_call_target="tpu_custom_call" | custom-call | tf_op jit(solution)/shard_map/attend/pallas_call | solution.py:167
  177.2 5.8 %back_rows.2 = bf16[64,72,128]{2,1,0:T(8,128)(2,1)S(1)} custom-call(s32[1,2048]{1,0:T(1,128)S(1)} %get-tuple-element.16.idx_ref, bf16[2048,256]{1,0:T(8,128)(2,1)S(1)} %attend.2.res_ref), custom_call_target="tpu_custom_call" | custom-call | tf_op jit(solution)/shard_map/back_rows/pallas_call | solution.py:209
  183.0 47.3 %all_to_all.25.refs_0_ = bf16[64,72,128]{2,1,0:T(8,128)(2,1)S(1)} all-to-all(bf16[64,72,128]{2,1,0:T(8,128)(2,1)S(1)} %back_rows.2), channel_id=1, replica_groups=mesh['zl'=4,'x'=4,'y'=4,'zh'=2,'c'=2] {'zl','x','y'}, dimensions={0} | all-to-all | bytes 2359296 | tf_op jit(solution)/shard_map/all_to_all | solution.py:325
  230.3 15.0 %home_rows.1 = f32[4,512,256]{2,1,0:T(8,128)S(1)} custom-call(s32[8,2,256]{2,1,0:T(2,128)S(1)} %bitcast.15, bf16[64,72,128]{2,1,0:T(8,128)(2,1)S(1)} %all_to_all.25.refs_0_, bf16[64,72,128]{2,1,0:T(8,128)(2,1)S(1)} %all-to-all-done.3.refs_1_), custom_call_target="tpu_custom_call" | custom-call | tf_op jit(solution)/shard_map/home_rows/pallas_call | solution.py:268
  245.3 60.1 %all_to_all.26.m_ref = f32[4,512,256]{2,1,0:T(8,128)S(1)} all-to-all(f32[4,512,256]{2,1,0:T(8,128)S(1)} %home_rows.1), channel_id=1, replica_groups=mesh['zl'=4,'x'=4,'y'=4,'zh'=2,'c'=2] {'zh','c'}, dimensions={0} | all-to-all | bytes 4194304 | tf_op jit(solution)/shard_map/all_to_all | solution.py:327
  305.4 2.1 finish.1
  (28 shorter events, 6.6 us)
Async XLA Ops:
  0.8 2.2 copy-start.4
  3.0 0.9 copy-start.5
  4.0 0.9 copy-start.6
  12.5 1.3 copy-start.3
  13.8 57.3 %all-to-all-start.2 = ((bf16[64,64,256]{2,1,0:T(8,128)(2,1)}), bf16[64,64,256]{2,1,0:T(8,128)(2,1)S(1)}, u32[]{:S(2)}, u32[]{:S(2)}) async-start(bf16[64,64,256]{2,1,0:T(8,128)(2,1)} %copy-done.3), calls=%async_computation.2 | async-start | bytes 4194304 | tf_op jit(solution)/shard_map/all_to_all | solution.py:318
  30.6 1.3 copy-start
  32.0 50.0 %copy-start.9 = (s32[2,2048]{1,0:T(2,128)S(1)}, s32[2,2048]{1,0:T(2,128)}, u32[]{:S(2)}) copy-start(s32[2,2048]{1,0:T(2,128)} %param.12) | copy-start | bytes 49156
  71.1 1.3 copy-start.1
  72.4 55.5 %all-to-all-start = ((bf16[64,64,256]{2,1,0:T(8,128)(2,1)}), bf16[64,64,256]{2,1,0:T(8,128)(2,1)S(1)}, u32[]{:S(2)}, u32[]{:S(2)}) async-start(bf16[64,64,256]{2,1,0:T(8,128)(2,1)} %copy-done), calls=%async_computation | async-start | bytes 4194304 | tf_op jit(solution)/shard_map/all_to_all | solution.py:318
  81.9 10.8 %copy-start.10 = (s32[2,8]{1,0:T(2,128)S(1)}, s32[2,8]{1,0:T(2,128)}, u32[]{:S(2)}) copy-start(s32[2,8]{1,0:T(2,128)} %param.13) | copy-start | bytes 196
  82.0 1.6 copy-start.2
  91.5 13.3 %collective-permute-start.1 = (bf16[512,256]{1,0:T(8,128)(2,1)S(1)}, bf16[512,256]{1,0:T(8,128)(2,1)S(1)}, u32[]{:S(2)}, u32[]{:S(2)}) collective-permute-start(bf16[512,256]{1,0:T(8,128)(2,1)S(1)} %slice.33), channel_id=1, source_target_pairs={{0,4},{4,8},{8,12},{12,16},{16,20},{20,24},{24,28},{28,32},{32,36}... | collective-permute-start | bytes 786440 | tf_op jit(solution)/shard_map/ppermute | solution.py:322
  127.9 55.0 %all-to-all-start.3 = ((bf16[64,72,128]{2,1,0:T(8,128)(2,1)}), bf16[64,72,128]{2,1,0:T(8,128)(2,1)S(1)}, u32[]{:S(2)}, u32[]{:S(2)}) async-start(bf16[64,72,128]{2,1,0:T(8,128)(2,1)} %back_rows.3), calls=%async_computation.3 | async-start | bytes 2359296 | tf_op jit(solution)/shard_map/all_to_all | solution.py:325
  160.5 12.2 %collective-permute-start = (bf16[512,256]{1,0:T(8,128)(2,1)S(1)}, bf16[512,256]{1,0:T(8,128)(2,1)S(1)}, u32[]{:S(2)}, u32[]{:S(2)}) collective-permute-start(bf16[512,256]{1,0:T(8,128)(2,1)S(1)} %slice.29), channel_id=1, source_target_pairs={{0,4},{4,8},{8,12},{12,16},{16,20},{20,24},{24,28},{28,32},{32,36}... | collective-permute-start | bytes 786440 | tf_op jit(solution)/shard_map/ppermute | solution.py:322
  177.2 53.1 %copy-start.8 = (s32[2,2048]{1,0:T(2,128)S(1)}, s32[2,2048]{1,0:T(2,128)}, u32[]{:S(2)}) copy-start(s32[2,2048]{1,0:T(2,128)} %param.11) | copy-start | bytes 49156
  245.3 60.1 %copy-start.7 = (bf16[128,1024]{1,0:T(8,128)(2,1)S(1)}, bf16[128,1024]{1,0:T(8,128)(2,1)}, u32[]{:S(2)}) copy-start(bf16[128,1024]{1,0:T(8,128)(2,1)} %w_ref.1) | copy-start | bytes 786436

commit v2 on v1

v2 whole, which is shorter than its diff:
```python
import functools

import jax
import jax.numpy as jnp
from jax import lax
from jax.experimental import pallas as pl
from jax.experimental.pallas import tpu as pltpu
from jax.sharding import Mesh
from jax.sharding import PartitionSpec as P

BLOCK = 256
SHIFTS = (0, 1, -1, 2, -2)
MASKED = -1000000000.0
SEQ = ("zl", "x", "y")
PLANE = ("x", "y")
ROUND = ("zh", "c")
BF = jnp.bfloat16
F32 = jnp.float32
VMEM_BYTES = 48 * 1024 * 1024


def params(n=1):
    return pltpu.CompilerParams(
        dimension_semantics=("arbitrary",) * n, vmem_limit_bytes=VMEM_BYTES
    )


def whole(shape):
    return pl.BlockSpec(shape, lambda *_: (0,) * len(shape))


def one_hot(a, b):
    return jnp.where(a == b, 1.0, 0.0).astype(BF)


def column(row):
    return jnp.transpose(jnp.broadcast_to(row, (8, row.shape[1])))[:, :1]


def project_kernel(x_ref, wqk_ref, wv_ref, out_ref, w_ref):
    @pl.when(pl.program_id(0) == 0)
    def _():
        w_ref[:, :128] = wqk_ref[...]
        w_ref[:, 128:] = wv_ref[...]

    out_ref[...] = jnp.dot(x_ref[...], w_ref[...], preferred_element_type=F32).astype(BF)


def project(x, w_qk, w_v):
    rows, model = x.shape
    step = 512
    return pl.pallas_call(
        project_kernel,
        grid=(rows // step,),
        in_specs=[
            pl.BlockSpec((step, model), lambda i: (i, 0)),
            whole(w_qk.shape),
            whole(w_v.shape),
        ],
        out_specs=pl.BlockSpec((step, 256), lambda i: (i, 0)),
        out_shape=jax.ShapeDtypeStruct((rows, 256), BF),
        scratch_shapes=[pltpu.VMEM((model, 256), BF)],
        compiler_params=params(),
        name="project",
    )(x, w_qk, w_v)


def ring(value, shift):
    def at(z):
        return (z % 4) * 2 + z // 4

    route = [(at(z), at((z + shift) % 8)) for z in range(8)]
    return lax.ppermute(value, ("zl", "zh"), route)


def ring_all(pieces, sign):
    return [pieces[0]] + [ring(p, sign * k) for p, k in zip(pieces[1:], SHIFTS[1:])]


def ring_first(split, sign):
    a, b, c, d, e = ring_all(split, sign)
    joint = jnp.stack([a, b, c, jnp.concatenate([d, e])], axis=1)
    return lax.all_to_all(joint, PLANE, 0, 0, tiled=True)


def plane_first(joint, sign):
    joint = lax.all_to_all(joint, PLANE, 0, 0, tiled=True)
    split = [joint[:, 0], joint[:, 1], joint[:, 2], joint[:8, 3], joint[8:, 3]]
    return ring_all(split, sign)


def emit_specs(split, width, lanes):
    if not split:
        return (
            [pl.BlockSpec((8, 1, width, lanes), lambda i: (i % 2, i // 2, 0, 0))],
            [jax.ShapeDtypeStruct((16, 4, width, lanes), BF)],
        )

    def spec(first):
        return pl.BlockSpec((8, width, lanes), lambda i: (jnp.clip(i - first, 0, 1), 0, 0))

    big = jax.ShapeDtypeStruct((16, width, lanes), BF)
    small = jax.ShapeDtypeStruct((8, width, lanes), BF)
    return [spec(0), spec(2), spec(4)] + [whole(small.shape)] * 2, [big] * 3 + [small] * 2


def emit(refs, store):
    if len(refs) == 1:
        store(refs[0].at[:, 0])
        return
    step = pl.program_id(0)
    for ref, (first, last) in zip(refs, ((0, 1), (2, 3), (4, 5), (6, 6), (7, 7))):

        @pl.when((step >= first) & (step <= last))
        def _(ref=ref):
            store(ref)


def scatter_kernel(width, idx_ref, rows_ref, *out_refs):
    n = 8 * width
    step = pl.program_id(0)
    line = idx_ref[pl.ds(jnp.where(step == 7, 4, step // 2), 1), :]
    place = lax.broadcasted_iota(jnp.int32, (n, rows_ref.shape[0]), 0)
    hot = one_hot(line - (step % 2) * n, place)
    got = jnp.dot(hot, rows_ref[...], preferred_element_type=F32).astype(BF)

    def store(ref):
        ref[...] = got.reshape(8, width, 256)

    emit(out_refs, store)


def scatter_rows(idx, rows, width, split):
    specs, shapes = emit_specs(split, width, 256)
    return pl.pallas_call(
        functools.partial(scatter_kernel, width),
        grid=(8,),
        in_specs=[whole(idx.shape), whole(rows.shape)],
        out_specs=specs,
        out_shape=shapes,
        compiler_params=params(),
        name="scatter_rows",
    )(idx, rows)


def sort_kernel(idx_ref, *refs):
    (*row_refs, q_ref, kv_ref) = refs
    col = column(idx_ref[0])
    got, base = 0.0, 0
    for ref in row_refs:
        rows = ref[...].reshape(-1, 256)
        n = rows.shape[0]
        place = lax.broadcasted_iota(jnp.int32, (BLOCK, n), 1) + base
        got += jnp.dot(one_hot(col, place), rows, preferred_element_type=F32)
        base += n
    qk = got[:, :128]
    keys = qk * lax.rsqrt(jnp.sum(qk * qk, axis=-1, keepdims=True) + 1e-06)
    q_ref[...] = qk.astype(BF)
    kv_ref[:, :128] = keys.astype(BF)
    kv_ref[:, 128:] = got[:, 128:].astype(BF)


def sort_rows(idx, rows):
    count = idx.shape[-1]
    blocks = count // BLOCK
    return pl.pallas_call(
        sort_kernel,
        grid=(blocks,),
        in_specs=[pl.BlockSpec((1, 1, BLOCK), lambda i: (i, 0, 0))]
        + [whole(r.shape) for r in rows],
        out_specs=[
            pl.BlockSpec((BLOCK, 128), lambda i: (i, 0)),
            pl.BlockSpec((BLOCK, 256), lambda i: (i, 0)),
        ],
        out_shape=[
            jax.ShapeDtypeStruct((count, 128), BF),
            jax.ShapeDtypeStruct((count, 256), BF),
        ],
        compiler_params=params(),
        name="sort_rows",
    )(idx.reshape(blocks, 1, BLOCK), *rows)


def terms_to_lines(terms, groups):
    terms = terms.reshape(groups, 32, 128)
    slot = lax.broadcasted_iota(jnp.int32, terms.shape, 1)
    lane = lax.broadcasted_iota(jnp.int32, terms.shape, 2) % 32
    return jnp.sum(jnp.where(slot == lane, terms, 0.0), axis=1, keepdims=True)


def lines_to_terms(line):
    n = line.shape[0]
    shape = (n, 32, 128)
    slot = lax.broadcasted_iota(jnp.int32, shape, 1)
    lane = lax.broadcasted_iota(jnp.int32, shape, 2) % 32
    spread = jnp.where(slot == lane, line, 0.0).reshape(n * 32, 128).astype(BF)
    group = lax.broadcasted_iota(jnp.int32, (128, 128), 0) // 32
    pick = one_hot(group, lax.broadcasted_iota(jnp.int32, (128, 128), 1))
    return jnp.dot(spread, pick, preferred_element_type=F32)


def three_terms(v):
    hi = v.astype(BF).astype(F32)
    mid = (v - hi).astype(BF).astype(F32)
    lo = v - hi - mid
    return hi, mid, lo


def term_lanes(v, rows):
    hi, mid, lo = three_terms(v)
    group = lax.broadcasted_iota(jnp.int32, (rows, 128), 1) // 32
    return jnp.where(
        group == 0, hi, jnp.where(group == 1, mid, jnp.where(group == 2, lo, 1.0))
    ).astype(BF)


def attend_block(q, own, behind, out_ref):
    nt = (((1,), (1,)), ((), ()))
    s1 = lax.dot_general(q, own[:, :128], nt, preferred_element_type=F32)
    s2 = lax.dot_general(q, behind[:, :128], nt, preferred_element_type=F32)
    r = lax.broadcasted_iota(jnp.int32, (BLOCK, BLOCK), 0)
    k = lax.broadcasted_iota(jnp.int32, (BLOCK, BLOCK), 1)
    s1 = jnp.where(r == k, MASKED, s1)
    top = jnp.maximum(
        jnp.max(s1, axis=-1, keepdims=True), jnp.max(s2, axis=-1, keepdims=True)
    )
    e1 = jnp.exp(s1 - top)
    e2 = jnp.exp(s2 - top)
    total = jnp.sum(e1, axis=-1, keepdims=True) + jnp.sum(e2, axis=-1, keepdims=True)
    o = jnp.dot(e1.astype(BF), own[:, 128:], preferred_element_type=F32) + jnp.dot(
        e2.astype(BF), behind[:, 128:], preferred_element_type=F32
    )
    out_ref[:, :128] = (o / total).astype(BF)
    out_ref[:, 128:] = term_lanes(top + jnp.log(total), BLOCK)


def inner_kernel(dist_ref, q_ref, kv_ref, out_ref):
    c = pl.program_id(0) + 2
    own = kv_ref[pl.ds(pl.multiple_of(c * BLOCK, BLOCK), BLOCK), :]
    behind = kv_ref[pl.ds(pl.multiple_of((c - dist_ref[c]) * BLOCK, BLOCK), BLOCK), :]
    attend_block(q_ref[...], own, behind, out_ref)


def edge_kernel(dist_ref, q_ref, kv_ref, halo_ref, out_ref):
    c = pl.program_id(0)
    own = kv_ref[pl.ds(pl.multiple_of(c * BLOCK, BLOCK), BLOCK), :]
    at = c + 2 - dist_ref[c]
    before = halo_ref[pl.ds(pl.multiple_of(jnp.minimum(at, 1) * BLOCK, BLOCK), BLOCK), :]
    behind = jnp.where(at < 2, before, kv_ref[:BLOCK, :])
    attend_block(q_ref[...], own, behind, out_ref)


def attend_inner(dist, q, kv):
    blocks = q.shape[0] // BLOCK - 2
    return pl.pallas_call(
        inner_kernel,
        grid_spec=pltpu.PrefetchScalarGridSpec(
            num_scalar_prefetch=1,
            grid=(blocks,),
            in_specs=[pl.BlockSpec((BLOCK, 128), lambda i, d: (i + 2, 0)), whole(kv.shape)],
            out_specs=pl.BlockSpec((BLOCK, 256), lambda i, d: (i, 0)),
        ),
        out_shape=jax.ShapeDtypeStruct((blocks * BLOCK, 256), BF),
        compiler_params=params(),
        name="attend_inner",
    )(dist, q, kv)


def attend_edge(dist, q, kv, halo):
    return pl.pallas_call(
        edge_kernel,
        grid_spec=pltpu.PrefetchScalarGridSpec(
            num_scalar_prefetch=1,
            grid=(2,),
            in_specs=[
                pl.BlockSpec((BLOCK, 128), lambda i, d: (i, 0)),
                whole((2 * BLOCK, 256)),
                whole(halo.shape),
            ],
            out_specs=pl.BlockSpec((BLOCK, 256), lambda i, d: (i, 0)),
        ),
        out_shape=jax.ShapeDtypeStruct((2 * BLOCK, 256), BF),
        compiler_params=params(),
        name="attend_edge",
    )(dist, q, kv, halo)


def back_kernel(width, idx_ref, *refs):
    edge_ref, inner_ref, *out_refs = refs
    n = 8 * width
    base = pl.program_id(0) * n
    idx = idx_ref[...] - base
    got = 0.0
    first = 0
    for ref in (edge_ref, inner_ref):
        count = ref.shape[0]
        place = lax.broadcasted_iota(jnp.int32, (n, count), 0)
        hot = one_hot(idx[:, first : first + count], place)
        got += jnp.dot(hot, ref[...], preferred_element_type=F32)
        first += count
    lines = terms_to_lines(got[:, 128:], n // 32).reshape(8, width // 32, 1, 128)
    row = lax.broadcasted_iota(jnp.int32, (8, 8, 128), 1)
    tail = jnp.zeros((8, 8, 128), F32)
    for part in range(width // 32):
        tail = jnp.where(row == part, lines[:, part], tail)

    def store(ref):
        ref[:, :width, :] = got[:, :128].astype(BF).reshape(8, width, 128)
        ref[:, width:, :] = tail.astype(BF)

    emit(out_refs, store)


def back_rows(idx, edge, inner, width, split):
    specs, shapes = emit_specs(split, width + 8, 128)
    return pl.pallas_call(
        functools.partial(back_kernel, width),
        grid=(8,),
        in_specs=[whole(idx.shape), whole(edge.shape), whole(inner.shape)],
        out_specs=specs,
        out_shape=shapes,
        compiler_params=params(),
        name="back_rows",
    )(idx, edge, inner)


ABSENT = -1e30


def home_kernel(width, splits, own_ref, idx_ref, *refs):
    (*home_refs, out_ref, x_ref) = refs
    jobs = len(splits)
    big, small = 16 * width, 8 * width
    sizes = (big, big, big, small, small)

    @pl.when(pl.program_id(0) == 0)
    def _():
        at = 0
        for job in range(jobs):
            if splits[job]:
                blocks = [home_refs[at + g] for g in range(5)]
                at += 5
            else:
                ref = home_refs[at]
                blocks = [ref.at[:, g] for g in range(3)] + [ref.at[:8, 3], ref.at[8:, 3]]
                at += 1
            row = 0
            for size, block in zip(sizes, blocks):
                x_ref[job, row : row + size, :128] = block[:, :width, :].reshape(size, 128)
                tail = block[:, width:, :].astype(F32)
                lines = jnp.concatenate(
                    [tail[:, p : p + 1][:, None] for p in range(width // 32)], axis=1
                ).reshape(size // 32, 1, 128)
                x_ref[job, row : row + size, 128:] = lines_to_terms(lines).astype(BF)
                row += size

    step = out_ref.shape[1] - out_ref.shape[1] // 33
    cols = jnp.transpose(idx_ref[0])
    states = {}
    for job in range(jobs):
        row = 0
        for g, size in enumerate(sizes):
            c = job * 5 + g
            first = small if g == 4 else 0
            place = lax.broadcasted_iota(jnp.int32, (step, size), 1) + first
            hot = one_hot(cols[:, c : c + 1], place)
            got = jnp.dot(hot, x_ref[job, row : row + size], preferred_element_type=F32)
            row += size
            key = ROUND_OF[job]
            if g == 0:
                states[key, 0] = states.get((key, 0), 0.0) + got
            else:
                mine = own_ref[c] == 1
                states[key, 0] = states[key, 0] + jnp.where(mine, got, 0.0)
                states[key, 1] = states.get((key, 1), 0.0) + jnp.where(mine, 0.0, got)
    states = list(states.values())
    here = [s[:, 131:132] > 0.5 for s in states]
    logs = [
        jnp.where(h, s[:, 128:129] + s[:, 129:130] + s[:, 130:131], ABSENT)
        for h, s in zip(here, states)
    ]
    top = functools.reduce(jnp.maximum, logs)
    scales = [jnp.where(h, jnp.exp(v - top), 0.0) for h, v in zip(here, logs)]
    total = sum(scales)
    some = total > 0.0
    summed = sum(s * p[:, :128] for s, p in zip(scales, states))
    safe = jnp.where(some, total, 1.0)
    log = jnp.where(some, top + jnp.log(safe), ABSENT)
    out_ref[0, :step, :] = (summed / safe).astype(BF)
    terms = term_lanes(log, step).astype(F32)
    out_ref[0, step:, :] = terms_to_lines(terms, step // 32).reshape(step // 32, 128).astype(BF)


def home_rows(own, idx, homes, width, splits):
    columns, count = idx.shape
    quarters = 4
    step = count // quarters
    flat = [h for home in homes for h in home]
    return pl.pallas_call(
        functools.partial(home_kernel, width, splits),
        grid_spec=pltpu.PrefetchScalarGridSpec(
            num_scalar_prefetch=1,
            grid=(quarters,),
            in_specs=[pl.BlockSpec((1, columns, step), lambda i, o: (i, 0, 0))]
            + [whole(h.shape) for h in flat],
            out_specs=pl.BlockSpec((1, step + step // 32, 128), lambda i, o: (i, 0, 0)),
            scratch_shapes=[pltpu.VMEM((len(homes), 64 * width, 256), BF)],
        ),
        out_shape=jax.ShapeDtypeStruct((quarters, step + step // 32, 128), BF),
        compiler_params=params(),
        name="home_rows",
    )(own, idx.reshape(columns, quarters, step).transpose(1, 0, 2), *flat)


def finish_kernel(m_ref, w_ref, out_ref):
    rows = out_ref.shape[0]
    logs = []
    for i in range(4):
        line = m_ref[i, rows:, :].astype(F32).reshape(rows // 32, 1, 128)
        terms = lines_to_terms(line)
        logs.append(terms[:, 0:1] + terms[:, 1:2] + terms[:, 2:3])
    top = functools.reduce(jnp.maximum, logs)
    scales = [jnp.exp(v - top) for v in logs]
    total = sum(scales)
    summed = sum(s * m_ref[i, :rows, :].astype(F32) for i, s in enumerate(scales))
    blended = (summed / total).astype(BF)
    out_ref[...] = jnp.dot(blended, w_ref[...], preferred_element_type=F32).astype(BF)


def finish(merged, w_out):
    parts, rows, _ = merged.shape
    rows -= rows // 33
    return pl.pallas_call(
        finish_kernel,
        in_specs=[whole(merged.shape), whole(w_out.shape)],
        out_specs=whole((rows, w_out.shape[1])),
        grid=(1,),
        out_shape=jax.ShapeDtypeStruct((rows, w_out.shape[1]), BF),
        compiler_params=params(),
        name="finish",
    )(merged, w_out)


def send_places(own_slots, other_slots, low, width, by_target):
    zl, zh = lax.axis_index("zl"), lax.axis_index("zh")
    late = lax.axis_index(PLANE) >= 8
    places, mine = [], []
    for g, shift in enumerate(SHIFTS):
        if by_target or g < 3:
            k = shift
        else:
            k = jnp.where(late, -2, 2)
        own = ((zh * 4 + zl + k + 8) & 7) // 4 == zh
        slot = jnp.where(own, own_slots, other_slots)
        place = (slot >> 6) & 15
        at = slot & 63
        hit = ((slot >> 10) == ((zl + k + 8) & 3)) & (at >= low) & (at < low + width)
        if g == 3:
            hit &= place < 8
        if g == 4:
            hit &= place >= 8
        places.append(jnp.where(hit, place * width + at - low, -1))
        mine.append(own)
    return jnp.stack(places), jnp.stack(mine).astype(jnp.int32)


def take_places(taken, low, width):
    zl = lax.axis_index("zl")
    away = (zl - (taken >> 10)) & 3
    group = jnp.where(away < 2, away, 5 - away)
    source = (taken >> 6) & 15
    at = taken & 63
    hit = (at >= low) & (at < low + width)
    by_group = jnp.where(hit, (group * 16 + source) * width + at - low, -1)
    by_source = jnp.where(hit, (source * 4 + group) * width + at - low, -1)
    return by_group, by_source


WIDTH = 64
JOBS = ((0, 0, True), (1, 0, False))
ROUND_OF = tuple(job[0] for job in JOBS)


def body(x, w_qk, w_v, w_out, slots, taken, looks):
    rounds, count = slots.shape
    peers = lax.axis_size(SEQ)
    blocks = count // BLOCK
    others = lax.ppermute(slots, "zh", [(0, 1), (1, 0)])
    packed = project(x, w_qk, w_v)
    mine = lax.axis_index(SEQ) * blocks + jnp.arange(blocks, dtype=jnp.int32)
    dist = (mine[None, :] - looks) % (peers * blocks)
    next_device = [(i, (i + 1) % peers) for i in range(peers)]
    sent, own, arrived = [], [], []
    for i, low, z_first in JOBS:
        places, flags = send_places(slots[i], others[i], low, WIDTH, z_first)
        sent.append(places)
        own.append(flags)
        out = scatter_rows(places, packed, WIDTH, z_first)
        if z_first:
            arrived.append([ring_first(out, 1)])
        else:
            arrived.append(plane_first(out[0], 1))
    homes = [None] * len(JOBS)
    for i in range(rounds):
        rows, spots, base = [], 0, 0
        back_spots = {}
        for job, (which, low, z_first) in enumerate(JOBS):
            if which != i:
                continue
            by_group, by_source = take_places(taken[i], low, WIDTH)
            back_spots[job] = by_group
            spot = by_source if z_first else by_group
            spots = jnp.where(spot >= 0, spot + base, spots)
            base += 64 * WIDTH
            rows += arrived[job]
        q, kv = sort_rows(spots, rows)
        halo = lax.ppermute(kv[count - 2 * BLOCK :], SEQ, next_device)
        inner = attend_inner(dist[i], q, kv)
        edge = attend_edge(dist[i], q, kv, halo)
        for job, spot in back_spots.items():
            z_first = JOBS[job][2]
            back = back_rows(spot[None], edge, inner, WIDTH, not z_first)
            if z_first:
                homes[job] = plane_first(back[0], -1)
            else:
                homes[job] = [ring_first(back, -1)]
    splits = tuple(z_first for _, _, z_first in JOBS)
    state = home_rows(jnp.concatenate(own), jnp.concatenate(sent), homes, WIDTH, splits)
    merged = lax.all_to_all(state, ROUND, 0, 0, tiled=True)
    return finish(merged, w_out)


def solution(mesh):
    fine = Mesh(mesh.devices.reshape(4, 4, 4, 2, 2), SEQ + ROUND)
    in_specs = (P(SEQ, None), P(), P(), P()) + (P(ROUND, SEQ),) * 3
    return jax.shard_map(
        body, mesh=fine, in_specs=in_specs, out_specs=P(SEQ + ROUND, None), check_vma=False
    )
```

time: 308 us -> 258 us (0.84)
  blocking collectives: 107 us -> 28.5 us
  starting transfers between devices: 47.8 us -> 61 us
  waiting for transfers between devices: 74.3 us -> 78.9 us
  Pallas kernels: 67.4 us -> 71.2 us
  other arithmetic: 0.01 us -> 3.41 us
  local copies, waits for them, and re-layouts: 10.5 us -> 13.9 us
    all_to_all x1 -> x0, blocking collectives: 47.3 us -> none  [body(): homes.append(lax.all_to_all(back, SEQ, 0, 0, tiled=True))]
    all_to_all x1, blocking collectives: 60.1 us -> 28.5 us  [body(): merged = lax.all_to_all(state, ROUND, 0, 0, tiled=True)]
    ppermute x2 -> x19, starting transfers between devices: 2.53 us -> 32.7 us  [the longest x16 24.3 us: ring(): return lax.ppermute(value, ('zl', 'zh'), route)]
    ppermute x2 -> x19, waiting for transfers between devices: 22.9 us -> 49.3 us  [the longest x16 46.4 us: ring(): return lax.ppermute(value, ('zl', 'zh'), route)]
    all_to_all x3 -> x4, waiting for transfers between devices: 51.4 us -> 29.6 us  [the longest x2 16.8 us: ring_first(): return lax.all_to_all(joint, PLANE, 0, 0, tiled=True)]
    all_to_all x3 -> x4, starting transfers between devices: 45.2 us -> 28.3 us  [the longest x2 15 us: plane_first(): joint = lax.all_to_all(joint, PLANE, 0, 0, tiled=True)]
    squeeze x1 -> x5, local copies, waits for them, and re-layouts: 0.01 us -> 6.47 us  [the longest x4 6.46 us: plane_first(): split = [joint[:, 0], joint[:, 1], joint[:, 2], joint[:8, 3], joint[8:, 3]]]
    pallas_call x8 -> x10, Pallas kernels: 49.7 us -> 53.5 us  [the longest x1 16.5 us: home_rows(): pl.pallas_call(functools.partial(home_kernel, width, splits), grid_spec=p...]
  transfers between devices with their start and end apart: 5 -> 23, of which waited for: 4 -> 10; matrix products, arithmetic and copies ran while one was open for 0% -> 4% of each run, Pallas kernels for 14% -> 18%
where the time goes in v2:
time: 258 us; the launch traced here: 257 us
  waiting for transfers between devices  78.9 us (31%)
  Pallas kernels  71.2 us (28%)
  starting transfers between devices  61 us (24%)
  blocking collectives  28.5 us (11%)
  local copies, waits for them, and re-layouts  13.9 us (5%)
  other arithmetic  3.41 us (1%)
    ppermute x16, waiting for transfers between devices, ring(): return lax.ppermute(value, ('zl', 'zh'), route)  46.4 us
    all_to_all x1, blocking collectives, body(): merged = lax.all_to_all(state, ROUND, 0, 0, tiled=True)  28.5 us
    ppermute x16, starting transfers between devices, ring(): return lax.ppermute(value, ('zl', 'zh'), route)  24.3 us
    all_to_all x2, waiting for transfers between devices, ring_first(): return lax.all_to_all(joint, PLANE, 0, 0, tiled=True)  16.8 us
    pallas_call x1, Pallas kernels, home_rows(): pl.pallas_call(functools.partial(home_kernel, width, splits), grid_spec=p...  16.5 us
    pallas_call x2, Pallas kernels, sort_rows(): pl.pallas_call(sort_kernel, grid=(blocks,), in_specs=[pl.BlockSpec((1, 1,...  15.8 us
    all_to_all x2, starting transfers between devices, plane_first(): joint = lax.all_to_all(joint, PLANE, 0, 0, tiled=True)  15 us
    all_to_all x2, starting transfers between devices, ring_first(): return lax.all_to_all(joint, PLANE, 0, 0, tiled=True)  13.3 us
  transfers between devices with their start and end apart: 23, of which 10 were waited for; matrix products, arithmetic and copies ran while one was open for 4% of the time, Pallas kernels for 18%

profile of v2, /device:TPU:35, one launch (start us, length us, event | category | flops | bytes accessed | tf_op | source)
XLA Modules:
  0.0 257.1 jit_solution(6149650865216129297)
XLA Ops:
  0.0 6.0 %collective-permute-start = (s32[2,2048]{1,0:T(2,128)}, s32[2,2048]{1,0:T(2,128)S(1)}, u32[]{:S(2)}, u32[]{:S(2)}) collective-permute-start(s32[2,2048]{1,0:T(2,128)} %param.11), channel_id=1, source_target_pairs={{0,2},{2,0},{1,3},{3,1},{4,6},{6,4},{5,7},{7,5},{8,10},{10,8},{9,1... | collective-permute-start | bytes 49160 | tf_op jit(solution)/shard_map/ppermute | solution.py:488
  12.5 6.0 %scatter_rows.2 = (bf16[16,64,256]{2,1,0:T(8,128)(2,1)S(1)}, bf16[16,64,256]{2,1,0:T(8,128)(2,1)S(1)}, bf16[16,64,256]{2,1,0:T(8,128)(2,1)S(1)}, bf16[8,64,256]{2,1,0:T(8,128)(2,1)S(1)}, bf16[8,64,256]{2,1,0:T(8,128)(2,1)S(1)}) custom-call(s32[5,2048]{1,0:T(8,128)S(1)} %stack.76.idx_ref, bf16[2048,256]{1,0:T(8,128)(2,1)S(1)} %project.1.rows_ref), custom_call_target="tpu_custom_call" | custom-call | tf_op jit(solution)/shard_map/scatter_rows/pallas_call | solution.py:135
  23.6 20.3 %collective-permute-done.3 = bf16[8,64,256]{2,1,0:T(8,128)(2,1)S(1)} collective-permute-done((bf16[8,64,256]{2,1,0:T(8,128)(2,1)S(1)}, bf16[8,64,256]{2,1,0:T(8,128)(2,1)S(1)}, u32[]{:S(2)}, u32[]{:S(2)}) %collective-permute-start.3) | collective-permute-done | bytes 262176 | tf_op jit(solution)/shard_map/ppermute | solution.py:73
  45.6 6.9 %all-to-all-start = ((bf16[16,4,64,256]{3,2,1,0:T(8,128)(2,1)}), bf16[16,4,64,256]{3,2,1,0:T(8,128)(2,1)S(1)}, u32[]{:S(2)}, u32[]{:S(2)}) async-start(bf16[16,4,64,256]{3,2,1,0:T(8,128)(2,1)} %pad_maximum_fusion), calls=%async_computation | async-start | bytes 4194304 | tf_op jit(solution)/shard_map/all_to_all | solution.py:83
  52.6 5.9 %scatter_rows.3 = bf16[16,4,64,256]{3,2,1,0:T(8,128)(2,1)S(1)} custom-call(s32[5,2048]{1,0:T(8,128)S(1)} %stack.82.idx_ref, bf16[2048,256]{1,0:T(8,128)(2,1)S(1)} %project.1.rows_ref), custom_call_target="tpu_custom_call" | custom-call | tf_op jit(solution)/shard_map/scatter_rows/pallas_call | solution.py:135
  59.9 16.8 %all-to-all-done.refs_0_ = bf16[16,4,64,256]{3,2,1,0:T(8,128)(2,1)S(1)} async-done(((bf16[16,4,64,256]{3,2,1,0:T(8,128)(2,1)}), bf16[16,4,64,256]{3,2,1,0:T(8,128)(2,1)S(1)}, u32[]{:S(2)}, u32[]{:S(2)}) %all-to-all-start) | async-done | bytes 2097184 | tf_op jit(solution)/shard_map/all_to_all | solution.py:83
  76.7 7.0 %all-to-all-start.2 = ((bf16[16,4,64,256]{3,2,1,0:T(8,128)(2,1)}), bf16[16,4,64,256]{3,2,1,0:T(8,128)(2,1)}, u32[]{:S(2)}, u32[]{:S(2)}) async-start(bf16[16,4,64,256]{3,2,1,0:T(8,128)(2,1)} %copy-done), calls=%async_computation.2 | async-start | bytes 4194304 | tf_op jit(solution)/shard_map/all_to_all | solution.py:87
  83.9 7.9 %sort_rows.2 = (bf16[2048,128]{1,0:T(8,128)(2,1)S(1)}, bf16[2048,256]{1,0:T(8,128)(2,1)S(1)}) custom-call(s32[8,1,256]{2,1,0:T(1,128)S(1)} %compare_select_fusion.3.idx_ref, bf16[16,4,64,256]{3,2,1,0:T(8,128)(2,1)S(1)} %all-to-all-done.refs_0_), custom_call_target="tpu_custom_call" | custom-call | tf_op jit(solution)/shard_map/sort_rows/pallas_call | solution.py:166
  94.5 12.8 %all-to-all-done.2 = bf16[16,4,64,256]{3,2,1,0:T(8,128)(2,1)} async-done(((bf16[16,4,64,256]{3,2,1,0:T(8,128)(2,1)}), bf16[16,4,64,256]{3,2,1,0:T(8,128)(2,1)}, u32[]{:S(2)}, u32[]{:S(2)}) %all-to-all-start.2) | async-done | bytes 2097184 | tf_op jit(solution)/shard_map/all_to_all | solution.py:87
  109.8 5.7 %collective-permute-start.10 = (bf16[16,64,256]{2,1,0:T(8,128)(2,1)}, bf16[16,64,256]{2,1,0:T(8,128)(2,1)S(1)}, u32[]{:S(2)}, u32[]{:S(2)}) collective-permute-start(bf16[16,64,256]{2,1,0:T(8,128)(2,1)} %get-tuple-element.42), channel_id=1, source_target_pairs={{0,64},{64,128},{128,192},{192,2},{2,66},{66,130},{130,194},{194,0... | collective-permute-start | bytes 1572872 | tf_op jit(solution)/shard_map/ppermute | solution.py:73
  115.6 3.4 %attend_inner.2.refs_1_ = bf16[1536,256]{1,0:T(8,128)(2,1)S(1)} custom-call(s32[8]{0:T(128)S(1)} %get-tuple-element.66.dist_ref, bf16[2048,128]{1,0:T(8,128)(2,1)S(1)} %copy-done.3, bf16[2048,256]{1,0:T(8,128)(2,1)S(1)} %get-tuple-element.25.kv_ref), custom_call_target="tpu_custom_call" | custom-call | tf_op jit(solution)/shard_map/attend_inner/pallas_call | solution.py:255
  120.6 6.7 %back_rows.2 = bf16[16,4,72,128]{3,2,1,0:T(8,128)(2,1)} custom-call(s32[1,2048]{1,0:T(1,128)S(1)} %get-tuple-element.61.idx_ref, bf16[512,256]{1,0:T(8,128)(2,1)S(1)} %attend_edge.2.refs_0_, bf16[1536,256]{1,0:T(8,128)(2,1)S(1)} %attend_inner.2.refs_1_), custom_call_target="tpu_custom_call" | custom-call | tf_op jit(solution)/shard_map/back_rows/pallas_call | solution.py:316
  127.2 8.0 %all-to-all-start.1 = ((bf16[16,4,72,128]{3,2,1,0:T(8,128)(2,1)}), bf16[16,4,72,128]{3,2,1,0:T(8,128)(2,1)}, u32[]{:S(2)}, u32[]{:S(2)}) async-start(bf16[16,4,72,128]{3,2,1,0:T(8,128)(2,1)} %back_rows.2), calls=%async_computation.1 | async-start | bytes 2359296 | tf_op jit(solution)/shard_map/all_to_all | solution.py:87
  140.2 7.5 %collective-permute-done.12.refs_3_ = bf16[8,64,256]{2,1,0:T(8,128)(2,1)S(1)} collective-permute-done((bf16[8,64,256]{2,1,0:T(8,128)(2,1)S(1)}, bf16[8,64,256]{2,1,0:T(8,128)(2,1)S(1)}, u32[]{:S(2)}, u32[]{:S(2)}) %collective-permute-start.12) | collective-permute-done | bytes 262176 | tf_op jit(solution)/shard_map/ppermute | solution.py:73
  150.3 7.9 %sort_rows.3 = (bf16[2048,128]{1,0:T(8,128)(2,1)S(1)}, bf16[2048,256]{1,0:T(8,128)(2,1)S(1)}) custom-call(s32[8,1,256]{2,1,0:T(1,128)S(1)} %compare_select_fusion.idx_ref, bf16[16,64,256]{2,1,0:T(8,128)(2,1)S(1)} %get-tuple-element.43.refs_0_, bf16[16,64,256]{2,1,0:T(8,128)(2,1)S(1)} %collective-permute-done.10.refs_1_, ...), custom_call_target="tpu_custom_call" | custom-call | tf_op jit(solution)/shard_map/sort_rows/pallas_call | solution.py:166
  159.4 3.4 %attend_inner.3.refs_1_ = bf16[1536,256]{1,0:T(8,128)(2,1)S(1)} custom-call(s32[8]{0:T(128)S(1)} %get-tuple-element.65.dist_ref, bf16[2048,128]{1,0:T(8,128)(2,1)S(1)} %get-tuple-element.26.q_ref, bf16[2048,256]{1,0:T(8,128)(2,1)S(1)} %get-tuple-element.27.kv_ref), custom_call_target="tpu_custom_call" | custom-call | tf_op jit(solution)/shard_map/attend_inner/pallas_call | solution.py:255
  167.2 6.0 %back_rows.3 = (bf16[16,72,128]{2,1,0:T(8,128)(2,1)S(1)}, bf16[16,72,128]{2,1,0:T(8,128)(2,1)S(1)}, bf16[16,72,128]{2,1,0:T(8,128)(2,1)S(1)}, bf16[8,72,128]{2,1,0:T(8,128)(2,1)S(1)}, bf16[8,72,128]{2,1,0:T(8,128)(2,1)S(1)}) custom-call(s32[1,2048]{1,0:T(1,128)S(1)} %get-tuple-element.33.idx_ref, bf16[512,256]{1,0:T(8,128)(2,1)S(1)} %attend_edge.3.refs_0_, ...), custom_call_target="tpu_custom_call" | custom-call | tf_op jit(solution)/shard_map/back_rows/pallas_call | solution.py:316
  174.8 4.2 %collective-permute-start.17 = (bf16[8,72,128]{2,1,0:T(8,128)(2,1)S(1)}, bf16[8,72,128]{2,1,0:T(8,128)(2,1)S(1)}, u32[]{:S(2)}, u32[]{:S(2)}) collective-permute-start(bf16[8,72,128]{2,1,0:T(8,128)(2,1)S(1)} %get-tuple-element.31), channel_id=1, source_target_pairs={{0,130},{64,194},{128,0},{192,64},{2,128},{66,192},{130,2},{194,66... | collective-permute-start | bytes 442376 | tf_op jit(solution)/shard_map/ppermute | solution.py:73
  179.0 5.0 %collective-permute-done.17 = bf16[8,72,128]{2,1,0:T(8,128)(2,1)S(1)} collective-permute-done((bf16[8,72,128]{2,1,0:T(8,128)(2,1)S(1)}, bf16[8,72,128]{2,1,0:T(8,128)(2,1)S(1)}, u32[]{:S(2)}, u32[]{:S(2)}) %collective-permute-start.17) | collective-permute-done | bytes 147488 | tf_op jit(solution)/shard_map/ppermute | solution.py:73
  184.0 3.9 %collective-permute-done.18 = bf16[8,72,128]{2,1,0:T(8,128)(2,1)S(1)} collective-permute-done((bf16[8,72,128]{2,1,0:T(8,128)(2,1)S(1)}, bf16[8,72,128]{2,1,0:T(8,128)(2,1)S(1)}, u32[]{:S(2)}, u32[]{:S(2)}) %collective-permute-start.18) | collective-permute-done | bytes 147488 | tf_op jit(solution)/shard_map/ppermute | solution.py:73
  189.2 6.3 %all-to-all-start.3 = ((bf16[16,4,72,128]{3,2,1,0:T(8,128)(2,1)}), bf16[16,4,72,128]{3,2,1,0:T(8,128)(2,1)S(1)}, u32[]{:S(2)}, u32[]{:S(2)}) async-start(bf16[16,4,72,128]{3,2,1,0:T(8,128)(2,1)} %pad_maximum_fusion.1), calls=%async_computation.3 | async-start | bytes 2359296 | tf_op jit(solution)/shard_map/all_to_all | solution.py:83
  202.6 5.2 %collective-permute-done.8.refs_3_ = bf16[8,72,128]{2,1,0:T(8,128)(2,1)S(1)} collective-permute-done((bf16[8,72,128]{2,1,0:T(8,128)(2,1)}, bf16[8,72,128]{2,1,0:T(8,128)(2,1)S(1)}, u32[]{:S(2)}, u32[]{:S(2)}) %collective-permute-start.8) | collective-permute-done | bytes 147488 | tf_op jit(solution)/shard_map/ppermute | solution.py:73
  209.7 16.5 %home_rows.1 = bf16[4,528,128]{2,1,0:T(8,128)(2,1)S(1)} custom-call(s32[10]{0:T(128)S(1)} %concatenate.38.own_ref, s32[4,10,512]{2,1,0:T(8,128)S(1)} %bitcast.77, bf16[16,72,128]{2,1,0:T(8,128)(2,1)S(1)} %get-tuple-element.48.refs_0_, bf16[16,72,128]{2,1,0:T(8,128)(2,1)S(1)} %collective-permute-done.6.refs_1_, ...), custom_call_target="tpu_custom_call" | custom-call | tf_op jit(solution)/shard_map/home_rows/pallas_call | solution.py:399
  226.1 28.5 %all_to_all.25.m_ref = bf16[4,528,128]{2,1,0:T(8,128)(2,1)S(1)} all-to-all(bf16[4,528,128]{2,1,0:T(8,128)(2,1)S(1)} %home_rows.1), channel_id=1, replica_groups=mesh['zl'=4,'x'=4,'y'=4,'zh'=2,'c'=2] {'zh','c'}, dimensions={0} | all-to-all | bytes 1081344 | tf_op jit(solution)/shard_map/all_to_all | solution.py:529
  (91 shorter events, 48.8 us)
Async XLA Ops:
  0.0 12.0 %collective-permute-start = (s32[2,2048]{1,0:T(2,128)}, s32[2,2048]{1,0:T(2,128)S(1)}, u32[]{:S(2)}, u32[]{:S(2)}) collective-permute-start(s32[2,2048]{1,0:T(2,128)} %param.11), channel_id=1, source_target_pairs={{0,2},{2,0},{1,3},{3,1},{4,6},{6,4},{5,7},{7,5},{8,10},{10,8},{9,1... | collective-permute-start | bytes 49160 | tf_op jit(solution)/shard_map/ppermute | solution.py:488
  18.5 25.5 %collective-permute-start.1 = (bf16[16,64,256]{2,1,0:T(8,128)(2,1)S(1)}, bf16[16,64,256]{2,1,0:T(8,128)(2,1)S(1)}, u32[]{:S(2)}, u32[]{:S(2)}) collective-permute-start(bf16[16,64,256]{2,1,0:T(8,128)(2,1)S(1)} %get-tuple-element.20), channel_id=1, source_target_pairs={{0,64},{64,128},{128,192},{192,2},{2,66},{66,130},{130,194},{194,0... | collective-permute-start | bytes 1572872 | tf_op jit(solution)/shard_map/ppermute | solution.py:73
  19.3 24.7 %collective-permute-start.2 = (bf16[16,64,256]{2,1,0:T(8,128)(2,1)S(1)}, bf16[16,64,256]{2,1,0:T(8,128)(2,1)S(1)}, u32[]{:S(2)}, u32[]{:S(2)}) collective-permute-start(bf16[16,64,256]{2,1,0:T(8,128)(2,1)S(1)} %get-tuple-element.21), channel_id=1, source_target_pairs={{0,194},{64,0},{128,64},{192,128},{2,192},{66,2},{130,66},{194,130... | collective-permute-start | bytes 1572872 | tf_op jit(solution)/shard_map/ppermute | solution.py:73
  20.1 23.9 %collective-permute-start.3 = (bf16[8,64,256]{2,1,0:T(8,128)(2,1)S(1)}, bf16[8,64,256]{2,1,0:T(8,128)(2,1)S(1)}, u32[]{:S(2)}, u32[]{:S(2)}) collective-permute-start(bf16[8,64,256]{2,1,0:T(8,128)(2,1)S(1)} %get-tuple-element.22), channel_id=1, source_target_pairs={{0,128},{64,192},{128,2},{192,66},{2,130},{66,194},{130,0},{194,64... | collective-permute-start | bytes 786440 | tf_op jit(solution)/shard_map/ppermute | solution.py:73
  21.3 22.7 %collective-permute-start.4 = (bf16[8,64,256]{2,1,0:T(8,128)(2,1)S(1)}, bf16[8,64,256]{2,1,0:T(8,128)(2,1)S(1)}, u32[]{:S(2)}, u32[]{:S(2)}) collective-permute-start(bf16[8,64,256]{2,1,0:T(8,128)(2,1)S(1)} %get-tuple-element.23), channel_id=1, source_target_pairs={{0,130},{64,194},{128,0},{192,64},{2,128},{66,192},{130,2},{194,66... | collective-permute-start | bytes 786440 | tf_op jit(solution)/shard_map/ppermute | solution.py:73
  45.6 31.0 %all-to-all-start = ((bf16[16,4,64,256]{3,2,1,0:T(8,128)(2,1)}), bf16[16,4,64,256]{3,2,1,0:T(8,128)(2,1)S(1)}, u32[]{:S(2)}, u32[]{:S(2)}) async-start(bf16[16,4,64,256]{3,2,1,0:T(8,128)(2,1)} %pad_maximum_fusion), calls=%async_computation | async-start | bytes 4194304 | tf_op jit(solution)/shard_map/all_to_all | solution.py:83
  76.7 30.7 %all-to-all-start.2 = ((bf16[16,4,64,256]{3,2,1,0:T(8,128)(2,1)}), bf16[16,4,64,256]{3,2,1,0:T(8,128)(2,1)}, u32[]{:S(2)}, u32[]{:S(2)}) async-start(bf16[16,4,64,256]{3,2,1,0:T(8,128)(2,1)} %copy-done), calls=%async_computation.2 | async-start | bytes 4194304 | tf_op jit(solution)/shard_map/all_to_all | solution.py:87
  93.3 25.7 %collective-permute-start.5 = (bf16[512,256]{1,0:T(8,128)(2,1)}, bf16[512,256]{1,0:T(8,128)(2,1)S(1)}, u32[]{:S(2)}, u32[]{:S(2)}) collective-permute-start(bf16[512,256]{1,0:T(8,128)(2,1)} %slice.68), channel_id=1, source_target_pairs={{0,4},{4,8},{8,12},{12,16},{16,20},{20,24},{24,28},{28,32},{32,36}... | collective-permute-start | bytes 786440 | tf_op jit(solution)/shard_map/ppermute | solution.py:517
  109.8 40.5 %collective-permute-start.10 = (bf16[16,64,256]{2,1,0:T(8,128)(2,1)}, bf16[16,64,256]{2,1,0:T(8,128)(2,1)S(1)}, u32[]{:S(2)}, u32[]{:S(2)}) collective-permute-start(bf16[16,64,256]{2,1,0:T(8,128)(2,1)} %get-tuple-element.42), channel_id=1, source_target_pairs={{0,64},{64,128},{128,192},{192,2},{2,66},{66,130},{130,194},{194,0... | collective-permute-start | bytes 1572872 | tf_op jit(solution)/shard_map/ppermute | solution.py:73
  115.6 34.8 %collective-permute-start.11 = (bf16[16,64,256]{2,1,0:T(8,128)(2,1)}, bf16[16,64,256]{2,1,0:T(8,128)(2,1)S(1)}, u32[]{:S(2)}, u32[]{:S(2)}) collective-permute-start(bf16[16,64,256]{2,1,0:T(8,128)(2,1)} %get-tuple-element.41), channel_id=1, source_target_pairs={{0,194},{64,0},{128,64},{192,128},{2,192},{66,2},{130,66},{194,130... | collective-permute-start | bytes 1572872 | tf_op jit(solution)/shard_map/ppermute | solution.py:73
  127.2 62.0 %all-to-all-start.1 = ((bf16[16,4,72,128]{3,2,1,0:T(8,128)(2,1)}), bf16[16,4,72,128]{3,2,1,0:T(8,128)(2,1)}, u32[]{:S(2)}, u32[]{:S(2)}) async-start(bf16[16,4,72,128]{3,2,1,0:T(8,128)(2,1)} %back_rows.2), calls=%async_computation.1 | async-start | bytes 2359296 | tf_op jit(solution)/shard_map/all_to_all | solution.py:87
  136.3 11.4 %collective-permute-start.12 = (bf16[8,64,256]{2,1,0:T(8,128)(2,1)S(1)}, bf16[8,64,256]{2,1,0:T(8,128)(2,1)S(1)}, u32[]{:S(2)}, u32[]{:S(2)}) collective-permute-start(bf16[8,64,256]{2,1,0:T(8,128)(2,1)S(1)} %get-tuple-element.40), channel_id=1, source_target_pairs={{0,128},{64,192},{128,2},{192,66},{2,130},{66,194},{130,0},{194,64... | collective-permute-start | bytes 786440 | tf_op jit(solution)/shard_map/ppermute | solution.py:73
  136.8 13.5 %collective-permute-start.13 = (bf16[8,64,256]{2,1,0:T(8,128)(2,1)S(1)}, bf16[8,64,256]{2,1,0:T(8,128)(2,1)S(1)}, u32[]{:S(2)}, u32[]{:S(2)}) collective-permute-start(bf16[8,64,256]{2,1,0:T(8,128)(2,1)S(1)} %get-tuple-element.39), channel_id=1, source_target_pairs={{0,130},{64,194},{128,0},{192,64},{2,128},{66,192},{130,2},{194,66... | collective-permute-start | bytes 786440 | tf_op jit(solution)/shard_map/ppermute | solution.py:73
  158.3 7.4 %collective-permute-start.14 = (bf16[512,256]{1,0:T(8,128)(2,1)S(1)}, bf16[512,256]{1,0:T(8,128)(2,1)S(1)}, u32[]{:S(2)}, u32[]{:S(2)}) collective-permute-start(bf16[512,256]{1,0:T(8,128)(2,1)S(1)} %slice.81), channel_id=1, source_target_pairs={{0,4},{4,8},{8,12},{12,16},{16,20},{20,24},{24,28},{28,32},{32,36}... | collective-permute-start | bytes 786440 | tf_op jit(solution)/shard_map/ppermute | solution.py:517
  173.2 14.7 %collective-permute-start.15 = (bf16[16,72,128]{2,1,0:T(8,128)(2,1)S(1)}, bf16[16,72,128]{2,1,0:T(8,128)(2,1)S(1)}, u32[]{:S(2)}, u32[]{:S(2)}) collective-permute-start(bf16[16,72,128]{2,1,0:T(8,128)(2,1)S(1)} %get-tuple-element.29), channel_id=1, source_target_pairs={{0,194},{64,0},{128,64},{192,128},{2,192},{66,2},{130,66},{194,130... | collective-permute-start | bytes 884744 | tf_op jit(solution)/shard_map/ppermute | solution.py:73
  173.3 14.6 %collective-permute-start.16 = (bf16[16,72,128]{2,1,0:T(8,128)(2,1)S(1)}, bf16[16,72,128]{2,1,0:T(8,128)(2,1)S(1)}, u32[]{:S(2)}, u32[]{:S(2)}) collective-permute-start(bf16[16,72,128]{2,1,0:T(8,128)(2,1)S(1)} %get-tuple-element.30), channel_id=1, source_target_pairs={{0,64},{64,128},{128,192},{192,2},{2,66},{66,130},{130,194},{194,0... | collective-permute-start | bytes 884744 | tf_op jit(solution)/shard_map/ppermute | solution.py:73
  174.8 9.2 %collective-permute-start.17 = (bf16[8,72,128]{2,1,0:T(8,128)(2,1)S(1)}, bf16[8,72,128]{2,1,0:T(8,128)(2,1)S(1)}, u32[]{:S(2)}, u32[]{:S(2)}) collective-permute-start(bf16[8,72,128]{2,1,0:T(8,128)(2,1)S(1)} %get-tuple-element.31), channel_id=1, source_target_pairs={{0,130},{64,194},{128,0},{192,64},{2,128},{66,192},{130,2},{194,66... | collective-permute-start | bytes 442376 | tf_op jit(solution)/shard_map/ppermute | solution.py:73
  179.0 8.9 %collective-permute-start.18 = (bf16[8,72,128]{2,1,0:T(8,128)(2,1)S(1)}, bf16[8,72,128]{2,1,0:T(8,128)(2,1)S(1)}, u32[]{:S(2)}, u32[]{:S(2)}) collective-permute-start(bf16[8,72,128]{2,1,0:T(8,128)(2,1)S(1)} %get-tuple-element.32), channel_id=1, source_target_pairs={{0,128},{64,192},{128,2},{192,66},{2,130},{66,194},{130,0},{194,64... | collective-permute-start | bytes 442376 | tf_op jit(solution)/shard_map/ppermute | solution.py:73
  189.2 20.5 %all-to-all-start.3 = ((bf16[16,4,72,128]{3,2,1,0:T(8,128)(2,1)}), bf16[16,4,72,128]{3,2,1,0:T(8,128)(2,1)S(1)}, u32[]{:S(2)}, u32[]{:S(2)}) async-start(bf16[16,4,72,128]{3,2,1,0:T(8,128)(2,1)} %pad_maximum_fusion.1), calls=%async_computation.3 | async-start | bytes 2359296 | tf_op jit(solution)/shard_map/all_to_all | solution.py:83
  196.7 12.9 %collective-permute-start.6 = (bf16[16,72,128]{2,1,0:T(8,128)(2,1)S(1)}, bf16[16,72,128]{2,1,0:T(8,128)(2,1)S(1)}, u32[]{:S(2)}, u32[]{:S(2)}) collective-permute-start(bf16[16,72,128]{2,1,0:T(8,128)(2,1)S(1)} %get-tuple-element.47), channel_id=1, source_target_pairs={{0,194},{64,0},{128,64},{192,128},{2,192},{66,2},{130,66},{194,130... | collective-permute-start | bytes 884744 | tf_op jit(solution)/shard_map/ppermute | solution.py:73
  196.8 12.8 %collective-permute-start.7 = (bf16[16,72,128]{2,1,0:T(8,128)(2,1)S(1)}, bf16[16,72,128]{2,1,0:T(8,128)(2,1)S(1)}, u32[]{:S(2)}, u32[]{:S(2)}) collective-permute-start(bf16[16,72,128]{2,1,0:T(8,128)(2,1)S(1)} %get-tuple-element.46), channel_id=1, source_target_pairs={{0,64},{64,128},{128,192},{192,2},{2,66},{66,130},{130,194},{194,0... | collective-permute-start | bytes 884744 | tf_op jit(solution)/shard_map/ppermute | solution.py:73
  200.0 7.9 %collective-permute-start.8 = (bf16[8,72,128]{2,1,0:T(8,128)(2,1)}, bf16[8,72,128]{2,1,0:T(8,128)(2,1)S(1)}, u32[]{:S(2)}, u32[]{:S(2)}) collective-permute-start(bf16[8,72,128]{2,1,0:T(8,128)(2,1)} %get-tuple-element.45), channel_id=1, source_target_pairs={{0,130},{64,194},{128,0},{192,64},{2,128},{66,192},{130,2},{194,66... | collective-permute-start | bytes 442376 | tf_op jit(solution)/shard_map/ppermute | solution.py:73
  201.0 8.6 %collective-permute-start.9 = (bf16[8,72,128]{2,1,0:T(8,128)(2,1)S(1)}, bf16[8,72,128]{2,1,0:T(8,128)(2,1)S(1)}, u32[]{:S(2)}, u32[]{:S(2)}) collective-permute-start(bf16[8,72,128]{2,1,0:T(8,128)(2,1)S(1)} %get-tuple-element.44), channel_id=1, source_target_pairs={{0,128},{64,192},{128,2},{192,66},{2,130},{66,194},{130,0},{194,64... | collective-permute-start | bytes 442376 | tf_op jit(solution)/shard_map/ppermute | solution.py:73
  202.6 52.0 %copy-start.6 = (bf16[128,1024]{1,0:T(8,128)(2,1)S(1)}, bf16[128,1024]{1,0:T(8,128)(2,1)}, u32[]{:S(2)}) copy-start(bf16[128,1024]{1,0:T(8,128)(2,1)} %w_ref.1) | copy-start | bytes 786436
  (15 other events, 232.2 us)

commit v3 on v2

--- a/solution.py
+++ b/solution.py
@@ -77,55 +77,61 @@
     return [pieces[0]] + [ring(p, sign * k) for p, k in zip(pieces[1:], SHIFTS[1:])]
 
 
-def ring_first(split, sign):
-    a, b, c, d, e = ring_all(split, sign)
-    joint = jnp.stack([a, b, c, jnp.concatenate([d, e])], axis=1)
+def join(split):
+    a, b, c, d, e = split
+    return jnp.stack([a, b, c, jnp.concatenate([d, e])], axis=1)
+
+
+def part(joint):
+    return [joint[:, 0], joint[:, 1], joint[:, 2], joint[:8, 3], joint[8:, 3]]
+
+
+def plane(joint):
     return lax.all_to_all(joint, PLANE, 0, 0, tiled=True)
 
 
-def plane_first(joint, sign):
-    joint = lax.all_to_all(joint, PLANE, 0, 0, tiled=True)
-    split = [joint[:, 0], joint[:, 1], joint[:, 2], joint[:8, 3], joint[8:, 3]]
-    return ring_all(split, sign)
+together = lax.optimization_barrier
 
 
 def emit_specs(split, width, lanes):
     if not split:
         return (
-            [pl.BlockSpec((8, 1, width, lanes), lambda i: (i % 2, i // 2, 0, 0))],
+            [pl.BlockSpec((16, 1, width, lanes), lambda i: (0, i, 0, 0))],
             [jax.ShapeDtypeStruct((16, 4, width, lanes), BF)],
         )
-
-    def spec(first):
-        return pl.BlockSpec((8, width, lanes), lambda i: (jnp.clip(i - first, 0, 1), 0, 0))
-
-    big = jax.ShapeDtypeStruct((16, width, lanes), BF)
-    small = jax.ShapeDtypeStruct((8, width, lanes), BF)
-    return [spec(0), spec(2), spec(4)] + [whole(small.shape)] * 2, [big] * 3 + [small] * 2
+    shapes = [(16, width, lanes)] * 3 + [(8, width, lanes)] * 2
+    return [whole(v) for v in shapes], [jax.ShapeDtypeStruct(v, BF) for v in shapes]
 
 
 def emit(refs, store):
     if len(refs) == 1:
-        store(refs[0].at[:, 0])
+        for half in range(2):
+            store(refs[0].at[8 * half : 8 * half + 8, 0], half)
         return
-    step = pl.program_id(0)
-    for ref, (first, last) in zip(refs, ((0, 1), (2, 3), (4, 5), (6, 6), (7, 7))):
-
-        @pl.when((step >= first) & (step <= last))
-        def _(ref=ref):
-            store(ref)
+    for group in range(4):
+
+        @pl.when(pl.program_id(0) == group)
+        def _(group=group):
+            for half in range(2):
+                if group < 3:
+                    store(refs[group].at[8 * half : 8 * half + 8], half)
+                else:
+                    store(refs[3 + half], half)
 
 
 def scatter_kernel(width, idx_ref, rows_ref, *out_refs):
     n = 8 * width
-    step = pl.program_id(0)
-    line = idx_ref[pl.ds(jnp.where(step == 7, 4, step // 2), 1), :]
+    group = pl.program_id(0)
     place = lax.broadcasted_iota(jnp.int32, (n, rows_ref.shape[0]), 0)
-    hot = one_hot(line - (step % 2) * n, place)
-    got = jnp.dot(hot, rows_ref[...], preferred_element_type=F32).astype(BF)
-
-    def store(ref):
-        ref[...] = got.reshape(8, width, 256)
+    halves = []
+    for half in range(2):
+        line = idx_ref[pl.ds(jnp.where(group == 3, 3 + half, group), 1), :]
+        hot = one_hot(line - half * n, place)
+        got = jnp.dot(hot, rows_ref[...], preferred_element_type=F32).astype(BF)
+        halves.append(got.reshape(8, width, 256))
+
+    def store(ref, half):
+        ref[...] = halves[half]
 
     emit(out_refs, store)
 
@@ -134,7 +140,7 @@
     specs, shapes = emit_specs(split, width, 256)
     return pl.pallas_call(
         functools.partial(scatter_kernel, width),
-        grid=(8,),
+        grid=(4,),
         in_specs=[whole(idx.shape), whole(rows.shape)],
         out_specs=specs,
         out_shape=shapes,
@@ -150,7 +156,7 @@
     for ref in row_refs:
         rows = ref[...].reshape(-1, 256)
         n = rows.shape[0]
-        place = lax.broadcasted_iota(jnp.int32, (BLOCK, n), 1) + base
+        place = lax.broadcasted_iota(jnp.int32, (q_ref.shape[0], n), 1) + base
         got += jnp.dot(one_hot(col, place), rows, preferred_element_type=F32)
         base += n
     qk = got[:, :128]
@@ -160,17 +166,17 @@
     kv_ref[:, 128:] = got[:, 128:].astype(BF)
 
 
-def sort_rows(idx, rows):
+def sort_rows(idx, rows, step):
     count = idx.shape[-1]
-    blocks = count // BLOCK
+    blocks = count // step
     return pl.pallas_call(
         sort_kernel,
         grid=(blocks,),
-        in_specs=[pl.BlockSpec((1, 1, BLOCK), lambda i: (i, 0, 0))]
+        in_specs=[pl.BlockSpec((1, 1, step), lambda i: (i, 0, 0))]
         + [whole(r.shape) for r in rows],
         out_specs=[
-            pl.BlockSpec((BLOCK, 128), lambda i: (i, 0)),
-            pl.BlockSpec((BLOCK, 256), lambda i: (i, 0)),
+            pl.BlockSpec((step, 128), lambda i: (i, 0)),
+            pl.BlockSpec((step, 256), lambda i: (i, 0)),
         ],
         out_shape=[
             jax.ShapeDtypeStruct((count, 128), BF),
@@ -178,7 +184,7 @@
         ],
         compiler_params=params(),
         name="sort_rows",
-    )(idx.reshape(blocks, 1, BLOCK), *rows)
+    )(idx.reshape(blocks, 1, step), *rows)
 
 
 def terms_to_lines(terms, groups):
@@ -234,11 +240,21 @@
     out_ref[:, 128:] = term_lanes(top + jnp.log(total), BLOCK)
 
 
-def inner_kernel(dist_ref, q_ref, kv_ref, out_ref):
+def inner_kernel(dist_ref, qh_ref, qt_ref, kvh_ref, kvt_ref, out_ref, q_ref, kv_ref):
+    head = kvh_ref.shape[0]
+
+    @pl.when(pl.program_id(0) == 0)
+    def _():
+        q_ref[:head] = qh_ref[...]
+        q_ref[head:] = qt_ref[...]
+        kv_ref[:head] = kvh_ref[...]
+        kv_ref[head:] = kvt_ref[...]
+
+    def block(ref, c):
+        return ref[pl.ds(pl.multiple_of(c * BLOCK, BLOCK), BLOCK), :]
+
     c = pl.program_id(0) + 2
-    own = kv_ref[pl.ds(pl.multiple_of(c * BLOCK, BLOCK), BLOCK), :]
-    behind = kv_ref[pl.ds(pl.multiple_of((c - dist_ref[c]) * BLOCK, BLOCK), BLOCK), :]
-    attend_block(q_ref[...], own, behind, out_ref)
+    attend_block(block(q_ref, c), block(kv_ref, c), block(kv_ref, c - dist_ref[c]), out_ref)
 
 
 def edge_kernel(dist_ref, q_ref, kv_ref, halo_ref, out_ref):
@@ -250,20 +266,22 @@
     attend_block(q_ref[...], own, behind, out_ref)
 
 
-def attend_inner(dist, q, kv):
-    blocks = q.shape[0] // BLOCK - 2
+def attend_inner(dist, q_head, q_tail, kv_head, kv_tail):
+    count = q_head.shape[0] + q_tail.shape[0]
+    blocks = count // BLOCK - 2
     return pl.pallas_call(
         inner_kernel,
         grid_spec=pltpu.PrefetchScalarGridSpec(
             num_scalar_prefetch=1,
             grid=(blocks,),
-            in_specs=[pl.BlockSpec((BLOCK, 128), lambda i, d: (i + 2, 0)), whole(kv.shape)],
+            in_specs=[whole(v.shape) for v in (q_head, q_tail, kv_head, kv_tail)],
             out_specs=pl.BlockSpec((BLOCK, 256), lambda i, d: (i, 0)),
+            scratch_shapes=[pltpu.VMEM((count, 128), BF), pltpu.VMEM((count, 256), BF)],
         ),
         out_shape=jax.ShapeDtypeStruct((blocks * BLOCK, 256), BF),
         compiler_params=params(),
         name="attend_inner",
-    )(dist, q, kv)
+    )(dist, q_head, q_tail, kv_head, kv_tail)
 
 
 def attend_edge(dist, q, kv, halo):
@@ -285,28 +303,29 @@
     )(dist, q, kv, halo)
 
 
-def back_kernel(width, idx_ref, *refs):
-    edge_ref, inner_ref, *out_refs = refs
+def back_kernel(width, idx_ref, edge_ref, inner_ref, *out_refs):
     n = 8 * width
-    base = pl.program_id(0) * n
-    idx = idx_ref[...] - base
-    got = 0.0
-    first = 0
-    for ref in (edge_ref, inner_ref):
-        count = ref.shape[0]
-        place = lax.broadcasted_iota(jnp.int32, (n, count), 0)
-        hot = one_hot(idx[:, first : first + count], place)
-        got += jnp.dot(hot, ref[...], preferred_element_type=F32)
-        first += count
-    lines = terms_to_lines(got[:, 128:], n // 32).reshape(8, width // 32, 1, 128)
-    row = lax.broadcasted_iota(jnp.int32, (8, 8, 128), 1)
-    tail = jnp.zeros((8, 8, 128), F32)
-    for part in range(width // 32):
-        tail = jnp.where(row == part, lines[:, part], tail)
-
-    def store(ref):
-        ref[:, :width, :] = got[:, :128].astype(BF).reshape(8, width, 128)
-        ref[:, width:, :] = tail.astype(BF)
+    halves = []
+    for half in range(2):
+        idx = idx_ref[...] - (pl.program_id(0) * 2 + half) * n
+        got = 0.0
+        first = 0
+        for ref in (edge_ref, inner_ref):
+            count = ref.shape[0]
+            place = lax.broadcasted_iota(jnp.int32, (n, count), 0)
+            hot = one_hot(idx[:, first : first + count], place)
+            got += jnp.dot(hot, ref[...], preferred_element_type=F32)
+            first += count
+        lines = terms_to_lines(got[:, 128:], n // 32).reshape(8, width // 32, 1, 128)
+        row = lax.broadcasted_iota(jnp.int32, (8, 8, 128), 1)
+        tail = jnp.zeros((8, 8, 128), F32)
+        for part in range(width // 32):
+            tail = jnp.where(row == part, lines[:, part], tail)
+        halves.append((got[:, :128].astype(BF).reshape(8, width, 128), tail.astype(BF)))
+
+    def store(ref, half):
+        ref[:, :width, :] = halves[half][0]
+        ref[:, width:, :] = halves[half][1]
 
     emit(out_refs, store)
 
@@ -315,7 +334,7 @@
     specs, shapes = emit_specs(split, width + 8, 128)
     return pl.pallas_call(
         functools.partial(back_kernel, width),
-        grid=(8,),
+        grid=(4,),
         in_specs=[whole(idx.shape), whole(edge.shape), whole(inner.shape)],
         out_specs=specs,
         out_shape=shapes,
@@ -327,53 +346,64 @@
 ABSENT = -1e30
 
 
-def home_kernel(width, splits, own_ref, idx_ref, *refs):
+def fill_home(x_ref, width, home_refs):
+    if len(home_refs) == 5:
+        blocks = home_refs
+    else:
+        ref = home_refs[0]
+        blocks = [ref.at[:, g] for g in range(3)] + [ref.at[:8, 3], ref.at[8:, 3]]
+    row = 0
+    for block in blocks:
+        size = block.shape[0] * width
+        x_ref[row : row + size, :128] = block[:, :width, :].reshape(size, 128)
+        tail = block[:, width:, :].astype(F32)
+        lines = jnp.concatenate(
+            [tail[:, p : p + 1][:, None] for p in range(width // 32)], axis=1
+        ).reshape(size // 32, 1, 128)
+        x_ref[row : row + size, 128:] = lines_to_terms(lines).astype(BF)
+        row += size
+
+
+def gather_home(own_ref, cols, x_ref, width):
+    near, far, row = 0.0, 0.0, 0
+    for g in range(5):
+        size = (16 if g < 3 else 8) * width
+        first = 8 * width if g == 4 else 0
+        place = lax.broadcasted_iota(jnp.int32, (cols.shape[0], size), 1) + first
+        hot = one_hot(cols[:, g : g + 1], place)
+        got = jnp.dot(hot, x_ref[row : row + size], preferred_element_type=F32)
+        row += size
+        if g == 0:
+            near = got
+        else:
+            mine = own_ref[g] == 1
+            near += jnp.where(mine, got, 0.0)
+            far += jnp.where(mine, 0.0, got)
+    return near, far
+
+
+def home_kernel(width, own_ref, idx_ref, *refs):
     (*home_refs, out_ref, x_ref) = refs
-    jobs = len(splits)
-    big, small = 16 * width, 8 * width
-    sizes = (big, big, big, small, small)
 
     @pl.when(pl.program_id(0) == 0)
     def _():
-        at = 0
-        for job in range(jobs):
-            if splits[job]:
-                blocks = [home_refs[at + g] for g in range(5)]
-                at += 5
-            else:
-                ref = home_refs[at]
-                blocks = [ref.at[:, g] for g in range(3)] + [ref.at[:8, 3], ref.at[8:, 3]]
-                at += 1
-            row = 0
-            for size, block in zip(sizes, blocks):
-                x_ref[job, row : row + size, :128] = block[:, :width, :].reshape(size, 128)
-                tail = block[:, width:, :].astype(F32)
-                lines = jnp.concatenate(
-                    [tail[:, p : p + 1][:, None] for p in range(width // 32)], axis=1
-                ).reshape(size // 32, 1, 128)
-                x_ref[job, row : row + size, 128:] = lines_to_terms(lines).astype(BF)
-                row += size
-
-    step = out_ref.shape[1] - out_ref.shape[1] // 33
-    cols = jnp.transpose(idx_ref[0])
-    states = {}
-    for job in range(jobs):
-        row = 0
-        for g, size in enumerate(sizes):
-            c = job * 5 + g
-            first = small if g == 4 else 0
-            place = lax.broadcasted_iota(jnp.int32, (step, size), 1) + first
-            hot = one_hot(cols[:, c : c + 1], place)
-            got = jnp.dot(hot, x_ref[job, row : row + size], preferred_element_type=F32)
-            row += size
-            key = ROUND_OF[job]
-            if g == 0:
-                states[key, 0] = states.get((key, 0), 0.0) + got
-            else:
-                mine = own_ref[c] == 1
-                states[key, 0] = states[key, 0] + jnp.where(mine, got, 0.0)
-                states[key, 1] = states.get((key, 1), 0.0) + jnp.where(mine, 0.0, got)
-    states = list(states.values())
+        fill_home(x_ref, width, home_refs)
+
+    near, far = gather_home(own_ref, jnp.transpose(idx_ref[0]), x_ref, width)
+    out_ref[0] = near.astype(BF)
+    out_ref[1] = far.astype(BF)
+
+
+def last_kernel(width, own_ref, idx_ref, before_ref, *refs):
+    (*home_refs, out_ref, x_ref) = refs
+
+    @pl.when(pl.program_id(0) == 0)
+    def _():
+        fill_home(x_ref, width, home_refs)
+
+    step = idx_ref.shape[2]
+    states = list(gather_home(own_ref, jnp.transpose(idx_ref[0]), x_ref, width))
+    states += [before_ref[i].astype(F32) for i in range(2)]
     here = [s[:, 131:132] > 0.5 for s in states]
     logs = [
         jnp.where(h, s[:, 128:129] + s[:, 129:130] + s[:, 130:131], ABSENT)
@@ -391,25 +421,35 @@
     out_ref[0, step:, :] = terms_to_lines(terms, step // 32).reshape(step // 32, 128).astype(BF)
 
 
-def home_rows(own, idx, homes, width, splits):
+def home_rows(own, idx, home, width, before=None):
     columns, count = idx.shape
     quarters = 4
     step = count // quarters
-    flat = [h for home in homes for h in home]
-    return pl.pallas_call(
-        functools.partial(home_kernel, width, splits),
+    args = [own, idx.reshape(columns, quarters, step).transpose(1, 0, 2)]
+    specs = [pl.BlockSpec((1, columns, step), lambda i, o: (i, 0, 0))]
+    if before is None:
+        kernel = home_kernel
+        out_spec = pl.BlockSpec((2, step, 256), lambda i, o: (0, i, 0))
+        out_shape = jax.ShapeDtypeStruct((2, count, 256), BF)
+    else:
+        kernel = last_kernel
+        args.append(before)
+        specs.append(pl.BlockSpec((2, step, 256), lambda i, o: (0, i, 0)))
+        out_spec = pl.BlockSpec((1, step + step // 32, 128), lambda i, o: (i, 0, 0))
+        out_shape = jax.ShapeDtypeStruct((quarters, step + step // 32, 128), BF)
+    return pl.pallas_call(
+        functools.partial(kernel, width),
         grid_spec=pltpu.PrefetchScalarGridSpec(
             num_scalar_prefetch=1,
             grid=(quarters,),
-            in_specs=[pl.BlockSpec((1, columns, step), lambda i, o: (i, 0, 0))]
-            + [whole(h.shape) for h in flat],
-            out_specs=pl.BlockSpec((1, step + step // 32, 128), lambda i, o: (i, 0, 0)),
-            scratch_shapes=[pltpu.VMEM((len(homes), 64 * width, 256), BF)],
+            in_specs=specs + [whole(h.shape) for h in home],
+            out_specs=out_spec,
+            scratch_shapes=[pltpu.VMEM((64 * width, 256), BF)],
         ),
-        out_shape=jax.ShapeDtypeStruct((quarters, step + step // 32, 128), BF),
+        out_shape=out_shape,
         compiler_params=params(),
         name="home_rows",
-    )(own, idx.reshape(columns, quarters, step).transpose(1, 0, 2), *flat)
+    )(*args, *home)
 
 
 def finish_kernel(m_ref, w_ref, out_ref):
@@ -476,56 +516,54 @@
     return by_group, by_source
 
 
-WIDTH = 64
-JOBS = ((0, 0, True), (1, 0, False))
-ROUND_OF = tuple(job[0] for job in JOBS)
-
-
 def body(x, w_qk, w_v, w_out, slots, taken, looks):
-    rounds, count = slots.shape
+    count = slots.shape[1]
     peers = lax.axis_size(SEQ)
+    width = 2 * count // peers
     blocks = count // BLOCK
+    tail = count - 2 * BLOCK
     others = lax.ppermute(slots, "zh", [(0, 1), (1, 0)])
     packed = project(x, w_qk, w_v)
     mine = lax.axis_index(SEQ) * blocks + jnp.arange(blocks, dtype=jnp.int32)
     dist = (mine[None, :] - looks) % (peers * blocks)
     next_device = [(i, (i + 1) % peers) for i in range(peers)]
-    sent, own, arrived = [], [], []
-    for i, low, z_first in JOBS:
-        places, flags = send_places(slots[i], others[i], low, WIDTH, z_first)
-        sent.append(places)
-        own.append(flags)
-        out = scatter_rows(places, packed, WIDTH, z_first)
-        if z_first:
-            arrived.append([ring_first(out, 1)])
-        else:
-            arrived.append(plane_first(out[0], 1))
-    homes = [None] * len(JOBS)
-    for i in range(rounds):
-        rows, spots, base = [], 0, 0
-        back_spots = {}
-        for job, (which, low, z_first) in enumerate(JOBS):
-            if which != i:
-                continue
-            by_group, by_source = take_places(taken[i], low, WIDTH)
-            back_spots[job] = by_group
-            spot = by_source if z_first else by_group
-            spots = jnp.where(spot >= 0, spot + base, spots)
-            base += 64 * WIDTH
-            rows += arrived[job]
-        q, kv = sort_rows(spots, rows)
-        halo = lax.ppermute(kv[count - 2 * BLOCK :], SEQ, next_device)
-        inner = attend_inner(dist[i], q, kv)
-        edge = attend_edge(dist[i], q, kv, halo)
-        for job, spot in back_spots.items():
-            z_first = JOBS[job][2]
-            back = back_rows(spot[None], edge, inner, WIDTH, not z_first)
-            if z_first:
-                homes[job] = plane_first(back[0], -1)
-            else:
-                homes[job] = [ring_first(back, -1)]
-    splits = tuple(z_first for _, _, z_first in JOBS)
-    state = home_rows(jnp.concatenate(own), jnp.concatenate(sent), homes, WIDTH, splits)
+    sent_0, own_0 = send_places(slots[0], others[0], 0, width, True)
+    sent_1, own_1 = send_places(slots[1], others[1], 0, width, False)
+    groups_0, _ = take_places(taken[0], 0, width)
+    _, spots_0 = take_places(taken[0], 0, width)
+    groups_1, _ = take_places(taken[1], 0, width)
+
+    out_0 = scatter_rows(sent_0, packed, width, True)
+    out_0, packed = together((out_0, packed))
+    rung_0 = ring_all(out_0, 1)
+    (out_1,) = scatter_rows(sent_1, packed, width, False)
+    half_1 = plane(out_1)
+    rung_0, half_1 = together((rung_0, half_1))
+    arrived_0 = [plane(join(rung_0))]
+    arrived_1 = ring_all(part(half_1), 1)
+
+    def sort_round(spots, rows):
+        q_tail, kv_tail = sort_rows(spots[tail:], rows, 2 * BLOCK)
+        halo = lax.ppermute(kv_tail, SEQ, next_device)
+        q_head, kv_head = sort_rows(spots[:tail], rows, 3 * BLOCK)
+        return q_head, q_tail, kv_head, kv_tail, halo
+
+    def attend_round(near, sorted_rows):
+        q_head, q_tail, kv_head, kv_tail, halo = sorted_rows
+        inner = attend_inner(near, q_head, q_tail, kv_head, kv_tail)
+        return attend_edge(near, q_head, kv_head, halo), inner
+
+    sorted_0 = sort_round(spots_0, arrived_0)
+    edge, inner = attend_round(dist[0], sorted_0)
+    (back_0,) = back_rows(groups_0[None], edge, inner, width, False)
+    sorted_1 = sort_round(groups_1, arrived_1)
+    edge, inner = attend_round(dist[1], sorted_1)
+    back_1 = back_rows(groups_1[None], edge, inner, width, True)
+
+    home_0 = ring_all(part(plane(back_0)), -1)
+    home_1 = [plane(join(ring_all(back_1, -1)))]
+    before = home_rows(own_0, sent_0, home_0, width)
+    state = home_rows(own_1, sent_1, home_1, width, before)
     merged = lax.all_to_all(state, ROUND, 0, 0, tiled=True)
     return finish(merged, w_out)
 

time: 258 us -> 251 us (0.973)
  waiting for transfers between devices: 78.9 us -> 60.9 us
  local copies, waits for them, and re-layouts: 13.9 us -> 21.5 us
  blocking collectives: 28.5 us -> 32.4 us
  starting transfers between devices: 61 us -> 57.8 us
  other arithmetic: 3.41 us -> 6.6 us
    ppermute x16, waiting for transfers between devices: 46.4 us -> 37.8 us  [ring(): return lax.ppermute(value, ('zl', 'zh'), route)]
    all_to_all x4, waiting for transfers between devices: 29.6 us -> 23.1 us  [plane(): return lax.all_to_all(joint, PLANE, 0, 0, tiled=True)]
    unnamed x32 -> x88, local copies, waits for them, and re-layouts: 6.27 us -> 12.7 us
    all_to_all x1, blocking collectives: 28.5 us -> 32.4 us  [body(): merged = lax.all_to_all(state, ROUND, 0, 0, tiled=True)]
    ppermute x16, starting transfers between devices: 24.3 us -> 20.9 us  [ring(): return lax.ppermute(value, ('zl', 'zh'), route)]
    ppermute x2, waiting for transfers between devices: 2.83 us -> 0.01 us  [sort_round(): halo = lax.ppermute(kv_tail, SEQ, next_device)]
    pallas_call x2 -> x4, Pallas kernels: 15.8 us -> 14 us  [sort_rows(): pl.pallas_call(sort_kernel, grid=(blocks,), in_specs=[pl.BlockSpec((1, 1,...]
    pallas_call x5 -> x6, Pallas kernels: 41.1 us -> 41.1 us  [the longest x2 18.9 us: home_rows(): pl.pallas_call(functools.partial(kernel, width), grid_spec=pltpu.Prefetch...]
  transfers between devices with their start and end apart: 23 -> 23, of which waited for: 10 -> 7; matrix products, arithmetic and copies ran while one was open for 4% -> 5% of each run, Pallas kernels for 18% -> 18%
where the time goes in v3:
time: 251 us; the launch traced here: 250 us
  Pallas kernels  70.6 us (28%)
  waiting for transfers between devices  60.9 us (24%)
  starting transfers between devices  57.8 us (23%)
  blocking collectives  32.4 us (13%)
  local copies, waits for them, and re-layouts  21.5 us (9%)
  other arithmetic  6.6 us (3%)
    ppermute x16, waiting for transfers between devices, ring(): return lax.ppermute(value, ('zl', 'zh'), route)  37.8 us
    all_to_all x1, blocking collectives, body(): merged = lax.all_to_all(state, ROUND, 0, 0, tiled=True)  32.4 us
    all_to_all x4, starting transfers between devices, plane(): return lax.all_to_all(joint, PLANE, 0, 0, tiled=True)  29.7 us
    all_to_all x4, waiting for transfers between devices, plane(): return lax.all_to_all(joint, PLANE, 0, 0, tiled=True)  23.1 us
    ppermute x16, starting transfers between devices, ring(): return lax.ppermute(value, ('zl', 'zh'), route)  20.9 us
    pallas_call x2, Pallas kernels, home_rows(): pl.pallas_call(functools.partial(kernel, width), grid_spec=pltpu.Prefetch...  18.9 us
    pallas_call x4, Pallas kernels, sort_rows(): pl.pallas_call(sort_kernel, grid=(blocks,), in_specs=[pl.BlockSpec((1, 1,...  14 us
    unnamed x88, local copies, waits for them, and re-layouts  12.7 us
  transfers between devices with their start and end apart: 23, of which 7 were waited for; matrix products, arithmetic and copies ran while one was open for 5% of the time, Pallas kernels for 18%

profile of v3, /device:TPU:35, one launch (start us, length us, event | category | flops | bytes accessed | tf_op | source)
XLA Modules:
  0.0 250.3 jit_solution(9938633347176375574)
XLA Ops:
  0.0 6.0 %collective-permute-start = (s32[2,2048]{1,0:T(2,128)}, s32[2,2048]{1,0:T(2,128)S(1)}, u32[]{:S(2)}, u32[]{:S(2)}) collective-permute-start(s32[2,2048]{1,0:T(2,128)} %param.11), channel_id=1, source_target_pairs={{0,2},{2,0},{1,3},{3,1},{4,6},{6,4},{5,7},{7,5},{8,10},{10,8},{9,1... | collective-permute-start | bytes 49160 | tf_op jit(solution)/shard_map/ppermute | solution.py:525
  13.1 5.3 %scatter_rows.2 = (bf16[16,64,256]{2,1,0:T(8,128)(2,1)S(1)}, bf16[16,64,256]{2,1,0:T(8,128)(2,1)S(1)}, bf16[16,64,256]{2,1,0:T(8,128)(2,1)S(1)}, bf16[8,64,256]{2,1,0:T(8,128)(2,1)S(1)}, bf16[8,64,256]{2,1,0:T(8,128)(2,1)S(1)}) custom-call(s32[5,2048]{1,0:T(8,128)S(1)} %stack.118.idx_ref, bf16[2048,256]{1,0:T(8,128)(2,1)S(1)} %project.1.rows_ref), custom_call_target="tpu_custom_call" | custom-call | tf_op jit(solution)/shard_map/scatter_rows/pallas_call | solution.py:141
  18.5 5.9 %scatter_rows.3 = bf16[16,4,64,256]{3,2,1,0:T(8,128)(2,1)} custom-call(s32[5,2048]{1,0:T(8,128)S(1)} %stack.119.idx_ref, bf16[2048,256]{1,0:T(8,128)(2,1)S(1)} %project.1.rows_ref), custom_call_target="tpu_custom_call" | custom-call | tf_op jit(solution)/shard_map/scatter_rows/pallas_call | solution.py:141
  24.4 6.9 %all-to-all-start = ((bf16[16,4,64,256]{3,2,1,0:T(8,128)(2,1)}), bf16[16,4,64,256]{3,2,1,0:T(8,128)(2,1)}, u32[]{:S(2)}, u32[]{:S(2)}) async-start(bf16[16,4,64,256]{3,2,1,0:T(8,128)(2,1)} %scatter_rows.3), calls=%async_computation | async-start | bytes 4194304 | tf_op jit(solution)/shard_map/all_to_all | solution.py:90
  36.4 19.8 %collective-permute-done.3 = bf16[8,64,256]{2,1,0:T(8,128)(2,1)S(1)} collective-permute-done((bf16[8,64,256]{2,1,0:T(8,128)(2,1)S(1)}, bf16[8,64,256]{2,1,0:T(8,128)(2,1)S(1)}, u32[]{:S(2)}, u32[]{:S(2)}) %collective-permute-start.3) | collective-permute-done | bytes 262176 | tf_op jit(solution)/shard_map/ppermute | solution.py:73
  58.9 6.9 %all-to-all-start.1 = ((bf16[16,4,64,256]{3,2,1,0:T(8,128)(2,1)}), bf16[16,4,64,256]{3,2,1,0:T(8,128)(2,1)S(1)}, u32[]{:S(2)}, u32[]{:S(2)}) async-start(bf16[16,4,64,256]{3,2,1,0:T(8,128)(2,1)} %pad_maximum_fusion), calls=%async_computation.1 | async-start | bytes 4194304 | tf_op jit(solution)/shard_map/all_to_all | solution.py:90
  67.1 23.0 %all-to-all-done.1.refs_0_ = bf16[16,4,64,256]{3,2,1,0:T(8,128)(2,1)S(1)} async-done(((bf16[16,4,64,256]{3,2,1,0:T(8,128)(2,1)}), bf16[16,4,64,256]{3,2,1,0:T(8,128)(2,1)S(1)}, u32[]{:S(2)}, u32[]{:S(2)}) %all-to-all-start.1) | async-done | bytes 2097184 | tf_op jit(solution)/shard_map/all_to_all | solution.py:90
  98.4 4.4 %sort_rows.4 = (bf16[1536,128]{1,0:T(8,128)(2,1)S(1)}, bf16[1536,256]{1,0:T(8,128)(2,1)S(1)}) custom-call(s32[2,1,768]{2,1,0:T(1,128)S(1)} %copy-done.11, bf16[16,4,64,256]{3,2,1,0:T(8,128)(2,1)S(1)} %all-to-all-done.1.refs_0_), custom_call_target="tpu_custom_call" | custom-call | tf_op jit(solution)/shard_map/sort_rows/pallas_call | solution.py:172
  102.8 3.5 %attend_inner.2.inner_ref = bf16[1536,256]{1,0:T(8,128)(2,1)S(1)} custom-call(s32[8]{0:T(128)S(1)} %copy-done.13, bf16[1536,128]{1,0:T(8,128)(2,1)S(1)} %get-tuple-element.51.q_ref.qh_ref, bf16[512,128]{1,0:T(8,128)(2,1)S(1)} %get-tuple-element.54.qt_ref, bf16[1536,256]{1,0:T(8,128)(2,1)S(1)} %get-tuple-element.52.kv_ref.kvh_ref, ...), custom_call_target="tpu_custom_call" | custom-call | tf_op jit(solution)/shard_map/attend_inner/pallas_call | solution.py:272
  108.8 5.8 %back_rows.2 = bf16[16,4,72,128]{3,2,1,0:T(8,128)(2,1)} custom-call(s32[1,2048]{1,0:T(1,128)S(1)} %get-tuple-element.95.idx_ref, bf16[512,256]{1,0:T(8,128)(2,1)S(1)} %attend_edge.2.edge_ref, bf16[1536,256]{1,0:T(8,128)(2,1)S(1)} %attend_inner.2.inner_ref), custom_call_target="tpu_custom_call" | custom-call | tf_op jit(solution)/shard_map/back_rows/pallas_call | solution.py:335
  114.6 7.9 %all-to-all-start.2 = ((bf16[16,4,72,128]{3,2,1,0:T(8,128)(2,1)}), bf16[16,4,72,128]{3,2,1,0:T(8,128)(2,1)}, u32[]{:S(2)}, u32[]{:S(2)}) async-start(bf16[16,4,72,128]{3,2,1,0:T(8,128)(2,1)} %back_rows.2), calls=%async_computation.2 | async-start | bytes 2359296 | tf_op jit(solution)/shard_map/all_to_all | solution.py:90
  127.2 6.8 %collective-permute-done.12.refs_3_ = bf16[8,64,256]{2,1,0:T(8,128)(2,1)S(1)} collective-permute-done((bf16[8,64,256]{2,1,0:T(8,128)(2,1)S(1)}, bf16[8,64,256]{2,1,0:T(8,128)(2,1)S(1)}, u32[]{:S(2)}, u32[]{:S(2)}) %collective-permute-start.12) | collective-permute-done | bytes 262176 | tf_op jit(solution)/shard_map/ppermute | solution.py:73
  134.1 2.6 %sort_rows.7 = (bf16[512,128]{1,0:T(8,128)(2,1)S(1)}, bf16[512,256]{1,0:T(8,128)(2,1)S(1)}) custom-call(s32[1,1,512]{2,1,0:T(1,128)S(1)} %bitcast.76, bf16[16,64,256]{2,1,0:T(8,128)(2,1)S(1)} %get-tuple-element.75.refs_0_, bf16[16,64,256]{2,1,0:T(8,128)(2,1)S(1)} %collective-permute-done.10.refs_1_, bf16[16,64,256]{2,1,0:T(8,128)(2,1)} %collective-permute-done.11.refs_2_, ...), custom_call_target="tpu_custom_call" | custom-call | tf_op jit(solution)/shard_map/sort_rows/pallas_call | solution.py:172
  137.8 5.4 %sort_rows.6 = (bf16[1536,128]{1,0:T(8,128)(2,1)S(1)}, bf16[1536,256]{1,0:T(8,128)(2,1)S(1)}) custom-call(s32[2,1,768]{2,1,0:T(1,128)S(1)} %reshape.56.idx_ref, bf16[16,64,256]{2,1,0:T(8,128)(2,1)S(1)} %get-tuple-element.75.refs_0_, bf16[16,64,256]{2,1,0:T(8,128)(2,1)S(1)} %collective-permute-done.10.refs_1_, ...), custom_call_target="tpu_custom_call" | custom-call | tf_op jit(solution)/shard_map/sort_rows/pallas_call | solution.py:172
  143.3 3.5 %attend_inner.3.inner_ref = bf16[1536,256]{1,0:T(8,128)(2,1)S(1)} custom-call(s32[8]{0:T(128)S(1)} %copy-done.12, bf16[1536,128]{1,0:T(8,128)(2,1)S(1)} %get-tuple-element.56.q_ref.qh_ref, bf16[512,128]{1,0:T(8,128)(2,1)S(1)} %get-tuple-element.59.qt_ref, bf16[1536,256]{1,0:T(8,128)(2,1)S(1)} %get-tuple-element.57.kv_ref.kvh_ref, ...), custom_call_target="tpu_custom_call" | custom-call | tf_op jit(solution)/shard_map/attend_inner/pallas_call | solution.py:272
  148.3 5.2 %back_rows.3 = (bf16[16,72,128]{2,1,0:T(8,128)(2,1)S(1)}, bf16[16,72,128]{2,1,0:T(8,128)(2,1)S(1)}, bf16[16,72,128]{2,1,0:T(8,128)(2,1)S(1)}, bf16[8,72,128]{2,1,0:T(8,128)(2,1)S(1)}, bf16[8,72,128]{2,1,0:T(8,128)(2,1)S(1)}) custom-call(s32[1,2048]{1,0:T(1,128)S(1)} %get-tuple-element.65.idx_ref, bf16[512,256]{1,0:T(8,128)(2,1)S(1)} %attend_edge.3.edge_ref, ...), custom_call_target="tpu_custom_call" | custom-call | tf_op jit(solution)/shard_map/back_rows/pallas_call | solution.py:335
  155.9 3.0 %collective-permute-start.17 = (bf16[8,72,128]{2,1,0:T(8,128)(2,1)S(1)}, bf16[8,72,128]{2,1,0:T(8,128)(2,1)S(1)}, u32[]{:S(2)}, u32[]{:S(2)}) collective-permute-start(bf16[8,72,128]{2,1,0:T(8,128)(2,1)S(1)} %get-tuple-element.63), channel_id=1, source_target_pairs={{0,130},{64,194},{128,0},{192,64},{2,128},{66,192},{130,2},{194,66... | collective-permute-start | bytes 442376 | tf_op jit(solution)/shard_map/ppermute | solution.py:73
  160.0 3.0 %collective-permute-done.17 = bf16[8,72,128]{2,1,0:T(8,128)(2,1)S(1)} collective-permute-done((bf16[8,72,128]{2,1,0:T(8,128)(2,1)S(1)}, bf16[8,72,128]{2,1,0:T(8,128)(2,1)S(1)}, u32[]{:S(2)}, u32[]{:S(2)}) %collective-permute-start.17) | collective-permute-done | bytes 147488 | tf_op jit(solution)/shard_map/ppermute | solution.py:73
  166.3 8.0 %all-to-all-start.3 = ((bf16[16,4,72,128]{3,2,1,0:T(8,128)(2,1)}), bf16[16,4,72,128]{3,2,1,0:T(8,128)(2,1)S(1)}, u32[]{:S(2)}, u32[]{:S(2)}) async-start(bf16[16,4,72,128]{3,2,1,0:T(8,128)(2,1)} %pad_maximum_fusion.1), calls=%async_computation.3 | async-start | bytes 2359296 | tf_op jit(solution)/shard_map/all_to_all | solution.py:90
  178.7 2.8 %collective-permute-start.8 = (bf16[8,72,128]{2,1,0:T(8,128)(2,1)S(1)}, bf16[8,72,128]{2,1,0:T(8,128)(2,1)S(1)}, u32[]{:S(2)}, u32[]{:S(2)}) collective-permute-start(bf16[8,72,128]{2,1,0:T(8,128)(2,1)S(1)} %get-tuple-element.77), channel_id=1, source_target_pairs={{0,130},{64,194},{128,0},{192,64},{2,128},{66,192},{130,2},{194,66... | collective-permute-start | bytes 442376 | tf_op jit(solution)/shard_map/ppermute | solution.py:73
  185.2 4.0 %collective-permute-done.9.refs_4_ = bf16[8,72,128]{2,1,0:T(8,128)(2,1)S(1)} collective-permute-done((bf16[8,72,128]{2,1,0:T(8,128)(2,1)S(1)}, bf16[8,72,128]{2,1,0:T(8,128)(2,1)S(1)}, u32[]{:S(2)}, u32[]{:S(2)}) %collective-permute-start.9) | collective-permute-done | bytes 147488 | tf_op jit(solution)/shard_map/ppermute | solution.py:73
  195.8 7.7 %home_rows.2.before_ref = bf16[2,2048,256]{2,1,0:T(8,128)(2,1)S(1)} custom-call(s32[5]{0:T(128)S(1)} %copy-done.15, s32[4,5,512]{2,1,0:T(8,128)S(1)} %bitcast.75, bf16[16,72,128]{2,1,0:T(8,128)(2,1)S(1)} %copy-done.1, bf16[16,72,128]{2,1,0:T(8,128)(2,1)S(1)} %copy-done.3, bf16[16,72,128]{2,1,0:T(8,128)(2,1)S(1)} %copy-done.5, ...), custom_call_target="tpu_custom_call" | custom-call | tf_op jit(solution)/shard_map/home_rows/pallas_call | solution.py:440
  204.2 11.1 %home_rows.3 = bf16[4,528,128]{2,1,0:T(8,128)(2,1)S(1)} custom-call(s32[5]{0:T(128)S(1)} %copy-done.14, s32[4,5,512]{2,1,0:T(8,128)S(1)} %bitcast.74, bf16[2,2048,256]{2,1,0:T(8,128)(2,1)S(1)} %home_rows.2.before_ref, bf16[16,4,72,128]{3,2,1,0:T(8,128)(2,1)S(1)} %all-to-all-done.3.refs_0_), custom_call_target="tpu_custom_call" | custom-call | tf_op jit(solution)/shard_map/home_rows/pallas_call | solution.py:440
  215.4 32.4 %all_to_all.25.m_ref = bf16[4,528,128]{2,1,0:T(8,128)(2,1)S(1)} all-to-all(bf16[4,528,128]{2,1,0:T(8,128)(2,1)S(1)} %home_rows.3), channel_id=1, replica_groups=mesh['zl'=4,'x'=4,'y'=4,'zh'=2,'c'=2] {'zh','c'}, dimensions={0} | all-to-all | bytes 1081344 | tf_op jit(solution)/shard_map/all_to_all | solution.py:567
  (156 shorter events, 58.6 us)
Async XLA Ops:
  0.0 12.0 %collective-permute-start = (s32[2,2048]{1,0:T(2,128)}, s32[2,2048]{1,0:T(2,128)S(1)}, u32[]{:S(2)}, u32[]{:S(2)}) collective-permute-start(s32[2,2048]{1,0:T(2,128)} %param.11), channel_id=1, source_target_pairs={{0,2},{2,0},{1,3},{3,1},{4,6},{6,4},{5,7},{7,5},{8,10},{10,8},{9,1... | collective-permute-start | bytes 49160 | tf_op jit(solution)/shard_map/ppermute | solution.py:525
  24.4 31.9 %all-to-all-start = ((bf16[16,4,64,256]{3,2,1,0:T(8,128)(2,1)}), bf16[16,4,64,256]{3,2,1,0:T(8,128)(2,1)}, u32[]{:S(2)}, u32[]{:S(2)}) async-start(bf16[16,4,64,256]{3,2,1,0:T(8,128)(2,1)} %scatter_rows.3), calls=%async_computation | async-start | bytes 4194304 | tf_op jit(solution)/shard_map/all_to_all | solution.py:90
  31.3 24.9 %collective-permute-start.1 = (bf16[16,64,256]{2,1,0:T(8,128)(2,1)S(1)}, bf16[16,64,256]{2,1,0:T(8,128)(2,1)S(1)}, u32[]{:S(2)}, u32[]{:S(2)}) collective-permute-start(bf16[16,64,256]{2,1,0:T(8,128)(2,1)S(1)} %get-tuple-element.41), channel_id=1, source_target_pairs={{0,64},{64,128},{128,192},{192,2},{2,66},{66,130},{130,194},{194,0... | collective-permute-start | bytes 1572872 | tf_op jit(solution)/shard_map/ppermute | solution.py:73
  32.1 24.2 %collective-permute-start.2 = (bf16[16,64,256]{2,1,0:T(8,128)(2,1)S(1)}, bf16[16,64,256]{2,1,0:T(8,128)(2,1)S(1)}, u32[]{:S(2)}, u32[]{:S(2)}) collective-permute-start(bf16[16,64,256]{2,1,0:T(8,128)(2,1)S(1)} %get-tuple-element.42), channel_id=1, source_target_pairs={{0,194},{64,0},{128,64},{192,128},{2,192},{66,2},{130,66},{194,130... | collective-permute-start | bytes 1572872 | tf_op jit(solution)/shard_map/ppermute | solution.py:73
  32.8 23.4 %collective-permute-start.3 = (bf16[8,64,256]{2,1,0:T(8,128)(2,1)S(1)}, bf16[8,64,256]{2,1,0:T(8,128)(2,1)S(1)}, u32[]{:S(2)}, u32[]{:S(2)}) collective-permute-start(bf16[8,64,256]{2,1,0:T(8,128)(2,1)S(1)} %get-tuple-element.43), channel_id=1, source_target_pairs={{0,128},{64,192},{128,2},{192,66},{2,130},{66,194},{130,0},{194,64... | collective-permute-start | bytes 786440 | tf_op jit(solution)/shard_map/ppermute | solution.py:73
  34.0 22.2 %collective-permute-start.4 = (bf16[8,64,256]{2,1,0:T(8,128)(2,1)S(1)}, bf16[8,64,256]{2,1,0:T(8,128)(2,1)}, u32[]{:S(2)}, u32[]{:S(2)}) collective-permute-start(bf16[8,64,256]{2,1,0:T(8,128)(2,1)S(1)} %get-tuple-element.44), channel_id=1, source_target_pairs={{0,130},{64,194},{128,0},{192,64},{2,128},{66,192},{130,2},{194,66... | collective-permute-start | bytes 786440 | tf_op jit(solution)/shard_map/ppermute | solution.py:73
  58.9 31.3 %all-to-all-start.1 = ((bf16[16,4,64,256]{3,2,1,0:T(8,128)(2,1)}), bf16[16,4,64,256]{3,2,1,0:T(8,128)(2,1)S(1)}, u32[]{:S(2)}, u32[]{:S(2)}) async-start(bf16[16,4,64,256]{3,2,1,0:T(8,128)(2,1)} %pad_maximum_fusion), calls=%async_computation.1 | async-start | bytes 4194304 | tf_op jit(solution)/shard_map/all_to_all | solution.py:90
  91.8 14.5 %collective-permute-start.5 = (bf16[512,256]{1,0:T(8,128)(2,1)S(1)}, bf16[512,256]{1,0:T(8,128)(2,1)}, u32[]{:S(2)}, u32[]{:S(2)}) collective-permute-start(bf16[512,256]{1,0:T(8,128)(2,1)S(1)} %get-tuple-element.53.kvt_ref), channel_id=1, source_target_pairs={{0,4},{4,8},{8,12},{12,16},{16,20},{20,24},{24,28},{28,32},{32,36}... | collective-permute-start | bytes 786440 | tf_op jit(solution)/shard_map/ppermute | solution.py:547
  94.4 39.7 %collective-permute-start.10 = (bf16[16,64,256]{2,1,0:T(8,128)(2,1)}, bf16[16,64,256]{2,1,0:T(8,128)(2,1)S(1)}, u32[]{:S(2)}, u32[]{:S(2)}) collective-permute-start(bf16[16,64,256]{2,1,0:T(8,128)(2,1)} %get-tuple-element.74), channel_id=1, source_target_pairs={{0,64},{64,128},{128,192},{192,2},{2,66},{66,130},{130,194},{194,0... | collective-permute-start | bytes 1572872 | tf_op jit(solution)/shard_map/ppermute | solution.py:73
  95.1 38.9 %collective-permute-start.11 = (bf16[16,64,256]{2,1,0:T(8,128)(2,1)}, bf16[16,64,256]{2,1,0:T(8,128)(2,1)}, u32[]{:S(2)}, u32[]{:S(2)}) collective-permute-start(bf16[16,64,256]{2,1,0:T(8,128)(2,1)} %get-tuple-element.73), channel_id=1, source_target_pairs={{0,194},{64,0},{128,64},{192,128},{2,192},{66,2},{130,66},{194,130... | collective-permute-start | bytes 1572872 | tf_op jit(solution)/shard_map/ppermute | solution.py:73
  114.6 51.7 %all-to-all-start.2 = ((bf16[16,4,72,128]{3,2,1,0:T(8,128)(2,1)}), bf16[16,4,72,128]{3,2,1,0:T(8,128)(2,1)}, u32[]{:S(2)}, u32[]{:S(2)}) async-start(bf16[16,4,72,128]{3,2,1,0:T(8,128)(2,1)} %back_rows.2), calls=%async_computation.2 | async-start | bytes 2359296 | tf_op jit(solution)/shard_map/all_to_all | solution.py:90
  123.6 10.5 %collective-permute-start.12 = (bf16[8,64,256]{2,1,0:T(8,128)(2,1)S(1)}, bf16[8,64,256]{2,1,0:T(8,128)(2,1)S(1)}, u32[]{:S(2)}, u32[]{:S(2)}) collective-permute-start(bf16[8,64,256]{2,1,0:T(8,128)(2,1)S(1)} %get-tuple-element.72), channel_id=1, source_target_pairs={{0,128},{64,192},{128,2},{192,66},{2,130},{66,194},{130,0},{194,64... | collective-permute-start | bytes 786440 | tf_op jit(solution)/shard_map/ppermute | solution.py:73
  125.4 8.7 %collective-permute-start.13 = (bf16[8,64,256]{2,1,0:T(8,128)(2,1)S(1)}, bf16[8,64,256]{2,1,0:T(8,128)(2,1)S(1)}, u32[]{:S(2)}, u32[]{:S(2)}) collective-permute-start(bf16[8,64,256]{2,1,0:T(8,128)(2,1)S(1)} %get-tuple-element.71), channel_id=1, source_target_pairs={{0,130},{64,194},{128,0},{192,64},{2,128},{66,192},{130,2},{194,66... | collective-permute-start | bytes 786440 | tf_op jit(solution)/shard_map/ppermute | solution.py:73
  136.7 10.1 %collective-permute-start.14 = (bf16[512,256]{1,0:T(8,128)(2,1)S(1)}, bf16[512,256]{1,0:T(8,128)(2,1)S(1)}, u32[]{:S(2)}, u32[]{:S(2)}) collective-permute-start(bf16[512,256]{1,0:T(8,128)(2,1)S(1)} %get-tuple-element.58.kvt_ref), channel_id=1, source_target_pairs={{0,4},{4,8},{8,12},{12,16},{16,20},{20,24},{24,28},{28,32},{32,36}... | collective-permute-start | bytes 786440 | tf_op jit(solution)/shard_map/ppermute | solution.py:547
  153.6 11.5 %collective-permute-start.15 = (bf16[16,72,128]{2,1,0:T(8,128)(2,1)S(1)}, bf16[16,72,128]{2,1,0:T(8,128)(2,1)S(1)}, u32[]{:S(2)}, u32[]{:S(2)}) collective-permute-start(bf16[16,72,128]{2,1,0:T(8,128)(2,1)S(1)} %get-tuple-element.61), channel_id=1, source_target_pairs={{0,194},{64,0},{128,64},{192,128},{2,192},{66,2},{130,66},{194,130... | collective-permute-start | bytes 884744 | tf_op jit(solution)/shard_map/ppermute | solution.py:73
  154.8 10.3 %collective-permute-start.16 = (bf16[16,72,128]{2,1,0:T(8,128)(2,1)S(1)}, bf16[16,72,128]{2,1,0:T(8,128)(2,1)S(1)}, u32[]{:S(2)}, u32[]{:S(2)}) collective-permute-start(bf16[16,72,128]{2,1,0:T(8,128)(2,1)S(1)} %get-tuple-element.62), channel_id=1, source_target_pairs={{0,64},{64,128},{128,192},{192,2},{2,66},{66,130},{130,194},{194,0... | collective-permute-start | bytes 884744 | tf_op jit(solution)/shard_map/ppermute | solution.py:73
  155.9 7.2 %collective-permute-start.17 = (bf16[8,72,128]{2,1,0:T(8,128)(2,1)S(1)}, bf16[8,72,128]{2,1,0:T(8,128)(2,1)S(1)}, u32[]{:S(2)}, u32[]{:S(2)}) collective-permute-start(bf16[8,72,128]{2,1,0:T(8,128)(2,1)S(1)} %get-tuple-element.63), channel_id=1, source_target_pairs={{0,130},{64,194},{128,0},{192,64},{2,128},{66,192},{130,2},{194,66... | collective-permute-start | bytes 442376 | tf_op jit(solution)/shard_map/ppermute | solution.py:73
  158.9 6.1 %collective-permute-start.18 = (bf16[8,72,128]{2,1,0:T(8,128)(2,1)S(1)}, bf16[8,72,128]{2,1,0:T(8,128)(2,1)S(1)}, u32[]{:S(2)}, u32[]{:S(2)}) collective-permute-start(bf16[8,72,128]{2,1,0:T(8,128)(2,1)S(1)} %get-tuple-element.64), channel_id=1, source_target_pairs={{0,128},{64,192},{128,2},{192,66},{2,130},{66,194},{130,0},{194,64... | collective-permute-start | bytes 442376 | tf_op jit(solution)/shard_map/ppermute | solution.py:73
  166.3 37.3 %all-to-all-start.3 = ((bf16[16,4,72,128]{3,2,1,0:T(8,128)(2,1)}), bf16[16,4,72,128]{3,2,1,0:T(8,128)(2,1)S(1)}, u32[]{:S(2)}, u32[]{:S(2)}) async-start(bf16[16,4,72,128]{3,2,1,0:T(8,128)(2,1)} %pad_maximum_fusion.1), calls=%async_computation.3 | async-start | bytes 2359296 | tf_op jit(solution)/shard_map/all_to_all | solution.py:90
  176.2 13.7 %collective-permute-start.6 = (bf16[16,72,128]{2,1,0:T(8,128)(2,1)S(1)}, bf16[16,72,128]{2,1,0:T(8,128)(2,1)S(1)}, u32[]{:S(2)}, u32[]{:S(2)}) collective-permute-start(bf16[16,72,128]{2,1,0:T(8,128)(2,1)S(1)} %get-tuple-element.79), channel_id=1, source_target_pairs={{0,194},{64,0},{128,64},{192,128},{2,192},{66,2},{130,66},{194,130... | collective-permute-start | bytes 884744 | tf_op jit(solution)/shard_map/ppermute | solution.py:73
  176.7 13.9 %collective-permute-start.7 = (bf16[16,72,128]{2,1,0:T(8,128)(2,1)S(1)}, bf16[16,72,128]{2,1,0:T(8,128)(2,1)S(1)}, u32[]{:S(2)}, u32[]{:S(2)}) collective-permute-start(bf16[16,72,128]{2,1,0:T(8,128)(2,1)S(1)} %get-tuple-element.78), channel_id=1, source_target_pairs={{0,64},{64,128},{128,192},{192,2},{2,66},{66,130},{130,194},{194,0... | collective-permute-start | bytes 884744 | tf_op jit(solution)/shard_map/ppermute | solution.py:73
  178.7 6.5 %collective-permute-start.8 = (bf16[8,72,128]{2,1,0:T(8,128)(2,1)S(1)}, bf16[8,72,128]{2,1,0:T(8,128)(2,1)S(1)}, u32[]{:S(2)}, u32[]{:S(2)}) collective-permute-start(bf16[8,72,128]{2,1,0:T(8,128)(2,1)S(1)} %get-tuple-element.77), channel_id=1, source_target_pairs={{0,130},{64,194},{128,0},{192,64},{2,128},{66,192},{130,2},{194,66... | collective-permute-start | bytes 442376 | tf_op jit(solution)/shard_map/ppermute | solution.py:73
  181.5 7.8 %collective-permute-start.9 = (bf16[8,72,128]{2,1,0:T(8,128)(2,1)S(1)}, bf16[8,72,128]{2,1,0:T(8,128)(2,1)S(1)}, u32[]{:S(2)}, u32[]{:S(2)}) collective-permute-start(bf16[8,72,128]{2,1,0:T(8,128)(2,1)S(1)} %get-tuple-element.76), channel_id=1, source_target_pairs={{0,128},{64,192},{128,2},{192,66},{2,130},{66,194},{130,0},{194,64... | collective-permute-start | bytes 442376 | tf_op jit(solution)/shard_map/ppermute | solution.py:73
  204.2 43.6 %copy-start.8 = (bf16[128,1024]{1,0:T(8,128)(2,1)S(1)}, bf16[128,1024]{1,0:T(8,128)(2,1)}, u32[]{:S(2)}) copy-start(bf16[128,1024]{1,0:T(8,128)(2,1)} %w_ref.1) | copy-start | bytes 786436
  (43 other events, 333.1 us)

commit v4 on v3

--- a/solution.py
+++ b/solution.py
@@ -35,6 +35,10 @@
 
 def column(row):
     return jnp.transpose(jnp.broadcast_to(row, (8, row.shape[1])))[:, :1]
+
+
+def in_hbm(v):
+    return pltpu.with_memory_space_constraint(v, pltpu.HBM)
 
 
 def project_kernel(x_ref, wqk_ref, wv_ref, out_ref, w_ref):
@@ -62,7 +66,7 @@
         scratch_shapes=[pltpu.VMEM((model, 256), BF)],
         compiler_params=params(),
         name="project",
-    )(x, w_qk, w_v)
+    )(in_hbm(x), in_hbm(w_qk), in_hbm(w_v))
 
 
 def ring(value, shift):
@@ -449,7 +453,7 @@
         out_shape=out_shape,
         compiler_params=params(),
         name="home_rows",
-    )(*args, *home)
+    )(*args, *[in_hbm(h) for h in home])
 
 
 def finish_kernel(m_ref, w_ref, out_ref):
@@ -539,8 +543,9 @@
     (out_1,) = scatter_rows(sent_1, packed, width, False)
     half_1 = plane(out_1)
     rung_0, half_1 = together((rung_0, half_1))
-    arrived_0 = [plane(join(rung_0))]
-    arrived_1 = ring_all(part(half_1), 1)
+    arrived_0, arrived_1 = together(
+        ([plane(join(rung_0))], ring_all(part(half_1), 1))
+    )
 
     def sort_round(spots, rows):
         q_tail, kv_tail = sort_rows(spots[tail:], rows, 2 * BLOCK)
@@ -557,10 +562,11 @@
     edge, inner = attend_round(dist[0], sorted_0)
     (back_0,) = back_rows(groups_0[None], edge, inner, width, False)
     sorted_1 = sort_round(groups_1, arrived_1)
-    edge, inner = attend_round(dist[1], sorted_1)
+    q_head, q_tail, kv_head, kv_tail, halo = sorted_1
+    half_0, q_head, kv_head = together((plane(back_0), q_head, kv_head))
+    edge, inner = attend_round(dist[1], (q_head, q_tail, kv_head, kv_tail, halo))
     back_1 = back_rows(groups_1[None], edge, inner, width, True)
-
-    home_0 = ring_all(part(plane(back_0)), -1)
+    home_0, back_1 = together((ring_all(part(half_0), -1), back_1))
     home_1 = [plane(join(ring_all(back_1, -1)))]
     before = home_rows(own_0, sent_0, home_0, width)
     state = home_rows(own_1, sent_1, home_1, width, before)

time: 251 us -> 235 us (0.936)
  waiting for transfers between devices: 60.9 us -> 42.7 us
  Pallas kernels: 70.6 us -> 77.2 us
  local copies, waits for them, and re-layouts: 21.5 us -> 15.2 us
    all_to_all x4, waiting for transfers between devices: 23.1 us -> 4.07 us  [plane(): return lax.all_to_all(joint, PLANE, 0, 0, tiled=True)]
    unnamed x88 -> x74, local copies, waits for them, and re-layouts: 12.7 us -> 4.37 us
    pallas_call x2, Pallas kernels: 18.9 us -> 21.4 us  [home_rows(): pl.pallas_call(functools.partial(kernel, width), grid_spec=pltpu.Prefetch...]
  transfers between devices with their start and end apart: 23 -> 23, of which waited for: 7 -> 7; matrix products, arithmetic and copies ran while one was open for 5% -> 6% of each run, Pallas kernels for 18% -> 17%
where the time goes in v4:
time: 235 us; the launch traced here: 233 us
  Pallas kernels  77.2 us (33%)
  starting transfers between devices  56.4 us (24%)
  waiting for transfers between devices  42.7 us (18%)
  blocking collectives  34.6 us (15%)
  local copies, waits for them, and re-layouts  15.2 us (6%)
  other arithmetic  6.53 us (3%)
    ppermute x16, waiting for transfers between devices, ring(): return lax.ppermute(value, ('zl', 'zh'), route)  38.6 us
    all_to_all x1, blocking collectives, body(): merged = lax.all_to_all(state, ROUND, 0, 0, tiled=True)  34.6 us
    all_to_all x4, starting transfers between devices, plane(): return lax.all_to_all(joint, PLANE, 0, 0, tiled=True)  27.3 us
    ppermute x16, starting transfers between devices, ring(): return lax.ppermute(value, ('zl', 'zh'), route)  21.8 us
    pallas_call x2, Pallas kernels, home_rows(): pl.pallas_call(functools.partial(kernel, width), grid_spec=pltpu.Prefetch...  21.4 us
    pallas_call x4, Pallas kernels, sort_rows(): pl.pallas_call(sort_kernel, grid=(blocks,), in_specs=[pl.BlockSpec((1, 1,...  14.9 us
    pallas_call x2, Pallas kernels, scatter_rows(): pl.pallas_call(functools.partial(scatter_kernel, width), grid=(4,), in_sp...  11.2 us
    pallas_call x2, Pallas kernels, back_rows(): pl.pallas_call(functools.partial(back_kernel, width), grid=(4,), in_specs...  11 us
  transfers between devices with their start and end apart: 23, of which 7 were waited for; matrix products, arithmetic and copies ran while one was open for 6% of the time, Pallas kernels for 17%

profile of v4, /device:TPU:35, one launch (start us, length us, event | category | flops | bytes accessed | tf_op | source)
XLA Modules:
  0.0 233.3 jit_solution(2302275968224062097)
XLA Ops:
  0.0 6.0 %collective-permute-start = (s32[2,2048]{1,0:T(2,128)}, s32[2,2048]{1,0:T(2,128)S(1)}, u32[]{:S(2)}, u32[]{:S(2)}) collective-permute-start(s32[2,2048]{1,0:T(2,128)} %param.11), channel_id=1, source_target_pairs={{0,2},{2,0},{1,3},{3,1},{4,6},{6,4},{5,7},{7,5},{8,10},{10,8},{9,1... | collective-permute-start | bytes 49160 | tf_op jit(solution)/shard_map/ppermute | solution.py:529
  6.0 4.1 %project.1.rows_ref = bf16[2048,256]{1,0:T(8,128)(2,1)S(1)} custom-call(bf16[2048,1024]{1,0:T(8,128)(2,1)} %x_ref.1, bf16[1024,128]{1,0:T(8,128)(2,1)} %wqk_ref.1, bf16[1024,128]{1,0:T(8,128)(2,1)} %wv_ref.1), custom_call_target="tpu_custom_call" | custom-call | tf_op jit(solution)/shard_map/project/pallas_call | solution.py:56
  11.2 5.3 %scatter_rows.2 = (bf16[16,64,256]{2,1,0:T(8,128)(2,1)S(1)}, bf16[16,64,256]{2,1,0:T(8,128)(2,1)S(1)}, bf16[16,64,256]{2,1,0:T(8,128)(2,1)S(1)}, bf16[8,64,256]{2,1,0:T(8,128)(2,1)S(1)}, bf16[8,64,256]{2,1,0:T(8,128)(2,1)S(1)}) custom-call(s32[5,2048]{1,0:T(8,128)S(1)} %stack.118.idx_ref, bf16[2048,256]{1,0:T(8,128)(2,1)S(1)} %project.1.rows_ref), custom_call_target="tpu_custom_call" | custom-call | tf_op jit(solution)/shard_map/scatter_rows/pallas_call | solution.py:145
  16.6 5.9 %scatter_rows.3 = bf16[16,4,64,256]{3,2,1,0:T(8,128)(2,1)} custom-call(s32[5,2048]{1,0:T(8,128)S(1)} %stack.119.idx_ref, bf16[2048,256]{1,0:T(8,128)(2,1)S(1)} %project.1.rows_ref), custom_call_target="tpu_custom_call" | custom-call | tf_op jit(solution)/shard_map/scatter_rows/pallas_call | solution.py:145
  22.5 6.9 %all-to-all-start = ((bf16[16,4,64,256]{3,2,1,0:T(8,128)(2,1)}), bf16[16,4,64,256]{3,2,1,0:T(8,128)(2,1)}, u32[]{:S(2)}, u32[]{:S(2)}) async-start(bf16[16,4,64,256]{3,2,1,0:T(8,128)(2,1)} %scatter_rows.3), calls=%async_computation | async-start | bytes 4194304 | tf_op jit(solution)/shard_map/all_to_all | solution.py:94
  34.5 19.9 %collective-permute-done.3 = bf16[8,64,256]{2,1,0:T(8,128)(2,1)S(1)} collective-permute-done((bf16[8,64,256]{2,1,0:T(8,128)(2,1)S(1)}, bf16[8,64,256]{2,1,0:T(8,128)(2,1)S(1)}, u32[]{:S(2)}, u32[]{:S(2)}) %collective-permute-start.3) | collective-permute-done | bytes 262176 | tf_op jit(solution)/shard_map/ppermute | solution.py:77
  57.6 6.7 %all-to-all-start.1 = ((bf16[16,4,64,256]{3,2,1,0:T(8,128)(2,1)}), bf16[16,4,64,256]{3,2,1,0:T(8,128)(2,1)S(1)}, u32[]{:S(2)}, u32[]{:S(2)}) async-start(bf16[16,4,64,256]{3,2,1,0:T(8,128)(2,1)} %pad_maximum_fusion), calls=%async_computation.1 | async-start | bytes 4194304 | tf_op jit(solution)/shard_map/all_to_all | solution.py:94
  71.6 2.8 %collective-permute-start.8 = (bf16[8,64,256]{2,1,0:T(8,128)(2,1)}, bf16[8,64,256]{2,1,0:T(8,128)(2,1)}, u32[]{:S(2)}, u32[]{:S(2)}) collective-permute-start(bf16[8,64,256]{2,1,0:T(8,128)(2,1)} %get-tuple-element.109), channel_id=1, source_target_pairs={{0,130},{64,194},{128,0},{192,64},{2,128},{66,192},{130,2},{194,66... | collective-permute-start | bytes 786440 | tf_op jit(solution)/shard_map/ppermute | solution.py:77
  76.1 11.0 %collective-permute-done.7.refs_3_ = bf16[8,64,256]{2,1,0:T(8,128)(2,1)S(1)} collective-permute-done((bf16[8,64,256]{2,1,0:T(8,128)(2,1)}, bf16[8,64,256]{2,1,0:T(8,128)(2,1)S(1)}, u32[]{:S(2)}, u32[]{:S(2)}) %collective-permute-start.7) | collective-permute-done | bytes 262176 | tf_op jit(solution)/shard_map/ppermute | solution.py:77
  95.5 4.4 %sort_rows.4 = (bf16[1536,128]{1,0:T(8,128)(2,1)S(1)}, bf16[1536,256]{1,0:T(8,128)(2,1)S(1)}) custom-call(s32[2,1,768]{2,1,0:T(1,128)S(1)} %copy-done.1, bf16[16,4,64,256]{3,2,1,0:T(8,128)(2,1)S(1)} %all-to-all-done.1.refs_0_), custom_call_target="tpu_custom_call" | custom-call | tf_op jit(solution)/shard_map/sort_rows/pallas_call | solution.py:176
  99.9 4.5 %attend_inner.2.inner_ref = bf16[1536,256]{1,0:T(8,128)(2,1)S(1)} custom-call(s32[8]{0:T(128)S(1)} %get-tuple-element.136.dist_ref, bf16[1536,128]{1,0:T(8,128)(2,1)S(1)} %get-tuple-element.72.q_ref.qh_ref, bf16[512,128]{1,0:T(8,128)(2,1)S(1)} %get-tuple-element.75.qt_ref, bf16[1536,256]{1,0:T(8,128)(2,1)S(1)} %get-tuple-element.73.kv_ref.kvh_ref, ...), custom_call_target="tpu_custom_call" | custom-call | tf_op jit(solution)/shard_map/attend_inner/pallas_call | solution.py:276
  107.0 5.8 %back_rows.2 = bf16[16,4,72,128]{3,2,1,0:T(8,128)(2,1)} custom-call(s32[1,2048]{1,0:T(1,128)S(1)} %get-tuple-element.129.idx_ref, bf16[512,256]{1,0:T(8,128)(2,1)S(1)} %attend_edge.2.edge_ref, bf16[1536,256]{1,0:T(8,128)(2,1)S(1)} %attend_inner.2.inner_ref), custom_call_target="tpu_custom_call" | custom-call | tf_op jit(solution)/shard_map/back_rows/pallas_call | solution.py:339
  112.8 8.2 %all-to-all-start.2 = ((bf16[16,4,72,128]{3,2,1,0:T(8,128)(2,1)}), bf16[16,4,72,128]{3,2,1,0:T(8,128)(2,1)}, u32[]{:S(2)}, u32[]{:S(2)}) async-start(bf16[16,4,72,128]{3,2,1,0:T(8,128)(2,1)} %back_rows.2), calls=%async_computation.2 | async-start | bytes 2359296 | tf_op jit(solution)/shard_map/all_to_all | solution.py:94
  123.7 5.5 %sort_rows.6 = (bf16[1536,128]{1,0:T(8,128)(2,1)S(1)}, bf16[1536,256]{1,0:T(8,128)(2,1)S(1)}) custom-call(s32[2,1,768]{2,1,0:T(1,128)S(1)} %reshape.56.idx_ref, bf16[16,64,256]{2,1,0:T(8,128)(2,1)S(1)} %get-tuple-element.76.refs_0_, bf16[16,64,256]{2,1,0:T(8,128)(2,1)S(1)} %collective-permute-done.5.refs_1_, ...), custom_call_target="tpu_custom_call" | custom-call | tf_op jit(solution)/shard_map/sort_rows/pallas_call | solution.py:176
  136.5 3.9 %collective-permute-start.12 = (bf16[8,72,128]{2,1,0:T(8,128)(2,1)S(1)}, bf16[8,72,128]{2,1,0:T(8,128)(2,1)S(1)}, u32[]{:S(2)}, u32[]{:S(2)}) collective-permute-start(bf16[8,72,128]{2,1,0:T(8,128)(2,1)S(1)} %get-tuple-element.115), channel_id=1, source_target_pairs={{0,130},{64,194},{128,0},{192,64},{2,128},{66,192},{130,2},{194,66... | collective-permute-start | bytes 442376 | tf_op jit(solution)/shard_map/ppermute | solution.py:77
  140.4 3.5 %attend_inner.3.inner_ref = bf16[1536,256]{1,0:T(8,128)(2,1)S(1)} custom-call(s32[8]{0:T(128)S(1)} %copy-done.3, bf16[1536,128]{1,0:T(8,128)(2,1)S(1)} %get-tuple-element.84.q_ref.qh_ref, bf16[512,128]{1,0:T(8,128)(2,1)S(1)} %get-tuple-element.87.qt_ref, bf16[1536,256]{1,0:T(8,128)(2,1)S(1)} %get-tuple-element.85.kv_ref.kvh_ref, ...), custom_call_target="tpu_custom_call" | custom-call | tf_op jit(solution)/shard_map/attend_inner/pallas_call | solution.py:276
  145.5 5.2 %back_rows.3 = (bf16[16,72,128]{2,1,0:T(8,128)(2,1)S(1)}, bf16[16,72,128]{2,1,0:T(8,128)(2,1)S(1)}, bf16[16,72,128]{2,1,0:T(8,128)(2,1)S(1)}, bf16[8,72,128]{2,1,0:T(8,128)(2,1)S(1)}, bf16[8,72,128]{2,1,0:T(8,128)(2,1)S(1)}) custom-call(s32[1,2048]{1,0:T(1,128)S(1)} %get-tuple-element.103.idx_ref, bf16[512,256]{1,0:T(8,128)(2,1)S(1)} %attend_edge.3.edge_ref, ...), custom_call_target="tpu_custom_call" | custom-call | tf_op jit(solution)/shard_map/back_rows/pallas_call | solution.py:339
  152.3 4.8 %collective-permute-start.17 = (bf16[8,72,128]{2,1,0:T(8,128)(2,1)S(1)}, bf16[8,72,128]{2,1,0:T(8,128)(2,1)S(1)}, u32[]{:S(2)}, u32[]{:S(2)}) collective-permute-start(bf16[8,72,128]{2,1,0:T(8,128)(2,1)S(1)} %get-tuple-element.101), channel_id=1, source_target_pairs={{0,130},{64,194},{128,0},{192,64},{2,128},{66,192},{130,2},{194,66... | collective-permute-start | bytes 442376 | tf_op jit(solution)/shard_map/ppermute | solution.py:77
  157.1 2.7 %collective-permute-done.17 = bf16[8,72,128]{2,1,0:T(8,128)(2,1)S(1)} collective-permute-done((bf16[8,72,128]{2,1,0:T(8,128)(2,1)S(1)}, bf16[8,72,128]{2,1,0:T(8,128)(2,1)S(1)}, u32[]{:S(2)}, u32[]{:S(2)}) %collective-permute-start.17) | collective-permute-done | bytes 147488 | tf_op jit(solution)/shard_map/ppermute | solution.py:77
  159.9 4.9 %collective-permute-done.18 = bf16[8,72,128]{2,1,0:T(8,128)(2,1)S(1)} collective-permute-done((bf16[8,72,128]{2,1,0:T(8,128)(2,1)S(1)}, bf16[8,72,128]{2,1,0:T(8,128)(2,1)S(1)}, u32[]{:S(2)}, u32[]{:S(2)}) %collective-permute-start.18) | collective-permute-done | bytes 147488 | tf_op jit(solution)/shard_map/ppermute | solution.py:77
  166.2 5.5 %all-to-all-start.3 = ((bf16[16,4,72,128]{3,2,1,0:T(8,128)(2,1)}), bf16[16,4,72,128]{3,2,1,0:T(8,128)(2,1)S(1)}, u32[]{:S(2)}, u32[]{:S(2)}) async-start(bf16[16,4,72,128]{3,2,1,0:T(8,128)(2,1)} %pad_maximum_fusion.1), calls=%async_computation.3 | async-start | bytes 2359296 | tf_op jit(solution)/shard_map/all_to_all | solution.py:94
  172.1 9.0 %home_rows.2.before_ref = bf16[2,2048,256]{2,1,0:T(8,128)(2,1)S(1)} custom-call(s32[5]{0:T(128)S(1)} %convert_element_type.7.own_ref, s32[4,5,512]{2,1,0:T(8,128)S(1)} %bitcast.65, bf16[16,72,128]{2,1,0:T(8,128)(2,1)} %get-tuple-element.93.refs_0_, bf16[16,72,128]{2,1,0:T(8,128)(2,1)} %copy-done.5, bf16[16,72,128]{2,1,0:T(8,128)(2,1)} %copy-done.6, ...), custom_call_target="tpu_custom_call" | custom-call | tf_op jit(solution)/shard_map/home_rows/pallas_call | solution.py:444
  183.7 12.4 %home_rows.3 = bf16[4,528,128]{2,1,0:T(8,128)(2,1)S(1)} custom-call(s32[5]{0:T(128)S(1)} %convert_element_type.6.own_ref, s32[4,5,512]{2,1,0:T(8,128)S(1)} %bitcast.64, bf16[2,2048,256]{2,1,0:T(8,128)(2,1)S(1)} %home_rows.2.before_ref, bf16[16,4,72,128]{3,2,1,0:T(8,128)(2,1)} %copy-done.4), custom_call_target="tpu_custom_call" | custom-call | tf_op jit(solution)/shard_map/home_rows/pallas_call | solution.py:444
  196.1 34.6 %all_to_all.25.m_ref = bf16[4,528,128]{2,1,0:T(8,128)(2,1)S(1)} all-to-all(bf16[4,528,128]{2,1,0:T(8,128)(2,1)S(1)} %home_rows.3), channel_id=1, replica_groups=mesh['zl'=4,'x'=4,'y'=4,'zh'=2,'c'=2] {'zh','c'}, dimensions={0} | all-to-all | bytes 1081344 | tf_op jit(solution)/shard_map/all_to_all | solution.py:573
  (142 shorter events, 49.0 us)
Async XLA Ops:
  0.0 10.1 %collective-permute-start = (s32[2,2048]{1,0:T(2,128)}, s32[2,2048]{1,0:T(2,128)S(1)}, u32[]{:S(2)}, u32[]{:S(2)}) collective-permute-start(s32[2,2048]{1,0:T(2,128)} %param.11), channel_id=1, source_target_pairs={{0,2},{2,0},{1,3},{3,1},{4,6},{6,4},{5,7},{7,5},{8,10},{10,8},{9,1... | collective-permute-start | bytes 49160 | tf_op jit(solution)/shard_map/ppermute | solution.py:529
  22.5 32.5 %all-to-all-start = ((bf16[16,4,64,256]{3,2,1,0:T(8,128)(2,1)}), bf16[16,4,64,256]{3,2,1,0:T(8,128)(2,1)}, u32[]{:S(2)}, u32[]{:S(2)}) async-start(bf16[16,4,64,256]{3,2,1,0:T(8,128)(2,1)} %scatter_rows.3), calls=%async_computation | async-start | bytes 4194304 | tf_op jit(solution)/shard_map/all_to_all | solution.py:94
  29.5 24.9 %collective-permute-start.1 = (bf16[16,64,256]{2,1,0:T(8,128)(2,1)S(1)}, bf16[16,64,256]{2,1,0:T(8,128)(2,1)S(1)}, u32[]{:S(2)}, u32[]{:S(2)}) collective-permute-start(bf16[16,64,256]{2,1,0:T(8,128)(2,1)S(1)} %get-tuple-element.60), channel_id=1, source_target_pairs={{0,64},{64,128},{128,192},{192,2},{2,66},{66,130},{130,194},{194,0... | collective-permute-start | bytes 1572872 | tf_op jit(solution)/shard_map/ppermute | solution.py:77
  30.2 24.9 %collective-permute-start.2 = (bf16[16,64,256]{2,1,0:T(8,128)(2,1)S(1)}, bf16[16,64,256]{2,1,0:T(8,128)(2,1)S(1)}, u32[]{:S(2)}, u32[]{:S(2)}) collective-permute-start(bf16[16,64,256]{2,1,0:T(8,128)(2,1)S(1)} %get-tuple-element.61), channel_id=1, source_target_pairs={{0,194},{64,0},{128,64},{192,128},{2,192},{66,2},{130,66},{194,130... | collective-permute-start | bytes 1572872 | tf_op jit(solution)/shard_map/ppermute | solution.py:77
  30.9 23.4 %collective-permute-start.3 = (bf16[8,64,256]{2,1,0:T(8,128)(2,1)S(1)}, bf16[8,64,256]{2,1,0:T(8,128)(2,1)S(1)}, u32[]{:S(2)}, u32[]{:S(2)}) collective-permute-start(bf16[8,64,256]{2,1,0:T(8,128)(2,1)S(1)} %get-tuple-element.62), channel_id=1, source_target_pairs={{0,128},{64,192},{128,2},{192,66},{2,130},{66,194},{130,0},{194,64... | collective-permute-start | bytes 786440 | tf_op jit(solution)/shard_map/ppermute | solution.py:77
  32.1 22.2 %collective-permute-start.4 = (bf16[8,64,256]{2,1,0:T(8,128)(2,1)S(1)}, bf16[8,64,256]{2,1,0:T(8,128)(2,1)S(1)}, u32[]{:S(2)}, u32[]{:S(2)}) collective-permute-start(bf16[8,64,256]{2,1,0:T(8,128)(2,1)S(1)} %get-tuple-element.63), channel_id=1, source_target_pairs={{0,130},{64,194},{128,0},{192,64},{2,128},{66,192},{130,2},{194,66... | collective-permute-start | bytes 786440 | tf_op jit(solution)/shard_map/ppermute | solution.py:77
  57.6 30.5 %all-to-all-start.1 = ((bf16[16,4,64,256]{3,2,1,0:T(8,128)(2,1)}), bf16[16,4,64,256]{3,2,1,0:T(8,128)(2,1)S(1)}, u32[]{:S(2)}, u32[]{:S(2)}) async-start(bf16[16,4,64,256]{3,2,1,0:T(8,128)(2,1)} %pad_maximum_fusion), calls=%async_computation.1 | async-start | bytes 4194304 | tf_op jit(solution)/shard_map/all_to_all | solution.py:94
  67.5 19.6 %collective-permute-start.5 = (bf16[16,64,256]{2,1,0:T(8,128)(2,1)}, bf16[16,64,256]{2,1,0:T(8,128)(2,1)S(1)}, u32[]{:S(2)}, u32[]{:S(2)}) collective-permute-start(bf16[16,64,256]{2,1,0:T(8,128)(2,1)} %get-tuple-element.112), channel_id=1, source_target_pairs={{0,64},{64,128},{128,192},{192,2},{2,66},{66,130},{130,194},{194,0... | collective-permute-start | bytes 1572872 | tf_op jit(solution)/shard_map/ppermute | solution.py:77
  68.2 18.9 %collective-permute-start.6 = (bf16[16,64,256]{2,1,0:T(8,128)(2,1)}, bf16[16,64,256]{2,1,0:T(8,128)(2,1)}, u32[]{:S(2)}, u32[]{:S(2)}) collective-permute-start(bf16[16,64,256]{2,1,0:T(8,128)(2,1)} %get-tuple-element.111), channel_id=1, source_target_pairs={{0,194},{64,0},{128,64},{192,128},{2,192},{66,2},{130,66},{194,130... | collective-permute-start | bytes 1572872 | tf_op jit(solution)/shard_map/ppermute | solution.py:77
  70.8 16.3 %collective-permute-start.7 = (bf16[8,64,256]{2,1,0:T(8,128)(2,1)}, bf16[8,64,256]{2,1,0:T(8,128)(2,1)S(1)}, u32[]{:S(2)}, u32[]{:S(2)}) collective-permute-start(bf16[8,64,256]{2,1,0:T(8,128)(2,1)} %get-tuple-element.110), channel_id=1, source_target_pairs={{0,128},{64,192},{128,2},{192,66},{2,130},{66,194},{130,0},{194,64... | collective-permute-start | bytes 786440 | tf_op jit(solution)/shard_map/ppermute | solution.py:77
  71.6 15.5 %collective-permute-start.8 = (bf16[8,64,256]{2,1,0:T(8,128)(2,1)}, bf16[8,64,256]{2,1,0:T(8,128)(2,1)}, u32[]{:S(2)}, u32[]{:S(2)}) collective-permute-start(bf16[8,64,256]{2,1,0:T(8,128)(2,1)} %get-tuple-element.109), channel_id=1, source_target_pairs={{0,130},{64,194},{128,0},{192,64},{2,128},{66,192},{130,2},{194,66... | collective-permute-start | bytes 786440 | tf_op jit(solution)/shard_map/ppermute | solution.py:77
  91.1 13.4 %collective-permute-start.9 = (bf16[512,256]{1,0:T(8,128)(2,1)}, bf16[512,256]{1,0:T(8,128)(2,1)}, u32[]{:S(2)}, u32[]{:S(2)}) collective-permute-start(bf16[512,256]{1,0:T(8,128)(2,1)} %get-tuple-element.74.kvt_ref), channel_id=1, source_target_pairs={{0,4},{4,8},{8,12},{12,16},{16,20},{20,24},{24,28},{28,32},{32,36}... | collective-permute-start | bytes 786440 | tf_op jit(solution)/shard_map/ppermute | solution.py:552
  112.8 19.3 %all-to-all-start.2 = ((bf16[16,4,72,128]{3,2,1,0:T(8,128)(2,1)}), bf16[16,4,72,128]{3,2,1,0:T(8,128)(2,1)}, u32[]{:S(2)}, u32[]{:S(2)}) async-start(bf16[16,4,72,128]{3,2,1,0:T(8,128)(2,1)} %back_rows.2), calls=%async_computation.2 | async-start | bytes 2359296 | tf_op jit(solution)/shard_map/all_to_all | solution.py:94
  129.2 14.7 %collective-permute-start.14 = (bf16[512,256]{1,0:T(8,128)(2,1)S(1)}, bf16[512,256]{1,0:T(8,128)(2,1)S(1)}, u32[]{:S(2)}, u32[]{:S(2)}) collective-permute-start(bf16[512,256]{1,0:T(8,128)(2,1)S(1)} %get-tuple-element.86.kvt_ref), channel_id=1, source_target_pairs={{0,4},{4,8},{8,12},{12,16},{16,20},{20,24},{24,28},{28,32},{32,36}... | collective-permute-start | bytes 786440 | tf_op jit(solution)/shard_map/ppermute | solution.py:552
  134.0 16.7 %collective-permute-start.10 = (bf16[16,72,128]{2,1,0:T(8,128)(2,1)S(1)}, bf16[16,72,128]{2,1,0:T(8,128)(2,1)S(1)}, u32[]{:S(2)}, u32[]{:S(2)}) collective-permute-start(bf16[16,72,128]{2,1,0:T(8,128)(2,1)S(1)} %get-tuple-element.117), channel_id=1, source_target_pairs={{0,194},{64,0},{128,64},{192,128},{2,192},{66,2},{130,66},{194,130... | collective-permute-start | bytes 884744 | tf_op jit(solution)/shard_map/ppermute | solution.py:77
  134.7 16.1 %collective-permute-start.11 = (bf16[16,72,128]{2,1,0:T(8,128)(2,1)S(1)}, bf16[16,72,128]{2,1,0:T(8,128)(2,1)S(1)}, u32[]{:S(2)}, u32[]{:S(2)}) collective-permute-start(bf16[16,72,128]{2,1,0:T(8,128)(2,1)S(1)} %get-tuple-element.116), channel_id=1, source_target_pairs={{0,64},{64,128},{128,192},{192,2},{2,66},{66,130},{130,194},{194,0... | collective-permute-start | bytes 884744 | tf_op jit(solution)/shard_map/ppermute | solution.py:77
  136.5 14.2 %collective-permute-start.12 = (bf16[8,72,128]{2,1,0:T(8,128)(2,1)S(1)}, bf16[8,72,128]{2,1,0:T(8,128)(2,1)S(1)}, u32[]{:S(2)}, u32[]{:S(2)}) collective-permute-start(bf16[8,72,128]{2,1,0:T(8,128)(2,1)S(1)} %get-tuple-element.115), channel_id=1, source_target_pairs={{0,130},{64,194},{128,0},{192,64},{2,128},{66,192},{130,2},{194,66... | collective-permute-start | bytes 442376 | tf_op jit(solution)/shard_map/ppermute | solution.py:77
  140.4 10.3 %collective-permute-start.13 = (bf16[8,72,128]{2,1,0:T(8,128)(2,1)S(1)}, bf16[8,72,128]{2,1,0:T(8,128)(2,1)S(1)}, u32[]{:S(2)}, u32[]{:S(2)}) collective-permute-start(bf16[8,72,128]{2,1,0:T(8,128)(2,1)S(1)} %get-tuple-element.114), channel_id=1, source_target_pairs={{0,128},{64,192},{128,2},{192,66},{2,130},{66,194},{130,0},{194,64... | collective-permute-start | bytes 442376 | tf_op jit(solution)/shard_map/ppermute | solution.py:77
  150.8 14.0 %collective-permute-start.15 = (bf16[16,72,128]{2,1,0:T(8,128)(2,1)S(1)}, bf16[16,72,128]{2,1,0:T(8,128)(2,1)S(1)}, u32[]{:S(2)}, u32[]{:S(2)}) collective-permute-start(bf16[16,72,128]{2,1,0:T(8,128)(2,1)S(1)} %get-tuple-element.99), channel_id=1, source_target_pairs={{0,194},{64,0},{128,64},{192,128},{2,192},{66,2},{130,66},{194,130... | collective-permute-start | bytes 884744 | tf_op jit(solution)/shard_map/ppermute | solution.py:77
  150.9 14.0 %collective-permute-start.16 = (bf16[16,72,128]{2,1,0:T(8,128)(2,1)S(1)}, bf16[16,72,128]{2,1,0:T(8,128)(2,1)S(1)}, u32[]{:S(2)}, u32[]{:S(2)}) collective-permute-start(bf16[16,72,128]{2,1,0:T(8,128)(2,1)S(1)} %get-tuple-element.100), channel_id=1, source_target_pairs={{0,64},{64,128},{128,192},{192,2},{2,66},{66,130},{130,194},{194,0... | collective-permute-start | bytes 884744 | tf_op jit(solution)/shard_map/ppermute | solution.py:77
  152.3 7.5 %collective-permute-start.17 = (bf16[8,72,128]{2,1,0:T(8,128)(2,1)S(1)}, bf16[8,72,128]{2,1,0:T(8,128)(2,1)S(1)}, u32[]{:S(2)}, u32[]{:S(2)}) collective-permute-start(bf16[8,72,128]{2,1,0:T(8,128)(2,1)S(1)} %get-tuple-element.101), channel_id=1, source_target_pairs={{0,130},{64,194},{128,0},{192,64},{2,128},{66,192},{130,2},{194,66... | collective-permute-start | bytes 442376 | tf_op jit(solution)/shard_map/ppermute | solution.py:77
  157.1 7.7 %collective-permute-start.18 = (bf16[8,72,128]{2,1,0:T(8,128)(2,1)S(1)}, bf16[8,72,128]{2,1,0:T(8,128)(2,1)S(1)}, u32[]{:S(2)}, u32[]{:S(2)}) collective-permute-start(bf16[8,72,128]{2,1,0:T(8,128)(2,1)S(1)} %get-tuple-element.102), channel_id=1, source_target_pairs={{0,128},{64,192},{128,2},{192,66},{2,130},{66,194},{130,0},{194,64... | collective-permute-start | bytes 442376 | tf_op jit(solution)/shard_map/ppermute | solution.py:77
  166.2 16.5 %all-to-all-start.3 = ((bf16[16,4,72,128]{3,2,1,0:T(8,128)(2,1)}), bf16[16,4,72,128]{3,2,1,0:T(8,128)(2,1)S(1)}, u32[]{:S(2)}, u32[]{:S(2)}) async-start(bf16[16,4,72,128]{3,2,1,0:T(8,128)(2,1)} %pad_maximum_fusion.1), calls=%async_computation.3 | async-start | bytes 2359296 | tf_op jit(solution)/shard_map/all_to_all | solution.py:94
  183.7 47.0 %copy-start = (bf16[128,1024]{1,0:T(8,128)(2,1)S(1)}, bf16[128,1024]{1,0:T(8,128)(2,1)}, u32[]{:S(2)}) copy-start(bf16[128,1024]{1,0:T(8,128)(2,1)} %w_ref.1) | copy-start | bytes 786436
  (36 other events, 263.3 us)

commit v5 on v4

--- a/solution.py
+++ b/solution.py
@@ -9,7 +9,6 @@
 from jax.sharding import PartitionSpec as P
 
 BLOCK = 256
-SHIFTS = (0, 1, -1, 2, -2)
 MASKED = -1000000000.0
 SEQ = ("zl", "x", "y")
 PLANE = ("x", "y")
@@ -77,17 +76,8 @@
     return lax.ppermute(value, ("zl", "zh"), route)
 
 
-def ring_all(pieces, sign):
-    return [pieces[0]] + [ring(p, sign * k) for p, k in zip(pieces[1:], SHIFTS[1:])]
-
-
-def join(split):
-    a, b, c, d, e = split
-    return jnp.stack([a, b, c, jnp.concatenate([d, e])], axis=1)
-
-
-def part(joint):
-    return [joint[:, 0], joint[:, 1], joint[:, 2], joint[:8, 3], joint[8:, 3]]
+def join(first, second):
+    return jnp.stack([first, second], axis=1)
 
 
 def plane(joint):
@@ -97,57 +87,29 @@
 together = lax.optimization_barrier
 
 
-def emit_specs(split, width, lanes):
-    if not split:
-        return (
-            [pl.BlockSpec((16, 1, width, lanes), lambda i: (0, i, 0, 0))],
-            [jax.ShapeDtypeStruct((16, 4, width, lanes), BF)],
-        )
-    shapes = [(16, width, lanes)] * 3 + [(8, width, lanes)] * 2
-    return [whole(v) for v in shapes], [jax.ShapeDtypeStruct(v, BF) for v in shapes]
-
-
-def emit(refs, store):
-    if len(refs) == 1:
-        for half in range(2):
-            store(refs[0].at[8 * half : 8 * half + 8, 0], half)
-        return
-    for group in range(4):
-
-        @pl.when(pl.program_id(0) == group)
-        def _(group=group):
-            for half in range(2):
-                if group < 3:
-                    store(refs[group].at[8 * half : 8 * half + 8], half)
-                else:
-                    store(refs[3 + half], half)
-
-
-def scatter_kernel(width, idx_ref, rows_ref, *out_refs):
-    n = 8 * width
+def scatter_kernel(idx_ref, rows_ref, even_ref, up_ref, down_ref):
+    peers, _, width, lanes = even_ref.shape
     group = pl.program_id(0)
-    place = lax.broadcasted_iota(jnp.int32, (n, rows_ref.shape[0]), 0)
-    halves = []
-    for half in range(2):
-        line = idx_ref[pl.ds(jnp.where(group == 3, 3 + half, group), 1), :]
-        hot = one_hot(line - half * n, place)
-        got = jnp.dot(hot, rows_ref[...], preferred_element_type=F32).astype(BF)
-        halves.append(got.reshape(8, width, 256))
-
-    def store(ref, half):
-        ref[...] = halves[half]
-
-    emit(out_refs, store)
-
-
-def scatter_rows(idx, rows, width, split):
-    specs, shapes = emit_specs(split, width, 256)
-    return pl.pallas_call(
-        functools.partial(scatter_kernel, width),
+    place = lax.broadcasted_iota(jnp.int32, (peers * width, rows_ref.shape[0]), 0)
+    hot = one_hot(idx_ref[pl.ds(group, 1), :], place)
+    got = jnp.dot(hot, rows_ref[...], preferred_element_type=F32)
+    got = got.astype(BF).reshape(peers, width, lanes)
+    places = (even_ref.at[:, 0], even_ref.at[:, 1], up_ref, down_ref)
+    for g, ref in enumerate(places):
+
+        @pl.when(group == g)
+        def _(ref=ref):
+            ref[...] = got
+
+
+def scatter_rows(idx, rows, width):
+    shapes = [(16, 2, width, 256)] + [(16, width, 256)] * 2
+    return pl.pallas_call(
+        scatter_kernel,
         grid=(4,),
         in_specs=[whole(idx.shape), whole(rows.shape)],
-        out_specs=specs,
-        out_shape=shapes,
+        out_specs=[whole(v) for v in shapes],
+        out_shape=[pltpu.HBM(v, BF) for v in shapes],
         compiler_params=params(),
         name="scatter_rows",
     )(idx, rows)
@@ -173,11 +135,13 @@
 def sort_rows(idx, rows, step):
     count = idx.shape[-1]
     blocks = count // step
+    peers, _, width, lanes = rows[0].shape
+    near = pl.BlockSpec((peers, 1, width, lanes), lambda i: (0, 0, 0, 0))
     return pl.pallas_call(
         sort_kernel,
         grid=(blocks,),
-        in_specs=[pl.BlockSpec((1, 1, step), lambda i: (i, 0, 0))]
-        + [whole(r.shape) for r in rows],
+        in_specs=[pl.BlockSpec((1, 1, step), lambda i: (i, 0, 0)), near]
+        + [whole(r.shape) for r in rows[1:]],
         out_specs=[
             pl.BlockSpec((step, 128), lambda i: (i, 0)),
             pl.BlockSpec((step, 256), lambda i: (i, 0)),
@@ -188,7 +152,7 @@
         ],
         compiler_params=params(),
         name="sort_rows",
-    )(idx.reshape(blocks, 1, step), *rows)
+    )(idx.reshape(blocks, 1, step), *[in_hbm(r) for r in rows])
 
 
 def terms_to_lines(terms, groups):
@@ -307,41 +271,59 @@
     )(dist, q, kv, halo)
 
 
-def back_kernel(width, idx_ref, edge_ref, inner_ref, *out_refs):
-    n = 8 * width
-    halves = []
-    for half in range(2):
-        idx = idx_ref[...] - (pl.program_id(0) * 2 + half) * n
-        got = 0.0
-        first = 0
-        for ref in (edge_ref, inner_ref):
-            count = ref.shape[0]
-            place = lax.broadcasted_iota(jnp.int32, (n, count), 0)
-            hot = one_hot(idx[:, first : first + count], place)
-            got += jnp.dot(hot, ref[...], preferred_element_type=F32)
-            first += count
-        lines = terms_to_lines(got[:, 128:], n // 32).reshape(8, width // 32, 1, 128)
-        row = lax.broadcasted_iota(jnp.int32, (8, 8, 128), 1)
-        tail = jnp.zeros((8, 8, 128), F32)
-        for part in range(width // 32):
-            tail = jnp.where(row == part, lines[:, part], tail)
-        halves.append((got[:, :128].astype(BF).reshape(8, width, 128), tail.astype(BF)))
-
-    def store(ref, half):
-        ref[:, :width, :] = halves[half][0]
-        ref[:, width:, :] = halves[half][1]
-
-    emit(out_refs, store)
-
-
-def back_rows(idx, edge, inner, width, split):
-    specs, shapes = emit_specs(split, width + 8, 128)
-    return pl.pallas_call(
-        functools.partial(back_kernel, width),
+def back_kernel(idx_ref, edge_ref, inner_ref, near_ref, low_ref, high_ref, odd_ref):
+    peers, ext, _ = near_ref.shape
+    width = ext - 8
+    n = peers * width
+    group = pl.program_id(0)
+    idx = idx_ref[...] - group * n
+    got = 0.0
+    first = 0
+    for ref in (edge_ref, inner_ref):
+        count = ref.shape[0]
+        place = lax.broadcasted_iota(jnp.int32, (n, count), 0)
+        hot = one_hot(idx[:, first : first + count], place)
+        got += jnp.dot(hot, ref[...], preferred_element_type=F32)
+        first += count
+    lines = terms_to_lines(got[:, 128:], n // 32).reshape(peers, width // 32, 1, 128)
+    row = lax.broadcasted_iota(jnp.int32, (peers, 8, 128), 1)
+    tail = jnp.zeros((peers, 8, 128), F32)
+    for part in range(width // 32):
+        tail = jnp.where(row == part, lines[:, part], tail)
+    tail = tail.astype(BF)
+    got = got[:, :128].astype(BF).reshape(peers, width, 128)
+
+    def store(ref, at):
+        ref[:, :width, :] = got[at]
+        ref[:, width:, :] = tail[at]
+
+    every, half = slice(None), peers // 2
+
+    @pl.when(group == 0)
+    def _():
+        store(near_ref, every)
+
+    @pl.when(group == 1)
+    def _():
+        store(low_ref, slice(0, half))
+        store(high_ref, slice(half, peers))
+
+    for g in range(2):
+
+        @pl.when(group == 2 + g)
+        def _(g=g):
+            store(odd_ref.at[:, g], every)
+
+
+def back_rows(idx, edge, inner, width):
+    ext = width + 8
+    shapes = [(16, ext, 128), (8, ext, 128), (8, ext, 128), (16, 2, ext, 128)]
+    return pl.pallas_call(
+        back_kernel,
         grid=(4,),
         in_specs=[whole(idx.shape), whole(edge.shape), whole(inner.shape)],
-        out_specs=specs,
-        out_shape=shapes,
+        out_specs=[whole(v) for v in shapes],
+        out_shape=[pltpu.HBM(v, BF) for v in shapes],
         compiler_params=params(),
         name="back_rows",
     )(idx, edge, inner)
@@ -350,14 +332,9 @@
 ABSENT = -1e30
 
 
-def fill_home(x_ref, width, home_refs):
-    if len(home_refs) == 5:
-        blocks = home_refs
-    else:
-        ref = home_refs[0]
-        blocks = [ref.at[:, g] for g in range(3)] + [ref.at[:8, 3], ref.at[8:, 3]]
+def fill_home(x_ref, width, even_ref, up_ref, down_ref):
     row = 0
-    for block in blocks:
+    for block in (even_ref.at[:, 0], even_ref.at[:, 1], up_ref, down_ref):
         size = block.shape[0] * width
         x_ref[row : row + size, :128] = block[:, :width, :].reshape(size, 128)
         tail = block[:, width:, :].astype(F32)
@@ -369,14 +346,12 @@
 
 
 def gather_home(own_ref, cols, x_ref, width):
-    near, far, row = 0.0, 0.0, 0
-    for g in range(5):
-        size = (16 if g < 3 else 8) * width
-        first = 8 * width if g == 4 else 0
-        place = lax.broadcasted_iota(jnp.int32, (cols.shape[0], size), 1) + first
+    near, far = 0.0, 0.0
+    size = 16 * width
+    place = lax.broadcasted_iota(jnp.int32, (cols.shape[0], size), 1)
+    for g in range(4):
         hot = one_hot(cols[:, g : g + 1], place)
-        got = jnp.dot(hot, x_ref[row : row + size], preferred_element_type=F32)
-        row += size
+        got = jnp.dot(hot, x_ref[g * size : (g + 1) * size], preferred_element_type=F32)
         if g == 0:
             near = got
         else:
@@ -391,7 +366,7 @@
 
     @pl.when(pl.program_id(0) == 0)
     def _():
-        fill_home(x_ref, width, home_refs)
+        fill_home(x_ref, width, *home_refs)
 
     near, far = gather_home(own_ref, jnp.transpose(idx_ref[0]), x_ref, width)
     out_ref[0] = near.astype(BF)
@@ -403,7 +378,7 @@
 
     @pl.when(pl.program_id(0) == 0)
     def _():
-        fill_home(x_ref, width, home_refs)
+        fill_home(x_ref, width, *home_refs)
 
     step = idx_ref.shape[2]
     states = list(gather_home(own_ref, jnp.transpose(idx_ref[0]), x_ref, width))
@@ -485,39 +460,27 @@
     )(merged, w_out)
 
 
-def send_places(own_slots, other_slots, low, width, by_target):
+def send_places(own_slots, other_slots, width):
     zl, zh = lax.axis_index("zl"), lax.axis_index("zh")
     late = lax.axis_index(PLANE) >= 8
     places, mine = [], []
-    for g, shift in enumerate(SHIFTS):
-        if by_target or g < 3:
-            k = shift
-        else:
-            k = jnp.where(late, -2, 2)
-        own = ((zh * 4 + zl + k + 8) & 7) // 4 == zh
+    for shift in (0, jnp.where(late, -2, 2), 1, -1):
+        own = ((zh * 4 + zl + shift + 8) & 7) // 4 == zh
         slot = jnp.where(own, own_slots, other_slots)
-        place = (slot >> 6) & 15
-        at = slot & 63
-        hit = ((slot >> 10) == ((zl + k + 8) & 3)) & (at >= low) & (at < low + width)
-        if g == 3:
-            hit &= place < 8
-        if g == 4:
-            hit &= place >= 8
-        places.append(jnp.where(hit, place * width + at - low, -1))
+        hit = (slot >> 10) == ((zl + shift + 8) & 3)
+        places.append(jnp.where(hit, ((slot >> 6) & 15) * width + (slot & 63), -1))
         mine.append(own)
     return jnp.stack(places), jnp.stack(mine).astype(jnp.int32)
 
 
-def take_places(taken, low, width):
-    zl = lax.axis_index("zl")
-    away = (zl - (taken >> 10)) & 3
-    group = jnp.where(away < 2, away, 5 - away)
+def take_places(taken, width):
+    away = (lax.axis_index("zl") - (taken >> 10)) & 3
+    group = jnp.where(away == 1, 2, jnp.where(away == 2, 1, away))
     source = (taken >> 6) & 15
     at = taken & 63
-    hit = (at >= low) & (at < low + width)
-    by_group = jnp.where(hit, (group * 16 + source) * width + at - low, -1)
-    by_source = jnp.where(hit, (source * 4 + group) * width + at - low, -1)
-    return by_group, by_source
+    by_group = (group * 16 + source) * width + at
+    odd = (32 + source * 2 + group - 2) * width + at
+    return jnp.where(group < 2, by_group, odd), by_group
 
 
 def body(x, w_qk, w_v, w_out, slots, taken, looks):
@@ -531,21 +494,25 @@
     mine = lax.axis_index(SEQ) * blocks + jnp.arange(blocks, dtype=jnp.int32)
     dist = (mine[None, :] - looks) % (peers * blocks)
     next_device = [(i, (i + 1) % peers) for i in range(peers)]
-    sent_0, own_0 = send_places(slots[0], others[0], 0, width, True)
-    sent_1, own_1 = send_places(slots[1], others[1], 0, width, False)
-    groups_0, _ = take_places(taken[0], 0, width)
-    _, spots_0 = take_places(taken[0], 0, width)
-    groups_1, _ = take_places(taken[1], 0, width)
-
-    out_0 = scatter_rows(sent_0, packed, width, True)
-    out_0, packed = together((out_0, packed))
-    rung_0 = ring_all(out_0, 1)
-    (out_1,) = scatter_rows(sent_1, packed, width, False)
-    half_1 = plane(out_1)
-    rung_0, half_1 = together((rung_0, half_1))
-    arrived_0, arrived_1 = together(
-        ([plane(join(rung_0))], ring_all(part(half_1), 1))
-    )
+    sent_0, own_0 = send_places(slots[0], others[0], width)
+    sent_1, own_1 = send_places(slots[1], others[1], width)
+    spots_0, groups_0 = take_places(taken[0], width)
+    spots_1, groups_1 = take_places(taken[1], width)
+
+    def leave(out):
+        even, up, down = out
+        return plane(even), [ring(up, 1), ring(down, -1)]
+
+    def arrive(half, rung):
+        return [ring(half[:8, 1], 2), ring(half[8:, 1], -2)], plane(join(*rung))
+
+    def turn(back):
+        _, low, high, odd = back
+        return [ring(low, -2), ring(high, 2)], plane(odd)
+
+    def land(back, rung, half):
+        even = plane(join(back[0], jnp.concatenate(rung)))
+        return [even, ring(half[:, 0], -1), ring(half[:, 1], 1)]
 
     def sort_round(spots, rows):
         q_tail, kv_tail = sort_rows(spots[tail:], rows, 2 * BLOCK)
@@ -553,21 +520,38 @@
         q_head, kv_head = sort_rows(spots[:tail], rows, 3 * BLOCK)
         return q_head, q_tail, kv_head, kv_tail, halo
 
-    def attend_round(near, sorted_rows):
-        q_head, q_tail, kv_head, kv_tail, halo = sorted_rows
-        inner = attend_inner(near, q_head, q_tail, kv_head, kv_tail)
-        return attend_edge(near, q_head, kv_head, halo), inner
-
-    sorted_0 = sort_round(spots_0, arrived_0)
-    edge, inner = attend_round(dist[0], sorted_0)
-    (back_0,) = back_rows(groups_0[None], edge, inner, width, False)
-    sorted_1 = sort_round(groups_1, arrived_1)
-    q_head, q_tail, kv_head, kv_tail, halo = sorted_1
-    half_0, q_head, kv_head = together((plane(back_0), q_head, kv_head))
-    edge, inner = attend_round(dist[1], (q_head, q_tail, kv_head, kv_tail, halo))
-    back_1 = back_rows(groups_1[None], edge, inner, width, True)
-    home_0, back_1 = together((ring_all(part(half_0), -1), back_1))
-    home_1 = [plane(join(ring_all(back_1, -1)))]
+    out_0 = scatter_rows(sent_0, packed, width)
+    out_0, packed = together((out_0, packed))
+    half_0, rung_0 = leave(out_0)
+    out_1 = scatter_rows(sent_1, packed, width)
+    half_0, rung_0, out_1 = together((half_0, rung_0, out_1))
+    far_0, odd_0 = arrive(half_0, rung_0)
+    far_0, odd_0, out_1 = together((far_0, odd_0, out_1))
+    half_1, rung_1 = leave(out_1)
+
+    q_head, q_tail, kv_head, kv_tail, halo = sort_round(spots_0, [half_0, *far_0, odd_0])
+    inner = attend_inner(dist[0], q_head, q_tail, kv_head, kv_tail)
+    inner, q_head, kv_head, halo, half_1, rung_1 = together(
+        (inner, q_head, kv_head, halo, half_1, rung_1)
+    )
+    far_1, odd_1 = arrive(half_1, rung_1)
+    edge = attend_edge(dist[0], q_head, kv_head, halo)
+    back_0 = back_rows(groups_0[None], edge, inner, width)
+    back_0, far_1, odd_1 = together((back_0, far_1, odd_1))
+    rung_0, half_0 = turn(back_0)
+
+    q_head, q_tail, kv_head, kv_tail, halo = sort_round(spots_1, [half_1, *far_1, odd_1])
+    inner = attend_inner(dist[1], q_head, q_tail, kv_head, kv_tail)
+    inner, q_head, kv_head, halo, half_0, rung_0 = together(
+        (inner, q_head, kv_head, halo, half_0, rung_0)
+    )
+    home_0 = land(back_0, rung_0, half_0)
+    edge = attend_edge(dist[1], q_head, kv_head, halo)
+    back_1 = back_rows(groups_1[None], edge, inner, width)
+    home_0, back_1 = together((home_0, back_1))
+    rung_1, half_1 = together(turn(back_1))
+    home_1 = land(back_1, rung_1, half_1)
+
     before = home_rows(own_0, sent_0, home_0, width)
     state = home_rows(own_1, sent_1, home_1, width, before)
     merged = lax.all_to_all(state, ROUND, 0, 0, tiled=True)

time: 235 us -> 236 us (level)
  starting transfers between devices: 56.4 us -> 79.9 us
  local copies, waits for them, and re-layouts: 15.2 us -> 2.73 us
  waiting for transfers between devices: 42.7 us -> 31.7 us
  Pallas kernels: 77.2 us -> 81.8 us
  blocking collectives: 34.6 us -> 30.7 us
    all_to_all x4 -> x8, starting transfers between devices: 27.3 us -> 53.1 us  [plane(): return lax.all_to_all(joint, PLANE, 0, 0, tiled=True)]
    ppermute x16, waiting for transfers between devices: 38.6 us -> 28.7 us  [ring(): return lax.ppermute(value, ('zl', 'zh'), route)]
    squeeze x5, local copies, waits for them, and re-layouts: 8.48 us -> 1.2 us  [the longest x2 1.11 us: arrive(): return ([ring(half[:8, 1], 2), ring(half[8:, 1], -2)], plane(join(*rung)))]
    all_to_all x1, blocking collectives: 34.6 us -> 30.7 us  [body(): merged = lax.all_to_all(state, ROUND, 0, 0, tiled=True)]
    ppermute x16, starting transfers between devices: 21.8 us -> 18.2 us  [ring(): return lax.ppermute(value, ('zl', 'zh'), route)]
    pallas_call x4, Pallas kernels: 22.2 us -> 25.8 us  [the longest x2 13.2 us: scatter_rows(): pl.pallas_call(scatter_kernel, grid=(4,), in_specs=[whole(idx.shape), who...]
    another operation x4 -> x7, other arithmetic: 3.77 us -> 7.27 us  [the longest x6 7.21 us: join(): return jnp.stack([first, second], axis=1)]
    pallas_call x4, Pallas kernels: 14.9 us -> 18.2 us  [sort_rows(): pl.pallas_call(sort_kernel, grid=(blocks,), in_specs=[pl.BlockSpec((1, 1,...]
  transfers between devices with their start and end apart: 23 -> 27, of which waited for: 7 -> 9; matrix products, arithmetic and copies ran while one was open for 6% -> 1% of each run, Pallas kernels for 17% -> 26%
where the time goes in v5:
time: 236 us; the launch traced here: 235 us
  Pallas kernels  81.8 us (35%)
  starting transfers between devices  79.9 us (34%)
  waiting for transfers between devices  31.7 us (13%)
  blocking collectives  30.7 us (13%)
  other arithmetic  7.72 us (3%)
  local copies, waits for them, and re-layouts  2.73 us (1%)
    all_to_all x8, starting transfers between devices, plane(): return lax.all_to_all(joint, PLANE, 0, 0, tiled=True)  53.1 us
    all_to_all x1, blocking collectives, body(): merged = lax.all_to_all(state, ROUND, 0, 0, tiled=True)  30.7 us
    ppermute x16, waiting for transfers between devices, ring(): return lax.ppermute(value, ('zl', 'zh'), route)  28.7 us
    pallas_call x2, Pallas kernels, home_rows(): pl.pallas_call(functools.partial(kernel, width), grid_spec=pltpu.Prefetch...  21.1 us
    pallas_call x4, Pallas kernels, sort_rows(): pl.pallas_call(sort_kernel, grid=(blocks,), in_specs=[pl.BlockSpec((1, 1,...  18.2 us
    ppermute x16, starting transfers between devices, ring(): return lax.ppermute(value, ('zl', 'zh'), route)  18.2 us
    pallas_call x2, Pallas kernels, scatter_rows(): pl.pallas_call(scatter_kernel, grid=(4,), in_specs=[whole(idx.shape), who...  13.2 us
    pallas_call x2, Pallas kernels, back_rows(): pl.pallas_call(back_kernel, grid=(4,), in_specs=[whole(idx.shape), whole(...  12.6 us
  transfers between devices with their start and end apart: 27, of which 9 were waited for; matrix products, arithmetic and copies ran while one was open for 1% of the time, Pallas kernels for 26%

profile of v5, /device:TPU:35, one launch (start us, length us, event | category | flops | bytes accessed | tf_op | source)
XLA Modules:
  0.0 235.1 jit_solution(15796541485639274220)
XLA Ops:
  0.0 6.0 %collective-permute-start = (s32[2,2048]{1,0:T(2,128)}, s32[2,2048]{1,0:T(2,128)S(1)}, u32[]{:S(2)}, u32[]{:S(2)}) collective-permute-start(s32[2,2048]{1,0:T(2,128)} %param.11), channel_id=1, source_target_pairs={{0,2},{2,0},{1,3},{3,1},{4,6},{6,4},{5,7},{7,5},{8,10},{10,8},{9,1... | collective-permute-start | bytes 49160 | tf_op jit(solution)/shard_map/ppermute | solution.py:492
  6.0 4.1 %project.1.rows_ref = bf16[2048,256]{1,0:T(8,128)(2,1)S(1)} custom-call(bf16[2048,1024]{1,0:T(8,128)(2,1)} %x_ref.1, bf16[1024,128]{1,0:T(8,128)(2,1)} %wqk_ref.1, bf16[1024,128]{1,0:T(8,128)(2,1)} %wv_ref.1), custom_call_target="tpu_custom_call" | custom-call | tf_op jit(solution)/shard_map/project/pallas_call | solution.py:55
  10.5 6.6 %scatter_rows.2 = (bf16[16,2,64,256]{3,2,1,0:T(8,128)(2,1)}, bf16[16,64,256]{2,1,0:T(8,128)(2,1)}, bf16[16,64,256]{2,1,0:T(8,128)(2,1)}) custom-call(s32[4,2048]{1,0:T(4,128)S(1)} %get-tuple-element.171.idx_ref, bf16[2048,256]{1,0:T(8,128)(2,1)S(1)} %project.1.rows_ref), custom_call_target="tpu_custom_call" | custom-call | tf_op jit(solution)/shard_map/scatter_rows/pallas_call | solution.py:107
  17.2 6.9 %all-to-all-start = ((bf16[16,2,64,256]{3,2,1,0:T(8,128)(2,1)}), bf16[16,2,64,256]{3,2,1,0:T(8,128)(2,1)S(1)}, u32[]{:S(2)}, u32[]{:S(2)}) async-start(bf16[16,2,64,256]{3,2,1,0:T(8,128)(2,1)} %get-tuple-element.77), calls=%async_computation | async-start | bytes 2097152 | tf_op jit(solution)/shard_map/all_to_all | solution.py:84
  25.6 6.6 %scatter_rows.3 = (bf16[16,2,64,256]{3,2,1,0:T(8,128)(2,1)}, bf16[16,64,256]{2,1,0:T(8,128)(2,1)}, bf16[16,64,256]{2,1,0:T(8,128)(2,1)}) custom-call(s32[4,2048]{1,0:T(4,128)S(1)} %get-tuple-element.172.idx_ref, bf16[2048,256]{1,0:T(8,128)(2,1)S(1)} %project.1.rows_ref), custom_call_target="tpu_custom_call" | custom-call | tf_op jit(solution)/shard_map/scatter_rows/pallas_call | solution.py:107
  32.1 4.1 %collective-permute-done.1 = bf16[16,64,256]{2,1,0:T(8,128)(2,1)S(1)} collective-permute-done((bf16[16,64,256]{2,1,0:T(8,128)(2,1)}, bf16[16,64,256]{2,1,0:T(8,128)(2,1)S(1)}, u32[]{:S(2)}, u32[]{:S(2)}) %collective-permute-start.1) | collective-permute-done | bytes 524320 | tf_op jit(solution)/shard_map/ppermute | solution.py:76
  39.0 5.7 %all-to-all-start.1 = ((bf16[16,2,64,256]{3,2,1,0:T(8,128)(2,1)}), bf16[16,2,64,256]{3,2,1,0:T(8,128)(2,1)S(1)}, u32[]{:S(2)}, u32[]{:S(2)}) async-start(bf16[16,2,64,256]{3,2,1,0:T(8,128)(2,1)} %pad_maximum_fusion), calls=%async_computation.1 | async-start | bytes 2097152 | tf_op jit(solution)/shard_map/all_to_all | solution.py:84
  44.7 3.7 %collective-permute-start.4 = (bf16[8,64,256]{2,1,0:T(8,128)(2,1)S(1)}, bf16[8,64,256]{2,1,0:T(8,128)(2,1)S(1)}, u32[]{:S(2)}, u32[]{:S(2)}) collective-permute-start(bf16[8,64,256]{2,1,0:T(8,128)(2,1)S(1)} %get-tuple-element.149), channel_id=1, source_target_pairs={{0,130},{64,194},{128,0},{192,64},{2,128},{66,192},{130,2},{194,66... | collective-permute-start | bytes 786440 | tf_op jit(solution)/shard_map/ppermute | solution.py:76
  48.4 9.9 %collective-permute-done.4.refs_2_ = bf16[8,64,256]{2,1,0:T(8,128)(2,1)S(1)} collective-permute-done((bf16[8,64,256]{2,1,0:T(8,128)(2,1)S(1)}, bf16[8,64,256]{2,1,0:T(8,128)(2,1)S(1)}, u32[]{:S(2)}, u32[]{:S(2)}) %collective-permute-start.4) | collective-permute-done | bytes 262176 | tf_op jit(solution)/shard_map/ppermute | solution.py:76
  61.0 6.7 %all-to-all-start.2 = ((bf16[16,2,64,256]{3,2,1,0:T(8,128)(2,1)}), bf16[16,2,64,256]{3,2,1,0:T(8,128)(2,1)}, u32[]{:S(2)}, u32[]{:S(2)}) async-start(bf16[16,2,64,256]{3,2,1,0:T(8,128)(2,1)} %get-tuple-element.97), calls=%async_computation.2 | async-start | bytes 2097152 | tf_op jit(solution)/shard_map/all_to_all | solution.py:84
  74.0 6.0 %sort_rows.4 = (bf16[1536,128]{1,0:T(8,128)(2,1)S(1)}, bf16[1536,256]{1,0:T(8,128)(2,1)S(1)}) custom-call(s32[2,1,768]{2,1,0:T(1,128)S(1)} %reshape.50.idx_ref, bf16[16,2,64,256]{3,2,1,0:T(8,128)(2,1)} %copy-done.1, bf16[8,64,256]{2,1,0:T(8,128)(2,1)} %copy-done.5, bf16[8,64,256]{2,1,0:T(8,128)(2,1)} %copy-done.4, bf16[16,2,64,256]{3,2,1,0:T(8,128)(2,1)} %copy-done.2), custom_call_target="tpu_custom_call" | custom-call | tf_op jit(solution)/shard_map/sort_rows/pallas_call | solution.py:140
  80.0 3.5 %attend_inner.2.inner_ref = bf16[1536,256]{1,0:T(8,128)(2,1)S(1)} custom-call(s32[8]{0:T(128)S(1)} %get-tuple-element.169.dist_ref, bf16[1536,128]{1,0:T(8,128)(2,1)S(1)} %get-tuple-element.100.qh_ref.q_ref, bf16[512,128]{1,0:T(8,128)(2,1)S(1)} %get-tuple-element.94.qt_ref, bf16[1536,256]{1,0:T(8,128)(2,1)S(1)} %get-tuple-element.101.kvh_ref.kv_ref, ...), custom_call_target="tpu_custom_call" | custom-call | tf_op jit(solution)/shard_map/attend_inner/pallas_call | solution.py:240
  87.6 7.4 %all-to-all-start.3 = ((bf16[16,2,64,256]{3,2,1,0:T(8,128)(2,1)}), bf16[16,2,64,256]{3,2,1,0:T(8,128)(2,1)}, u32[]{:S(2)}, u32[]{:S(2)}) async-start(bf16[16,2,64,256]{3,2,1,0:T(8,128)(2,1)} %pad_maximum_fusion.1), calls=%async_computation.3 | async-start | bytes 2097152 | tf_op jit(solution)/shard_map/all_to_all | solution.py:84
  100.2 6.3 %back_rows.2 = (bf16[16,72,128]{2,1,0:T(8,128)(2,1)}, bf16[8,72,128]{2,1,0:T(8,128)(2,1)}, bf16[8,72,128]{2,1,0:T(8,128)(2,1)}, bf16[16,2,72,128]{3,2,1,0:T(8,128)(2,1)}) custom-call(s32[1,2048]{1,0:T(1,128)S(1)} %get-tuple-element.145.idx_ref, bf16[512,256]{1,0:T(8,128)(2,1)S(1)} %attend_edge.2.edge_ref, bf16[1536,256]{1,0:T(8,128)(2,1)S(1)} %attend_inner.2.inner_ref), custom_call_target="tpu_custom_call" | custom-call | tf_op jit(solution)/shard_map/back_rows/pallas_call | solution.py:321
  106.5 5.5 %collective-permute-done.8.refs_1_ = bf16[8,64,256]{2,1,0:T(8,128)(2,1)S(1)} collective-permute-done((bf16[8,64,256]{2,1,0:T(8,128)(2,1)S(1)}, bf16[8,64,256]{2,1,0:T(8,128)(2,1)S(1)}, u32[]{:S(2)}, u32[]{:S(2)}) %collective-permute-start.8) | collective-permute-done | bytes 262176 | tf_op jit(solution)/shard_map/ppermute | solution.py:76
  112.0 6.6 %all-to-all-start.4 = ((bf16[16,2,72,128]{3,2,1,0:T(8,128)(2,1)}), bf16[16,2,72,128]{3,2,1,0:T(8,128)(2,1)S(1)}, u32[]{:S(2)}, u32[]{:S(2)}) async-start(bf16[16,2,72,128]{3,2,1,0:T(8,128)(2,1)} %get-tuple-element.119), calls=%async_computation.4 | async-start | bytes 1179648 | tf_op jit(solution)/shard_map/all_to_all | solution.py:84
  125.4 6.0 %sort_rows.6 = (bf16[1536,128]{1,0:T(8,128)(2,1)S(1)}, bf16[1536,256]{1,0:T(8,128)(2,1)S(1)}) custom-call(s32[2,1,768]{2,1,0:T(1,128)S(1)} %reshape.52.idx_ref, bf16[16,2,64,256]{3,2,1,0:T(8,128)(2,1)} %all-to-all-done.2.refs_0_, bf16[8,64,256]{2,1,0:T(8,128)(2,1)} %copy-done.7, bf16[8,64,256]{2,1,0:T(8,128)(2,1)} %copy-done.6, ...), custom_call_target="tpu_custom_call" | custom-call | tf_op jit(solution)/shard_map/sort_rows/pallas_call | solution.py:140
  136.9 6.4 %all-to-all-start.5 = ((bf16[16,2,72,128]{3,2,1,0:T(8,128)(2,1)}), bf16[16,2,72,128]{3,2,1,0:T(8,128)(2,1)S(1)}, u32[]{:S(2)}, u32[]{:S(2)}) async-start(bf16[16,2,72,128]{3,2,1,0:T(8,128)(2,1)} %pad_maximum_fusion.2), calls=%async_computation.5 | async-start | bytes 1179648 | tf_op jit(solution)/shard_map/all_to_all | solution.py:84
  146.6 6.3 %back_rows.3 = (bf16[16,72,128]{2,1,0:T(8,128)(2,1)}, bf16[8,72,128]{2,1,0:T(8,128)(2,1)}, bf16[8,72,128]{2,1,0:T(8,128)(2,1)}, bf16[16,2,72,128]{3,2,1,0:T(8,128)(2,1)}) custom-call(s32[1,2048]{1,0:T(1,128)S(1)} %get-tuple-element.167.idx_ref, bf16[512,256]{1,0:T(8,128)(2,1)S(1)} %attend_edge.3.edge_ref, bf16[1536,256]{1,0:T(8,128)(2,1)S(1)} %attend_inner.3.inner_ref), custom_call_target="tpu_custom_call" | custom-call | tf_op jit(solution)/shard_map/back_rows/pallas_call | solution.py:321
  153.7 6.7 %all-to-all-start.6 = ((bf16[16,2,72,128]{3,2,1,0:T(8,128)(2,1)}), bf16[16,2,72,128]{3,2,1,0:T(8,128)(2,1)S(1)}, u32[]{:S(2)}, u32[]{:S(2)}) async-start(bf16[16,2,72,128]{3,2,1,0:T(8,128)(2,1)} %get-tuple-element.139), calls=%async_computation.6 | async-start | bytes 1179648 | tf_op jit(solution)/shard_map/all_to_all | solution.py:84
  170.7 6.7 %all-to-all-start.7 = ((bf16[16,2,72,128]{3,2,1,0:T(8,128)(2,1)}), bf16[16,2,72,128]{3,2,1,0:T(8,128)(2,1)}, u32[]{:S(2)}, u32[]{:S(2)}) async-start(bf16[16,2,72,128]{3,2,1,0:T(8,128)(2,1)} %pad_maximum_fusion.3), calls=%async_computation.7 | async-start | bytes 1179648 | tf_op jit(solution)/shard_map/all_to_all | solution.py:84
  180.1 9.2 %home_rows.2.before_ref = bf16[2,2048,256]{2,1,0:T(8,128)(2,1)S(1)} custom-call(s32[4]{0:T(128)S(1)} %add_convert_fusion.own_ref, s32[4,4,512]{2,1,0:T(4,128)S(1)} %add_bitcast_fusion.1.idx_ref, bf16[16,2,72,128]{3,2,1,0:T(8,128)(2,1)} %copy-done.3, bf16[16,72,128]{2,1,0:T(8,128)(2,1)} %collective-permute-done.13.refs_1_, bf16[16,72,128]{2,1,0:T(8,128)(2,1)} %copy-done.9), custom_call_target="tpu_custom_call" | custom-call | tf_op jit(solution)/shard_map/home_rows/pallas_call | solution.py:419
  190.0 11.9 %home_rows.3 = bf16[4,528,128]{2,1,0:T(8,128)(2,1)S(1)} custom-call(s32[4]{0:T(128)S(1)} %add_convert_fusion.own_ref, s32[4,4,512]{2,1,0:T(4,128)S(1)} %add_bitcast_fusion.idx_ref, bf16[2,2048,256]{2,1,0:T(8,128)(2,1)S(1)} %home_rows.2.before_ref, bf16[16,2,72,128]{3,2,1,0:T(8,128)(2,1)} %all-to-all-done.7.refs_0_, ...), custom_call_target="tpu_custom_call" | custom-call | tf_op jit(solution)/shard_map/home_rows/pallas_call | solution.py:419
  201.9 30.7 %all_to_all.45.m_ref = bf16[4,528,128]{2,1,0:T(8,128)(2,1)S(1)} all-to-all(bf16[4,528,128]{2,1,0:T(8,128)(2,1)S(1)} %home_rows.3), channel_id=1, replica_groups=mesh['zl'=4,'x'=4,'y'=4,'zh'=2,'c'=2] {'zh','c'}, dimensions={0} | all-to-all | bytes 1081344 | tf_op jit(solution)/shard_map/all_to_all | solution.py:557
  (131 shorter events, 55.2 us)
Async XLA Ops:
  0.0 10.1 %collective-permute-start = (s32[2,2048]{1,0:T(2,128)}, s32[2,2048]{1,0:T(2,128)S(1)}, u32[]{:S(2)}, u32[]{:S(2)}) collective-permute-start(s32[2,2048]{1,0:T(2,128)} %param.11), channel_id=1, source_target_pairs={{0,2},{2,0},{1,3},{3,1},{4,6},{6,4},{5,7},{7,5},{8,10},{10,8},{9,1... | collective-permute-start | bytes 49160 | tf_op jit(solution)/shard_map/ppermute | solution.py:492
  17.2 20.6 %all-to-all-start = ((bf16[16,2,64,256]{3,2,1,0:T(8,128)(2,1)}), bf16[16,2,64,256]{3,2,1,0:T(8,128)(2,1)S(1)}, u32[]{:S(2)}, u32[]{:S(2)}) async-start(bf16[16,2,64,256]{3,2,1,0:T(8,128)(2,1)} %get-tuple-element.77), calls=%async_computation | async-start | bytes 2097152 | tf_op jit(solution)/shard_map/all_to_all | solution.py:84
  24.1 12.1 %collective-permute-start.1 = (bf16[16,64,256]{2,1,0:T(8,128)(2,1)}, bf16[16,64,256]{2,1,0:T(8,128)(2,1)S(1)}, u32[]{:S(2)}, u32[]{:S(2)}) collective-permute-start(bf16[16,64,256]{2,1,0:T(8,128)(2,1)} %get-tuple-element.78), channel_id=1, source_target_pairs={{0,64},{64,128},{128,192},{192,2},{2,66},{66,130},{130,194},{194,0... | collective-permute-start | bytes 1572872 | tf_op jit(solution)/shard_map/ppermute | solution.py:76
  24.8 11.8 %collective-permute-start.2 = (bf16[16,64,256]{2,1,0:T(8,128)(2,1)}, bf16[16,64,256]{2,1,0:T(8,128)(2,1)S(1)}, u32[]{:S(2)}, u32[]{:S(2)}) collective-permute-start(bf16[16,64,256]{2,1,0:T(8,128)(2,1)} %get-tuple-element.79), channel_id=1, source_target_pairs={{0,194},{64,0},{128,64},{192,128},{2,192},{66,2},{130,66},{194,130... | collective-permute-start | bytes 1572872 | tf_op jit(solution)/shard_map/ppermute | solution.py:76
  39.0 22.1 %all-to-all-start.1 = ((bf16[16,2,64,256]{3,2,1,0:T(8,128)(2,1)}), bf16[16,2,64,256]{3,2,1,0:T(8,128)(2,1)S(1)}, u32[]{:S(2)}, u32[]{:S(2)}) async-start(bf16[16,2,64,256]{3,2,1,0:T(8,128)(2,1)} %pad_maximum_fusion), calls=%async_computation.1 | async-start | bytes 2097152 | tf_op jit(solution)/shard_map/all_to_all | solution.py:84
  44.7 13.6 %collective-permute-start.4 = (bf16[8,64,256]{2,1,0:T(8,128)(2,1)S(1)}, bf16[8,64,256]{2,1,0:T(8,128)(2,1)S(1)}, u32[]{:S(2)}, u32[]{:S(2)}) collective-permute-start(bf16[8,64,256]{2,1,0:T(8,128)(2,1)S(1)} %get-tuple-element.149), channel_id=1, source_target_pairs={{0,130},{64,194},{128,0},{192,64},{2,128},{66,192},{130,2},{194,66... | collective-permute-start | bytes 786440 | tf_op jit(solution)/shard_map/ppermute | solution.py:76
  48.4 12.6 %collective-permute-start.3 = (bf16[8,64,256]{2,1,0:T(8,128)(2,1)S(1)}, bf16[8,64,256]{2,1,0:T(8,128)(2,1)S(1)}, u32[]{:S(2)}, u32[]{:S(2)}) collective-permute-start(bf16[8,64,256]{2,1,0:T(8,128)(2,1)S(1)} %get-tuple-element.150), channel_id=1, source_target_pairs={{0,128},{64,192},{128,2},{192,66},{2,130},{66,194},{130,0},{194,64... | collective-permute-start | bytes 786440 | tf_op jit(solution)/shard_map/ppermute | solution.py:76
  61.0 24.3 %all-to-all-start.2 = ((bf16[16,2,64,256]{3,2,1,0:T(8,128)(2,1)}), bf16[16,2,64,256]{3,2,1,0:T(8,128)(2,1)}, u32[]{:S(2)}, u32[]{:S(2)}) async-start(bf16[16,2,64,256]{3,2,1,0:T(8,128)(2,1)} %get-tuple-element.97), calls=%async_computation.2 | async-start | bytes 2097152 | tf_op jit(solution)/shard_map/all_to_all | solution.py:84
  67.8 17.5 %collective-permute-start.6 = (bf16[16,64,256]{2,1,0:T(8,128)(2,1)}, bf16[16,64,256]{2,1,0:T(8,128)(2,1)}, u32[]{:S(2)}, u32[]{:S(2)}) collective-permute-start(bf16[16,64,256]{2,1,0:T(8,128)(2,1)} %get-tuple-element.98), channel_id=1, source_target_pairs={{0,64},{64,128},{128,192},{192,2},{2,66},{66,130},{130,194},{194,0... | collective-permute-start | bytes 1572872 | tf_op jit(solution)/shard_map/ppermute | solution.py:76
  67.9 17.4 %collective-permute-start.7 = (bf16[16,64,256]{2,1,0:T(8,128)(2,1)}, bf16[16,64,256]{2,1,0:T(8,128)(2,1)}, u32[]{:S(2)}, u32[]{:S(2)}) collective-permute-start(bf16[16,64,256]{2,1,0:T(8,128)(2,1)} %get-tuple-element.99), channel_id=1, source_target_pairs={{0,194},{64,0},{128,64},{192,128},{2,192},{66,2},{130,66},{194,130... | collective-permute-start | bytes 1572872 | tf_op jit(solution)/shard_map/ppermute | solution.py:76
  72.5 12.8 %collective-permute-start.5 = (bf16[512,256]{1,0:T(8,128)(2,1)S(1)}, bf16[512,256]{1,0:T(8,128)(2,1)S(1)}, u32[]{:S(2)}, u32[]{:S(2)}) collective-permute-start(bf16[512,256]{1,0:T(8,128)(2,1)S(1)} %get-tuple-element.96.kvt_ref), channel_id=1, source_target_pairs={{0,4},{4,8},{8,12},{12,16},{16,20},{20,24},{24,28},{28,32},{32,36}... | collective-permute-start | bytes 786440 | tf_op jit(solution)/shard_map/ppermute | solution.py:519
  87.6 24.4 %all-to-all-start.3 = ((bf16[16,2,64,256]{3,2,1,0:T(8,128)(2,1)}), bf16[16,2,64,256]{3,2,1,0:T(8,128)(2,1)}, u32[]{:S(2)}, u32[]{:S(2)}) async-start(bf16[16,2,64,256]{3,2,1,0:T(8,128)(2,1)} %pad_maximum_fusion.1), calls=%async_computation.3 | async-start | bytes 2097152 | tf_op jit(solution)/shard_map/all_to_all | solution.py:84
  96.1 10.4 %collective-permute-start.9 = (bf16[8,64,256]{2,1,0:T(8,128)(2,1)S(1)}, bf16[8,64,256]{2,1,0:T(8,128)(2,1)S(1)}, u32[]{:S(2)}, u32[]{:S(2)}) collective-permute-start(bf16[8,64,256]{2,1,0:T(8,128)(2,1)S(1)} %get-tuple-element.147), channel_id=1, source_target_pairs={{0,130},{64,194},{128,0},{192,64},{2,128},{66,192},{130,2},{194,66... | collective-permute-start | bytes 786440 | tf_op jit(solution)/shard_map/ppermute | solution.py:76
  98.7 13.3 %collective-permute-start.8 = (bf16[8,64,256]{2,1,0:T(8,128)(2,1)S(1)}, bf16[8,64,256]{2,1,0:T(8,128)(2,1)S(1)}, u32[]{:S(2)}, u32[]{:S(2)}) collective-permute-start(bf16[8,64,256]{2,1,0:T(8,128)(2,1)S(1)} %get-tuple-element.148), channel_id=1, source_target_pairs={{0,128},{64,192},{128,2},{192,66},{2,130},{66,194},{130,0},{194,64... | collective-permute-start | bytes 786440 | tf_op jit(solution)/shard_map/ppermute | solution.py:76
  112.0 23.0 %all-to-all-start.4 = ((bf16[16,2,72,128]{3,2,1,0:T(8,128)(2,1)}), bf16[16,2,72,128]{3,2,1,0:T(8,128)(2,1)S(1)}, u32[]{:S(2)}, u32[]{:S(2)}) async-start(bf16[16,2,72,128]{3,2,1,0:T(8,128)(2,1)} %get-tuple-element.119), calls=%async_computation.4 | async-start | bytes 1179648 | tf_op jit(solution)/shard_map/all_to_all | solution.py:84
  121.8 13.2 %collective-permute-start.10 = (bf16[512,256]{1,0:T(8,128)(2,1)S(1)}, bf16[512,256]{1,0:T(8,128)(2,1)S(1)}, u32[]{:S(2)}, u32[]{:S(2)}) collective-permute-start(bf16[512,256]{1,0:T(8,128)(2,1)S(1)} %get-tuple-element.118.kvt_ref), channel_id=1, source_target_pairs={{0,4},{4,8},{8,12},{12,16},{16,20},{20,24},{24,28},{28,32},{32,36}... | collective-permute-start | bytes 786440 | tf_op jit(solution)/shard_map/ppermute | solution.py:519
  123.1 11.9 %collective-permute-start.11 = (bf16[8,72,128]{2,1,0:T(8,128)(2,1)}, bf16[8,72,128]{2,1,0:T(8,128)(2,1)S(1)}, u32[]{:S(2)}, u32[]{:S(2)}) collective-permute-start(bf16[8,72,128]{2,1,0:T(8,128)(2,1)} %get-tuple-element.120), channel_id=1, source_target_pairs={{0,130},{64,194},{128,0},{192,64},{2,128},{66,192},{130,2},{194,66... | collective-permute-start | bytes 442376 | tf_op jit(solution)/shard_map/ppermute | solution.py:76
  123.1 11.9 %collective-permute-start.12 = (bf16[8,72,128]{2,1,0:T(8,128)(2,1)}, bf16[8,72,128]{2,1,0:T(8,128)(2,1)S(1)}, u32[]{:S(2)}, u32[]{:S(2)}) collective-permute-start(bf16[8,72,128]{2,1,0:T(8,128)(2,1)} %get-tuple-element.121), channel_id=1, source_target_pairs={{0,128},{64,192},{128,2},{192,66},{2,130},{66,194},{130,0},{194,64... | collective-permute-start | bytes 442376 | tf_op jit(solution)/shard_map/ppermute | solution.py:76
  136.9 16.1 %all-to-all-start.5 = ((bf16[16,2,72,128]{3,2,1,0:T(8,128)(2,1)}), bf16[16,2,72,128]{3,2,1,0:T(8,128)(2,1)S(1)}, u32[]{:S(2)}, u32[]{:S(2)}) async-start(bf16[16,2,72,128]{3,2,1,0:T(8,128)(2,1)} %pad_maximum_fusion.2), calls=%async_computation.5 | async-start | bytes 1179648 | tf_op jit(solution)/shard_map/all_to_all | solution.py:84
  143.4 9.6 %collective-permute-start.14 = (bf16[16,72,128]{2,1,0:T(8,128)(2,1)S(1)}, bf16[16,72,128]{2,1,0:T(8,128)(2,1)S(1)}, u32[]{:S(2)}, u32[]{:S(2)}) collective-permute-start(bf16[16,72,128]{2,1,0:T(8,128)(2,1)S(1)} %get-tuple-element.153), channel_id=1, source_target_pairs={{0,64},{64,128},{128,192},{192,2},{2,66},{66,130},{130,194},{194,0... | collective-permute-start | bytes 884744 | tf_op jit(solution)/shard_map/ppermute | solution.py:76
  153.7 15.1 %all-to-all-start.6 = ((bf16[16,2,72,128]{3,2,1,0:T(8,128)(2,1)}), bf16[16,2,72,128]{3,2,1,0:T(8,128)(2,1)S(1)}, u32[]{:S(2)}, u32[]{:S(2)}) async-start(bf16[16,2,72,128]{3,2,1,0:T(8,128)(2,1)} %get-tuple-element.139), calls=%async_computation.6 | async-start | bytes 1179648 | tf_op jit(solution)/shard_map/all_to_all | solution.py:84
  170.7 18.6 %all-to-all-start.7 = ((bf16[16,2,72,128]{3,2,1,0:T(8,128)(2,1)}), bf16[16,2,72,128]{3,2,1,0:T(8,128)(2,1)}, u32[]{:S(2)}, u32[]{:S(2)}) async-start(bf16[16,2,72,128]{3,2,1,0:T(8,128)(2,1)} %pad_maximum_fusion.3), calls=%async_computation.7 | async-start | bytes 1179648 | tf_op jit(solution)/shard_map/all_to_all | solution.py:84
  177.4 11.9 %collective-permute-start.18 = (bf16[16,72,128]{2,1,0:T(8,128)(2,1)S(1)}, bf16[16,72,128]{2,1,0:T(8,128)(2,1)S(1)}, u32[]{:S(2)}, u32[]{:S(2)}) collective-permute-start(bf16[16,72,128]{2,1,0:T(8,128)(2,1)S(1)} %get-tuple-element.151), channel_id=1, source_target_pairs={{0,64},{64,128},{128,192},{192,2},{2,66},{66,130},{130,194},{194,0... | collective-permute-start | bytes 884744 | tf_op jit(solution)/shard_map/ppermute | solution.py:76
  177.9 11.4 %collective-permute-start.17 = (bf16[16,72,128]{2,1,0:T(8,128)(2,1)S(1)}, bf16[16,72,128]{2,1,0:T(8,128)(2,1)}, u32[]{:S(2)}, u32[]{:S(2)}) collective-permute-start(bf16[16,72,128]{2,1,0:T(8,128)(2,1)S(1)} %get-tuple-element.152), channel_id=1, source_target_pairs={{0,194},{64,0},{128,64},{192,128},{2,192},{66,2},{130,66},{194,130... | collective-permute-start | bytes 884744 | tf_op jit(solution)/shard_map/ppermute | solution.py:76
  (32 other events, 614.7 us)

commit v6 on v5

v6 whole, which is shorter than its diff:
```python
import functools

import jax
import jax.numpy as jnp
from jax import lax
from jax.experimental import pallas as pl
from jax.experimental.pallas import tpu as pltpu
from jax.sharding import Mesh
from jax.sharding import PartitionSpec as P

BLOCK = 256
MASKED = -1000000000.0
SEQ = ("zl", "x", "y")
PLANE = ("x", "y")
ROUND = ("zh", "c")
BF = jnp.bfloat16
F32 = jnp.float32
VMEM_BYTES = 48 * 1024 * 1024


def params(n=1):
    return pltpu.CompilerParams(
        dimension_semantics=("arbitrary",) * n, vmem_limit_bytes=VMEM_BYTES
    )


def whole(shape):
    return pl.BlockSpec(shape, lambda *_: (0,) * len(shape))


def one_hot(a, b):
    return jnp.where(a == b, 1.0, 0.0).astype(BF)


def column(row):
    return jnp.transpose(jnp.broadcast_to(row, (8, row.shape[1])))[:, :1]


def in_hbm(v):
    return pltpu.with_memory_space_constraint(v, pltpu.HBM)


def project_kernel(x_ref, wqk_ref, wv_ref, out_ref, w_ref):
    @pl.when(pl.program_id(0) == 0)
    def _():
        w_ref[:, :128] = wqk_ref[...]
        w_ref[:, 128:] = wv_ref[...]

    out_ref[...] = jnp.dot(x_ref[...], w_ref[...], preferred_element_type=F32).astype(BF)


def project(x, w_qk, w_v):
    rows, model = x.shape
    step = 512
    return pl.pallas_call(
        project_kernel,
        grid=(rows // step,),
        in_specs=[
            pl.BlockSpec((step, model), lambda i: (i, 0)),
            whole(w_qk.shape),
            whole(w_v.shape),
        ],
        out_specs=pl.BlockSpec((step, 256), lambda i: (i, 0)),
        out_shape=jax.ShapeDtypeStruct((rows, 256), BF),
        scratch_shapes=[pltpu.VMEM((model, 256), BF)],
        compiler_params=params(),
        name="project",
    )(in_hbm(x), in_hbm(w_qk), in_hbm(w_v))


def ring(value, shift):
    def at(z):
        return (z % 4) * 2 + z // 4

    route = [(at(z), at((z + shift) % 8)) for z in range(8)]
    return lax.ppermute(value, ("zl", "zh"), route)


def join(first, second):
    return jnp.stack([first, second], axis=1)


def plane(joint):
    return lax.all_to_all(joint, PLANE, 0, 0, tiled=True)


together = lax.optimization_barrier


def scatter_kernel(idx_ref, rows_ref, *out_refs):
    peers, _, width, lanes = out_refs[0].shape[:2] + out_refs[0].shape[-2:]
    group = pl.program_id(1)
    place = lax.broadcasted_iota(jnp.int32, (peers * width, rows_ref.shape[0]), 0)
    hot = one_hot(idx_ref[0, pl.ds(group, 1), :], place)
    got = jnp.dot(hot, rows_ref[...], preferred_element_type=F32)
    got = got.astype(BF).reshape(peers, width, lanes)
    if len(out_refs) == 1:
        out_refs[0][:, 0, 0] = got
        return
    for g, ref in enumerate(out_refs):

        @pl.when(group == g)
        def _(ref=ref):
            ref[:, 0] = got


def scatter_rows(idx, rows, width, even):
    rounds, groups, count = idx.shape
    if even:
        shapes = [(16, groups, rounds, width, 256)]
        specs = [pl.BlockSpec((16, 1, 1, width, 256), lambda r, g: (0, g, r, 0, 0))]
    else:
        shapes = [(16, rounds, width, 256)] * groups
        specs = [pl.BlockSpec((16, 1, width, 256), lambda r, g: (0, r, 0, 0))] * groups
    return pl.pallas_call(
        scatter_kernel,
        grid=(rounds, groups),
        in_specs=[pl.BlockSpec((1, groups, count), lambda r, g: (r, 0, 0)), whole(rows.shape)],
        out_specs=specs,
        out_shape=[pltpu.HBM(v, BF) for v in shapes],
        compiler_params=params(2),
        name="scatter_rows",
    )(idx, rows)


def sort_kernel(idx_ref, *refs):
    (*row_refs, q_ref, kv_ref) = refs
    col = column(idx_ref[0, 0])
    got, base = 0.0, 0
    for ref in row_refs:
        rows = ref[...].reshape(-1, 256)
        n = rows.shape[0]
        place = lax.broadcasted_iota(jnp.int32, (q_ref.shape[1], n), 1) + base
        got += jnp.dot(one_hot(col, place), rows, preferred_element_type=F32)
        base += n
    qk = got[:, :128]
    keys = qk * lax.rsqrt(jnp.sum(qk * qk, axis=-1, keepdims=True) + 1e-06)
    q_ref[0] = qk.astype(BF)
    kv_ref[0, :, :128] = keys.astype(BF)
    kv_ref[0, :, 128:] = got[:, 128:].astype(BF)


def sort_rows(idx, even, low, high, odd, step):
    rounds, count = idx.shape
    blocks = count // step
    peers, _, _, width, lanes = even.shape
    four = lambda r, b: (0, r, 0, 0)
    five = lambda r, b: (0, 0, r, 0, 0)
    return pl.pallas_call(
        sort_kernel,
        grid=(rounds, blocks),
        in_specs=[
            pl.BlockSpec((1, 1, 1, step), lambda r, b: (r, b, 0, 0)),
            pl.BlockSpec((peers, 1, 1, width, lanes), five),
            pl.BlockSpec((peers // 2, 1, width, lanes), four),
            pl.BlockSpec((peers // 2, 1, width, lanes), four),
            pl.BlockSpec((peers, 2, 1, width, lanes), five),
        ],
        out_specs=[
            pl.BlockSpec((1, step, 128), lambda r, b: (r, b, 0)),
            pl.BlockSpec((1, step, 256), lambda r, b: (r, b, 0)),
        ],
        out_shape=[
            jax.ShapeDtypeStruct((rounds, count, 128), BF),
            jax.ShapeDtypeStruct((rounds, count, 256), BF),
        ],
        compiler_params=params(2),
        name="sort_rows",
    )(idx.reshape(rounds, blocks, 1, step), even, low, high, odd)


def terms_to_lines(terms, groups):
    terms = terms.reshape(groups, 32, 128)
    slot = lax.broadcasted_iota(jnp.int32, terms.shape, 1)
    lane = lax.broadcasted_iota(jnp.int32, terms.shape, 2) % 32
    return jnp.sum(jnp.where(slot == lane, terms, 0.0), axis=1, keepdims=True)


def lines_to_terms(line):
    n = line.shape[0]
    shape = (n, 32, 128)
    slot = lax.broadcasted_iota(jnp.int32, shape, 1)
    lane = lax.broadcasted_iota(jnp.int32, shape, 2) % 32
    spread = jnp.where(slot == lane, line, 0.0).reshape(n * 32, 128).astype(BF)
    group = lax.broadcasted_iota(jnp.int32, (128, 128), 0) // 32
    pick = one_hot(group, lax.broadcasted_iota(jnp.int32, (128, 128), 1))
    return jnp.dot(spread, pick, preferred_element_type=F32)


def three_terms(v):
    hi = v.astype(BF).astype(F32)
    mid = (v - hi).astype(BF).astype(F32)
    lo = v - hi - mid
    return hi, mid, lo


def term_lanes(v, rows):
    hi, mid, lo = three_terms(v)
    group = lax.broadcasted_iota(jnp.int32, (rows, 128), 1) // 32
    return jnp.where(
        group == 0, hi, jnp.where(group == 1, mid, jnp.where(group == 2, lo, 1.0))
    ).astype(BF)


def attend_block(q, own, behind, out_ref):
    nt = (((1,), (1,)), ((), ()))
    s1 = lax.dot_general(q, own[:, :128], nt, preferred_element_type=F32)
    s2 = lax.dot_general(q, behind[:, :128], nt, preferred_element_type=F32)
    r = lax.broadcasted_iota(jnp.int32, (BLOCK, BLOCK), 0)
    k = lax.broadcasted_iota(jnp.int32, (BLOCK, BLOCK), 1)
    s1 = jnp.where(r == k, MASKED, s1)
    top = jnp.maximum(
        jnp.max(s1, axis=-1, keepdims=True), jnp.max(s2, axis=-1, keepdims=True)
    )
    e1 = jnp.exp(s1 - top)
    e2 = jnp.exp(s2 - top)
    total = jnp.sum(e1, axis=-1, keepdims=True) + jnp.sum(e2, axis=-1, keepdims=True)
    o = jnp.dot(e1.astype(BF), own[:, 128:], preferred_element_type=F32) + jnp.dot(
        e2.astype(BF), behind[:, 128:], preferred_element_type=F32
    )
    out_ref[0, :, :128] = (o / total).astype(BF)
    out_ref[0, :, 128:] = term_lanes(top + jnp.log(total), BLOCK)


def inner_kernel(dist_ref, qh_ref, qt_ref, kvh_ref, kvt_ref, out_ref, q_ref, kv_ref):
    head = kvh_ref.shape[1]

    @pl.when(pl.program_id(1) == 0)
    def _():
        q_ref[:head] = qh_ref[0]
        q_ref[head:] = qt_ref[0]
        kv_ref[:head] = kvh_ref[0]
        kv_ref[head:] = kvt_ref[0]

    def block(ref, c):
        return ref[pl.ds(pl.multiple_of(c * BLOCK, BLOCK), BLOCK), :]

    c = pl.program_id(1) + 2
    at = c - dist_ref[pl.program_id(0), c]
    attend_block(block(q_ref, c), block(kv_ref, c), block(kv_ref, at), out_ref)


def edge_kernel(dist_ref, q_ref, kv_ref, halo_ref, out_ref):
    c = pl.program_id(1)
    own = kv_ref[0, pl.ds(pl.multiple_of(c * BLOCK, BLOCK), BLOCK), :]
    at = c + 2 - dist_ref[pl.program_id(0), c]
    before = halo_ref[0, pl.ds(pl.multiple_of(jnp.minimum(at, 1) * BLOCK, BLOCK), BLOCK), :]
    behind = jnp.where(at < 2, before, kv_ref[0, :BLOCK, :])
    attend_block(q_ref[0], own, behind, out_ref)


def of_round(shape):
    return pl.BlockSpec((1,) + shape[1:], lambda r, b, d: (r, 0, 0))


def attend_inner(dist, q_head, q_tail, kv_head, kv_tail):
    rounds = q_head.shape[0]
    count = q_head.shape[1] + q_tail.shape[1]
    blocks = count // BLOCK - 2
    return pl.pallas_call(
        inner_kernel,
        grid_spec=pltpu.PrefetchScalarGridSpec(
            num_scalar_prefetch=1,
            grid=(rounds, blocks),
            in_specs=[of_round(v.shape) for v in (q_head, q_tail, kv_head, kv_tail)],
            out_specs=pl.BlockSpec((1, BLOCK, 256), lambda r, b, d: (r, b, 0)),
            scratch_shapes=[pltpu.VMEM((count, 128), BF), pltpu.VMEM((count, 256), BF)],
        ),
        out_shape=jax.ShapeDtypeStruct((rounds, blocks * BLOCK, 256), BF),
        compiler_params=params(2),
        name="attend_inner",
    )(dist, q_head, q_tail, kv_head, kv_tail)


def attend_edge(dist, q, kv, halo):
    rounds = q.shape[0]
    return pl.pallas_call(
        edge_kernel,
        grid_spec=pltpu.PrefetchScalarGridSpec(
            num_scalar_prefetch=1,
            grid=(rounds, 2),
            in_specs=[
                pl.BlockSpec((1, BLOCK, 128), lambda r, b, d: (r, b, 0)),
                of_round((rounds, 2 * BLOCK, 256)),
                of_round(halo.shape),
            ],
            out_specs=pl.BlockSpec((1, BLOCK, 256), lambda r, b, d: (r, b, 0)),
        ),
        out_shape=jax.ShapeDtypeStruct((rounds, 2 * BLOCK, 256), BF),
        compiler_params=params(2),
        name="attend_edge",
    )(dist, q, kv, halo)


def back_kernel(first_group, idx_ref, edge_ref, inner_ref, *out_refs):
    width, peers = out_refs[0].shape[-2] - 8, 16
    n = peers * width
    group = pl.program_id(1)
    idx = idx_ref[0] - (first_group + group) * n
    got = 0.0
    first = 0
    for ref in (edge_ref, inner_ref):
        count = ref.shape[1]
        place = lax.broadcasted_iota(jnp.int32, (n, count), 0)
        hot = one_hot(idx[:, first : first + count], place)
        got += jnp.dot(hot, ref[0], preferred_element_type=F32)
        first += count
    lines = terms_to_lines(got[:, 128:], n // 32).reshape(peers, width // 32, 1, 128)
    row = lax.broadcasted_iota(jnp.int32, (peers, 8, 128), 1)
    tail = jnp.zeros((peers, 8, 128), F32)
    for part in range(width // 32):
        tail = jnp.where(row == part, lines[:, part], tail)
    tail = tail.astype(BF)
    got = got[:, :128].astype(BF).reshape(peers, width, 128)

    def store(ref, at):
        ref[:, :width, :] = got[at]
        ref[:, width:, :] = tail[at]

    every, half = slice(None), peers // 2
    if len(out_refs) == 1:
        store(out_refs[0].at[:, 0, 0], every)
        return
    near_ref, low_ref, high_ref = out_refs

    @pl.when(group == 0)
    def _():
        store(near_ref.at[:, 0], every)

    @pl.when(group == 1)
    def _():
        store(low_ref.at[:, 0], slice(0, half))
        store(high_ref.at[:, 0], slice(half, peers))


def back_rows(idx, edge, inner, width, even):
    rounds = idx.shape[0]
    ext = width + 8
    if even:
        shapes = [(n, rounds, ext, 128) for n in (16, 8, 8)]
        specs = [pl.BlockSpec((v[0], 1, ext, 128), lambda r, g: (0, r, 0, 0)) for v in shapes]
    else:
        shapes = [(16, 2, rounds, ext, 128)]
        specs = [pl.BlockSpec((16, 1, 1, ext, 128), lambda r, g: (0, g, r, 0, 0))]
    one = lambda v: pl.BlockSpec((1,) + v.shape[1:], lambda r, g: (r, 0, 0))
    return pl.pallas_call(
        functools.partial(back_kernel, 0 if even else 2),
        grid=(rounds, 2),
        in_specs=[one(idx), one(edge), one(inner)],
        out_specs=specs,
        out_shape=[pltpu.HBM(v, BF) for v in shapes],
        compiler_params=params(2),
        name="back_rows",
    )(idx, edge, inner)


ABSENT = -1e30


def fill_home(x_ref, width, blocks):
    row = 0
    for block in blocks:
        size = block.shape[0] * width
        x_ref[row : row + size, :128] = block[:, :width, :].reshape(size, 128)
        tail = block[:, width:, :].astype(F32)
        lines = jnp.concatenate(
            [tail[:, p : p + 1][:, None] for p in range(width // 32)], axis=1
        ).reshape(size // 32, 1, 128)
        x_ref[row : row + size, 128:] = lines_to_terms(lines).astype(BF)
        row += size


def gather_home(own_ref, cols, x_ref, width):
    near, far = 0.0, 0.0
    size = 16 * width
    place = lax.broadcasted_iota(jnp.int32, (cols.shape[0], size), 1)
    for g in range(4):
        hot = one_hot(cols[:, g : g + 1], place)
        got = jnp.dot(hot, x_ref[g * size : (g + 1) * size], preferred_element_type=F32)
        if g == 0:
            near = got
        else:
            mine = own_ref[g] == 1
            near += jnp.where(mine, got, 0.0)
            far += jnp.where(mine, 0.0, got)
    return [near, far]


def home_kernel(width, own_ref, idx_ref, even_ref, up_ref, down_ref, out_ref, x_ref):
    rounds = even_ref.shape[2]

    @pl.when(pl.program_id(0) == 0)
    def _():
        for r in range(rounds):
            blocks = [even_ref.at[:, 0, r], even_ref.at[:, 1, r], up_ref.at[:, r], down_ref.at[:, r]]
            fill_home(x_ref.at[r], width, blocks)

    step = idx_ref.shape[2]
    cols = jnp.transpose(idx_ref[0])
    states = []
    for r in range(rounds):
        states += gather_home(own_ref, cols[:, 4 * r : 4 * r + 4], x_ref.at[r], width)
    here = [s[:, 131:132] > 0.5 for s in states]
    logs = [
        jnp.where(h, s[:, 128:129] + s[:, 129:130] + s[:, 130:131], ABSENT)
        for h, s in zip(here, states)
    ]
    top = functools.reduce(jnp.maximum, logs)
    scales = [jnp.where(h, jnp.exp(v - top), 0.0) for h, v in zip(here, logs)]
    total = sum(scales)
    some = total > 0.0
    summed = sum(s * p[:, :128] for s, p in zip(scales, states))
    safe = jnp.where(some, total, 1.0)
    log = jnp.where(some, top + jnp.log(safe), ABSENT)
    out_ref[0, :step, :] = (summed / safe).astype(BF)
    terms = term_lanes(log, step).astype(F32)
    out_ref[0, step:, :] = terms_to_lines(terms, step // 32).reshape(step // 32, 128).astype(BF)


def home_rows(own, idx, even, up, down, width):
    rounds, groups, count = idx.shape
    quarters = 4
    step = count // quarters
    columns = rounds * groups
    idx = idx.reshape(columns, quarters, step).transpose(1, 0, 2)
    return pl.pallas_call(
        functools.partial(home_kernel, width),
        grid_spec=pltpu.PrefetchScalarGridSpec(
            num_scalar_prefetch=1,
            grid=(quarters,),
            in_specs=[pl.BlockSpec((1, columns, step), lambda i, o: (i, 0, 0))]
            + [whole(v.shape) for v in (even, up, down)],
            out_specs=pl.BlockSpec((1, step + step // 32, 128), lambda i, o: (i, 0, 0)),
            scratch_shapes=[pltpu.VMEM((rounds, 64 * width, 256), BF)],
        ),
        out_shape=jax.ShapeDtypeStruct((quarters, step + step // 32, 128), BF),
        compiler_params=params(),
        name="home_rows",
    )(own, idx, even, up, down)


def finish_kernel(m_ref, w_ref, out_ref):
    rows = out_ref.shape[0]
    logs = []
    for i in range(4):
        line = m_ref[i, rows:, :].astype(F32).reshape(rows // 32, 1, 128)
        terms = lines_to_terms(line)
        logs.append(terms[:, 0:1] + terms[:, 1:2] + terms[:, 2:3])
    top = functools.reduce(jnp.maximum, logs)
    scales = [jnp.exp(v - top) for v in logs]
    total = sum(scales)
    summed = sum(s * m_ref[i, :rows, :].astype(F32) for i, s in enumerate(scales))
    blended = (summed / total).astype(BF)
    out_ref[...] = jnp.dot(blended, w_ref[...], preferred_element_type=F32).astype(BF)


def finish(merged, w_out):
    parts, rows, _ = merged.shape
    rows -= rows // 33
    return pl.pallas_call(
        finish_kernel,
        in_specs=[whole(merged.shape), whole(w_out.shape)],
        out_specs=whole((rows, w_out.shape[1])),
        grid=(1,),
        out_shape=jax.ShapeDtypeStruct((rows, w_out.shape[1]), BF),
        compiler_params=params(),
        name="finish",
    )(merged, w_out)


def send_places(own_slots, other_slots, width):
    zl, zh = lax.axis_index("zl"), lax.axis_index("zh")
    late = lax.axis_index(PLANE) >= 8
    group = jnp.arange(4, dtype=jnp.int32)
    shift = jnp.where(group == 0, 0, jnp.where(group == 1, jnp.where(late, -2, 2), 5 - 2 * group))
    own = ((zh * 4 + zl + shift + 8) & 7) // 4 == zh
    slot = jnp.where(own[:, None], own_slots[:, None], other_slots[:, None])
    hit = (slot >> 10) == ((zl + shift + 8) & 3)[:, None]
    return jnp.where(hit, ((slot >> 6) & 15) * width + (slot & 63), -1), own.astype(jnp.int32)


def take_places(taken, width):
    away = (lax.axis_index("zl") - (taken >> 10)) & 3
    group = jnp.where(away == 1, 2, jnp.where(away == 2, 1, away))
    source = (taken >> 6) & 15
    at = taken & 63
    by_group = (group * 16 + source) * width + at
    odd = (32 + source * 2 + group - 2) * width + at
    return jnp.where(group < 2, by_group, odd), by_group


def body(x, w_qk, w_v, w_out, slots, taken, looks):
    count = slots.shape[1]
    peers = lax.axis_size(SEQ)
    width = 2 * count // peers
    blocks = count // BLOCK
    tail = count - 2 * BLOCK
    others = lax.ppermute(slots, "zh", [(0, 1), (1, 0)])
    packed = project(x, w_qk, w_v)
    mine = lax.axis_index(SEQ) * blocks + jnp.arange(blocks, dtype=jnp.int32)
    dist = (mine[None, :] - looks) % (peers * blocks)
    next_device = [(i, (i + 1) % peers) for i in range(peers)]
    sent, own = send_places(slots, others, width)
    spots, groups = take_places(taken, width)

    (even,) = scatter_rows(sent[:, :2], packed, width, True)
    even, packed = together((even, packed))
    half = plane(even)
    up, down = scatter_rows(sent[:, 2:], packed, width, False)
    half, up, down = together((half, ring(up, 1), ring(down, -1)))
    rows = half, ring(half[:8, 1], 2), ring(half[8:, 1], -2), plane(join(up, down))
    rows = together(rows)

    q_tail, kv_tail = sort_rows(spots[:, tail:], *rows, 2 * BLOCK)
    halo = lax.ppermute(kv_tail, SEQ, next_device)
    q_head, kv_head = sort_rows(spots[:, :tail], *rows, 3 * BLOCK)
    inner = attend_inner(dist, q_head, q_tail, kv_head, kv_tail)
    edge = attend_edge(dist, q_head, kv_head, halo)

    (odd,) = back_rows(groups[:, None], edge, inner, width, False)
    odd, edge = together((odd, edge))
    half = plane(odd)
    near, low, high = back_rows(groups[:, None], edge, inner, width, True)
    half, low, high = together((half, ring(low, -2), ring(high, 2)))
    even = plane(join(near, jnp.concatenate([low, high])))
    state = home_rows(own, sent, even, ring(half[:, 0], -1), ring(half[:, 1], 1), width)
    merged = lax.all_to_all(state, ROUND, 0, 0, tiled=True)
    return finish(merged, w_out)


def solution(mesh):
    fine = Mesh(mesh.devices.reshape(4, 4, 4, 2, 2), SEQ + ROUND)
    in_specs = (P(SEQ, None), P(), P(), P()) + (P(ROUND, SEQ),) * 3
    return jax.shard_map(
        body, mesh=fine, in_specs=in_specs, out_specs=P(SEQ + ROUND, None), check_vma=False
    )
```

time: 236 us -> 220 us (0.932)
  waiting for transfers between devices: 31.7 us -> 65.2 us
  starting transfers between devices: 79.9 us -> 47.2 us
  Pallas kernels: 81.8 us -> 73.7 us
  blocking collectives: 30.7 us -> 26.7 us
  other arithmetic: 7.72 us -> 4.22 us
    ppermute x16 -> x8, waiting for transfers between devices: 28.7 us -> 65.2 us  [ring(): return lax.ppermute(value, ('zl', 'zh'), route)]
    all_to_all x8 -> x4, starting transfers between devices: 53.1 us -> 26.6 us  [plane(): return lax.all_to_all(joint, PLANE, 0, 0, tiled=True)]
    pallas_call x10 -> x7, Pallas kernels: 65.1 us -> 55 us  [the longest x1 15.5 us: home_rows(): pl.pallas_call(functools.partial(home_kernel, width), grid_spec=pltpu.Pre...]
    ppermute x16 -> x8, starting transfers between devices: 18.2 us -> 13.4 us  [ring(): return lax.ppermute(value, ('zl', 'zh'), route)]
    all_to_all x1, blocking collectives: 30.7 us -> 26.7 us  [body(): merged = lax.all_to_all(state, ROUND, 0, 0, tiled=True)]
    another operation x6 -> x3, other arithmetic: 7.21 us -> 3.92 us  [join(): return jnp.stack([first, second], axis=1)]
    pallas_call x2 -> x1, Pallas kernels: 7.05 us -> 8.12 us  [attend_inner(): pl.pallas_call(inner_kernel, grid_spec=pltpu.PrefetchScalarGridSpec(num_s...]
  transfers between devices with their start and end apart: 27 -> 14, of which waited for: 9 -> 7; matrix products, arithmetic and copies ran while one was open for 1% -> 1% of each run, Pallas kernels for 26% -> 16%
where the time goes in v6:
time: 220 us; the launch traced here: 219 us
  Pallas kernels  73.7 us (34%)
  waiting for transfers between devices  65.2 us (30%)
  starting transfers between devices  47.2 us (21%)
  blocking collectives  26.7 us (12%)
  other arithmetic  4.22 us (2%)
    ppermute x8, waiting for transfers between devices, ring(): return lax.ppermute(value, ('zl', 'zh'), route)  65.2 us
    all_to_all x1, blocking collectives, body(): merged = lax.all_to_all(state, ROUND, 0, 0, tiled=True)  26.7 us
    all_to_all x4, starting transfers between devices, plane(): return lax.all_to_all(joint, PLANE, 0, 0, tiled=True)  26.6 us
    pallas_call x1, Pallas kernels, home_rows(): pl.pallas_call(functools.partial(home_kernel, width), grid_spec=pltpu.Pre...  15.5 us
    pallas_call x2, Pallas kernels, sort_rows(): pl.pallas_call(sort_kernel, grid=(rounds, blocks), in_specs=[pl.BlockSpec...  15.5 us
    ppermute x8, starting transfers between devices, ring(): return lax.ppermute(value, ('zl', 'zh'), route)  13.4 us
    pallas_call x2, Pallas kernels, scatter_rows(): pl.pallas_call(scatter_kernel, grid=(rounds, groups), in_specs=[pl.BlockS...  12.1 us
    pallas_call x2, Pallas kernels, back_rows(): pl.pallas_call(functools.partial(back_kernel, 0 if even else 2), grid=(ro...  11.9 us
  transfers between devices with their start and end apart: 14, of which 7 were waited for; matrix products, arithmetic and copies ran while one was open for 1% of the time, Pallas kernels for 16%

profile of v6, /device:TPU:35, one launch (start us, length us, event | category | flops | bytes accessed | tf_op | source)
XLA Modules:
  0.0 218.9 jit_solution(1526018478039563742)
XLA Ops:
  0.0 6.0 %collective-permute-start = (s32[2,2048]{1,0:T(2,128)}, s32[2,2048]{1,0:T(2,128)S(1)}, u32[]{:S(2)}, u32[]{:S(2)}) collective-permute-start(s32[2,2048]{1,0:T(2,128)} %param.11), channel_id=1, source_target_pairs={{0,2},{2,0},{1,3},{3,1},{4,6},{6,4},{5,7},{7,5},{8,10},{10,8},{9,1... | collective-permute-start | bytes 49160 | tf_op jit(solution)/shard_map/ppermute | solution.py:498
  6.1 4.1 %project.1.rows_ref = bf16[2048,256]{1,0:T(8,128)(2,1)S(1)} custom-call(bf16[2048,1024]{1,0:T(8,128)(2,1)} %x_ref.1, bf16[1024,128]{1,0:T(8,128)(2,1)} %wqk_ref.1, bf16[1024,128]{1,0:T(8,128)(2,1)} %wv_ref.1), custom_call_target="tpu_custom_call" | custom-call | tf_op jit(solution)/shard_map/project/pallas_call | solution.py:55
  10.4 5.9 %scatter_rows.2 = bf16[16,2,2,64,256]{4,3,2,1,0:T(8,128)(2,1)} custom-call(s32[2,2,2048]{2,1,0:T(2,128)S(1)} %get-tuple-element.60.idx_ref, bf16[2048,256]{1,0:T(8,128)(2,1)S(1)} %project.1.rows_ref), custom_call_target="tpu_custom_call" | custom-call | tf_op jit(solution)/shard_map/scatter_rows/pallas_call | solution.py:115
  16.2 6.9 %all-to-all-start = ((bf16[16,2,2,64,256]{4,3,2,1,0:T(8,128)(2,1)}), bf16[16,2,2,64,256]{4,3,2,1,0:T(8,128)(2,1)S(1)}, u32[]{:S(2)}, u32[]{:S(2)}) async-start(bf16[16,2,2,64,256]{4,3,2,1,0:T(8,128)(2,1)} %scatter_rows.2), calls=%async_computation | async-start | bytes 4194304 | tf_op jit(solution)/shard_map/all_to_all | solution.py:84
  23.2 6.2 %scatter_rows.3 = (bf16[16,2,64,256]{3,2,1,0:T(8,128)(2,1)}, bf16[16,2,64,256]{3,2,1,0:T(8,128)(2,1)}) custom-call(s32[2,2,2048]{2,1,0:T(2,128)S(1)} %get-tuple-element.59.idx_ref, bf16[2048,256]{1,0:T(8,128)(2,1)S(1)} %project.1.rows_ref), custom_call_target="tpu_custom_call" | custom-call | tf_op jit(solution)/shard_map/scatter_rows/pallas_call | solution.py:115
  30.9 22.0 %collective-permute-done.1 = bf16[16,2,64,256]{3,2,1,0:T(8,128)(2,1)S(1)} collective-permute-done((bf16[16,2,64,256]{3,2,1,0:T(8,128)(2,1)}, bf16[16,2,64,256]{3,2,1,0:T(8,128)(2,1)S(1)}, u32[]{:S(2)}, u32[]{:S(2)}) %collective-permute-start.1) | collective-permute-done | bytes 1048608 | tf_op jit(solution)/shard_map/ppermute | solution.py:76
  53.3 2.7 %pad_maximum_fusion = bf16[16,2,2,64,256]{4,3,2,1,0:T(8,128)(2,1)} fusion(bf16[16,1,2,64,256]{4,3,2,1,0:T(8,128)(2,1)} %bitcast.4, bf16[16,1,2,64,256]{4,3,2,1,0:T(8,128)(2,1)S(1)} %bitcast.17), kind=kLoop, calls=%fused_computation | loop fusion | flops 1048576 | bytes 4194304 | tf_op jit(solution)/shard_map/stack | solution.py:80
  56.1 6.7 %all-to-all-start.1 = ((bf16[16,2,2,64,256]{4,3,2,1,0:T(8,128)(2,1)}), bf16[16,2,2,64,256]{4,3,2,1,0:T(8,128)(2,1)}, u32[]{:S(2)}, u32[]{:S(2)}) async-start(bf16[16,2,2,64,256]{4,3,2,1,0:T(8,128)(2,1)} %pad_maximum_fusion), calls=%async_computation.1 | async-start | bytes 4194304 | tf_op jit(solution)/shard_map/all_to_all | solution.py:84
  66.7 21.0 %collective-permute-done.3.refs_1_ = bf16[8,2,64,256]{3,2,1,0:T(8,128)(2,1)S(1)} collective-permute-done((bf16[8,2,64,256]{3,2,1,0:T(8,128)(2,1)S(1)}, bf16[8,2,64,256]{3,2,1,0:T(8,128)(2,1)S(1)}, u32[]{:S(2)}, u32[]{:S(2)}) %collective-permute-start.3) | collective-permute-done | bytes 524320 | tf_op jit(solution)/shard_map/ppermute | solution.py:76
  88.3 5.2 %sort_rows.3 = (bf16[2,512,128]{2,1,0:T(8,128)(2,1)S(1)}, bf16[2,512,256]{2,1,0:T(8,128)(2,1)}) custom-call(s32[2,1,1,512]{3,2,1,0:T(1,128)S(1)} %copy.27.idx_ref, bf16[16,2,2,64,256]{4,3,2,1,0:T(8,128)(2,1)S(1)} %all-to-all-done.refs_0_, bf16[8,2,64,256]{3,2,1,0:T(8,128)(2,1)S(1)} %collective-permute-done.3.refs_1_, ...), custom_call_target="tpu_custom_call" | custom-call | tf_op jit(solution)/shard_map/sort_rows/pallas_call | solution.py:149
  94.8 10.2 %sort_rows.2 = (bf16[2,1536,128]{2,1,0:T(8,128)(2,1)S(1)}, bf16[2,1536,256]{2,1,0:T(8,128)(2,1)S(1)}) custom-call(s32[2,2,1,768]{3,2,1,0:T(1,128)S(1)} %reshape.33.idx_ref, bf16[16,2,2,64,256]{4,3,2,1,0:T(8,128)(2,1)S(1)} %all-to-all-done.refs_0_, bf16[8,2,64,256]{3,2,1,0:T(8,128)(2,1)S(1)} %collective-permute-done.3.refs_1_, ...), custom_call_target="tpu_custom_call" | custom-call | tf_op jit(solution)/shard_map/sort_rows/pallas_call | solution.py:149
  105.0 8.1 %attend_inner.1.inner_ref = bf16[2,1536,256]{2,1,0:T(8,128)(2,1)S(1)} custom-call(s32[2,8]{1,0:T(2,128)S(1)} %and_select_fusion.dist_ref, bf16[2,1536,128]{2,1,0:T(8,128)(2,1)S(1)} %get-tuple-element.39.q_ref.qh_ref, bf16[2,512,128]{2,1,0:T(8,128)(2,1)S(1)} %get-tuple-element.42.qt_ref, bf16[2,1536,256]{2,1,0:T(8,128)(2,1)S(1)} %get-tuple-element.40.kv_ref.kvh_ref, ...), custom_call_target="tpu_custom_call" | custom-call | tf_op jit(solution)/shard_map/attend_inner/pallas_call | solution.py:260
  113.2 3.9 %attend_edge.1.edge_ref = bf16[2,512,256]{2,1,0:T(8,128)(2,1)S(1)} custom-call(s32[2,8]{1,0:T(2,128)S(1)} %and_select_fusion.dist_ref, bf16[2,1536,128]{2,1,0:T(8,128)(2,1)S(1)} %get-tuple-element.39.q_ref.qh_ref, bf16[2,1536,256]{2,1,0:T(8,128)(2,1)S(1)} %get-tuple-element.40.kv_ref.kvh_ref, bf16[2,512,256]{2,1,0:T(8,128)(2,1)} %collective-permute-done.5.halo_ref), custom_call_target="tpu_custom_call" | custom-call | tf_op jit(solution)/shard_map/attend_edge/pallas_call | solution.py:277
  117.1 5.8 %back_rows.2 = bf16[16,2,2,72,128]{4,3,2,1,0:T(8,128)(2,1)} custom-call(s32[2,1,2048]{2,1,0:T(1,128)S(1)} %broadcast_in_dim.69.idx_ref, bf16[2,512,256]{2,1,0:T(8,128)(2,1)S(1)} %attend_edge.1.edge_ref, bf16[2,1536,256]{2,1,0:T(8,128)(2,1)S(1)} %attend_inner.1.inner_ref), custom_call_target="tpu_custom_call" | custom-call | tf_op jit(solution)/shard_map/back_rows/pallas_call | solution.py:346
  122.9 6.4 %all-to-all-start.2 = ((bf16[16,2,2,72,128]{4,3,2,1,0:T(8,128)(2,1)}), bf16[16,2,2,72,128]{4,3,2,1,0:T(8,128)(2,1)S(1)}, u32[]{:S(2)}, u32[]{:S(2)}) async-start(bf16[16,2,2,72,128]{4,3,2,1,0:T(8,128)(2,1)} %back_rows.2), calls=%async_computation.2 | async-start | bytes 2359296 | tf_op jit(solution)/shard_map/all_to_all | solution.py:84
  129.3 6.1 %back_rows.3 = (bf16[16,2,72,128]{3,2,1,0:T(8,128)(2,1)}, bf16[8,2,72,128]{3,2,1,0:T(8,128)(2,1)}, bf16[8,2,72,128]{3,2,1,0:T(8,128)(2,1)}) custom-call(s32[2,1,2048]{2,1,0:T(1,128)S(1)} %broadcast_in_dim.69.idx_ref, bf16[2,512,256]{2,1,0:T(8,128)(2,1)S(1)} %attend_edge.1.edge_ref, bf16[2,1536,256]{2,1,0:T(8,128)(2,1)S(1)} %attend_inner.1.inner_ref), custom_call_target="tpu_custom_call" | custom-call | tf_op jit(solution)/shard_map/back_rows/pallas_call | solution.py:346
  135.4 3.3 %collective-permute-start.6 = (bf16[8,2,72,128]{3,2,1,0:T(8,128)(2,1)}, bf16[8,2,72,128]{3,2,1,0:T(8,128)(2,1)S(1)}, u32[]{:S(2)}, u32[]{:S(2)}) collective-permute-start(bf16[8,2,72,128]{3,2,1,0:T(8,128)(2,1)} %get-tuple-element.46), channel_id=1, source_target_pairs={{0,130},{64,194},{128,0},{192,64},{2,128},{66,192},{130,2},{194,66... | collective-permute-start | bytes 884744 | tf_op jit(solution)/shard_map/ppermute | solution.py:76
  138.7 10.3 %collective-permute-done.6 = bf16[8,2,72,128]{3,2,1,0:T(8,128)(2,1)S(1)} collective-permute-done((bf16[8,2,72,128]{3,2,1,0:T(8,128)(2,1)}, bf16[8,2,72,128]{3,2,1,0:T(8,128)(2,1)S(1)}, u32[]{:S(2)}, u32[]{:S(2)}) %collective-permute-start.6) | collective-permute-done | bytes 294944 | tf_op jit(solution)/shard_map/ppermute | solution.py:76
  150.2 6.7 %all-to-all-start.3 = ((bf16[16,2,2,72,128]{4,3,2,1,0:T(8,128)(2,1)}), bf16[16,2,2,72,128]{4,3,2,1,0:T(8,128)(2,1)S(1)}, u32[]{:S(2)}, u32[]{:S(2)}) async-start(bf16[16,2,2,72,128]{4,3,2,1,0:T(8,128)(2,1)} %pad_maximum_fusion.1), calls=%async_computation.3 | async-start | bytes 2359296 | tf_op jit(solution)/shard_map/all_to_all | solution.py:84
  158.0 4.8 %collective-permute-start.8 = (bf16[16,2,72,128]{3,2,1,0:T(8,128)(2,1)}, bf16[16,2,72,128]{3,2,1,0:T(8,128)(2,1)S(1)}, u32[]{:S(2)}, u32[]{:S(2)}) collective-permute-start(bf16[16,2,72,128]{3,2,1,0:T(8,128)(2,1)} %get-tuple-element.58), channel_id=1, source_target_pairs={{0,194},{64,0},{128,64},{192,128},{2,192},{66,2},{130,66},{194,130... | collective-permute-start | bytes 1769480 | tf_op jit(solution)/shard_map/ppermute | solution.py:76
  163.2 9.1 %collective-permute-done.8.up_ref = bf16[16,2,72,128]{3,2,1,0:T(8,128)(2,1)S(1)} collective-permute-done((bf16[16,2,72,128]{3,2,1,0:T(8,128)(2,1)}, bf16[16,2,72,128]{3,2,1,0:T(8,128)(2,1)S(1)}, u32[]{:S(2)}, u32[]{:S(2)}) %collective-permute-start.8) | collective-permute-done | bytes 589856 | tf_op jit(solution)/shard_map/ppermute | solution.py:76
  174.1 15.5 %home_rows.1 = bf16[4,528,128]{2,1,0:T(8,128)(2,1)S(1)} custom-call(s32[4]{0:T(128)S(1)} %get-tuple-element.53.own_ref, s32[4,8,512]{2,1,0:T(8,128)S(1)} %select_bitcast_fusion.idx_ref, bf16[16,2,2,72,128]{4,3,2,1,0:T(8,128)(2,1)S(1)} %all-to-all-done.3.even_ref, bf16[16,2,72,128]{3,2,1,0:T(8,128)(2,1)S(1)} %collective-permute-done.8.up_ref, ...), custom_call_target="tpu_custom_call" | custom-call | tf_op jit(solution)/shard_map/home_rows/pallas_call | solution.py:426
  189.6 26.7 %all_to_all.25.m_ref = bf16[4,528,128]{2,1,0:T(8,128)(2,1)S(1)} all-to-all(bf16[4,528,128]{2,1,0:T(8,128)(2,1)S(1)} %home_rows.1), channel_id=1, replica_groups=mesh['zl'=4,'x'=4,'y'=4,'zh'=2,'c'=2] {'zh','c'}, dimensions={0} | all-to-all | bytes 1081344 | tf_op jit(solution)/shard_map/all_to_all | solution.py:527
  216.4 2.5 %finish.1 = bf16[512,1024]{1,0:T(8,128)(2,1)} custom-call(bf16[4,528,128]{2,1,0:T(8,128)(2,1)S(1)} %all_to_all.25.m_ref, bf16[128,1024]{1,0:T(8,128)(2,1)S(1)} %copy-done), custom_call_target="tpu_custom_call" | custom-call | tf_op jit(solution)/shard_map/finish/pallas_call | solution.py:460
  (52 shorter events, 12.4 us)
Async XLA Ops:
  0.0 10.2 %collective-permute-start = (s32[2,2048]{1,0:T(2,128)}, s32[2,2048]{1,0:T(2,128)S(1)}, u32[]{:S(2)}, u32[]{:S(2)}) collective-permute-start(s32[2,2048]{1,0:T(2,128)} %param.11), channel_id=1, source_target_pairs={{0,2},{2,0},{1,3},{3,1},{4,6},{6,4},{5,7},{7,5},{8,10},{10,8},{9,1... | collective-permute-start | bytes 49160 | tf_op jit(solution)/shard_map/ppermute | solution.py:498
  6.0 4.1 %copy-start.2 = (s32[2,2048]{1,0:T(2,128)S(1)}, s32[2,2048]{1,0:T(2,128)}, u32[]{:S(2)}) copy-start(s32[2,2048]{1,0:T(2,128)} %param.11) | copy-start | bytes 49156
  16.2 37.1 %all-to-all-start = ((bf16[16,2,2,64,256]{4,3,2,1,0:T(8,128)(2,1)}), bf16[16,2,2,64,256]{4,3,2,1,0:T(8,128)(2,1)S(1)}, u32[]{:S(2)}, u32[]{:S(2)}) async-start(bf16[16,2,2,64,256]{4,3,2,1,0:T(8,128)(2,1)} %scatter_rows.2), calls=%async_computation | async-start | bytes 4194304 | tf_op jit(solution)/shard_map/all_to_all | solution.py:84
  29.4 23.5 %collective-permute-start.1 = (bf16[16,2,64,256]{3,2,1,0:T(8,128)(2,1)}, bf16[16,2,64,256]{3,2,1,0:T(8,128)(2,1)S(1)}, u32[]{:S(2)}, u32[]{:S(2)}) collective-permute-start(bf16[16,2,64,256]{3,2,1,0:T(8,128)(2,1)} %get-tuple-element.30), channel_id=1, source_target_pairs={{0,64},{64,128},{128,192},{192,2},{2,66},{66,130},{130,194},{194,0... | collective-permute-start | bytes 3145736 | tf_op jit(solution)/shard_map/ppermute | solution.py:76
  30.2 23.2 %collective-permute-start.2 = (bf16[16,2,64,256]{3,2,1,0:T(8,128)(2,1)}, bf16[16,2,64,256]{3,2,1,0:T(8,128)(2,1)}, u32[]{:S(2)}, u32[]{:S(2)}) collective-permute-start(bf16[16,2,64,256]{3,2,1,0:T(8,128)(2,1)} %get-tuple-element.31), channel_id=1, source_target_pairs={{0,194},{64,0},{128,64},{192,128},{2,192},{66,2},{130,66},{194,130... | collective-permute-start | bytes 3145736 | tf_op jit(solution)/shard_map/ppermute | solution.py:76
  56.1 32.2 %all-to-all-start.1 = ((bf16[16,2,2,64,256]{4,3,2,1,0:T(8,128)(2,1)}), bf16[16,2,2,64,256]{4,3,2,1,0:T(8,128)(2,1)}, u32[]{:S(2)}, u32[]{:S(2)}) async-start(bf16[16,2,2,64,256]{4,3,2,1,0:T(8,128)(2,1)} %pad_maximum_fusion), calls=%async_computation.1 | async-start | bytes 4194304 | tf_op jit(solution)/shard_map/all_to_all | solution.py:84
  62.7 3.9 %copy-start.3 = (s32[2,2048]{1,0:T(2,128)S(1)}, s32[2,2048]{1,0:T(2,128)}, u32[]{:S(2)}) copy-start(s32[2,2048]{1,0:T(2,128)} %param.12) | copy-start | bytes 49156
  62.9 24.9 %collective-permute-start.3 = (bf16[8,2,64,256]{3,2,1,0:T(8,128)(2,1)S(1)}, bf16[8,2,64,256]{3,2,1,0:T(8,128)(2,1)S(1)}, u32[]{:S(2)}, u32[]{:S(2)}) collective-permute-start(bf16[8,2,64,256]{3,2,1,0:T(8,128)(2,1)S(1)} %get-tuple-element.56), channel_id=1, source_target_pairs={{0,128},{64,192},{128,2},{192,66},{2,130},{66,194},{130,0},{194,64... | collective-permute-start | bytes 1572872 | tf_op jit(solution)/shard_map/ppermute | solution.py:76
  64.9 23.4 %collective-permute-start.4 = (bf16[8,2,64,256]{3,2,1,0:T(8,128)(2,1)S(1)}, bf16[8,2,64,256]{3,2,1,0:T(8,128)(2,1)S(1)}, u32[]{:S(2)}, u32[]{:S(2)}) collective-permute-start(bf16[8,2,64,256]{3,2,1,0:T(8,128)(2,1)S(1)} %get-tuple-element.55), channel_id=1, source_target_pairs={{0,130},{64,194},{128,0},{192,64},{2,128},{66,192},{130,2},{194,66... | collective-permute-start | bytes 1572872 | tf_op jit(solution)/shard_map/ppermute | solution.py:76
  66.7 28.1 %copy-start.4 = (s32[2,8]{1,0:T(2,128)S(1)}, s32[2,8]{1,0:T(2,128)}, u32[]{:S(2)}) copy-start(s32[2,8]{1,0:T(2,128)} %param.13) | copy-start | bytes 196
  93.5 19.7 %collective-permute-start.5 = (bf16[2,512,256]{2,1,0:T(8,128)(2,1)}, bf16[2,512,256]{2,1,0:T(8,128)(2,1)}, u32[]{:S(2)}, u32[]{:S(2)}) collective-permute-start(bf16[2,512,256]{2,1,0:T(8,128)(2,1)} %get-tuple-element.41.kvt_ref), channel_id=1, source_target_pairs={{0,4},{4,8},{8,12},{12,16},{16,20},{20,24},{24,28},{28,32},{32,36}... | collective-permute-start | bytes 1572872 | tf_op jit(solution)/shard_map/ppermute | solution.py:515
  122.9 26.0 %all-to-all-start.2 = ((bf16[16,2,2,72,128]{4,3,2,1,0:T(8,128)(2,1)}), bf16[16,2,2,72,128]{4,3,2,1,0:T(8,128)(2,1)S(1)}, u32[]{:S(2)}, u32[]{:S(2)}) async-start(bf16[16,2,2,72,128]{4,3,2,1,0:T(8,128)(2,1)} %back_rows.2), calls=%async_computation.2 | async-start | bytes 2359296 | tf_op jit(solution)/shard_map/all_to_all | solution.py:84
  135.4 13.7 %copy-start.1 = (bf16[16,2,72,128]{3,2,1,0:T(8,128)(2,1)S(1)}, bf16[16,2,72,128]{3,2,1,0:T(8,128)(2,1)}, u32[]{:S(2)}) copy-start(bf16[16,2,72,128]{3,2,1,0:T(8,128)(2,1)} %get-tuple-element.44) | copy-start | bytes 1769476
  135.4 13.6 %collective-permute-start.6 = (bf16[8,2,72,128]{3,2,1,0:T(8,128)(2,1)}, bf16[8,2,72,128]{3,2,1,0:T(8,128)(2,1)S(1)}, u32[]{:S(2)}, u32[]{:S(2)}) collective-permute-start(bf16[8,2,72,128]{3,2,1,0:T(8,128)(2,1)} %get-tuple-element.46), channel_id=1, source_target_pairs={{0,130},{64,194},{128,0},{192,64},{2,128},{66,192},{130,2},{194,66... | collective-permute-start | bytes 884744 | tf_op jit(solution)/shard_map/ppermute | solution.py:76
  138.7 10.3 %collective-permute-start.7 = (bf16[8,2,72,128]{3,2,1,0:T(8,128)(2,1)}, bf16[8,2,72,128]{3,2,1,0:T(8,128)(2,1)S(1)}, u32[]{:S(2)}, u32[]{:S(2)}) collective-permute-start(bf16[8,2,72,128]{3,2,1,0:T(8,128)(2,1)} %get-tuple-element.47), channel_id=1, source_target_pairs={{0,128},{64,192},{128,2},{192,66},{2,130},{66,194},{130,0},{194,64... | collective-permute-start | bytes 884744 | tf_op jit(solution)/shard_map/ppermute | solution.py:76
  150.2 23.9 %all-to-all-start.3 = ((bf16[16,2,2,72,128]{4,3,2,1,0:T(8,128)(2,1)}), bf16[16,2,2,72,128]{4,3,2,1,0:T(8,128)(2,1)S(1)}, u32[]{:S(2)}, u32[]{:S(2)}) async-start(bf16[16,2,2,72,128]{4,3,2,1,0:T(8,128)(2,1)} %pad_maximum_fusion.1), calls=%async_computation.3 | async-start | bytes 2359296 | tf_op jit(solution)/shard_map/all_to_all | solution.py:84
  158.0 14.4 %collective-permute-start.8 = (bf16[16,2,72,128]{3,2,1,0:T(8,128)(2,1)}, bf16[16,2,72,128]{3,2,1,0:T(8,128)(2,1)S(1)}, u32[]{:S(2)}, u32[]{:S(2)}) collective-permute-start(bf16[16,2,72,128]{3,2,1,0:T(8,128)(2,1)} %get-tuple-element.58), channel_id=1, source_target_pairs={{0,194},{64,0},{128,64},{192,128},{2,192},{66,2},{130,66},{194,130... | collective-permute-start | bytes 1769480 | tf_op jit(solution)/shard_map/ppermute | solution.py:76
  162.8 11.3 %collective-permute-start.9 = (bf16[16,2,72,128]{3,2,1,0:T(8,128)(2,1)}, bf16[16,2,72,128]{3,2,1,0:T(8,128)(2,1)S(1)}, u32[]{:S(2)}, u32[]{:S(2)}) collective-permute-start(bf16[16,2,72,128]{3,2,1,0:T(8,128)(2,1)} %get-tuple-element.57), channel_id=1, source_target_pairs={{0,64},{64,128},{128,192},{192,2},{2,66},{66,130},{130,194},{194,0... | collective-permute-start | bytes 1769480 | tf_op jit(solution)/shard_map/ppermute | solution.py:76
  174.1 42.2 %copy-start = (bf16[128,1024]{1,0:T(8,128)(2,1)S(1)}, bf16[128,1024]{1,0:T(8,128)(2,1)}, u32[]{:S(2)}) copy-start(bf16[128,1024]{1,0:T(8,128)(2,1)} %w_ref.1) | copy-start | bytes 786436

commit v7 on v6

--- a/solution.py
+++ b/solution.py
@@ -123,16 +123,46 @@
     )(idx, rows)
 
 
-def sort_kernel(idx_ref, *refs):
-    (*row_refs, q_ref, kv_ref) = refs
+def pick_rows(idx_ref, row_refs, base):
     col = column(idx_ref[0, 0])
-    got, base = 0.0, 0
+    got = 0.0
     for ref in row_refs:
         rows = ref[...].reshape(-1, 256)
         n = rows.shape[0]
-        place = lax.broadcasted_iota(jnp.int32, (q_ref.shape[1], n), 1) + base
+        place = lax.broadcasted_iota(jnp.int32, (col.shape[0], n), 1) + base
         got += jnp.dot(one_hot(col, place), rows, preferred_element_type=F32)
         base += n
+    return got
+
+
+def early_kernel(idx_ref, near_ref, low_ref, high_ref, out_ref):
+    out_ref[0] = pick_rows(idx_ref, (near_ref, low_ref, high_ref), 0).astype(BF)
+
+
+def early_rows(idx, even, low, high):
+    rounds, count = idx.shape
+    step = count // 2
+    peers, _, _, width, lanes = even.shape
+    four = lambda r, b: (0, r, 0, 0)
+    return pl.pallas_call(
+        early_kernel,
+        grid=(rounds, 2),
+        in_specs=[
+            pl.BlockSpec((1, 1, 1, step), lambda r, b: (r, b, 0, 0)),
+            pl.BlockSpec((peers, 1, 1, width, lanes), lambda r, b: (0, 0, r, 0, 0)),
+            pl.BlockSpec((peers // 2, 1, width, lanes), four),
+            pl.BlockSpec((peers // 2, 1, width, lanes), four),
+        ],
+        out_specs=pl.BlockSpec((1, step, 256), lambda r, b: (r, b, 0)),
+        out_shape=pltpu.HBM((rounds, count, 256), BF),
+        compiler_params=params(2),
+        name="early_rows",
+    )(idx.reshape(rounds, 2, 1, step), in_hbm(even), low, high)
+
+
+def sort_kernel(idx_ref, early_ref, odd_ref, q_ref, kv_ref):
+    n = odd_ref.shape[0] * odd_ref.shape[1] * odd_ref.shape[3]
+    got = early_ref[0].astype(F32) + pick_rows(idx_ref, (odd_ref,), n)
     qk = got[:, :128]
     keys = qk * lax.rsqrt(jnp.sum(qk * qk, axis=-1, keepdims=True) + 1e-06)
     q_ref[0] = qk.astype(BF)
@@ -140,21 +170,17 @@
     kv_ref[0, :, 128:] = got[:, 128:].astype(BF)
 
 
-def sort_rows(idx, even, low, high, odd, step):
+def sort_rows(idx, early, odd, first, step):
     rounds, count = idx.shape
     blocks = count // step
-    peers, _, _, width, lanes = even.shape
-    four = lambda r, b: (0, r, 0, 0)
-    five = lambda r, b: (0, 0, r, 0, 0)
+    peers, _, _, width, lanes = odd.shape
     return pl.pallas_call(
         sort_kernel,
         grid=(rounds, blocks),
         in_specs=[
             pl.BlockSpec((1, 1, 1, step), lambda r, b: (r, b, 0, 0)),
-            pl.BlockSpec((peers, 1, 1, width, lanes), five),
-            pl.BlockSpec((peers // 2, 1, width, lanes), four),
-            pl.BlockSpec((peers // 2, 1, width, lanes), four),
-            pl.BlockSpec((peers, 2, 1, width, lanes), five),
+            pl.BlockSpec((1, step, 256), lambda r, b: (r, first // step + b, 0)),
+            pl.BlockSpec((peers, 2, 1, width, lanes), lambda r, b: (0, 0, r, 0, 0)),
         ],
         out_specs=[
             pl.BlockSpec((1, step, 128), lambda r, b: (r, b, 0)),
@@ -166,7 +192,7 @@
         ],
         compiler_params=params(2),
         name="sort_rows",
-    )(idx.reshape(rounds, blocks, 1, step), even, low, high, odd)
+    )(idx.reshape(rounds, blocks, 1, step), in_hbm(early), in_hbm(odd))
 
 
 def terms_to_lines(terms, groups):
@@ -370,36 +396,48 @@
         row += size
 
 
-def gather_home(own_ref, cols, x_ref, width):
+def gather_home(own_ref, cols, x_ref, width, groups):
     near, far = 0.0, 0.0
     size = 16 * width
     place = lax.broadcasted_iota(jnp.int32, (cols.shape[0], size), 1)
-    for g in range(4):
-        hot = one_hot(cols[:, g : g + 1], place)
-        got = jnp.dot(hot, x_ref[g * size : (g + 1) * size], preferred_element_type=F32)
-        if g == 0:
-            near = got
-        else:
-            mine = own_ref[g] == 1
-            near += jnp.where(mine, got, 0.0)
-            far += jnp.where(mine, 0.0, got)
+    for at, g in enumerate(groups):
+        hot = one_hot(cols[:, at : at + 1], place)
+        got = jnp.dot(hot, x_ref[at * size : (at + 1) * size], preferred_element_type=F32)
+        mine = own_ref[g] == 1
+        near += jnp.where(mine, got, 0.0)
+        far += jnp.where(mine, 0.0, got)
     return [near, far]
 
 
-def home_kernel(width, own_ref, idx_ref, even_ref, up_ref, down_ref, out_ref, x_ref):
-    rounds = even_ref.shape[2]
+def odd_home_kernel(width, own_ref, idx_ref, up_ref, down_ref, out_ref, x_ref):
+    rounds = up_ref.shape[1]
 
     @pl.when(pl.program_id(0) == 0)
     def _():
         for r in range(rounds):
-            blocks = [even_ref.at[:, 0, r], even_ref.at[:, 1, r], up_ref.at[:, r], down_ref.at[:, r]]
-            fill_home(x_ref.at[r], width, blocks)
+            fill_home(x_ref.at[r], width, [up_ref.at[:, r], down_ref.at[:, r]])
+
+    cols = jnp.transpose(idx_ref[0])
+    for r in range(rounds):
+        states = gather_home(own_ref, cols[:, 2 * r : 2 * r + 2], x_ref.at[r], width, (2, 3))
+        for at, state in enumerate(states):
+            out_ref[2 * r + at] = state.astype(BF)
+
+
+def home_kernel(width, own_ref, idx_ref, odd_ref, even_ref, out_ref, x_ref):
+    rounds = even_ref.shape[2]
+
+    @pl.when(pl.program_id(0) == 0)
+    def _():
+        for r in range(rounds):
+            fill_home(x_ref.at[r], width, [even_ref.at[:, 0, r], even_ref.at[:, 1, r]])
 
     step = idx_ref.shape[2]
     cols = jnp.transpose(idx_ref[0])
     states = []
     for r in range(rounds):
-        states += gather_home(own_ref, cols[:, 4 * r : 4 * r + 4], x_ref.at[r], width)
+        states += gather_home(own_ref, cols[:, 2 * r : 2 * r + 2], x_ref.at[r], width, (0, 1))
+    states = [s + odd_ref[at].astype(F32) for at, s in enumerate(states)]
     here = [s[:, 131:132] > 0.5 for s in states]
     logs = [
         jnp.where(h, s[:, 128:129] + s[:, 129:130] + s[:, 130:131], ABSENT)
@@ -417,26 +455,38 @@
     out_ref[0, step:, :] = terms_to_lines(terms, step // 32).reshape(step // 32, 128).astype(BF)
 
 
-def home_rows(own, idx, even, up, down, width):
+def home_rows(own, idx, width, homes, odd=None):
     rounds, groups, count = idx.shape
     quarters = 4
     step = count // quarters
     columns = rounds * groups
     idx = idx.reshape(columns, quarters, step).transpose(1, 0, 2)
-    return pl.pallas_call(
-        functools.partial(home_kernel, width),
+    partial = pl.BlockSpec((2 * rounds, step, 256), lambda i, o: (0, i, 0))
+    specs = [pl.BlockSpec((1, columns, step), lambda i, o: (i, 0, 0))]
+    if odd is None:
+        kernel, out_spec = odd_home_kernel, partial
+        out_shape = pltpu.HBM((2 * rounds, count, 256), BF)
+    else:
+        kernel = home_kernel
+        odd = in_hbm(odd)
+        homes = (odd, *homes)
+        out_spec = pl.BlockSpec((1, step + step // 32, 128), lambda i, o: (i, 0, 0))
+        out_shape = jax.ShapeDtypeStruct((quarters, step + step // 32, 128), BF)
+    for v in homes:
+        specs.append(partial if v is odd else whole(v.shape))
+    return pl.pallas_call(
+        functools.partial(kernel, width),
         grid_spec=pltpu.PrefetchScalarGridSpec(
             num_scalar_prefetch=1,
             grid=(quarters,),
-            in_specs=[pl.BlockSpec((1, columns, step), lambda i, o: (i, 0, 0))]
-            + [whole(v.shape) for v in (even, up, down)],
-            out_specs=pl.BlockSpec((1, step + step // 32, 128), lambda i, o: (i, 0, 0)),
-            scratch_shapes=[pltpu.VMEM((rounds, 64 * width, 256), BF)],
+            in_specs=specs,
+            out_specs=out_spec,
+            scratch_shapes=[pltpu.VMEM((rounds, 32 * width, 256), BF)],
         ),
-        out_shape=jax.ShapeDtypeStruct((quarters, step + step // 32, 128), BF),
+        out_shape=out_shape,
         compiler_params=params(),
         name="home_rows",
-    )(own, idx, even, up, down)
+    )(own, idx, *homes)
 
 
 def finish_kernel(m_ref, w_ref, out_ref):
@@ -507,13 +557,15 @@
     even, packed = together((even, packed))
     half = plane(even)
     up, down = scatter_rows(sent[:, 2:], packed, width, False)
-    half, up, down = together((half, ring(up, 1), ring(down, -1)))
-    rows = half, ring(half[:8, 1], 2), ring(half[8:, 1], -2), plane(join(up, down))
-    rows = together(rows)
-
-    q_tail, kv_tail = sort_rows(spots[:, tail:], *rows, 2 * BLOCK)
+    up, down = ring(up, 1), ring(down, -1)
+    low, high = ring(half[:8, 1], 2), ring(half[8:, 1], -2)
+    odd = plane(join(up, down))
+    early = early_rows(spots, half, low, high)
+    early, odd = together((early, odd))
+
+    q_tail, kv_tail = sort_rows(spots[:, tail:], early, odd, tail, 2 * BLOCK)
     halo = lax.ppermute(kv_tail, SEQ, next_device)
-    q_head, kv_head = sort_rows(spots[:, :tail], *rows, 3 * BLOCK)
+    q_head, kv_head = sort_rows(spots[:, :tail], early, odd, 0, 3 * BLOCK)
     inner = attend_inner(dist, q_head, q_tail, kv_head, kv_tail)
     edge = attend_edge(dist, q_head, kv_head, halo)
 
@@ -521,9 +573,12 @@
     odd, edge = together((odd, edge))
     half = plane(odd)
     near, low, high = back_rows(groups[:, None], edge, inner, width, True)
-    half, low, high = together((half, ring(low, -2), ring(high, 2)))
+    low, high = ring(low, -2), ring(high, 2)
+    up, down = ring(half[:, 0], -1), ring(half[:, 1], 1)
     even = plane(join(near, jnp.concatenate([low, high])))
-    state = home_rows(own, sent, even, ring(half[:, 0], -1), ring(half[:, 1], 1), width)
+    late = home_rows(own, sent[:, 2:], width, (up, down))
+    late, even = together((late, even))
+    state = home_rows(own, sent[:, :2], width, (even,), late)
     merged = lax.all_to_all(state, ROUND, 0, 0, tiled=True)
     return finish(merged, w_out)
 

time: 220 us -> 232 us (1.055)
  waiting for transfers between devices: 65.2 us -> 75.7 us
  Pallas kernels: 73.7 us -> 80.3 us
  starting transfers between devices: 47.2 us -> 43.1 us
    pallas_call x1 -> x3, Pallas kernels: 15.5 us -> 30 us  [the longest x2 21.3 us: home_rows(): pl.pallas_call(functools.partial(kernel, width), grid_spec=pltpu.Prefetch...]
    ppermute x8, waiting for transfers between devices: 65.2 us -> 75.5 us  [ring(): return lax.ppermute(value, ('zl', 'zh'), route)]
    pallas_call x2, Pallas kernels: 15.5 us -> 10.5 us  [sort_rows(): pl.pallas_call(sort_kernel, grid=(rounds, blocks), in_specs=[pl.BlockSpec...]
    ppermute x8, starting transfers between devices: 13.4 us -> 8.95 us  [ring(): return lax.ppermute(value, ('zl', 'zh'), route)]
  transfers between devices with their start and end apart: 14 -> 14, of which waited for: 7 -> 8; matrix products, arithmetic and copies ran while one was open for 1% -> 3% of each run, Pallas kernels for 16% -> 20%
where the time goes in v7:
time: 232 us
  Pallas kernels  80.3 us (35%)
  waiting for transfers between devices  75.7 us (33%)
  starting transfers between devices  43.1 us (19%)
  blocking collectives  24.5 us (11%)
  other arithmetic  4.04 us (2%)
  local copies, waits for them, and re-layouts  3.66 us (2%)
    ppermute x8, waiting for transfers between devices, ring(): return lax.ppermute(value, ('zl', 'zh'), route)  75.5 us
    all_to_all x4, starting transfers between devices, plane(): return lax.all_to_all(joint, PLANE, 0, 0, tiled=True)  26.7 us
    all_to_all x1, blocking collectives, body(): merged = lax.all_to_all(state, ROUND, 0, 0, tiled=True)  24.5 us
    pallas_call x2, Pallas kernels, home_rows(): pl.pallas_call(functools.partial(kernel, width), grid_spec=pltpu.Prefetch...  21.3 us
    pallas_call x2, Pallas kernels, scatter_rows(): pl.pallas_call(scatter_kernel, grid=(rounds, groups), in_specs=[pl.BlockS...  12.2 us
    pallas_call x2, Pallas kernels, back_rows(): pl.pallas_call(functools.partial(back_kernel, 0 if even else 2), grid=(ro...  11.9 us
    pallas_call x2, Pallas kernels, sort_rows(): pl.pallas_call(sort_kernel, grid=(rounds, blocks), in_specs=[pl.BlockSpec...  10.5 us
    ppermute x8, starting transfers between devices, ring(): return lax.ppermute(value, ('zl', 'zh'), route)  8.95 us
  transfers between devices with their start and end apart: 14, of which 8 were waited for; matrix products, arithmetic and copies ran while one was open for 3% of the time, Pallas kernels for 20%

profile of v7, /device:TPU:35, one launch (start us, length us, event | category | flops | bytes accessed | tf_op | source)
XLA Modules:
  0.0 231.6 jit_solution(8122825087157882786)
XLA Ops:
  0.0 6.0 %collective-permute-start = (s32[2,2048]{1,0:T(2,128)}, s32[2,2048]{1,0:T(2,128)S(1)}, u32[]{:S(2)}, u32[]{:S(2)}) collective-permute-start(s32[2,2048]{1,0:T(2,128)} %param.11), channel_id=1, source_target_pairs={{0,2},{2,0},{1,3},{3,1},{4,6},{6,4},{5,7},{7,5},{8,10},{10,8},{9,1... | collective-permute-start | bytes 49160 | tf_op jit(solution)/shard_map/ppermute | solution.py:548
  6.1 4.1 %project.1.rows_ref = bf16[2048,256]{1,0:T(8,128)(2,1)S(1)} custom-call(bf16[2048,1024]{1,0:T(8,128)(2,1)} %x_ref.1, bf16[1024,128]{1,0:T(8,128)(2,1)} %wqk_ref.1, bf16[1024,128]{1,0:T(8,128)(2,1)} %wv_ref.1), custom_call_target="tpu_custom_call" | custom-call | tf_op jit(solution)/shard_map/project/pallas_call | solution.py:55
  10.4 5.9 %scatter_rows.2 = bf16[16,2,2,64,256]{4,3,2,1,0:T(8,128)(2,1)} custom-call(s32[2,2,2048]{2,1,0:T(2,128)S(1)} %get-tuple-element.48.idx_ref, bf16[2048,256]{1,0:T(8,128)(2,1)S(1)} %project.1.rows_ref), custom_call_target="tpu_custom_call" | custom-call | tf_op jit(solution)/shard_map/scatter_rows/pallas_call | solution.py:115
  16.3 6.9 %all-to-all-start = ((bf16[16,2,2,64,256]{4,3,2,1,0:T(8,128)(2,1)}), bf16[16,2,2,64,256]{4,3,2,1,0:T(8,128)(2,1)}, u32[]{:S(2)}, u32[]{:S(2)}) async-start(bf16[16,2,2,64,256]{4,3,2,1,0:T(8,128)(2,1)} %scatter_rows.2), calls=%async_computation | async-start | bytes 4194304 | tf_op jit(solution)/shard_map/all_to_all | solution.py:84
  23.2 6.3 %scatter_rows.3 = (bf16[16,2,64,256]{3,2,1,0:T(8,128)(2,1)}, bf16[16,2,64,256]{3,2,1,0:T(8,128)(2,1)}) custom-call(s32[2,2,2048]{2,1,0:T(2,128)S(1)} %get-tuple-element.47.idx_ref, bf16[2048,256]{1,0:T(8,128)(2,1)S(1)} %project.1.rows_ref), custom_call_target="tpu_custom_call" | custom-call | tf_op jit(solution)/shard_map/scatter_rows/pallas_call | solution.py:115
  30.9 21.9 %collective-permute-done.3 = bf16[16,2,64,256]{3,2,1,0:T(8,128)(2,1)S(1)} collective-permute-done((bf16[16,2,64,256]{3,2,1,0:T(8,128)(2,1)}, bf16[16,2,64,256]{3,2,1,0:T(8,128)(2,1)S(1)}, u32[]{:S(2)}, u32[]{:S(2)}) %collective-permute-start.3) | collective-permute-done | bytes 1048608 | tf_op jit(solution)/shard_map/ppermute | solution.py:76
  54.8 6.7 %all-to-all-start.1 = ((bf16[16,2,2,64,256]{4,3,2,1,0:T(8,128)(2,1)}), bf16[16,2,2,64,256]{4,3,2,1,0:T(8,128)(2,1)}, u32[]{:S(2)}, u32[]{:S(2)}) async-start(bf16[16,2,2,64,256]{4,3,2,1,0:T(8,128)(2,1)} %pad_maximum_fusion), calls=%async_computation.1 | async-start | bytes 4194304 | tf_op jit(solution)/shard_map/all_to_all | solution.py:84
  62.8 3.7 %collective-permute-start.2 = (bf16[8,2,64,256]{3,2,1,0:T(8,128)(2,1)S(1)}, bf16[8,2,64,256]{3,2,1,0:T(8,128)(2,1)S(1)}, u32[]{:S(2)}, u32[]{:S(2)}) collective-permute-start(bf16[8,2,64,256]{3,2,1,0:T(8,128)(2,1)S(1)} %get-tuple-element.43), channel_id=1, source_target_pairs={{0,130},{64,194},{128,0},{192,64},{2,128},{66,192},{130,2},{194,66... | collective-permute-start | bytes 1572872 | tf_op jit(solution)/shard_map/ppermute | solution.py:76
  66.5 22.6 %collective-permute-done.2.high_ref = bf16[8,2,64,256]{3,2,1,0:T(8,128)(2,1)S(1)} collective-permute-done((bf16[8,2,64,256]{3,2,1,0:T(8,128)(2,1)S(1)}, bf16[8,2,64,256]{3,2,1,0:T(8,128)(2,1)S(1)}, u32[]{:S(2)}, u32[]{:S(2)}) %collective-permute-start.2) | collective-permute-done | bytes 524320 | tf_op jit(solution)/shard_map/ppermute | solution.py:76
  91.4 8.7 %early_rows.1.early_ref = bf16[2,2048,256]{2,1,0:T(8,128)(2,1)} custom-call(s32[2,2,1,1024]{3,2,1,0:T(1,128)S(1)} %reshape.41.idx_ref, bf16[16,2,2,64,256]{4,3,2,1,0:T(8,128)(2,1)} %all-to-all-done.near_ref, bf16[8,2,64,256]{3,2,1,0:T(8,128)(2,1)S(1)} %collective-permute-done.1.low_ref, bf16[8,2,64,256]{3,2,1,0:T(8,128)(2,1)S(1)} %collective-permute-done.2.high_ref), custom_call_target="tpu_custom_call" | custom-call | tf_op jit(solution)/shard_map/early_rows/pallas_call | solution.py:147
  100.1 3.5 %sort_rows.3 = (bf16[2,512,128]{2,1,0:T(8,128)(2,1)S(1)}, bf16[2,512,256]{2,1,0:T(8,128)(2,1)S(1)}) custom-call(s32[2,1,1,512]{3,2,1,0:T(1,128)S(1)} %copy.28.idx_ref, bf16[2,2048,256]{2,1,0:T(8,128)(2,1)} %early_rows.1.early_ref, bf16[16,2,2,64,256]{4,3,2,1,0:T(8,128)(2,1)} %all-to-all-done.1.odd_ref), custom_call_target="tpu_custom_call" | custom-call | tf_op jit(solution)/shard_map/sort_rows/pallas_call | solution.py:177
  105.1 7.0 %sort_rows.2 = (bf16[2,1536,128]{2,1,0:T(8,128)(2,1)S(1)}, bf16[2,1536,256]{2,1,0:T(8,128)(2,1)S(1)}) custom-call(s32[2,2,1,768]{3,2,1,0:T(1,128)S(1)} %reshape.40.idx_ref, bf16[2,2048,256]{2,1,0:T(8,128)(2,1)} %early_rows.1.early_ref, bf16[16,2,2,64,256]{4,3,2,1,0:T(8,128)(2,1)} %all-to-all-done.1.odd_ref), custom_call_target="tpu_custom_call" | custom-call | tf_op jit(solution)/shard_map/sort_rows/pallas_call | solution.py:177
  112.2 6.6 %attend_inner.1.inner_ref = bf16[2,1536,256]{2,1,0:T(8,128)(2,1)S(1)} custom-call(s32[2,8]{1,0:T(2,128)S(1)} %and_select_fusion.dist_ref, bf16[2,1536,128]{2,1,0:T(8,128)(2,1)S(1)} %get-tuple-element.28.q_ref.qh_ref, bf16[2,512,128]{2,1,0:T(8,128)(2,1)S(1)} %get-tuple-element.31.qt_ref, bf16[2,1536,256]{2,1,0:T(8,128)(2,1)S(1)} %get-tuple-element.29.kv_ref.kvh_ref, ...), custom_call_target="tpu_custom_call" | custom-call | tf_op jit(solution)/shard_map/attend_inner/pallas_call | solution.py:286
  121.5 5.9 %back_rows.2 = bf16[16,2,2,72,128]{4,3,2,1,0:T(8,128)(2,1)} custom-call(s32[2,1,2048]{2,1,0:T(1,128)S(1)} %broadcast_in_dim.53.idx_ref, bf16[2,512,256]{2,1,0:T(8,128)(2,1)S(1)} %attend_edge.1.edge_ref, bf16[2,1536,256]{2,1,0:T(8,128)(2,1)S(1)} %attend_inner.1.inner_ref), custom_call_target="tpu_custom_call" | custom-call | tf_op jit(solution)/shard_map/back_rows/pallas_call | solution.py:372
  127.3 6.4 %all-to-all-start.2 = ((bf16[16,2,2,72,128]{4,3,2,1,0:T(8,128)(2,1)}), bf16[16,2,2,72,128]{4,3,2,1,0:T(8,128)(2,1)}, u32[]{:S(2)}, u32[]{:S(2)}) async-start(bf16[16,2,2,72,128]{4,3,2,1,0:T(8,128)(2,1)} %back_rows.2), calls=%async_computation.2 | async-start | bytes 2359296 | tf_op jit(solution)/shard_map/all_to_all | solution.py:84
  133.8 6.1 %back_rows.3 = (bf16[16,2,72,128]{3,2,1,0:T(8,128)(2,1)}, bf16[8,2,72,128]{3,2,1,0:T(8,128)(2,1)}, bf16[8,2,72,128]{3,2,1,0:T(8,128)(2,1)}) custom-call(s32[2,1,2048]{2,1,0:T(1,128)S(1)} %broadcast_in_dim.53.idx_ref, bf16[2,512,256]{2,1,0:T(8,128)(2,1)S(1)} %attend_edge.1.edge_ref, bf16[2,1536,256]{2,1,0:T(8,128)(2,1)S(1)} %attend_inner.1.inner_ref), custom_call_target="tpu_custom_call" | custom-call | tf_op jit(solution)/shard_map/back_rows/pallas_call | solution.py:372
  142.2 8.3 %collective-permute-done.8 = bf16[8,2,72,128]{3,2,1,0:T(8,128)(2,1)S(1)} collective-permute-done((bf16[8,2,72,128]{3,2,1,0:T(8,128)(2,1)}, bf16[8,2,72,128]{3,2,1,0:T(8,128)(2,1)S(1)}, u32[]{:S(2)}, u32[]{:S(2)}) %collective-permute-start.8) | collective-permute-done | bytes 294944 | tf_op jit(solution)/shard_map/ppermute | solution.py:76
  150.5 8.4 %collective-permute-done.9 = bf16[8,2,72,128]{3,2,1,0:T(8,128)(2,1)S(1)} collective-permute-done((bf16[8,2,72,128]{3,2,1,0:T(8,128)(2,1)}, bf16[8,2,72,128]{3,2,1,0:T(8,128)(2,1)S(1)}, u32[]{:S(2)}, u32[]{:S(2)}) %collective-permute-start.9) | collective-permute-done | bytes 294944 | tf_op jit(solution)/shard_map/ppermute | solution.py:76
  161.1 6.7 %all-to-all-start.3 = ((bf16[16,2,2,72,128]{4,3,2,1,0:T(8,128)(2,1)}), bf16[16,2,2,72,128]{4,3,2,1,0:T(8,128)(2,1)S(1)}, u32[]{:S(2)}, u32[]{:S(2)}) async-start(bf16[16,2,2,72,128]{4,3,2,1,0:T(8,128)(2,1)} %pad_maximum_fusion.1), calls=%async_computation.3 | async-start | bytes 2359296 | tf_op jit(solution)/shard_map/all_to_all | solution.py:84
  171.6 11.7 %collective-permute-done.7.down_ref = bf16[16,2,72,128]{3,2,1,0:T(8,128)(2,1)S(1)} collective-permute-done((bf16[16,2,72,128]{3,2,1,0:T(8,128)(2,1)}, bf16[16,2,72,128]{3,2,1,0:T(8,128)(2,1)S(1)}, u32[]{:S(2)}, u32[]{:S(2)}) %collective-permute-start.7) | collective-permute-done | bytes 589856 | tf_op jit(solution)/shard_map/ppermute | solution.py:76
  183.2 8.4 %home_rows.2.odd_ref = bf16[4,2048,256]{2,1,0:T(8,128)(2,1)} custom-call(s32[4]{0:T(128)S(1)} %get-tuple-element.41.own_ref, s32[4,4,512]{2,1,0:T(4,128)S(1)} %bitcast.30, bf16[16,2,72,128]{3,2,1,0:T(8,128)(2,1)S(1)} %collective-permute-done.6.up_ref, bf16[16,2,72,128]{3,2,1,0:T(8,128)(2,1)S(1)} %collective-permute-done.7.down_ref), custom_call_target="tpu_custom_call" | custom-call | tf_op jit(solution)/shard_map/home_rows/pallas_call | solution.py:477
  191.6 12.9 %home_rows.3 = bf16[4,528,128]{2,1,0:T(8,128)(2,1)S(1)} custom-call(s32[4]{0:T(128)S(1)} %get-tuple-element.41.own_ref, s32[4,4,512]{2,1,0:T(4,128)S(1)} %bitcast.29, bf16[4,2048,256]{2,1,0:T(8,128)(2,1)} %home_rows.2.odd_ref, bf16[16,2,2,72,128]{4,3,2,1,0:T(8,128)(2,1)S(1)} %all-to-all-done.3.even_ref), custom_call_target="tpu_custom_call" | custom-call | tf_op jit(solution)/shard_map/home_rows/pallas_call | solution.py:477
  204.5 24.5 %all_to_all.25.m_ref = bf16[4,528,128]{2,1,0:T(8,128)(2,1)S(1)} all-to-all(bf16[4,528,128]{2,1,0:T(8,128)(2,1)S(1)} %home_rows.3), channel_id=1, replica_groups=mesh['zl'=4,'x'=4,'y'=4,'zh'=2,'c'=2] {'zh','c'}, dimensions={0} | all-to-all | bytes 1081344 | tf_op jit(solution)/shard_map/all_to_all | solution.py:582
  229.1 2.5 %finish.1 = bf16[512,1024]{1,0:T(8,128)(2,1)} custom-call(bf16[4,528,128]{2,1,0:T(8,128)(2,1)S(1)} %all_to_all.25.m_ref, bf16[128,1024]{1,0:T(8,128)(2,1)S(1)} %copy-done), custom_call_target="tpu_custom_call" | custom-call | tf_op jit(solution)/shard_map/finish/pallas_call | solution.py:510
  (48 shorter events, 19.9 us)
Async XLA Ops:
  0.0 10.2 %collective-permute-start = (s32[2,2048]{1,0:T(2,128)}, s32[2,2048]{1,0:T(2,128)S(1)}, u32[]{:S(2)}, u32[]{:S(2)}) collective-permute-start(s32[2,2048]{1,0:T(2,128)} %param.11), channel_id=1, source_target_pairs={{0,2},{2,0},{1,3},{3,1},{4,6},{6,4},{5,7},{7,5},{8,10},{10,8},{9,1... | collective-permute-start | bytes 49160 | tf_op jit(solution)/shard_map/ppermute | solution.py:548
  6.0 4.1 %copy-start.1 = (s32[2,2048]{1,0:T(2,128)S(1)}, s32[2,2048]{1,0:T(2,128)}, u32[]{:S(2)}) copy-start(s32[2,2048]{1,0:T(2,128)} %param.11) | copy-start | bytes 49156
  16.3 38.5 %all-to-all-start = ((bf16[16,2,2,64,256]{4,3,2,1,0:T(8,128)(2,1)}), bf16[16,2,2,64,256]{4,3,2,1,0:T(8,128)(2,1)}, u32[]{:S(2)}, u32[]{:S(2)}) async-start(bf16[16,2,2,64,256]{4,3,2,1,0:T(8,128)(2,1)} %scatter_rows.2), calls=%async_computation | async-start | bytes 4194304 | tf_op jit(solution)/shard_map/all_to_all | solution.py:84
  29.4 23.4 %collective-permute-start.3 = (bf16[16,2,64,256]{3,2,1,0:T(8,128)(2,1)}, bf16[16,2,64,256]{3,2,1,0:T(8,128)(2,1)S(1)}, u32[]{:S(2)}, u32[]{:S(2)}) collective-permute-start(bf16[16,2,64,256]{3,2,1,0:T(8,128)(2,1)} %get-tuple-element.24), channel_id=1, source_target_pairs={{0,64},{64,128},{128,192},{192,2},{2,66},{66,130},{130,194},{194,0... | collective-permute-start | bytes 3145736 | tf_op jit(solution)/shard_map/ppermute | solution.py:76
  30.2 23.1 %collective-permute-start.4 = (bf16[16,2,64,256]{3,2,1,0:T(8,128)(2,1)}, bf16[16,2,64,256]{3,2,1,0:T(8,128)(2,1)S(1)}, u32[]{:S(2)}, u32[]{:S(2)}) collective-permute-start(bf16[16,2,64,256]{3,2,1,0:T(8,128)(2,1)} %get-tuple-element.25), channel_id=1, source_target_pairs={{0,194},{64,0},{128,64},{192,128},{2,192},{66,2},{130,66},{194,130... | collective-permute-start | bytes 3145736 | tf_op jit(solution)/shard_map/ppermute | solution.py:76
  54.8 45.3 %all-to-all-start.1 = ((bf16[16,2,2,64,256]{4,3,2,1,0:T(8,128)(2,1)}), bf16[16,2,2,64,256]{4,3,2,1,0:T(8,128)(2,1)}, u32[]{:S(2)}, u32[]{:S(2)}) async-start(bf16[16,2,2,64,256]{4,3,2,1,0:T(8,128)(2,1)} %pad_maximum_fusion), calls=%async_computation.1 | async-start | bytes 4194304 | tf_op jit(solution)/shard_map/all_to_all | solution.py:84
  61.5 4.9 %copy-start.2 = (s32[2,2048]{1,0:T(2,128)S(1)}, s32[2,2048]{1,0:T(2,128)}, u32[]{:S(2)}) copy-start(s32[2,2048]{1,0:T(2,128)} %param.12) | copy-start | bytes 49156
  62.8 26.3 %collective-permute-start.2 = (bf16[8,2,64,256]{3,2,1,0:T(8,128)(2,1)S(1)}, bf16[8,2,64,256]{3,2,1,0:T(8,128)(2,1)S(1)}, u32[]{:S(2)}, u32[]{:S(2)}) collective-permute-start(bf16[8,2,64,256]{3,2,1,0:T(8,128)(2,1)S(1)} %get-tuple-element.43), channel_id=1, source_target_pairs={{0,130},{64,194},{128,0},{192,64},{2,128},{66,192},{130,2},{194,66... | collective-permute-start | bytes 1572872 | tf_op jit(solution)/shard_map/ppermute | solution.py:76
  66.4 25.0 %collective-permute-start.1 = (bf16[8,2,64,256]{3,2,1,0:T(8,128)(2,1)S(1)}, bf16[8,2,64,256]{3,2,1,0:T(8,128)(2,1)S(1)}, u32[]{:S(2)}, u32[]{:S(2)}) collective-permute-start(bf16[8,2,64,256]{3,2,1,0:T(8,128)(2,1)S(1)} %get-tuple-element.44), channel_id=1, source_target_pairs={{0,128},{64,192},{128,2},{192,66},{2,130},{66,194},{130,0},{194,64... | collective-permute-start | bytes 1572872 | tf_op jit(solution)/shard_map/ppermute | solution.py:76
  100.1 5.0 %copy-start.3 = (s32[2,8]{1,0:T(2,128)S(1)}, s32[2,8]{1,0:T(2,128)}, u32[]{:S(2)}) copy-start(s32[2,8]{1,0:T(2,128)} %param.13) | copy-start | bytes 196
  103.6 15.4 %collective-permute-start.5 = (bf16[2,512,256]{2,1,0:T(8,128)(2,1)S(1)}, bf16[2,512,256]{2,1,0:T(8,128)(2,1)S(1)}, u32[]{:S(2)}, u32[]{:S(2)}) collective-permute-start(bf16[2,512,256]{2,1,0:T(8,128)(2,1)S(1)} %get-tuple-element.30.kvt_ref), channel_id=1, source_target_pairs={{0,4},{4,8},{8,12},{12,16},{16,20},{20,24},{24,28},{28,32},{32,36}... | collective-permute-start | bytes 1572872 | tf_op jit(solution)/shard_map/ppermute | solution.py:567
  127.3 33.8 %all-to-all-start.2 = ((bf16[16,2,2,72,128]{4,3,2,1,0:T(8,128)(2,1)}), bf16[16,2,2,72,128]{4,3,2,1,0:T(8,128)(2,1)}, u32[]{:S(2)}, u32[]{:S(2)}) async-start(bf16[16,2,2,72,128]{4,3,2,1,0:T(8,128)(2,1)} %back_rows.2), calls=%async_computation.2 | async-start | bytes 2359296 | tf_op jit(solution)/shard_map/all_to_all | solution.py:84
  139.8 10.6 %collective-permute-start.8 = (bf16[8,2,72,128]{3,2,1,0:T(8,128)(2,1)}, bf16[8,2,72,128]{3,2,1,0:T(8,128)(2,1)S(1)}, u32[]{:S(2)}, u32[]{:S(2)}) collective-permute-start(bf16[8,2,72,128]{3,2,1,0:T(8,128)(2,1)} %get-tuple-element.35), channel_id=1, source_target_pairs={{0,130},{64,194},{128,0},{192,64},{2,128},{66,192},{130,2},{194,66... | collective-permute-start | bytes 884744 | tf_op jit(solution)/shard_map/ppermute | solution.py:76
  142.0 16.9 %collective-permute-start.9 = (bf16[8,2,72,128]{3,2,1,0:T(8,128)(2,1)}, bf16[8,2,72,128]{3,2,1,0:T(8,128)(2,1)S(1)}, u32[]{:S(2)}, u32[]{:S(2)}) collective-permute-start(bf16[8,2,72,128]{3,2,1,0:T(8,128)(2,1)} %get-tuple-element.36), channel_id=1, source_target_pairs={{0,128},{64,192},{128,2},{192,66},{2,130},{66,194},{130,0},{194,64... | collective-permute-start | bytes 884744 | tf_op jit(solution)/shard_map/ppermute | solution.py:76
  161.1 30.5 %all-to-all-start.3 = ((bf16[16,2,2,72,128]{4,3,2,1,0:T(8,128)(2,1)}), bf16[16,2,2,72,128]{4,3,2,1,0:T(8,128)(2,1)S(1)}, u32[]{:S(2)}, u32[]{:S(2)}) async-start(bf16[16,2,2,72,128]{4,3,2,1,0:T(8,128)(2,1)} %pad_maximum_fusion.1), calls=%async_computation.3 | async-start | bytes 2359296 | tf_op jit(solution)/shard_map/all_to_all | solution.py:84
  170.0 13.3 %collective-permute-start.7 = (bf16[16,2,72,128]{3,2,1,0:T(8,128)(2,1)}, bf16[16,2,72,128]{3,2,1,0:T(8,128)(2,1)S(1)}, u32[]{:S(2)}, u32[]{:S(2)}) collective-permute-start(bf16[16,2,72,128]{3,2,1,0:T(8,128)(2,1)} %get-tuple-element.45), channel_id=1, source_target_pairs={{0,64},{64,128},{128,192},{192,2},{2,66},{66,130},{130,194},{194,0... | collective-permute-start | bytes 1769480 | tf_op jit(solution)/shard_map/ppermute | solution.py:76
  170.0 13.3 %collective-permute-start.6 = (bf16[16,2,72,128]{3,2,1,0:T(8,128)(2,1)S(1)}, bf16[16,2,72,128]{3,2,1,0:T(8,128)(2,1)S(1)}, u32[]{:S(2)}, u32[]{:S(2)}) collective-permute-start(bf16[16,2,72,128]{3,2,1,0:T(8,128)(2,1)S(1)} %get-tuple-element.46), channel_id=1, source_target_pairs={{0,194},{64,0},{128,64},{192,128},{2,192},{66,2},{130,66},{194,130... | collective-permute-start | bytes 1769480 | tf_op jit(solution)/shard_map/ppermute | solution.py:76
  191.6 37.4 %copy-start = (bf16[128,1024]{1,0:T(8,128)(2,1)S(1)}, bf16[128,1024]{1,0:T(8,128)(2,1)}, u32[]{:S(2)}) copy-start(bf16[128,1024]{1,0:T(8,128)(2,1)} %w_ref.1) | copy-start | bytes 786436

commit v8 on v6

--- a/solution.py
+++ b/solution.py
@@ -123,16 +123,53 @@
     )(idx, rows)
 
 
-def sort_kernel(idx_ref, *refs):
-    (*row_refs, q_ref, kv_ref) = refs
+def pick_rows(idx_ref, row_refs, base):
     col = column(idx_ref[0, 0])
-    got, base = 0.0, 0
+    got = 0.0
     for ref in row_refs:
         rows = ref[...].reshape(-1, 256)
         n = rows.shape[0]
-        place = lax.broadcasted_iota(jnp.int32, (q_ref.shape[1], n), 1) + base
+        place = lax.broadcasted_iota(jnp.int32, (col.shape[0], n), 1) + base
         got += jnp.dot(one_hot(col, place), rows, preferred_element_type=F32)
         base += n
+    return got
+
+
+def near_kernel(idx_ref, near_ref, out_ref):
+    out_ref[0] = pick_rows(idx_ref, (near_ref,), 0).astype(BF)
+
+
+def odd_kernel(idx_ref, early_ref, odd_ref, out_ref):
+    n = odd_ref.shape[0] * odd_ref.shape[1] * odd_ref.shape[3]
+    out_ref[0] = (early_ref[0].astype(F32) + pick_rows(idx_ref, (odd_ref,), n)).astype(BF)
+
+
+def early_rows(idx, rows, early=None):
+    rounds, count = idx.shape
+    step = count // 2
+    peers, _, _, width, lanes = rows.shape
+    wide = pl.BlockSpec((1, step, 256), lambda r, b: (r, b, 0))
+    groups = 1 if early is None else 2
+    specs = [pl.BlockSpec((1, 1, 1, step), lambda r, b: (r, b, 0, 0))]
+    args = [idx.reshape(rounds, 2, 1, step)]
+    if early is not None:
+        specs.append(wide)
+        args.append(in_hbm(early))
+    specs.append(pl.BlockSpec((peers, groups, 1, width, lanes), lambda r, b: (0, 0, r, 0, 0)))
+    return pl.pallas_call(
+        near_kernel if early is None else odd_kernel,
+        grid=(rounds, 2),
+        in_specs=specs,
+        out_specs=wide,
+        out_shape=pltpu.HBM((rounds, count, 256), BF),
+        compiler_params=params(2),
+        name="early_rows",
+    )(*args, in_hbm(rows))
+
+
+def sort_kernel(idx_ref, early_ref, low_ref, high_ref, q_ref, kv_ref):
+    n = 2 * low_ref.shape[0] * low_ref.shape[2]
+    got = early_ref[0].astype(F32) + pick_rows(idx_ref, (low_ref, high_ref), n)
     qk = got[:, :128]
     keys = qk * lax.rsqrt(jnp.sum(qk * qk, axis=-1, keepdims=True) + 1e-06)
     q_ref[0] = qk.astype(BF)
@@ -140,21 +177,19 @@
     kv_ref[0, :, 128:] = got[:, 128:].astype(BF)
 
 
-def sort_rows(idx, even, low, high, odd, step):
+def sort_rows(idx, early, low, high, first, step):
     rounds, count = idx.shape
     blocks = count // step
-    peers, _, _, width, lanes = even.shape
-    four = lambda r, b: (0, r, 0, 0)
-    five = lambda r, b: (0, 0, r, 0, 0)
+    peers, _, width, lanes = low.shape
+    half = pl.BlockSpec((peers, 1, width, lanes), lambda r, b: (0, r, 0, 0))
     return pl.pallas_call(
         sort_kernel,
         grid=(rounds, blocks),
         in_specs=[
             pl.BlockSpec((1, 1, 1, step), lambda r, b: (r, b, 0, 0)),
-            pl.BlockSpec((peers, 1, 1, width, lanes), five),
-            pl.BlockSpec((peers // 2, 1, width, lanes), four),
-            pl.BlockSpec((peers // 2, 1, width, lanes), four),
-            pl.BlockSpec((peers, 2, 1, width, lanes), five),
+            pl.BlockSpec((1, step, 256), lambda r, b: (r, first // step + b, 0)),
+            half,
+            half,
         ],
         out_specs=[
             pl.BlockSpec((1, step, 128), lambda r, b: (r, b, 0)),
@@ -166,7 +201,7 @@
         ],
         compiler_params=params(2),
         name="sort_rows",
-    )(idx.reshape(rounds, blocks, 1, step), even, low, high, odd)
+    )(idx.reshape(rounds, blocks, 1, step), in_hbm(early), low, high)
 
 
 def terms_to_lines(terms, groups):
@@ -507,13 +542,15 @@
     even, packed = together((even, packed))
     half = plane(even)
     up, down = scatter_rows(sent[:, 2:], packed, width, False)
-    half, up, down = together((half, ring(up, 1), ring(down, -1)))
-    rows = half, ring(half[:8, 1], 2), ring(half[8:, 1], -2), plane(join(up, down))
-    rows = together(rows)
-
-    q_tail, kv_tail = sort_rows(spots[:, tail:], *rows, 2 * BLOCK)
+    up, down = ring(up, 1), ring(down, -1)
+    low, high = ring(half[:8, 1], 2), ring(half[8:, 1], -2)
+    odd = plane(join(up, down))
+    early = early_rows(spots, odd, early_rows(spots, half))
+    early, low, high = together((early, low, high))
+
+    q_tail, kv_tail = sort_rows(spots[:, tail:], early, low, high, tail, 2 * BLOCK)
     halo = lax.ppermute(kv_tail, SEQ, next_device)
-    q_head, kv_head = sort_rows(spots[:, :tail], *rows, 3 * BLOCK)
+    q_head, kv_head = sort_rows(spots[:, :tail], early, low, high, 0, 3 * BLOCK)
     inner = attend_inner(dist, q_head, q_tail, kv_head, kv_tail)
     edge = attend_edge(dist, q_head, kv_head, halo)
 
@@ -521,9 +558,10 @@
     odd, edge = together((odd, edge))
     half = plane(odd)
     near, low, high = back_rows(groups[:, None], edge, inner, width, True)
-    half, low, high = together((half, ring(low, -2), ring(high, 2)))
+    low, high = ring(low, -2), ring(high, 2)
+    up, down = ring(half[:, 0], -1), ring(half[:, 1], 1)
     even = plane(join(near, jnp.concatenate([low, high])))
-    state = home_rows(own, sent, even, ring(half[:, 0], -1), ring(half[:, 1], 1), width)
+    state = home_rows(own, sent, even, up, down, width)
     merged = lax.all_to_all(state, ROUND, 0, 0, tiled=True)
     return finish(merged, w_out)
 

time: 220 us -> 219 us (level)
  waiting for transfers between devices: 65.2 us -> 52.5 us
  Pallas kernels: 73.7 us -> 78.6 us
  starting transfers between devices: 47.2 us -> 49.6 us
  local copies, waits for them, and re-layouts: 1.63 us -> 3.91 us
    ppermute x8, waiting for transfers between devices: 65.2 us -> 38.2 us  [ring(): return lax.ppermute(value, ('zl', 'zh'), route)]
    pallas_call x0 -> x2, Pallas kernels: none -> 15.6 us  [early_rows(): pl.pallas_call(near_kernel if early is None else odd_kernel, grid=(rounds...]
    all_to_all x4, waiting for transfers between devices: 0.01 us -> 14.3 us  [plane(): return lax.all_to_all(joint, PLANE, 0, 0, tiled=True)]
    pallas_call x2, Pallas kernels: 15.5 us -> 7.6 us  [sort_rows(): pl.pallas_call(sort_kernel, grid=(rounds, blocks), in_specs=[pl.BlockSpec...]
    squeeze x2, local copies, waits for them, and re-layouts: 1.2 us -> 3.46 us  [the longest x1 2.15 us: body(): up, down = (ring(half[:, 0], -1), ring(half[:, 1], 1))]
  transfers between devices with their start and end apart: 14 -> 14, of which waited for: 7 -> 7; matrix products, arithmetic and copies ran while one was open for 1% -> 4% of each run, Pallas kernels for 16% -> 20%
where the time goes in v8:
time: 219 us; the launch traced here: 216 us
  Pallas kernels  78.6 us (36%)
  waiting for transfers between devices  52.5 us (24%)
  starting transfers between devices  49.6 us (23%)
  blocking collectives  26.7 us (12%)
  other arithmetic  4.11 us (2%)
  local copies, waits for them, and re-layouts  3.91 us (2%)
    ppermute x8, waiting for transfers between devices, ring(): return lax.ppermute(value, ('zl', 'zh'), route)  38.2 us
    all_to_all x4, starting transfers between devices, plane(): return lax.all_to_all(joint, PLANE, 0, 0, tiled=True)  28.3 us
    all_to_all x1, blocking collectives, body(): merged = lax.all_to_all(state, ROUND, 0, 0, tiled=True)  26.7 us
    pallas_call x2, Pallas kernels, early_rows(): pl.pallas_call(near_kernel if early is None else odd_kernel, grid=(rounds...  15.6 us
    pallas_call x1, Pallas kernels, home_rows(): pl.pallas_call(functools.partial(home_kernel, width), grid_spec=pltpu.Pre...  15.5 us
    ppermute x8, starting transfers between devices, ring(): return lax.ppermute(value, ('zl', 'zh'), route)  15 us
    all_to_all x4, waiting for transfers between devices, plane(): return lax.all_to_all(joint, PLANE, 0, 0, tiled=True)  14.3 us
    pallas_call x2, Pallas kernels, scatter_rows(): pl.pallas_call(scatter_kernel, grid=(rounds, groups), in_specs=[pl.BlockS...  12.2 us
  transfers between devices with their start and end apart: 14, of which 7 were waited for; matrix products, arithmetic and copies ran while one was open for 4% of the time, Pallas kernels for 20%

profile of v8, /device:TPU:35, one launch (start us, length us, event | category | flops | bytes accessed | tf_op | source)
XLA Modules:
  0.0 215.7 jit_solution(8811675982115321251)
XLA Ops:
  0.0 6.0 %collective-permute-start = (s32[2,2048]{1,0:T(2,128)}, s32[2,2048]{1,0:T(2,128)S(1)}, u32[]{:S(2)}, u32[]{:S(2)}) collective-permute-start(s32[2,2048]{1,0:T(2,128)} %param.11), channel_id=1, source_target_pairs={{0,2},{2,0},{1,3},{3,1},{4,6},{6,4},{5,7},{7,5},{8,10},{10,8},{9,1... | collective-permute-start | bytes 49160 | tf_op jit(solution)/shard_map/ppermute | solution.py:533
  6.1 4.1 %project.1.rows_ref = bf16[2048,256]{1,0:T(8,128)(2,1)S(1)} custom-call(bf16[2048,1024]{1,0:T(8,128)(2,1)} %x_ref.1, bf16[1024,128]{1,0:T(8,128)(2,1)} %wqk_ref.1, bf16[1024,128]{1,0:T(8,128)(2,1)} %wv_ref.1), custom_call_target="tpu_custom_call" | custom-call | tf_op jit(solution)/shard_map/project/pallas_call | solution.py:55
  10.4 5.9 %scatter_rows.2 = bf16[16,2,2,64,256]{4,3,2,1,0:T(8,128)(2,1)} custom-call(s32[2,2,2048]{2,1,0:T(2,128)S(1)} %get-tuple-element.46.idx_ref, bf16[2048,256]{1,0:T(8,128)(2,1)S(1)} %project.1.rows_ref), custom_call_target="tpu_custom_call" | custom-call | tf_op jit(solution)/shard_map/scatter_rows/pallas_call | solution.py:115
  16.3 6.9 %all-to-all-start = ((bf16[16,2,2,64,256]{4,3,2,1,0:T(8,128)(2,1)}), bf16[16,2,2,64,256]{4,3,2,1,0:T(8,128)(2,1)}, u32[]{:S(2)}, u32[]{:S(2)}) async-start(bf16[16,2,2,64,256]{4,3,2,1,0:T(8,128)(2,1)} %scatter_rows.2), calls=%async_computation | async-start | bytes 4194304 | tf_op jit(solution)/shard_map/all_to_all | solution.py:84
  23.2 6.3 %scatter_rows.3 = (bf16[16,2,64,256]{3,2,1,0:T(8,128)(2,1)}, bf16[16,2,64,256]{3,2,1,0:T(8,128)(2,1)}) custom-call(s32[2,2,2048]{2,1,0:T(2,128)S(1)} %get-tuple-element.45.idx_ref, bf16[2048,256]{1,0:T(8,128)(2,1)S(1)} %project.1.rows_ref), custom_call_target="tpu_custom_call" | custom-call | tf_op jit(solution)/shard_map/scatter_rows/pallas_call | solution.py:115
  30.9 21.9 %collective-permute-done.1 = bf16[16,2,64,256]{3,2,1,0:T(8,128)(2,1)S(1)} collective-permute-done((bf16[16,2,64,256]{3,2,1,0:T(8,128)(2,1)}, bf16[16,2,64,256]{3,2,1,0:T(8,128)(2,1)S(1)}, u32[]{:S(2)}, u32[]{:S(2)}) %collective-permute-start.1) | collective-permute-done | bytes 1048608 | tf_op jit(solution)/shard_map/ppermute | solution.py:76
  54.9 6.7 %all-to-all-start.1 = ((bf16[16,2,2,64,256]{4,3,2,1,0:T(8,128)(2,1)}), bf16[16,2,2,64,256]{4,3,2,1,0:T(8,128)(2,1)}, u32[]{:S(2)}, u32[]{:S(2)}) async-start(bf16[16,2,2,64,256]{4,3,2,1,0:T(8,128)(2,1)} %pad_maximum_fusion), calls=%async_computation.1 | async-start | bytes 4194304 | tf_op jit(solution)/shard_map/all_to_all | solution.py:84
  62.8 3.7 %collective-permute-start.4 = (bf16[8,2,64,256]{3,2,1,0:T(8,128)(2,1)S(1)}, bf16[8,2,64,256]{3,2,1,0:T(8,128)(2,1)S(1)}, u32[]{:S(2)}, u32[]{:S(2)}) collective-permute-start(bf16[8,2,64,256]{3,2,1,0:T(8,128)(2,1)S(1)} %get-tuple-element.41), channel_id=1, source_target_pairs={{0,130},{64,194},{128,0},{192,64},{2,128},{66,192},{130,2},{194,66... | collective-permute-start | bytes 1572872 | tf_op jit(solution)/shard_map/ppermute | solution.py:76
  66.6 6.6 %early_rows.2.early_ref = bf16[2,2048,256]{2,1,0:T(8,128)(2,1)} custom-call(s32[2,2,1,1024]{3,2,1,0:T(1,128)S(1)} %reshape.39.idx_ref, bf16[16,2,2,64,256]{4,3,2,1,0:T(8,128)(2,1)} %all-to-all-done.near_ref), custom_call_target="tpu_custom_call" | custom-call | tf_op jit(solution)/shard_map/early_rows/pallas_call | solution.py:159
  73.3 12.1 %all-to-all-done.1.odd_ref = bf16[16,2,2,64,256]{4,3,2,1,0:T(8,128)(2,1)} async-done(((bf16[16,2,2,64,256]{4,3,2,1,0:T(8,128)(2,1)}), bf16[16,2,2,64,256]{4,3,2,1,0:T(8,128)(2,1)}, u32[]{:S(2)}, u32[]{:S(2)}) %all-to-all-start.1) | async-done | bytes 2097184 | tf_op jit(solution)/shard_map/all_to_all | solution.py:84
  85.4 9.0 %early_rows.3.early_ref = bf16[2,2048,256]{2,1,0:T(8,128)(2,1)} custom-call(s32[2,2,1,1024]{3,2,1,0:T(1,128)S(1)} %reshape.39.idx_ref, bf16[2,2048,256]{2,1,0:T(8,128)(2,1)} %early_rows.2.early_ref, bf16[16,2,2,64,256]{4,3,2,1,0:T(8,128)(2,1)} %all-to-all-done.1.odd_ref), custom_call_target="tpu_custom_call" | custom-call | tf_op jit(solution)/shard_map/early_rows/pallas_call | solution.py:159
  97.4 5.0 %sort_rows.2 = (bf16[2,1536,128]{2,1,0:T(8,128)(2,1)S(1)}, bf16[2,1536,256]{2,1,0:T(8,128)(2,1)S(1)}) custom-call(s32[2,2,1,768]{3,2,1,0:T(1,128)S(1)} %reshape.38.idx_ref, bf16[2,2048,256]{2,1,0:T(8,128)(2,1)} %early_rows.3.early_ref, bf16[8,2,64,256]{3,2,1,0:T(8,128)(2,1)S(1)} %collective-permute-done.3.low_ref, ...), custom_call_target="tpu_custom_call" | custom-call | tf_op jit(solution)/shard_map/sort_rows/pallas_call | solution.py:185
  102.4 6.6 %attend_inner.1.inner_ref = bf16[2,1536,256]{2,1,0:T(8,128)(2,1)S(1)} custom-call(s32[2,8]{1,0:T(2,128)S(1)} %and_select_fusion.dist_ref, bf16[2,1536,128]{2,1,0:T(8,128)(2,1)S(1)} %get-tuple-element.28.q_ref.qh_ref, bf16[2,512,128]{2,1,0:T(8,128)(2,1)S(1)} %get-tuple-element.31.qt_ref, bf16[2,1536,256]{2,1,0:T(8,128)(2,1)S(1)} %get-tuple-element.29.kv_ref.kvh_ref, ...), custom_call_target="tpu_custom_call" | custom-call | tf_op jit(solution)/shard_map/attend_inner/pallas_call | solution.py:295
  111.6 5.9 %back_rows.2 = bf16[16,2,2,72,128]{4,3,2,1,0:T(8,128)(2,1)} custom-call(s32[2,1,2048]{2,1,0:T(1,128)S(1)} %broadcast_in_dim.69.idx_ref, bf16[2,512,256]{2,1,0:T(8,128)(2,1)S(1)} %attend_edge.1.edge_ref, bf16[2,1536,256]{2,1,0:T(8,128)(2,1)S(1)} %attend_inner.1.inner_ref), custom_call_target="tpu_custom_call" | custom-call | tf_op jit(solution)/shard_map/back_rows/pallas_call | solution.py:381
  117.5 8.1 %all-to-all-start.3 = ((bf16[16,2,2,72,128]{4,3,2,1,0:T(8,128)(2,1)}), bf16[16,2,2,72,128]{4,3,2,1,0:T(8,128)(2,1)}, u32[]{:S(2)}, u32[]{:S(2)}) async-start(bf16[16,2,2,72,128]{4,3,2,1,0:T(8,128)(2,1)} %back_rows.2), calls=%async_computation.3 | async-start | bytes 2359296 | tf_op jit(solution)/shard_map/all_to_all | solution.py:84
  125.5 6.1 %back_rows.3 = (bf16[16,2,72,128]{3,2,1,0:T(8,128)(2,1)}, bf16[8,2,72,128]{3,2,1,0:T(8,128)(2,1)}, bf16[8,2,72,128]{3,2,1,0:T(8,128)(2,1)}) custom-call(s32[2,1,2048]{2,1,0:T(1,128)S(1)} %broadcast_in_dim.69.idx_ref, bf16[2,512,256]{2,1,0:T(8,128)(2,1)S(1)} %attend_edge.1.edge_ref, bf16[2,1536,256]{2,1,0:T(8,128)(2,1)S(1)} %attend_inner.1.inner_ref), custom_call_target="tpu_custom_call" | custom-call | tf_op jit(solution)/shard_map/back_rows/pallas_call | solution.py:381
  131.6 3.6 %collective-permute-start.6 = (bf16[8,2,72,128]{3,2,1,0:T(8,128)(2,1)}, bf16[8,2,72,128]{3,2,1,0:T(8,128)(2,1)S(1)}, u32[]{:S(2)}, u32[]{:S(2)}) collective-permute-start(bf16[8,2,72,128]{3,2,1,0:T(8,128)(2,1)} %get-tuple-element.34), channel_id=1, source_target_pairs={{0,130},{64,194},{128,0},{192,64},{2,128},{66,192},{130,2},{194,66... | collective-permute-start | bytes 884744 | tf_op jit(solution)/shard_map/ppermute | solution.py:76
  135.2 6.8 %collective-permute-done.6 = bf16[8,2,72,128]{3,2,1,0:T(8,128)(2,1)S(1)} collective-permute-done((bf16[8,2,72,128]{3,2,1,0:T(8,128)(2,1)}, bf16[8,2,72,128]{3,2,1,0:T(8,128)(2,1)S(1)}, u32[]{:S(2)}, u32[]{:S(2)}) %collective-permute-start.6) | collective-permute-done | bytes 294944 | tf_op jit(solution)/shard_map/ppermute | solution.py:76
  142.0 3.0 %collective-permute-done.7 = bf16[8,2,72,128]{3,2,1,0:T(8,128)(2,1)S(1)} collective-permute-done((bf16[8,2,72,128]{3,2,1,0:T(8,128)(2,1)}, bf16[8,2,72,128]{3,2,1,0:T(8,128)(2,1)S(1)}, u32[]{:S(2)}, u32[]{:S(2)}) %collective-permute-start.7) | collective-permute-done | bytes 294944 | tf_op jit(solution)/shard_map/ppermute | solution.py:76
  147.2 6.7 %all-to-all-start.2 = ((bf16[16,2,2,72,128]{4,3,2,1,0:T(8,128)(2,1)}), bf16[16,2,2,72,128]{4,3,2,1,0:T(8,128)(2,1)S(1)}, u32[]{:S(2)}, u32[]{:S(2)}) async-start(bf16[16,2,2,72,128]{4,3,2,1,0:T(8,128)(2,1)} %pad_maximum_fusion.1), calls=%async_computation.2 | async-start | bytes 2359296 | tf_op jit(solution)/shard_map/all_to_all | solution.py:84
  156.0 6.3 %collective-permute-start.8 = (bf16[16,2,72,128]{3,2,1,0:T(8,128)(2,1)S(1)}, bf16[16,2,72,128]{3,2,1,0:T(8,128)(2,1)S(1)}, u32[]{:S(2)}, u32[]{:S(2)}) collective-permute-start(bf16[16,2,72,128]{3,2,1,0:T(8,128)(2,1)S(1)} %get-tuple-element.44), channel_id=1, source_target_pairs={{0,194},{64,0},{128,64},{192,128},{2,192},{66,2},{130,66},{194,130... | collective-permute-start | bytes 1769480 | tf_op jit(solution)/shard_map/ppermute | solution.py:76
  164.9 6.0 %collective-permute-done.9.down_ref = bf16[16,2,72,128]{3,2,1,0:T(8,128)(2,1)S(1)} collective-permute-done((bf16[16,2,72,128]{3,2,1,0:T(8,128)(2,1)}, bf16[16,2,72,128]{3,2,1,0:T(8,128)(2,1)S(1)}, u32[]{:S(2)}, u32[]{:S(2)}) %collective-permute-start.9) | collective-permute-done | bytes 589856 | tf_op jit(solution)/shard_map/ppermute | solution.py:76
  171.0 15.5 %home_rows.1 = bf16[4,528,128]{2,1,0:T(8,128)(2,1)S(1)} custom-call(s32[4]{0:T(128)S(1)} %get-tuple-element.39.own_ref, s32[4,8,512]{2,1,0:T(8,128)S(1)} %select_bitcast_fusion.idx_ref, bf16[16,2,2,72,128]{4,3,2,1,0:T(8,128)(2,1)S(1)} %all-to-all-done.2.even_ref, bf16[16,2,72,128]{3,2,1,0:T(8,128)(2,1)S(1)} %collective-permute-done.8.up_ref, ...), custom_call_target="tpu_custom_call" | custom-call | tf_op jit(solution)/shard_map/home_rows/pallas_call | solution.py:461
  186.5 26.7 %all_to_all.25.m_ref = bf16[4,528,128]{2,1,0:T(8,128)(2,1)S(1)} all-to-all(bf16[4,528,128]{2,1,0:T(8,128)(2,1)S(1)} %home_rows.1), channel_id=1, replica_groups=mesh['zl'=4,'x'=4,'y'=4,'zh'=2,'c'=2] {'zh','c'}, dimensions={0} | all-to-all | bytes 1081344 | tf_op jit(solution)/shard_map/all_to_all | solution.py:565
  (53 shorter events, 20.0 us)
Async XLA Ops:
  0.0 10.2 %collective-permute-start = (s32[2,2048]{1,0:T(2,128)}, s32[2,2048]{1,0:T(2,128)S(1)}, u32[]{:S(2)}, u32[]{:S(2)}) collective-permute-start(s32[2,2048]{1,0:T(2,128)} %param.11), channel_id=1, source_target_pairs={{0,2},{2,0},{1,3},{3,1},{4,6},{6,4},{5,7},{7,5},{8,10},{10,8},{9,1... | collective-permute-start | bytes 49160 | tf_op jit(solution)/shard_map/ppermute | solution.py:533
  6.0 4.1 %copy-start.1 = (s32[2,2048]{1,0:T(2,128)S(1)}, s32[2,2048]{1,0:T(2,128)}, u32[]{:S(2)}) copy-start(s32[2,2048]{1,0:T(2,128)} %param.11) | copy-start | bytes 49156
  16.3 38.6 %all-to-all-start = ((bf16[16,2,2,64,256]{4,3,2,1,0:T(8,128)(2,1)}), bf16[16,2,2,64,256]{4,3,2,1,0:T(8,128)(2,1)}, u32[]{:S(2)}, u32[]{:S(2)}) async-start(bf16[16,2,2,64,256]{4,3,2,1,0:T(8,128)(2,1)} %scatter_rows.2), calls=%async_computation | async-start | bytes 4194304 | tf_op jit(solution)/shard_map/all_to_all | solution.py:84
  29.4 23.4 %collective-permute-start.1 = (bf16[16,2,64,256]{3,2,1,0:T(8,128)(2,1)}, bf16[16,2,64,256]{3,2,1,0:T(8,128)(2,1)S(1)}, u32[]{:S(2)}, u32[]{:S(2)}) collective-permute-start(bf16[16,2,64,256]{3,2,1,0:T(8,128)(2,1)} %get-tuple-element.23), channel_id=1, source_target_pairs={{0,64},{64,128},{128,192},{192,2},{2,66},{66,130},{130,194},{194,0... | collective-permute-start | bytes 3145736 | tf_op jit(solution)/shard_map/ppermute | solution.py:76
  30.2 23.1 %collective-permute-start.2 = (bf16[16,2,64,256]{3,2,1,0:T(8,128)(2,1)}, bf16[16,2,64,256]{3,2,1,0:T(8,128)(2,1)S(1)}, u32[]{:S(2)}, u32[]{:S(2)}) collective-permute-start(bf16[16,2,64,256]{3,2,1,0:T(8,128)(2,1)} %get-tuple-element.24), channel_id=1, source_target_pairs={{0,194},{64,0},{128,64},{192,128},{2,192},{66,2},{130,66},{194,130... | collective-permute-start | bytes 3145736 | tf_op jit(solution)/shard_map/ppermute | solution.py:76
  54.9 30.5 %all-to-all-start.1 = ((bf16[16,2,2,64,256]{4,3,2,1,0:T(8,128)(2,1)}), bf16[16,2,2,64,256]{4,3,2,1,0:T(8,128)(2,1)}, u32[]{:S(2)}, u32[]{:S(2)}) async-start(bf16[16,2,2,64,256]{4,3,2,1,0:T(8,128)(2,1)} %pad_maximum_fusion), calls=%async_computation.1 | async-start | bytes 4194304 | tf_op jit(solution)/shard_map/all_to_all | solution.py:84
  61.5 5.0 %copy-start.2 = (s32[2,2048]{1,0:T(2,128)S(1)}, s32[2,2048]{1,0:T(2,128)}, u32[]{:S(2)}) copy-start(s32[2,2048]{1,0:T(2,128)} %param.12) | copy-start | bytes 49156
  62.8 31.6 %collective-permute-start.4 = (bf16[8,2,64,256]{3,2,1,0:T(8,128)(2,1)S(1)}, bf16[8,2,64,256]{3,2,1,0:T(8,128)(2,1)S(1)}, u32[]{:S(2)}, u32[]{:S(2)}) collective-permute-start(bf16[8,2,64,256]{3,2,1,0:T(8,128)(2,1)S(1)} %get-tuple-element.41), channel_id=1, source_target_pairs={{0,130},{64,194},{128,0},{192,64},{2,128},{66,192},{130,2},{194,66... | collective-permute-start | bytes 1572872 | tf_op jit(solution)/shard_map/ppermute | solution.py:76
  66.5 27.9 %collective-permute-start.3 = (bf16[8,2,64,256]{3,2,1,0:T(8,128)(2,1)S(1)}, bf16[8,2,64,256]{3,2,1,0:T(8,128)(2,1)S(1)}, u32[]{:S(2)}, u32[]{:S(2)}) collective-permute-start(bf16[8,2,64,256]{3,2,1,0:T(8,128)(2,1)S(1)} %get-tuple-element.42), channel_id=1, source_target_pairs={{0,128},{64,192},{128,2},{192,66},{2,130},{66,194},{130,0},{194,64... | collective-permute-start | bytes 1572872 | tf_op jit(solution)/shard_map/ppermute | solution.py:76
  94.4 3.0 %copy-start.3 = (s32[2,8]{1,0:T(2,128)S(1)}, s32[2,8]{1,0:T(2,128)}, u32[]{:S(2)}) copy-start(s32[2,8]{1,0:T(2,128)} %param.13) | copy-start | bytes 196
  97.0 12.1 %collective-permute-start.5 = (bf16[2,512,256]{2,1,0:T(8,128)(2,1)S(1)}, bf16[2,512,256]{2,1,0:T(8,128)(2,1)S(1)}, u32[]{:S(2)}, u32[]{:S(2)}) collective-permute-start(bf16[2,512,256]{2,1,0:T(8,128)(2,1)S(1)} %get-tuple-element.30.kvt_ref), channel_id=1, source_target_pairs={{0,4},{4,8},{8,12},{12,16},{16,20},{20,24},{24,28},{28,32},{32,36}... | collective-permute-start | bytes 1572872 | tf_op jit(solution)/shard_map/ppermute | solution.py:552
  117.5 29.8 %all-to-all-start.3 = ((bf16[16,2,2,72,128]{4,3,2,1,0:T(8,128)(2,1)}), bf16[16,2,2,72,128]{4,3,2,1,0:T(8,128)(2,1)}, u32[]{:S(2)}, u32[]{:S(2)}) async-start(bf16[16,2,2,72,128]{4,3,2,1,0:T(8,128)(2,1)} %back_rows.2), calls=%async_computation.3 | async-start | bytes 2359296 | tf_op jit(solution)/shard_map/all_to_all | solution.py:84
  131.6 10.4 %collective-permute-start.6 = (bf16[8,2,72,128]{3,2,1,0:T(8,128)(2,1)}, bf16[8,2,72,128]{3,2,1,0:T(8,128)(2,1)S(1)}, u32[]{:S(2)}, u32[]{:S(2)}) collective-permute-start(bf16[8,2,72,128]{3,2,1,0:T(8,128)(2,1)} %get-tuple-element.34), channel_id=1, source_target_pairs={{0,130},{64,194},{128,0},{192,64},{2,128},{66,192},{130,2},{194,66... | collective-permute-start | bytes 884744 | tf_op jit(solution)/shard_map/ppermute | solution.py:76
  135.2 9.8 %collective-permute-start.7 = (bf16[8,2,72,128]{3,2,1,0:T(8,128)(2,1)}, bf16[8,2,72,128]{3,2,1,0:T(8,128)(2,1)S(1)}, u32[]{:S(2)}, u32[]{:S(2)}) collective-permute-start(bf16[8,2,72,128]{3,2,1,0:T(8,128)(2,1)} %get-tuple-element.35), channel_id=1, source_target_pairs={{0,128},{64,192},{128,2},{192,66},{2,130},{66,194},{130,0},{194,64... | collective-permute-start | bytes 884744 | tf_op jit(solution)/shard_map/ppermute | solution.py:76
  147.2 17.7 %all-to-all-start.2 = ((bf16[16,2,2,72,128]{4,3,2,1,0:T(8,128)(2,1)}), bf16[16,2,2,72,128]{4,3,2,1,0:T(8,128)(2,1)S(1)}, u32[]{:S(2)}, u32[]{:S(2)}) async-start(bf16[16,2,2,72,128]{4,3,2,1,0:T(8,128)(2,1)} %pad_maximum_fusion.1), calls=%async_computation.2 | async-start | bytes 2359296 | tf_op jit(solution)/shard_map/all_to_all | solution.py:84
  156.0 14.9 %collective-permute-start.9 = (bf16[16,2,72,128]{3,2,1,0:T(8,128)(2,1)}, bf16[16,2,72,128]{3,2,1,0:T(8,128)(2,1)S(1)}, u32[]{:S(2)}, u32[]{:S(2)}) collective-permute-start(bf16[16,2,72,128]{3,2,1,0:T(8,128)(2,1)} %get-tuple-element.43), channel_id=1, source_target_pairs={{0,64},{64,128},{128,192},{192,2},{2,66},{66,130},{130,194},{194,0... | collective-permute-start | bytes 1769480 | tf_op jit(solution)/shard_map/ppermute | solution.py:76
  156.0 14.9 %collective-permute-start.8 = (bf16[16,2,72,128]{3,2,1,0:T(8,128)(2,1)S(1)}, bf16[16,2,72,128]{3,2,1,0:T(8,128)(2,1)S(1)}, u32[]{:S(2)}, u32[]{:S(2)}) collective-permute-start(bf16[16,2,72,128]{3,2,1,0:T(8,128)(2,1)S(1)} %get-tuple-element.44), channel_id=1, source_target_pairs={{0,194},{64,0},{128,64},{192,128},{2,192},{66,2},{130,66},{194,130... | collective-permute-start | bytes 1769480 | tf_op jit(solution)/shard_map/ppermute | solution.py:76
  162.6 50.6 %copy-start = (bf16[128,1024]{1,0:T(8,128)(2,1)S(1)}, bf16[128,1024]{1,0:T(8,128)(2,1)}, u32[]{:S(2)}) copy-start(bf16[128,1024]{1,0:T(8,128)(2,1)} %w_ref.1) | copy-start | bytes 786436

commit v9 on v8

--- a/solution.py
+++ b/solution.py
@@ -40,13 +40,16 @@
     return pltpu.with_memory_space_constraint(v, pltpu.HBM)
 
 
-def project_kernel(x_ref, wqk_ref, wv_ref, out_ref, w_ref):
+def project_kernel(left_ref, right_ref, wqk_ref, wv_ref, out_ref, w_ref):
     @pl.when(pl.program_id(0) == 0)
     def _():
         w_ref[:, :128] = wqk_ref[...]
         w_ref[:, 128:] = wv_ref[...]
 
-    out_ref[...] = jnp.dot(x_ref[...], w_ref[...], preferred_element_type=F32).astype(BF)
+    half = left_ref.shape[1]
+    got = jnp.dot(left_ref[...], w_ref[:half], preferred_element_type=F32)
+    got += jnp.dot(right_ref[...], w_ref[half:], preferred_element_type=F32)
+    out_ref[...] = got.astype(BF)
 
 
 def project(x, w_qk, w_v):
@@ -56,7 +59,8 @@
         project_kernel,
         grid=(rows // step,),
         in_specs=[
-            pl.BlockSpec((step, model), lambda i: (i, 0)),
+            pl.BlockSpec((step, model // 2), lambda i: (i, 0)),
+            pl.BlockSpec((step, model // 2), lambda i: (i, 1)),
             whole(w_qk.shape),
             whole(w_v.shape),
         ],
@@ -65,7 +69,7 @@
         scratch_shapes=[pltpu.VMEM((model, 256), BF)],
         compiler_params=params(),
         name="project",
-    )(in_hbm(x), in_hbm(w_qk), in_hbm(w_v))
+    )(in_hbm(x), in_hbm(x), in_hbm(w_qk), in_hbm(w_v))
 
 
 def ring(value, shift):
@@ -447,28 +451,33 @@
     summed = sum(s * p[:, :128] for s, p in zip(scales, states))
     safe = jnp.where(some, total, 1.0)
     log = jnp.where(some, top + jnp.log(safe), ABSENT)
-    out_ref[0, :step, :] = (summed / safe).astype(BF)
+    mean = (summed / safe).astype(BF)
     terms = term_lanes(log, step).astype(F32)
-    out_ref[0, step:, :] = terms_to_lines(terms, step // 32).reshape(step // 32, 128).astype(BF)
+    lines = terms_to_lines(terms, step // 32).reshape(step // 32, 128).astype(BF)
+    part = step // out_ref.shape[0]
+    for q in range(out_ref.shape[0]):
+        out_ref[q, :part, :] = mean[q * part : (q + 1) * part]
+        out_ref[q, part:, :] = lines[q * part // 32 : (q + 1) * part // 32]
 
 
 def home_rows(own, idx, even, up, down, width):
     rounds, groups, count = idx.shape
-    quarters = 4
-    step = count // quarters
+    quarters, steps = 4, 2
+    step = count // steps
+    part = count // quarters
     columns = rounds * groups
-    idx = idx.reshape(columns, quarters, step).transpose(1, 0, 2)
+    idx = idx.reshape(columns, steps, step).transpose(1, 0, 2)
     return pl.pallas_call(
         functools.partial(home_kernel, width),
         grid_spec=pltpu.PrefetchScalarGridSpec(
             num_scalar_prefetch=1,
-            grid=(quarters,),
+            grid=(steps,),
             in_specs=[pl.BlockSpec((1, columns, step), lambda i, o: (i, 0, 0))]
             + [whole(v.shape) for v in (even, up, down)],
-            out_specs=pl.BlockSpec((1, step + step // 32, 128), lambda i, o: (i, 0, 0)),
+            out_specs=pl.BlockSpec((quarters // steps, part + part // 32, 128), lambda i, o: (i, 0, 0)),
             scratch_shapes=[pltpu.VMEM((rounds, 64 * width, 256), BF)],
         ),
-        out_shape=jax.ShapeDtypeStruct((quarters, step + step // 32, 128), BF),
+        out_shape=jax.ShapeDtypeStruct((quarters, part + part // 32, 128), BF),
         compiler_params=params(),
         name="home_rows",
     )(own, idx, even, up, down)
@@ -543,7 +552,8 @@
     half = plane(even)
     up, down = scatter_rows(sent[:, 2:], packed, width, False)
     up, down = ring(up, 1), ring(down, -1)
-    low, high = ring(half[:8, 1], 2), ring(half[8:, 1], -2)
+    low, high, up, down = together((half[:8, 1], half[8:, 1], up, down))
+    low, high = ring(low, 2), ring(high, -2)
     odd = plane(join(up, down))
     early = early_rows(spots, odd, early_rows(spots, half))
     early, low, high = together((early, low, high))
@@ -559,7 +569,8 @@
     half = plane(odd)
     near, low, high = back_rows(groups[:, None], edge, inner, width, True)
     low, high = ring(low, -2), ring(high, 2)
-    up, down = ring(half[:, 0], -1), ring(half[:, 1], 1)
+    up, down, low, high = together((half[:, 0], half[:, 1], low, high))
+    up, down = ring(up, -1), ring(down, 1)
     even = plane(join(near, jnp.concatenate([low, high])))
     state = home_rows(own, sent, even, up, down, width)
     merged = lax.all_to_all(state, ROUND, 0, 0, tiled=True)

time: 219 us -> 215 us (0.982)
    all_to_all x4, waiting for transfers between devices: 14.3 us -> 32.1 us  [plane(): return lax.all_to_all(joint, PLANE, 0, 0, tiled=True)]
    ppermute x8, waiting for transfers between devices: 38.2 us -> 20.6 us  [ring(): return lax.ppermute(value, ('zl', 'zh'), route)]
  transfers between devices with their start and end apart: 14 -> 14, of which waited for: 7 -> 9; matrix products, arithmetic and copies ran while one was open for 4% -> 2% of each run, Pallas kernels for 20% -> 20%
where the time goes in v9:
time: 215 us; the launch traced here: 214 us
  Pallas kernels  77.9 us (36%)
  waiting for transfers between devices  52.7 us (25%)
  starting transfers between devices  49.7 us (23%)
  blocking collectives  26.3 us (12%)
  local copies, waits for them, and re-layouts  3.91 us (2%)
  other arithmetic  3.05 us (1%)
    all_to_all x4, waiting for transfers between devices, plane(): return lax.all_to_all(joint, PLANE, 0, 0, tiled=True)  32.1 us
    all_to_all x4, starting transfers between devices, plane(): return lax.all_to_all(joint, PLANE, 0, 0, tiled=True)  28.4 us
    all_to_all x1, blocking collectives, body(): merged = lax.all_to_all(state, ROUND, 0, 0, tiled=True)  26.3 us
    ppermute x8, waiting for transfers between devices, ring(): return lax.ppermute(value, ('zl', 'zh'), route)  20.6 us
    pallas_call x2, Pallas kernels, early_rows(): pl.pallas_call(near_kernel if early is None else odd_kernel, grid=(rounds...  15.6 us
    ppermute x8, starting transfers between devices, ring(): return lax.ppermute(value, ('zl', 'zh'), route)  14.9 us
    pallas_call x1, Pallas kernels, home_rows(): pl.pallas_call(functools.partial(home_kernel, width), grid_spec=pltpu.Pre...  14.7 us
    pallas_call x2, Pallas kernels, scatter_rows(): pl.pallas_call(scatter_kernel, grid=(rounds, groups), in_specs=[pl.BlockS...  12.2 us
  transfers between devices with their start and end apart: 14, of which 9 were waited for; matrix products, arithmetic and copies ran while one was open for 2% of the time, Pallas kernels for 20%

profile of v9, /device:TPU:35, one launch (start us, length us, event | category | flops | bytes accessed | tf_op | source)
XLA Modules:
  0.0 213.8 jit_solution(10794238010057237433)
XLA Ops:
  0.0 6.0 %collective-permute-start = (s32[2,2048]{1,0:T(2,128)}, s32[2,2048]{1,0:T(2,128)S(1)}, u32[]{:S(2)}, u32[]{:S(2)}) collective-permute-start(s32[2,2048]{1,0:T(2,128)} %param.11), channel_id=1, source_target_pairs={{0,2},{2,0},{1,3},{3,1},{4,6},{6,4},{5,7},{7,5},{8,10},{10,8},{9,1... | collective-permute-start | bytes 49160 | tf_op jit(solution)/shard_map/ppermute | solution.py:542
  6.1 4.1 %project.1.rows_ref = bf16[2048,256]{1,0:T(8,128)(2,1)S(1)} custom-call(bf16[2048,1024]{1,0:T(8,128)(2,1)} %right_ref.1, bf16[2048,1024]{1,0:T(8,128)(2,1)} %right_ref.1, bf16[1024,128]{1,0:T(8,128)(2,1)} %wqk_ref.1, bf16[1024,128]{1,0:T(8,128)(2,1)} %wv_ref.1), custom_call_target="tpu_custom_call" | custom-call | tf_op jit(solution)/shard_map/project/pallas_call | solution.py:58
  10.3 5.9 %scatter_rows.2 = bf16[16,2,2,64,256]{4,3,2,1,0:T(8,128)(2,1)} custom-call(s32[2,2,2048]{2,1,0:T(2,128)S(1)} %get-tuple-element.62.idx_ref, bf16[2048,256]{1,0:T(8,128)(2,1)S(1)} %project.1.rows_ref), custom_call_target="tpu_custom_call" | custom-call | tf_op jit(solution)/shard_map/scatter_rows/pallas_call | solution.py:119
  16.2 6.9 %all-to-all-start = ((bf16[16,2,2,64,256]{4,3,2,1,0:T(8,128)(2,1)}), bf16[16,2,2,64,256]{4,3,2,1,0:T(8,128)(2,1)}, u32[]{:S(2)}, u32[]{:S(2)}) async-start(bf16[16,2,2,64,256]{4,3,2,1,0:T(8,128)(2,1)} %scatter_rows.2), calls=%async_computation | async-start | bytes 4194304 | tf_op jit(solution)/shard_map/all_to_all | solution.py:88
  23.2 6.3 %scatter_rows.3 = (bf16[16,2,64,256]{3,2,1,0:T(8,128)(2,1)}, bf16[16,2,64,256]{3,2,1,0:T(8,128)(2,1)}) custom-call(s32[2,2,2048]{2,1,0:T(2,128)S(1)} %get-tuple-element.61.idx_ref, bf16[2048,256]{1,0:T(8,128)(2,1)S(1)} %project.1.rows_ref), custom_call_target="tpu_custom_call" | custom-call | tf_op jit(solution)/shard_map/scatter_rows/pallas_call | solution.py:119
  30.9 17.2 %all-to-all-done.near_ref = bf16[16,2,2,64,256]{4,3,2,1,0:T(8,128)(2,1)} async-done(((bf16[16,2,2,64,256]{4,3,2,1,0:T(8,128)(2,1)}), bf16[16,2,2,64,256]{4,3,2,1,0:T(8,128)(2,1)}, u32[]{:S(2)}, u32[]{:S(2)}) %all-to-all-start) | async-done | bytes 2097184 | tf_op jit(solution)/shard_map/all_to_all | solution.py:88
  49.4 3.4 %collective-permute-done.1 = bf16[16,2,64,256]{3,2,1,0:T(8,128)(2,1)S(1)} collective-permute-done((bf16[16,2,64,256]{3,2,1,0:T(8,128)(2,1)}, bf16[16,2,64,256]{3,2,1,0:T(8,128)(2,1)S(1)}, u32[]{:S(2)}, u32[]{:S(2)}) %collective-permute-start.1) | collective-permute-done | bytes 1048608 | tf_op jit(solution)/shard_map/ppermute | solution.py:80
  54.8 6.8 %all-to-all-start.1 = ((bf16[16,2,2,64,256]{4,3,2,1,0:T(8,128)(2,1)}), bf16[16,2,2,64,256]{4,3,2,1,0:T(8,128)(2,1)}, u32[]{:S(2)}, u32[]{:S(2)}) async-start(bf16[16,2,2,64,256]{4,3,2,1,0:T(8,128)(2,1)} %pad_maximum_fusion), calls=%async_computation.1 | async-start | bytes 4194304 | tf_op jit(solution)/shard_map/all_to_all | solution.py:88
  65.4 6.6 %early_rows.2.early_ref = bf16[2,2048,256]{2,1,0:T(8,128)(2,1)} custom-call(s32[2,2,1,1024]{3,2,1,0:T(1,128)S(1)} %reshape.39.idx_ref, bf16[16,2,2,64,256]{4,3,2,1,0:T(8,128)(2,1)} %all-to-all-done.near_ref), custom_call_target="tpu_custom_call" | custom-call | tf_op jit(solution)/shard_map/early_rows/pallas_call | solution.py:163
  72.1 13.4 %all-to-all-done.1.odd_ref = bf16[16,2,2,64,256]{4,3,2,1,0:T(8,128)(2,1)} async-done(((bf16[16,2,2,64,256]{4,3,2,1,0:T(8,128)(2,1)}), bf16[16,2,2,64,256]{4,3,2,1,0:T(8,128)(2,1)}, u32[]{:S(2)}, u32[]{:S(2)}) %all-to-all-start.1) | async-done | bytes 2097184 | tf_op jit(solution)/shard_map/all_to_all | solution.py:88
  85.5 9.0 %early_rows.3.early_ref = bf16[2,2048,256]{2,1,0:T(8,128)(2,1)} custom-call(s32[2,2,1,1024]{3,2,1,0:T(1,128)S(1)} %reshape.39.idx_ref, bf16[2,2048,256]{2,1,0:T(8,128)(2,1)} %early_rows.2.early_ref, bf16[16,2,2,64,256]{4,3,2,1,0:T(8,128)(2,1)} %all-to-all-done.1.odd_ref), custom_call_target="tpu_custom_call" | custom-call | tf_op jit(solution)/shard_map/early_rows/pallas_call | solution.py:163
  97.5 5.0 %sort_rows.2 = (bf16[2,1536,128]{2,1,0:T(8,128)(2,1)S(1)}, bf16[2,1536,256]{2,1,0:T(8,128)(2,1)S(1)}) custom-call(s32[2,2,1,768]{3,2,1,0:T(1,128)S(1)} %reshape.38.idx_ref, bf16[2,2048,256]{2,1,0:T(8,128)(2,1)} %early_rows.3.early_ref, bf16[8,2,64,256]{3,2,1,0:T(8,128)(2,1)S(1)} %collective-permute-done.3.low_ref, ...), custom_call_target="tpu_custom_call" | custom-call | tf_op jit(solution)/shard_map/sort_rows/pallas_call | solution.py:189
  102.5 6.6 %attend_inner.1.inner_ref = bf16[2,1536,256]{2,1,0:T(8,128)(2,1)S(1)} custom-call(s32[2,8]{1,0:T(2,128)S(1)} %and_select_fusion.dist_ref, bf16[2,1536,128]{2,1,0:T(8,128)(2,1)S(1)} %get-tuple-element.40.q_ref.qh_ref, bf16[2,512,128]{2,1,0:T(8,128)(2,1)S(1)} %get-tuple-element.43.qt_ref, bf16[2,1536,256]{2,1,0:T(8,128)(2,1)S(1)} %get-tuple-element.41.kv_ref.kvh_ref, ...), custom_call_target="tpu_custom_call" | custom-call | tf_op jit(solution)/shard_map/attend_inner/pallas_call | solution.py:299
  111.7 5.8 %back_rows.2 = bf16[16,2,2,72,128]{4,3,2,1,0:T(8,128)(2,1)} custom-call(s32[2,1,2048]{2,1,0:T(1,128)S(1)} %broadcast_in_dim.69.idx_ref, bf16[2,512,256]{2,1,0:T(8,128)(2,1)S(1)} %attend_edge.1.edge_ref, bf16[2,1536,256]{2,1,0:T(8,128)(2,1)S(1)} %attend_inner.1.inner_ref), custom_call_target="tpu_custom_call" | custom-call | tf_op jit(solution)/shard_map/back_rows/pallas_call | solution.py:385
  117.5 8.0 %all-to-all-start.2 = ((bf16[16,2,2,72,128]{4,3,2,1,0:T(8,128)(2,1)}), bf16[16,2,2,72,128]{4,3,2,1,0:T(8,128)(2,1)}, u32[]{:S(2)}, u32[]{:S(2)}) async-start(bf16[16,2,2,72,128]{4,3,2,1,0:T(8,128)(2,1)} %back_rows.2), calls=%async_computation.2 | async-start | bytes 2359296 | tf_op jit(solution)/shard_map/all_to_all | solution.py:88
  125.6 6.1 %back_rows.3 = (bf16[16,2,72,128]{3,2,1,0:T(8,128)(2,1)}, bf16[8,2,72,128]{3,2,1,0:T(8,128)(2,1)}, bf16[8,2,72,128]{3,2,1,0:T(8,128)(2,1)}) custom-call(s32[2,1,2048]{2,1,0:T(1,128)S(1)} %broadcast_in_dim.69.idx_ref, bf16[2,512,256]{2,1,0:T(8,128)(2,1)S(1)} %attend_edge.1.edge_ref, bf16[2,1536,256]{2,1,0:T(8,128)(2,1)S(1)} %attend_inner.1.inner_ref), custom_call_target="tpu_custom_call" | custom-call | tf_op jit(solution)/shard_map/back_rows/pallas_call | solution.py:385
  131.7 3.6 %collective-permute-start.6 = (bf16[8,2,72,128]{3,2,1,0:T(8,128)(2,1)}, bf16[8,2,72,128]{3,2,1,0:T(8,128)(2,1)S(1)}, u32[]{:S(2)}, u32[]{:S(2)}) collective-permute-start(bf16[8,2,72,128]{3,2,1,0:T(8,128)(2,1)} %get-tuple-element.47), channel_id=1, source_target_pairs={{0,130},{64,194},{128,0},{192,64},{2,128},{66,192},{130,2},{194,66... | collective-permute-start | bytes 884744 | tf_op jit(solution)/shard_map/ppermute | solution.py:80
  138.9 3.1 %collective-permute-done.6 = bf16[8,2,72,128]{3,2,1,0:T(8,128)(2,1)S(1)} collective-permute-done((bf16[8,2,72,128]{3,2,1,0:T(8,128)(2,1)}, bf16[8,2,72,128]{3,2,1,0:T(8,128)(2,1)S(1)}, u32[]{:S(2)}, u32[]{:S(2)}) %collective-permute-start.6) | collective-permute-done | bytes 294944 | tf_op jit(solution)/shard_map/ppermute | solution.py:80
  142.1 3.0 %collective-permute-done.7 = bf16[8,2,72,128]{3,2,1,0:T(8,128)(2,1)S(1)} collective-permute-done((bf16[8,2,72,128]{3,2,1,0:T(8,128)(2,1)}, bf16[8,2,72,128]{3,2,1,0:T(8,128)(2,1)S(1)}, u32[]{:S(2)}, u32[]{:S(2)}) %collective-permute-start.7) | collective-permute-done | bytes 294944 | tf_op jit(solution)/shard_map/ppermute | solution.py:80
  146.3 6.7 %all-to-all-start.3 = ((bf16[16,2,2,72,128]{4,3,2,1,0:T(8,128)(2,1)}), bf16[16,2,2,72,128]{4,3,2,1,0:T(8,128)(2,1)S(1)}, u32[]{:S(2)}, u32[]{:S(2)}) async-start(bf16[16,2,2,72,128]{4,3,2,1,0:T(8,128)(2,1)} %pad_maximum_fusion.1), calls=%async_computation.3 | async-start | bytes 2359296 | tf_op jit(solution)/shard_map/all_to_all | solution.py:88
  153.0 6.2 %collective-permute-start.8 = (bf16[16,2,72,128]{3,2,1,0:T(8,128)(2,1)}, bf16[16,2,72,128]{3,2,1,0:T(8,128)(2,1)S(1)}, u32[]{:S(2)}, u32[]{:S(2)}) collective-permute-start(bf16[16,2,72,128]{3,2,1,0:T(8,128)(2,1)} %get-tuple-element.51), channel_id=1, source_target_pairs={{0,194},{64,0},{128,64},{192,128},{2,192},{66,2},{130,66},{194,130... | collective-permute-start | bytes 1769480 | tf_op jit(solution)/shard_map/ppermute | solution.py:80
  159.6 9.2 %collective-permute-done.8.up_ref = bf16[16,2,72,128]{3,2,1,0:T(8,128)(2,1)S(1)} collective-permute-done((bf16[16,2,72,128]{3,2,1,0:T(8,128)(2,1)}, bf16[16,2,72,128]{3,2,1,0:T(8,128)(2,1)S(1)}, u32[]{:S(2)}, u32[]{:S(2)}) %collective-permute-start.8) | collective-permute-done | bytes 589856 | tf_op jit(solution)/shard_map/ppermute | solution.py:80
  170.2 14.7 %home_rows.1 = bf16[4,528,128]{2,1,0:T(8,128)(2,1)S(1)} custom-call(s32[4]{0:T(128)S(1)} %get-tuple-element.55.own_ref, s32[2,8,1024]{2,1,0:T(8,128)S(1)} %select_bitcast_fusion.idx_ref, bf16[16,2,2,72,128]{4,3,2,1,0:T(8,128)(2,1)S(1)} %all-to-all-done.3.even_ref, bf16[16,2,72,128]{3,2,1,0:T(8,128)(2,1)S(1)} %collective-permute-done.8.up_ref, ...), custom_call_target="tpu_custom_call" | custom-call | tf_op jit(solution)/shard_map/home_rows/pallas_call | solution.py:470
  184.9 26.3 %all_to_all.25.m_ref = bf16[4,528,128]{2,1,0:T(8,128)(2,1)S(1)} all-to-all(bf16[4,528,128]{2,1,0:T(8,128)(2,1)S(1)} %home_rows.1), channel_id=1, replica_groups=mesh['zl'=4,'x'=4,'y'=4,'zh'=2,'c'=2] {'zh','c'}, dimensions={0} | all-to-all | bytes 1081344 | tf_op jit(solution)/shard_map/all_to_all | solution.py:576
  (55 shorter events, 23.4 us)
Async XLA Ops:
  0.0 10.2 %collective-permute-start = (s32[2,2048]{1,0:T(2,128)}, s32[2,2048]{1,0:T(2,128)S(1)}, u32[]{:S(2)}, u32[]{:S(2)}) collective-permute-start(s32[2,2048]{1,0:T(2,128)} %param.11), channel_id=1, source_target_pairs={{0,2},{2,0},{1,3},{3,1},{4,6},{6,4},{5,7},{7,5},{8,10},{10,8},{9,1... | collective-permute-start | bytes 49160 | tf_op jit(solution)/shard_map/ppermute | solution.py:542
  6.0 4.1 %copy-start.2 = (s32[2,2048]{1,0:T(2,128)S(1)}, s32[2,2048]{1,0:T(2,128)}, u32[]{:S(2)}) copy-start(s32[2,2048]{1,0:T(2,128)} %param.11) | copy-start | bytes 49156
  16.2 31.9 %all-to-all-start = ((bf16[16,2,2,64,256]{4,3,2,1,0:T(8,128)(2,1)}), bf16[16,2,2,64,256]{4,3,2,1,0:T(8,128)(2,1)}, u32[]{:S(2)}, u32[]{:S(2)}) async-start(bf16[16,2,2,64,256]{4,3,2,1,0:T(8,128)(2,1)} %scatter_rows.2), calls=%async_computation | async-start | bytes 4194304 | tf_op jit(solution)/shard_map/all_to_all | solution.py:88
  29.4 23.3 %collective-permute-start.1 = (bf16[16,2,64,256]{3,2,1,0:T(8,128)(2,1)}, bf16[16,2,64,256]{3,2,1,0:T(8,128)(2,1)S(1)}, u32[]{:S(2)}, u32[]{:S(2)}) collective-permute-start(bf16[16,2,64,256]{3,2,1,0:T(8,128)(2,1)} %get-tuple-element.31), channel_id=1, source_target_pairs={{0,64},{64,128},{128,192},{192,2},{2,66},{66,130},{130,194},{194,0... | collective-permute-start | bytes 3145736 | tf_op jit(solution)/shard_map/ppermute | solution.py:80
  30.2 23.1 %collective-permute-start.2 = (bf16[16,2,64,256]{3,2,1,0:T(8,128)(2,1)}, bf16[16,2,64,256]{3,2,1,0:T(8,128)(2,1)S(1)}, u32[]{:S(2)}, u32[]{:S(2)}) collective-permute-start(bf16[16,2,64,256]{3,2,1,0:T(8,128)(2,1)} %get-tuple-element.32), channel_id=1, source_target_pairs={{0,194},{64,0},{128,64},{192,128},{2,192},{66,2},{130,66},{194,130... | collective-permute-start | bytes 3145736 | tf_op jit(solution)/shard_map/ppermute | solution.py:80
  54.8 10.5 %copy-start.3 = (s32[2,2048]{1,0:T(2,128)S(1)}, s32[2,2048]{1,0:T(2,128)}, u32[]{:S(2)}) copy-start(s32[2,2048]{1,0:T(2,128)} %param.12) | copy-start | bytes 49156
  54.8 30.7 %all-to-all-start.1 = ((bf16[16,2,2,64,256]{4,3,2,1,0:T(8,128)(2,1)}), bf16[16,2,2,64,256]{4,3,2,1,0:T(8,128)(2,1)}, u32[]{:S(2)}, u32[]{:S(2)}) async-start(bf16[16,2,2,64,256]{4,3,2,1,0:T(8,128)(2,1)} %pad_maximum_fusion), calls=%async_computation.1 | async-start | bytes 4194304 | tf_op jit(solution)/shard_map/all_to_all | solution.py:88
  61.6 32.9 %collective-permute-start.3 = (bf16[8,2,64,256]{3,2,1,0:T(8,128)(2,1)S(1)}, bf16[8,2,64,256]{3,2,1,0:T(8,128)(2,1)S(1)}, u32[]{:S(2)}, u32[]{:S(2)}) collective-permute-start(bf16[8,2,64,256]{3,2,1,0:T(8,128)(2,1)S(1)} %get-tuple-element.35), channel_id=1, source_target_pairs={{0,128},{64,192},{128,2},{192,66},{2,130},{66,194},{130,0},{194,64... | collective-permute-start | bytes 1572872 | tf_op jit(solution)/shard_map/ppermute | solution.py:80
  63.6 30.9 %collective-permute-start.4 = (bf16[8,2,64,256]{3,2,1,0:T(8,128)(2,1)S(1)}, bf16[8,2,64,256]{3,2,1,0:T(8,128)(2,1)S(1)}, u32[]{:S(2)}, u32[]{:S(2)}) collective-permute-start(bf16[8,2,64,256]{3,2,1,0:T(8,128)(2,1)S(1)} %get-tuple-element.36), channel_id=1, source_target_pairs={{0,130},{64,194},{128,0},{192,64},{2,128},{66,192},{130,2},{194,66... | collective-permute-start | bytes 1572872 | tf_op jit(solution)/shard_map/ppermute | solution.py:80
  94.5 3.0 %copy-start.4 = (s32[2,8]{1,0:T(2,128)S(1)}, s32[2,8]{1,0:T(2,128)}, u32[]{:S(2)}) copy-start(s32[2,8]{1,0:T(2,128)} %param.13) | copy-start | bytes 196
  97.1 12.1 %collective-permute-start.5 = (bf16[2,512,256]{2,1,0:T(8,128)(2,1)S(1)}, bf16[2,512,256]{2,1,0:T(8,128)(2,1)S(1)}, u32[]{:S(2)}, u32[]{:S(2)}) collective-permute-start(bf16[2,512,256]{2,1,0:T(8,128)(2,1)S(1)} %get-tuple-element.42.kvt_ref), channel_id=1, source_target_pairs={{0,4},{4,8},{8,12},{12,16},{16,20},{20,24},{24,28},{28,32},{32,36}... | collective-permute-start | bytes 1572872 | tf_op jit(solution)/shard_map/ppermute | solution.py:562
  117.5 19.2 %all-to-all-start.2 = ((bf16[16,2,2,72,128]{4,3,2,1,0:T(8,128)(2,1)}), bf16[16,2,2,72,128]{4,3,2,1,0:T(8,128)(2,1)}, u32[]{:S(2)}, u32[]{:S(2)}) async-start(bf16[16,2,2,72,128]{4,3,2,1,0:T(8,128)(2,1)} %back_rows.2), calls=%async_computation.2 | async-start | bytes 2359296 | tf_op jit(solution)/shard_map/all_to_all | solution.py:88
  131.7 13.5 %copy-start.1 = (bf16[16,2,72,128]{3,2,1,0:T(8,128)(2,1)S(1)}, bf16[16,2,72,128]{3,2,1,0:T(8,128)(2,1)}, u32[]{:S(2)}) copy-start(bf16[16,2,72,128]{3,2,1,0:T(8,128)(2,1)} %get-tuple-element.45) | copy-start | bytes 1769476
  131.7 10.4 %collective-permute-start.6 = (bf16[8,2,72,128]{3,2,1,0:T(8,128)(2,1)}, bf16[8,2,72,128]{3,2,1,0:T(8,128)(2,1)S(1)}, u32[]{:S(2)}, u32[]{:S(2)}) collective-permute-start(bf16[8,2,72,128]{3,2,1,0:T(8,128)(2,1)} %get-tuple-element.47), channel_id=1, source_target_pairs={{0,130},{64,194},{128,0},{192,64},{2,128},{66,192},{130,2},{194,66... | collective-permute-start | bytes 884744 | tf_op jit(solution)/shard_map/ppermute | solution.py:80
  135.3 9.8 %collective-permute-start.7 = (bf16[8,2,72,128]{3,2,1,0:T(8,128)(2,1)}, bf16[8,2,72,128]{3,2,1,0:T(8,128)(2,1)S(1)}, u32[]{:S(2)}, u32[]{:S(2)}) collective-permute-start(bf16[8,2,72,128]{3,2,1,0:T(8,128)(2,1)} %get-tuple-element.48), channel_id=1, source_target_pairs={{0,128},{64,192},{128,2},{192,66},{2,130},{66,194},{130,0},{194,64... | collective-permute-start | bytes 884744 | tf_op jit(solution)/shard_map/ppermute | solution.py:80
  146.3 23.9 %all-to-all-start.3 = ((bf16[16,2,2,72,128]{4,3,2,1,0:T(8,128)(2,1)}), bf16[16,2,2,72,128]{4,3,2,1,0:T(8,128)(2,1)S(1)}, u32[]{:S(2)}, u32[]{:S(2)}) async-start(bf16[16,2,2,72,128]{4,3,2,1,0:T(8,128)(2,1)} %pad_maximum_fusion.1), calls=%async_computation.3 | async-start | bytes 2359296 | tf_op jit(solution)/shard_map/all_to_all | solution.py:88
  153.0 15.8 %collective-permute-start.8 = (bf16[16,2,72,128]{3,2,1,0:T(8,128)(2,1)}, bf16[16,2,72,128]{3,2,1,0:T(8,128)(2,1)S(1)}, u32[]{:S(2)}, u32[]{:S(2)}) collective-permute-start(bf16[16,2,72,128]{3,2,1,0:T(8,128)(2,1)} %get-tuple-element.51), channel_id=1, source_target_pairs={{0,194},{64,0},{128,64},{192,128},{2,192},{66,2},{130,66},{194,130... | collective-permute-start | bytes 1769480 | tf_op jit(solution)/shard_map/ppermute | solution.py:80
  159.2 11.0 %collective-permute-start.9 = (bf16[16,2,72,128]{3,2,1,0:T(8,128)(2,1)S(1)}, bf16[16,2,72,128]{3,2,1,0:T(8,128)(2,1)S(1)}, u32[]{:S(2)}, u32[]{:S(2)}) collective-permute-start(bf16[16,2,72,128]{3,2,1,0:T(8,128)(2,1)S(1)} %get-tuple-element.52), channel_id=1, source_target_pairs={{0,64},{64,128},{128,192},{192,2},{2,66},{66,130},{130,194},{194,0... | collective-permute-start | bytes 1769480 | tf_op jit(solution)/shard_map/ppermute | solution.py:80
  159.5 51.7 %copy-start = (bf16[128,1024]{1,0:T(8,128)(2,1)S(1)}, bf16[128,1024]{1,0:T(8,128)(2,1)}, u32[]{:S(2)}) copy-start(bf16[128,1024]{1,0:T(8,128)(2,1)} %w_ref.1) | copy-start | bytes 786436

commit v10 on v9

--- a/solution.py
+++ b/solution.py
@@ -143,37 +143,27 @@
     out_ref[0] = pick_rows(idx_ref, (near_ref,), 0).astype(BF)
 
 
-def odd_kernel(idx_ref, early_ref, odd_ref, out_ref):
-    n = odd_ref.shape[0] * odd_ref.shape[1] * odd_ref.shape[3]
-    out_ref[0] = (early_ref[0].astype(F32) + pick_rows(idx_ref, (odd_ref,), n)).astype(BF)
-
-
-def early_rows(idx, rows, early=None):
+def near_rows(idx, rows):
     rounds, count = idx.shape
     step = count // 2
     peers, _, _, width, lanes = rows.shape
-    wide = pl.BlockSpec((1, step, 256), lambda r, b: (r, b, 0))
-    groups = 1 if early is None else 2
-    specs = [pl.BlockSpec((1, 1, 1, step), lambda r, b: (r, b, 0, 0))]
-    args = [idx.reshape(rounds, 2, 1, step)]
-    if early is not None:
-        specs.append(wide)
-        args.append(in_hbm(early))
-    specs.append(pl.BlockSpec((peers, groups, 1, width, lanes), lambda r, b: (0, 0, r, 0, 0)))
-    return pl.pallas_call(
-        near_kernel if early is None else odd_kernel,
+    return pl.pallas_call(
+        near_kernel,
         grid=(rounds, 2),
-        in_specs=specs,
-        out_specs=wide,
+        in_specs=[
+            pl.BlockSpec((1, 1, 1, step), lambda r, b: (r, b, 0, 0)),
+            pl.BlockSpec((peers, 1, 1, width, lanes), lambda r, b: (0, 0, r, 0, 0)),
+        ],
+        out_specs=pl.BlockSpec((1, step, 256), lambda r, b: (r, b, 0)),
         out_shape=pltpu.HBM((rounds, count, 256), BF),
         compiler_params=params(2),
-        name="early_rows",
-    )(*args, in_hbm(rows))
-
-
-def sort_kernel(idx_ref, early_ref, low_ref, high_ref, q_ref, kv_ref):
+        name="near_rows",
+    )(idx.reshape(rounds, 2, 1, step), in_hbm(rows))
+
+
+def sort_kernel(idx_ref, early_ref, low_ref, high_ref, odd_ref, q_ref, kv_ref):
     n = 2 * low_ref.shape[0] * low_ref.shape[2]
-    got = early_ref[0].astype(F32) + pick_rows(idx_ref, (low_ref, high_ref), n)
+    got = early_ref[0].astype(F32) + pick_rows(idx_ref, (low_ref, high_ref, odd_ref), n)
     qk = got[:, :128]
     keys = qk * lax.rsqrt(jnp.sum(qk * qk, axis=-1, keepdims=True) + 1e-06)
     q_ref[0] = qk.astype(BF)
@@ -181,7 +171,7 @@
     kv_ref[0, :, 128:] = got[:, 128:].astype(BF)
 
 
-def sort_rows(idx, early, low, high, first, step):
+def sort_rows(idx, early, low, high, odd, first, step):
     rounds, count = idx.shape
     blocks = count // step
     peers, _, width, lanes = low.shape
@@ -194,6 +184,7 @@
             pl.BlockSpec((1, step, 256), lambda r, b: (r, first // step + b, 0)),
             half,
             half,
+            pl.BlockSpec((2 * peers, 2, 1, width, lanes), lambda r, b: (0, 0, r, 0, 0)),
         ],
         out_specs=[
             pl.BlockSpec((1, step, 128), lambda r, b: (r, b, 0)),
@@ -205,7 +196,7 @@
         ],
         compiler_params=params(2),
         name="sort_rows",
-    )(idx.reshape(rounds, blocks, 1, step), in_hbm(early), low, high)
+    )(idx.reshape(rounds, blocks, 1, step), in_hbm(early), low, high, in_hbm(odd))
 
 
 def terms_to_lines(terms, groups):
@@ -555,12 +546,12 @@
     low, high, up, down = together((half[:8, 1], half[8:, 1], up, down))
     low, high = ring(low, 2), ring(high, -2)
     odd = plane(join(up, down))
-    early = early_rows(spots, odd, early_rows(spots, half))
-    early, low, high = together((early, low, high))
-
-    q_tail, kv_tail = sort_rows(spots[:, tail:], early, low, high, tail, 2 * BLOCK)
+    early = near_rows(spots, half)
+    early, low, high, odd = together((early, low, high, odd))
+
+    q_tail, kv_tail = sort_rows(spots[:, tail:], early, low, high, odd, tail, 2 * BLOCK)
     halo = lax.ppermute(kv_tail, SEQ, next_device)
-    q_head, kv_head = sort_rows(spots[:, :tail], early, low, high, 0, 3 * BLOCK)
+    q_head, kv_head = sort_rows(spots[:, :tail], early, low, high, odd, 0, 3 * BLOCK)
     inner = attend_inner(dist, q_head, q_tail, kv_head, kv_tail)
     edge = attend_edge(dist, q_head, kv_head, halo)
 

time: 215 us -> 212 us (0.986)
  Pallas kernels: 77.9 us -> 73.9 us
  starting transfers between devices: 49.7 us -> 46.2 us
  blocking collectives: 26.3 us -> 29.1 us
    ppermute x8, waiting for transfers between devices: 20.6 us -> 35.6 us  [ring(): return lax.ppermute(value, ('zl', 'zh'), route)]
    all_to_all x4, waiting for transfers between devices: 32.1 us -> 18.4 us  [plane(): return lax.all_to_all(joint, PLANE, 0, 0, tiled=True)]
    pallas_call x2 -> x1, Pallas kernels: 15.6 us -> 6.65 us  [near_rows(): pl.pallas_call(near_kernel, grid=(rounds, 2), in_specs=[pl.BlockSpec((1,...]
    pallas_call x2, Pallas kernels: 7.61 us -> 12.7 us  [sort_rows(): pl.pallas_call(sort_kernel, grid=(rounds, blocks), in_specs=[pl.BlockSpec...]
    ppermute x8, starting transfers between devices: 14.9 us -> 12 us  [ring(): return lax.ppermute(value, ('zl', 'zh'), route)]
    all_to_all x1, blocking collectives: 26.3 us -> 29.1 us  [body(): merged = lax.all_to_all(state, ROUND, 0, 0, tiled=True)]
  transfers between devices with their start and end apart: 14 -> 14, of which waited for: 9 -> 8; matrix products, arithmetic and copies ran while one was open for 2% -> 2% of each run, Pallas kernels for 20% -> 18%
where the time goes in v10:
time: 212 us; the launch traced here: 210 us
  Pallas kernels  73.9 us (35%)
  waiting for transfers between devices  54 us (25%)
  starting transfers between devices  46.2 us (22%)
  blocking collectives  29.1 us (14%)
  local copies, waits for them, and re-layouts  3.91 us (2%)
  other arithmetic  3.05 us (1%)
    ppermute x8, waiting for transfers between devices, ring(): return lax.ppermute(value, ('zl', 'zh'), route)  35.6 us
    all_to_all x1, blocking collectives, body(): merged = lax.all_to_all(state, ROUND, 0, 0, tiled=True)  29.1 us
    all_to_all x4, starting transfers between devices, plane(): return lax.all_to_all(joint, PLANE, 0, 0, tiled=True)  26.8 us
    all_to_all x4, waiting for transfers between devices, plane(): return lax.all_to_all(joint, PLANE, 0, 0, tiled=True)  18.4 us
    pallas_call x1, Pallas kernels, home_rows(): pl.pallas_call(functools.partial(home_kernel, width), grid_spec=pltpu.Pre...  14.7 us
    pallas_call x2, Pallas kernels, sort_rows(): pl.pallas_call(sort_kernel, grid=(rounds, blocks), in_specs=[pl.BlockSpec...  12.7 us
    pallas_call x2, Pallas kernels, scatter_rows(): pl.pallas_call(scatter_kernel, grid=(rounds, groups), in_specs=[pl.BlockS...  12.2 us
    ppermute x8, starting transfers between devices, ring(): return lax.ppermute(value, ('zl', 'zh'), route)  12 us
  transfers between devices with their start and end apart: 14, of which 8 were waited for; matrix products, arithmetic and copies ran while one was open for 2% of the time, Pallas kernels for 18%

profile of v10, /device:TPU:35, one launch (start us, length us, event | category | flops | bytes accessed | tf_op | source)
XLA Modules:
  0.0 210.4 jit_solution(5446996750841348826)
XLA Ops:
  0.0 6.0 %collective-permute-start = (s32[2,2048]{1,0:T(2,128)}, s32[2,2048]{1,0:T(2,128)S(1)}, u32[]{:S(2)}, u32[]{:S(2)}) collective-permute-start(s32[2,2048]{1,0:T(2,128)} %param.11), channel_id=1, source_target_pairs={{0,2},{2,0},{1,3},{3,1},{4,6},{6,4},{5,7},{7,5},{8,10},{10,8},{9,1... | collective-permute-start | bytes 49160 | tf_op jit(solution)/shard_map/ppermute | solution.py:533
  6.1 4.1 %project.1.rows_ref = bf16[2048,256]{1,0:T(8,128)(2,1)S(1)} custom-call(bf16[2048,1024]{1,0:T(8,128)(2,1)} %right_ref.1, bf16[2048,1024]{1,0:T(8,128)(2,1)} %right_ref.1, bf16[1024,128]{1,0:T(8,128)(2,1)} %wqk_ref.1, bf16[1024,128]{1,0:T(8,128)(2,1)} %wv_ref.1), custom_call_target="tpu_custom_call" | custom-call | tf_op jit(solution)/shard_map/project/pallas_call | solution.py:58
  10.3 5.9 %scatter_rows.2 = bf16[16,2,2,64,256]{4,3,2,1,0:T(8,128)(2,1)} custom-call(s32[2,2,2048]{2,1,0:T(2,128)S(1)} %get-tuple-element.64.idx_ref, bf16[2048,256]{1,0:T(8,128)(2,1)S(1)} %project.1.rows_ref), custom_call_target="tpu_custom_call" | custom-call | tf_op jit(solution)/shard_map/scatter_rows/pallas_call | solution.py:119
  16.2 6.9 %all-to-all-start = ((bf16[16,2,2,64,256]{4,3,2,1,0:T(8,128)(2,1)}), bf16[16,2,2,64,256]{4,3,2,1,0:T(8,128)(2,1)}, u32[]{:S(2)}, u32[]{:S(2)}) async-start(bf16[16,2,2,64,256]{4,3,2,1,0:T(8,128)(2,1)} %scatter_rows.2), calls=%async_computation | async-start | bytes 4194304 | tf_op jit(solution)/shard_map/all_to_all | solution.py:88
  23.2 6.3 %scatter_rows.3 = (bf16[16,2,64,256]{3,2,1,0:T(8,128)(2,1)}, bf16[16,2,64,256]{3,2,1,0:T(8,128)(2,1)}) custom-call(s32[2,2,2048]{2,1,0:T(2,128)S(1)} %get-tuple-element.63.idx_ref, bf16[2048,256]{1,0:T(8,128)(2,1)S(1)} %project.1.rows_ref), custom_call_target="tpu_custom_call" | custom-call | tf_op jit(solution)/shard_map/scatter_rows/pallas_call | solution.py:119
  30.9 17.2 %all-to-all-done.near_ref = bf16[16,2,2,64,256]{4,3,2,1,0:T(8,128)(2,1)} async-done(((bf16[16,2,2,64,256]{4,3,2,1,0:T(8,128)(2,1)}), bf16[16,2,2,64,256]{4,3,2,1,0:T(8,128)(2,1)}, u32[]{:S(2)}, u32[]{:S(2)}) %all-to-all-start) | async-done | bytes 2097184 | tf_op jit(solution)/shard_map/all_to_all | solution.py:88
  49.4 3.4 %collective-permute-done.1 = bf16[16,2,64,256]{3,2,1,0:T(8,128)(2,1)S(1)} collective-permute-done((bf16[16,2,64,256]{3,2,1,0:T(8,128)(2,1)}, bf16[16,2,64,256]{3,2,1,0:T(8,128)(2,1)S(1)}, u32[]{:S(2)}, u32[]{:S(2)}) %collective-permute-start.1) | collective-permute-done | bytes 1048608 | tf_op jit(solution)/shard_map/ppermute | solution.py:80
  54.8 6.8 %all-to-all-start.1 = ((bf16[16,2,2,64,256]{4,3,2,1,0:T(8,128)(2,1)}), bf16[16,2,2,64,256]{4,3,2,1,0:T(8,128)(2,1)}, u32[]{:S(2)}, u32[]{:S(2)}) async-start(bf16[16,2,2,64,256]{4,3,2,1,0:T(8,128)(2,1)} %pad_maximum_fusion), calls=%async_computation.1 | async-start | bytes 4194304 | tf_op jit(solution)/shard_map/all_to_all | solution.py:88
  65.4 6.6 %near_rows.1.early_ref = bf16[2,2048,256]{2,1,0:T(8,128)(2,1)} custom-call(s32[2,2,1,1024]{3,2,1,0:T(1,128)S(1)} %reshape.38.idx_ref, bf16[16,2,2,64,256]{4,3,2,1,0:T(8,128)(2,1)} %all-to-all-done.near_ref), custom_call_target="tpu_custom_call" | custom-call | tf_op jit(solution)/shard_map/near_rows/pallas_call | solution.py:150
  72.1 14.2 %collective-permute-done.3.low_ref = bf16[8,2,64,256]{3,2,1,0:T(8,128)(2,1)S(1)} collective-permute-done((bf16[8,2,64,256]{3,2,1,0:T(8,128)(2,1)S(1)}, bf16[8,2,64,256]{3,2,1,0:T(8,128)(2,1)S(1)}, u32[]{:S(2)}, u32[]{:S(2)}) %collective-permute-start.3) | collective-permute-done | bytes 524320 | tf_op jit(solution)/shard_map/ppermute | solution.py:80
  86.3 4.0 %sort_rows.3 = (bf16[2,512,128]{2,1,0:T(8,128)(2,1)S(1)}, bf16[2,512,256]{2,1,0:T(8,128)(2,1)S(1)}) custom-call(s32[2,1,1,512]{3,2,1,0:T(1,128)S(1)} %copy.28.idx_ref, bf16[2,2048,256]{2,1,0:T(8,128)(2,1)} %near_rows.1.early_ref, bf16[8,2,64,256]{3,2,1,0:T(8,128)(2,1)S(1)} %collective-permute-done.3.low_ref, ...), custom_call_target="tpu_custom_call" | custom-call | tf_op jit(solution)/shard_map/sort_rows/pallas_call | solution.py:179
  91.8 8.7 %sort_rows.2 = (bf16[2,1536,128]{2,1,0:T(8,128)(2,1)S(1)}, bf16[2,1536,256]{2,1,0:T(8,128)(2,1)S(1)}) custom-call(s32[2,2,1,768]{3,2,1,0:T(1,128)S(1)} %reshape.37.idx_ref, bf16[2,2048,256]{2,1,0:T(8,128)(2,1)} %near_rows.1.early_ref, bf16[8,2,64,256]{3,2,1,0:T(8,128)(2,1)S(1)} %collective-permute-done.3.low_ref, ...), custom_call_target="tpu_custom_call" | custom-call | tf_op jit(solution)/shard_map/sort_rows/pallas_call | solution.py:179
  100.5 6.6 %attend_inner.1.inner_ref = bf16[2,1536,256]{2,1,0:T(8,128)(2,1)S(1)} custom-call(s32[2,8]{1,0:T(2,128)S(1)} %and_select_fusion.dist_ref, bf16[2,1536,128]{2,1,0:T(8,128)(2,1)S(1)} %get-tuple-element.42.q_ref.qh_ref, bf16[2,512,128]{2,1,0:T(8,128)(2,1)S(1)} %get-tuple-element.45.qt_ref, bf16[2,1536,256]{2,1,0:T(8,128)(2,1)S(1)} %get-tuple-element.43.kv_ref.kvh_ref, ...), custom_call_target="tpu_custom_call" | custom-call | tf_op jit(solution)/shard_map/attend_inner/pallas_call | solution.py:290
  109.6 5.8 %back_rows.2 = bf16[16,2,2,72,128]{4,3,2,1,0:T(8,128)(2,1)} custom-call(s32[2,1,2048]{2,1,0:T(1,128)S(1)} %broadcast_in_dim.69.idx_ref, bf16[2,512,256]{2,1,0:T(8,128)(2,1)S(1)} %attend_edge.1.edge_ref, bf16[2,1536,256]{2,1,0:T(8,128)(2,1)S(1)} %attend_inner.1.inner_ref), custom_call_target="tpu_custom_call" | custom-call | tf_op jit(solution)/shard_map/back_rows/pallas_call | solution.py:376
  115.5 6.4 %all-to-all-start.2 = ((bf16[16,2,2,72,128]{4,3,2,1,0:T(8,128)(2,1)}), bf16[16,2,2,72,128]{4,3,2,1,0:T(8,128)(2,1)}, u32[]{:S(2)}, u32[]{:S(2)}) async-start(bf16[16,2,2,72,128]{4,3,2,1,0:T(8,128)(2,1)} %back_rows.2), calls=%async_computation.2 | async-start | bytes 2359296 | tf_op jit(solution)/shard_map/all_to_all | solution.py:88
  121.9 6.1 %back_rows.3 = (bf16[16,2,72,128]{3,2,1,0:T(8,128)(2,1)}, bf16[8,2,72,128]{3,2,1,0:T(8,128)(2,1)}, bf16[8,2,72,128]{3,2,1,0:T(8,128)(2,1)}) custom-call(s32[2,1,2048]{2,1,0:T(1,128)S(1)} %broadcast_in_dim.69.idx_ref, bf16[2,512,256]{2,1,0:T(8,128)(2,1)S(1)} %attend_edge.1.edge_ref, bf16[2,1536,256]{2,1,0:T(8,128)(2,1)S(1)} %attend_inner.1.inner_ref), custom_call_target="tpu_custom_call" | custom-call | tf_op jit(solution)/shard_map/back_rows/pallas_call | solution.py:376
  128.0 4.0 %collective-permute-start.6 = (bf16[8,2,72,128]{3,2,1,0:T(8,128)(2,1)}, bf16[8,2,72,128]{3,2,1,0:T(8,128)(2,1)S(1)}, u32[]{:S(2)}, u32[]{:S(2)}) collective-permute-start(bf16[8,2,72,128]{3,2,1,0:T(8,128)(2,1)} %get-tuple-element.49), channel_id=1, source_target_pairs={{0,130},{64,194},{128,0},{192,64},{2,128},{66,192},{130,2},{194,66... | collective-permute-start | bytes 884744 | tf_op jit(solution)/shard_map/ppermute | solution.py:80
  135.3 7.8 %collective-permute-done.6 = bf16[8,2,72,128]{3,2,1,0:T(8,128)(2,1)S(1)} collective-permute-done((bf16[8,2,72,128]{3,2,1,0:T(8,128)(2,1)}, bf16[8,2,72,128]{3,2,1,0:T(8,128)(2,1)S(1)}, u32[]{:S(2)}, u32[]{:S(2)}) %collective-permute-start.6) | collective-permute-done | bytes 294944 | tf_op jit(solution)/shard_map/ppermute | solution.py:80
  144.3 6.7 %all-to-all-start.3 = ((bf16[16,2,2,72,128]{4,3,2,1,0:T(8,128)(2,1)}), bf16[16,2,2,72,128]{4,3,2,1,0:T(8,128)(2,1)S(1)}, u32[]{:S(2)}, u32[]{:S(2)}) async-start(bf16[16,2,2,72,128]{4,3,2,1,0:T(8,128)(2,1)} %pad_maximum_fusion.1), calls=%async_computation.3 | async-start | bytes 2359296 | tf_op jit(solution)/shard_map/all_to_all | solution.py:88
  150.9 2.9 %collective-permute-start.8 = (bf16[16,2,72,128]{3,2,1,0:T(8,128)(2,1)}, bf16[16,2,72,128]{3,2,1,0:T(8,128)(2,1)S(1)}, u32[]{:S(2)}, u32[]{:S(2)}) collective-permute-start(bf16[16,2,72,128]{3,2,1,0:T(8,128)(2,1)} %get-tuple-element.53), channel_id=1, source_target_pairs={{0,194},{64,0},{128,64},{192,128},{2,192},{66,2},{130,66},{194,130... | collective-permute-start | bytes 1769480 | tf_op jit(solution)/shard_map/ppermute | solution.py:80
  154.3 8.1 %collective-permute-done.8.up_ref = bf16[16,2,72,128]{3,2,1,0:T(8,128)(2,1)S(1)} collective-permute-done((bf16[16,2,72,128]{3,2,1,0:T(8,128)(2,1)}, bf16[16,2,72,128]{3,2,1,0:T(8,128)(2,1)S(1)}, u32[]{:S(2)}, u32[]{:S(2)}) %collective-permute-start.8) | collective-permute-done | bytes 589856 | tf_op jit(solution)/shard_map/ppermute | solution.py:80
  164.1 14.7 %home_rows.1 = bf16[4,528,128]{2,1,0:T(8,128)(2,1)S(1)} custom-call(s32[4]{0:T(128)S(1)} %get-tuple-element.57.own_ref, s32[2,8,1024]{2,1,0:T(8,128)S(1)} %select_bitcast_fusion.idx_ref, bf16[16,2,2,72,128]{4,3,2,1,0:T(8,128)(2,1)S(1)} %all-to-all-done.3.even_ref, bf16[16,2,72,128]{3,2,1,0:T(8,128)(2,1)S(1)} %collective-permute-done.8.up_ref, ...), custom_call_target="tpu_custom_call" | custom-call | tf_op jit(solution)/shard_map/home_rows/pallas_call | solution.py:461
  178.8 29.1 %all_to_all.25.m_ref = bf16[4,528,128]{2,1,0:T(8,128)(2,1)S(1)} all-to-all(bf16[4,528,128]{2,1,0:T(8,128)(2,1)S(1)} %home_rows.1), channel_id=1, replica_groups=mesh['zl'=4,'x'=4,'y'=4,'zh'=2,'c'=2] {'zh','c'}, dimensions={0} | all-to-all | bytes 1081344 | tf_op jit(solution)/shard_map/all_to_all | solution.py:567
  207.9 2.5 %finish.1 = bf16[512,1024]{1,0:T(8,128)(2,1)} custom-call(bf16[4,528,128]{2,1,0:T(8,128)(2,1)S(1)} %all_to_all.25.m_ref, bf16[128,1024]{1,0:T(8,128)(2,1)S(1)} %copy-done), custom_call_target="tpu_custom_call" | custom-call | tf_op jit(solution)/shard_map/finish/pallas_call | solution.py:495
  (54 shorter events, 19.3 us)
Async XLA Ops:
  0.0 10.2 %collective-permute-start = (s32[2,2048]{1,0:T(2,128)}, s32[2,2048]{1,0:T(2,128)S(1)}, u32[]{:S(2)}, u32[]{:S(2)}) collective-permute-start(s32[2,2048]{1,0:T(2,128)} %param.11), channel_id=1, source_target_pairs={{0,2},{2,0},{1,3},{3,1},{4,6},{6,4},{5,7},{7,5},{8,10},{10,8},{9,1... | collective-permute-start | bytes 49160 | tf_op jit(solution)/shard_map/ppermute | solution.py:533
  6.0 4.1 %copy-start.2 = (s32[2,2048]{1,0:T(2,128)S(1)}, s32[2,2048]{1,0:T(2,128)}, u32[]{:S(2)}) copy-start(s32[2,2048]{1,0:T(2,128)} %param.11) | copy-start | bytes 49156
  16.2 31.9 %all-to-all-start = ((bf16[16,2,2,64,256]{4,3,2,1,0:T(8,128)(2,1)}), bf16[16,2,2,64,256]{4,3,2,1,0:T(8,128)(2,1)}, u32[]{:S(2)}, u32[]{:S(2)}) async-start(bf16[16,2,2,64,256]{4,3,2,1,0:T(8,128)(2,1)} %scatter_rows.2), calls=%async_computation | async-start | bytes 4194304 | tf_op jit(solution)/shard_map/all_to_all | solution.py:88
  29.4 23.3 %collective-permute-start.1 = (bf16[16,2,64,256]{3,2,1,0:T(8,128)(2,1)}, bf16[16,2,64,256]{3,2,1,0:T(8,128)(2,1)S(1)}, u32[]{:S(2)}, u32[]{:S(2)}) collective-permute-start(bf16[16,2,64,256]{3,2,1,0:T(8,128)(2,1)} %get-tuple-element.32), channel_id=1, source_target_pairs={{0,64},{64,128},{128,192},{192,2},{2,66},{66,130},{130,194},{194,0... | collective-permute-start | bytes 3145736 | tf_op jit(solution)/shard_map/ppermute | solution.py:80
  30.2 23.1 %collective-permute-start.2 = (bf16[16,2,64,256]{3,2,1,0:T(8,128)(2,1)}, bf16[16,2,64,256]{3,2,1,0:T(8,128)(2,1)S(1)}, u32[]{:S(2)}, u32[]{:S(2)}) collective-permute-start(bf16[16,2,64,256]{3,2,1,0:T(8,128)(2,1)} %get-tuple-element.33), channel_id=1, source_target_pairs={{0,194},{64,0},{128,64},{192,128},{2,192},{66,2},{130,66},{194,130... | collective-permute-start | bytes 3145736 | tf_op jit(solution)/shard_map/ppermute | solution.py:80
  54.8 10.5 %copy-start.3 = (s32[2,2048]{1,0:T(2,128)S(1)}, s32[2,2048]{1,0:T(2,128)}, u32[]{:S(2)}) copy-start(s32[2,2048]{1,0:T(2,128)} %param.12) | copy-start | bytes 49156
  54.8 31.5 %all-to-all-start.1 = ((bf16[16,2,2,64,256]{4,3,2,1,0:T(8,128)(2,1)}), bf16[16,2,2,64,256]{4,3,2,1,0:T(8,128)(2,1)}, u32[]{:S(2)}, u32[]{:S(2)}) async-start(bf16[16,2,2,64,256]{4,3,2,1,0:T(8,128)(2,1)} %pad_maximum_fusion), calls=%async_computation.1 | async-start | bytes 4194304 | tf_op jit(solution)/shard_map/all_to_all | solution.py:88
  61.6 24.7 %collective-permute-start.3 = (bf16[8,2,64,256]{3,2,1,0:T(8,128)(2,1)S(1)}, bf16[8,2,64,256]{3,2,1,0:T(8,128)(2,1)S(1)}, u32[]{:S(2)}, u32[]{:S(2)}) collective-permute-start(bf16[8,2,64,256]{3,2,1,0:T(8,128)(2,1)S(1)} %get-tuple-element.34), channel_id=1, source_target_pairs={{0,128},{64,192},{128,2},{192,66},{2,130},{66,194},{130,0},{194,64... | collective-permute-start | bytes 1572872 | tf_op jit(solution)/shard_map/ppermute | solution.py:80
  63.6 22.7 %collective-permute-start.4 = (bf16[8,2,64,256]{3,2,1,0:T(8,128)(2,1)S(1)}, bf16[8,2,64,256]{3,2,1,0:T(8,128)(2,1)S(1)}, u32[]{:S(2)}, u32[]{:S(2)}) collective-permute-start(bf16[8,2,64,256]{3,2,1,0:T(8,128)(2,1)S(1)} %get-tuple-element.35), channel_id=1, source_target_pairs={{0,130},{64,194},{128,0},{192,64},{2,128},{66,192},{130,2},{194,66... | collective-permute-start | bytes 1572872 | tf_op jit(solution)/shard_map/ppermute | solution.py:80
  72.1 19.7 %copy-start.4 = (s32[2,8]{1,0:T(2,128)S(1)}, s32[2,8]{1,0:T(2,128)}, u32[]{:S(2)}) copy-start(s32[2,8]{1,0:T(2,128)} %param.13) | copy-start | bytes 196
  90.3 16.8 %collective-permute-start.5 = (bf16[2,512,256]{2,1,0:T(8,128)(2,1)S(1)}, bf16[2,512,256]{2,1,0:T(8,128)(2,1)S(1)}, u32[]{:S(2)}, u32[]{:S(2)}) collective-permute-start(bf16[2,512,256]{2,1,0:T(8,128)(2,1)S(1)} %get-tuple-element.44.kvt_ref), channel_id=1, source_target_pairs={{0,4},{4,8},{8,12},{12,16},{16,20},{20,24},{24,28},{28,32},{32,36}... | collective-permute-start | bytes 1572872 | tf_op jit(solution)/shard_map/ppermute | solution.py:553
  115.5 17.6 %all-to-all-start.2 = ((bf16[16,2,2,72,128]{4,3,2,1,0:T(8,128)(2,1)}), bf16[16,2,2,72,128]{4,3,2,1,0:T(8,128)(2,1)}, u32[]{:S(2)}, u32[]{:S(2)}) async-start(bf16[16,2,2,72,128]{4,3,2,1,0:T(8,128)(2,1)} %back_rows.2), calls=%async_computation.2 | async-start | bytes 2359296 | tf_op jit(solution)/shard_map/all_to_all | solution.py:88
  128.0 15.2 %copy-start.1 = (bf16[16,2,72,128]{3,2,1,0:T(8,128)(2,1)S(1)}, bf16[16,2,72,128]{3,2,1,0:T(8,128)(2,1)}, u32[]{:S(2)}) copy-start(bf16[16,2,72,128]{3,2,1,0:T(8,128)(2,1)} %get-tuple-element.47) | copy-start | bytes 1769476
  128.0 15.1 %collective-permute-start.6 = (bf16[8,2,72,128]{3,2,1,0:T(8,128)(2,1)}, bf16[8,2,72,128]{3,2,1,0:T(8,128)(2,1)S(1)}, u32[]{:S(2)}, u32[]{:S(2)}) collective-permute-start(bf16[8,2,72,128]{3,2,1,0:T(8,128)(2,1)} %get-tuple-element.49), channel_id=1, source_target_pairs={{0,130},{64,194},{128,0},{192,64},{2,128},{66,192},{130,2},{194,66... | collective-permute-start | bytes 884744 | tf_op jit(solution)/shard_map/ppermute | solution.py:80
  131.9 11.2 %collective-permute-start.7 = (bf16[8,2,72,128]{3,2,1,0:T(8,128)(2,1)}, bf16[8,2,72,128]{3,2,1,0:T(8,128)(2,1)S(1)}, u32[]{:S(2)}, u32[]{:S(2)}) collective-permute-start(bf16[8,2,72,128]{3,2,1,0:T(8,128)(2,1)} %get-tuple-element.50), channel_id=1, source_target_pairs={{0,128},{64,192},{128,2},{192,66},{2,130},{66,194},{130,0},{194,64... | collective-permute-start | bytes 884744 | tf_op jit(solution)/shard_map/ppermute | solution.py:80
  144.3 19.8 %all-to-all-start.3 = ((bf16[16,2,2,72,128]{4,3,2,1,0:T(8,128)(2,1)}), bf16[16,2,2,72,128]{4,3,2,1,0:T(8,128)(2,1)S(1)}, u32[]{:S(2)}, u32[]{:S(2)}) async-start(bf16[16,2,2,72,128]{4,3,2,1,0:T(8,128)(2,1)} %pad_maximum_fusion.1), calls=%async_computation.3 | async-start | bytes 2359296 | tf_op jit(solution)/shard_map/all_to_all | solution.py:88
  150.9 11.4 %collective-permute-start.8 = (bf16[16,2,72,128]{3,2,1,0:T(8,128)(2,1)}, bf16[16,2,72,128]{3,2,1,0:T(8,128)(2,1)S(1)}, u32[]{:S(2)}, u32[]{:S(2)}) collective-permute-start(bf16[16,2,72,128]{3,2,1,0:T(8,128)(2,1)} %get-tuple-element.53), channel_id=1, source_target_pairs={{0,194},{64,0},{128,64},{192,128},{2,192},{66,2},{130,66},{194,130... | collective-permute-start | bytes 1769480 | tf_op jit(solution)/shard_map/ppermute | solution.py:80
  153.8 10.3 %collective-permute-start.9 = (bf16[16,2,72,128]{3,2,1,0:T(8,128)(2,1)S(1)}, bf16[16,2,72,128]{3,2,1,0:T(8,128)(2,1)S(1)}, u32[]{:S(2)}, u32[]{:S(2)}) collective-permute-start(bf16[16,2,72,128]{3,2,1,0:T(8,128)(2,1)S(1)} %get-tuple-element.54), channel_id=1, source_target_pairs={{0,64},{64,128},{128,192},{192,2},{2,66},{66,130},{130,194},{194,0... | collective-permute-start | bytes 1769480 | tf_op jit(solution)/shard_map/ppermute | solution.py:80
  154.2 53.7 %copy-start = (bf16[128,1024]{1,0:T(8,128)(2,1)S(1)}, bf16[128,1024]{1,0:T(8,128)(2,1)}, u32[]{:S(2)}) copy-start(bf16[128,1024]{1,0:T(8,128)(2,1)} %w_ref.1) | copy-start | bytes 786436
